TPU v7x, 32 devices: a whole 2x2x4 slice. The times are simulated.
32 devices in a mesh: gx: 4 (over z), gy: 4 (over x, core), ma: 2 (over y).
Axes of the slice: x: 2, y: 2, z: 4, core: 2. Of those that a mesh axis runs over, the one named last changes fastest.
Arguments:
- right_side: float32 [128, 128, 4, 256], P('gx', 'gy', None, 'ma'), may hold values from -6 to 6
- start_field: float32 [128, 128, 4, 256], P('gx', 'gy', None, 'ma'), may hold values from -1.8 to 1.8
- coefficients: float32 [3, 128, 128, 4], P(None, 'gx', 'gy'), may hold values from -0.8 to 3, as said below
- couplings: float32 [3, 256, 256], replicated, may hold values from -0.25 to 2.25, as said below
Outputs:
- solution_field: float32 [128, 128, 4, 256], P('gx', 'gy', None, 'ma')
- residual: float32 [128, 128, 4, 256], P('gx', 'gy', None, 'ma')
Inputs may be any that keep to these rules, and one draw needn't show every extreme that they name: coefficients[0] lies between 1 and 3, coefficients[1] and coefficients[2] between -0.8 and 0.8. couplings[0] is 2 on its diagonal plus entries of size about 256 ** -0.5; couplings[1] and couplings[2] have entries of size about 256 ** -0.5.
All inputs are finite; a program needn't handle non-finite values.
Results may differ from a plain program's by a relative error of at most 0.00016.
Values sent between devices are 32-bit elements; how exact they have to be, the bound alone decides.
No kernel may reach another device: no remote copies, remote signals or barrier semaphores. Data moves between devices by JAX's collectives and lax.ppermute only.
A program may use at most 128 MiB of HBM per device.

v0:
```python
import jax
import jax.numpy as jnp
from jax import lax
from jax.sharding import PartitionSpec as P

step_size = 0.02


def extended(block, sides, width, periodic):
    for axis, dim in sides:
        count = lax.axis_size(axis)
        forward = [(i, i + 1) for i in range(count - 1)]
        if periodic:
            forward.append((count - 1, 0))
        backward = [(target, source) for source, target in forward]
        low = lax.ppermute(
            lax.slice_in_dim(block, block.shape[dim] - width, None, axis=dim), axis, forward
        )
        high = lax.ppermute(lax.slice_in_dim(block, 0, width, axis=dim), axis, backward)
        block = jnp.concatenate([low, block, high], axis=dim)
    return block


def moved(array, offset_x, offset_y, offset_z):
    size_x, size_y, size_z = (array.shape[0], array.shape[1], array.shape[2])
    return array[
        1 + offset_x : size_x - 1 + offset_x,
        1 + offset_y : size_y - 1 + offset_y,
        1 + offset_z : size_z - 1 + offset_z,
    ]


def stencil(field_pad, coef_pad):
    center = moved(field_pad, 0, 0, 0)
    coef_center = moved(coef_pad, 0, 0, 0)
    total = jnp.zeros(center.shape, jnp.float32)
    for offsets in ((1, 0, 0), (-1, 0, 0), (0, 1, 0), (0, -1, 0), (0, 0, 1), (0, 0, -1)):
        neighbour = moved(field_pad, offsets[0], offsets[1], offsets[2])
        face = 0.5 * (coef_center + moved(coef_pad, offsets[0], offsets[1], offsets[2]))
        total = total + face[..., None] * (center - neighbour)
    return total


def pad_planes(array, axis):
    widths = [(0, 0)] * array.ndim
    widths[axis] = (1, 1)
    return jnp.pad(array, widths)


def apply_operator(field, coef_pads, couplings):
    local_modes = field.shape[3]
    offset = lax.axis_index("ma") * local_modes
    coupling_rows = lax.dynamic_slice_in_dim(couplings, offset, local_modes, 1)
    mixed = jnp.einsum(
        "xyzj,kij->kxyzi",
        lax.all_gather(field, "ma", axis=3, tiled=True),
        coupling_rows,
        precision=lax.Precision.HIGHEST,
        preferred_element_type=jnp.float32,
    )
    mixed_x = extended(mixed, (("gx", 1),), 1, False)
    mixed_y = extended(mixed_x, (("gy", 2),), 1, True)
    mixed_pad = pad_planes(mixed_y, 3)
    total = stencil(mixed_pad[0], coef_pads[0])
    total = total + stencil(mixed_pad[1], coef_pads[1])
    return total + stencil(mixed_pad[2], coef_pads[2])


def shards(right_side, start_field, coefficients, couplings):
    coef_x = extended(coefficients, (("gx", 1),), 1, False)
    coef_y = extended(coef_x, (("gy", 2),), 1, True)
    coef_all = pad_planes(coef_y, 3)
    coef_pads = [coef_all[index] for index in range(3)]
    first = start_field + step_size * (
        right_side - apply_operator(start_field, coef_pads, couplings)
    )
    residual = right_side - apply_operator(first, coef_pads, couplings)
    solution_field = first + step_size * residual
    return (solution_field, residual)


def solution(mesh):
    placed = (P("gx", "gy", None, "ma"), P("gx", "gy", None, "ma"), P(None, "gx", "gy", None), P())
    return jax.shard_map(
        shards,
        mesh=mesh,
        in_specs=placed,
        out_specs=(P("gx", "gy", None, "ma"), P("gx", "gy", None, "ma")),
        check_vma=False,
    )
```

profile of v0, /device:TPU:0, one launch (start us, length us, event | category | flops | bytes accessed | tf_op | source)
XLA Modules:
  0.0 266.1 jit_solution(12603050348678972208)
XLA Ops:
  7.2 3.2 %copy.8 = f32[32,32,4,128]{3,1,2,0:T(8,128)} copy(f32[32,32,4,128]{3,2,1,0:T(4,128)} %param.5) | data formatting | bytes 4194304 | tf_op args[1]
  11.4 4.9 %collective-permute-start = (f32[3,1,32,4]{2,3,1,0:T(4,128)S(1)}, f32[3,1,32,4]{2,3,1,0:T(4,128)S(1)}, u32[]{:S(2)}, u32[]{:S(2)}) collective-permute-start(f32[3,1,32,4]{2,3,1,0:T(4,128)S(1)} %get-tuple-element.26), channel_id=1, source_target_pairs={{0,8},{8,16},{16,24},{1,9},{9,17},{17,25},{2,10},{10,18},{18,26},{... | collective-permute-start | bytes 4616 | tf_op jit(solution)/shard_map/ppermute | solution.py:16
  17.7 4.2 %collective-permute-done.1 = f32[3,1,32,4]{2,3,1,0:T(4,128)S(1)} collective-permute-done((f32[3,1,32,4]{2,3,1,0:T(4,128)S(1)}, f32[3,1,32,4]{2,3,1,0:T(4,128)S(1)}, u32[]{:S(2)}, u32[]{:S(2)}) %collective-permute-start.1) | collective-permute-done | bytes 1568 | tf_op jit(solution)/shard_map/ppermute | solution.py:19
  23.8 3.9 %collective-permute-done.2 = f32[3,34,1,4]{2,3,1,0:T(4,128)S(1)} collective-permute-done((f32[3,34,1,4]{2,3,1,0:T(4,128)S(1)}, f32[3,34,1,4]{2,3,1,0:T(4,128)S(1)}, u32[]{:S(2)}, u32[]{:S(2)}) %collective-permute-start.2) | collective-permute-done | bytes 1664 | tf_op jit(solution)/shard_map/ppermute | solution.py:16
  29.2 40.9 %all-gather.3.cloned.1.call-done = f32[32,32,4,256]{3,1,2,0:T(8,128)} async-done(((f32[32,32,4,128]{3,1,2,0:T(8,128)}), f32[32,32,4,256]{3,1,2,0:T(8,128)}) %all-gather.3.cloned.1.call-update) | async-done | bytes 4194320 | tf_op jit(solution)/shard_map/all_gather | solution.py:56
  70.1 9.9 %fusion.5 = f32[3,32,32,4,128]{4,2,3,1,0:T(8,128)S(1)} fusion(f32[32,32,4,256]{3,1,2,0:T(8,128)} %all-gather.3.cloned.1.call-done, f32[3,256,256]{2,1,0:T(8,128)S(1)} %copy-done, s32[]{:T(128)S(6)} %select_n.4), kind=kOutput, calls=%fused_computation.21 | convolution fusion | flops 4831838208 | bytes 10878980 | tf_op jit(solution)/shard_map/xyzj,kij->kxyzi/dot_general | solution.py:54
  80.0 3.4 %collective-permute-start.4 = (f32[3,1,32,4,128]{4,2,3,1,0:T(8,128)S(1)}, f32[3,1,32,4,128]{4,2,3,1,0:T(8,128)S(1)}, u32[]{:S(2)}, u32[]{:S(2)}) collective-permute-start(f32[3,1,32,4,128]{4,2,3,1,0:T(8,128)S(1)} %get-tuple-element.18), channel_id=1, source_target_pairs={{0,8},{8,16},{16,24},{1,9},{9,17},{17,25},{2,10},{10,18},{18,26},{... | collective-permute-start | bytes 589832 | tf_op jit(solution)/shard_map/ppermute | solution.py:16
  85.0 2.6 collective-permute-done.4
  87.6 4.1 %collective-permute-done.5 = f32[3,1,32,4,128]{4,2,3,1,0:T(8,128)S(1)} collective-permute-done((f32[3,1,32,4,128]{4,2,3,1,0:T(8,128)S(1)}, f32[3,1,32,4,128]{4,2,3,1,0:T(8,128)S(1)}, u32[]{:S(2)}, u32[]{:S(2)}) %collective-permute-start.5) | collective-permute-done | bytes 196640 | tf_op jit(solution)/shard_map/ppermute | solution.py:19
  94.1 3.6 %collective-permute-done.6 = f32[3,34,1,4,128]{4,2,3,1,0:T(1,128)S(1)} collective-permute-done((f32[3,34,1,4,128]{4,2,3,1,0:T(1,128)S(1)}, f32[3,34,1,4,128]{4,2,3,1,0:T(1,128)S(1)}, u32[]{:S(2)}, u32[]{:S(2)}) %collective-permute-start.6) | collective-permute-done | bytes 208928 | tf_op jit(solution)/shard_map/ppermute | solution.py:16
  98.5 9.3 %select_maximum_fusion.4 = f32[3,34,34,6,128]{4,2,3,1,0:T(8,128)} fusion(f32[3,34,1,4,128]{4,2,3,1,0:T(1,128)S(1)} %collective-permute-done.7, f32[3,34,1,4,128]{4,2,3,1,0:T(1,128)S(1)} %collective-permute-done.6, f32[3,1,32,4,128]{4,2,3,1,0:T(8,128)S(1)} %collective-permute-done.5, f32[3,32,32,4,128]{4,2,3,1,0:T(8,128)S(1)} %fusion.5, ...), kind=kLoop, calls=%fused_computation.6 | loop fusion | flops 31961088 | bytes 17756160 | tf_op jit(solution)/shard_map/concatenate | solution.py:20
  107.8 8.8 %slice_bitcast_fusion.5 = (f32[34,34,6,128]{3,1,2,0:T(8,128)S(1)}, f32[34,34,6,128]{3,1,2,0:T(8,128)}, f32[34,34,6,128]{3,1,2,0:T(8,128)}) fusion(f32[3,34,34,6,128]{4,2,3,1,0:T(8,128)} %select_maximum_fusion.4), kind=kLoop, calls=%fused_computation.20 | loop fusion | bytes 21307392 | tf_op jit(solution)/shard_map/squeeze | solution.py:64
  116.6 17.2 %fusion.52 = f32[32,32,4,128]{3,1,2,0:T(8,128)} fusion(f32[34,34,6,128]{3,1,2,0:T(8,128)} %get-tuple-element.11, f32[34,34,6,128]{3,1,2,0:T(8,128)} %get-tuple-element.10, f32[34,34,6,128]{3,1,2,0:T(8,128)S(1)} %get-tuple-element.9, f32[32,32,4,128]{3,2,1,0:T(4,128)} %param.4, f32[32,32,4]{1,2,0:T(4,128)S(1)} %get-tuple-element.44, ...), kind=kLoop, calls=%fused_computation.83 | loop fusion | flops 29360128 | bytes 50626560 | tf_op jit(solution)/shard_map/add | solution.py:74
  133.8 56.4 %all-gather.5.cloned.1.call-done = f32[32,32,4,256]{3,1,2,0:T(8,128)} async-done(((f32[32,32,4,128]{3,1,2,0:T(8,128)}), f32[32,32,4,256]{3,1,2,0:T(8,128)}) %all-gather.5.cloned.1.call-update) | async-done | bytes 4194320 | tf_op jit(solution)/shard_map/all_gather | solution.py:56
  190.2 9.9 %fusion.8 = f32[3,32,32,4,128]{4,2,3,1,0:T(8,128)S(1)} fusion(f32[32,32,4,256]{3,1,2,0:T(8,128)} %all-gather.5.cloned.1.call-done, f32[3,256,256]{2,1,0:T(8,128)S(1)} %copy-done, s32[]{:T(128)S(6)} %select_n.4), kind=kOutput, calls=%fused_computation.22 | convolution fusion | flops 4831838208 | bytes 10878980 | tf_op jit(solution)/shard_map/xyzj,kij->kxyzi/dot_general | solution.py:54
  200.2 3.4 %collective-permute-start.8 = (f32[3,1,32,4,128]{4,2,3,1,0:T(8,128)S(1)}, f32[3,1,32,4,128]{4,2,3,1,0:T(8,128)S(1)}, u32[]{:S(2)}, u32[]{:S(2)}) collective-permute-start(f32[3,1,32,4,128]{4,2,3,1,0:T(8,128)S(1)} %get-tuple-element.16), channel_id=1, source_target_pairs={{0,8},{8,16},{16,24},{1,9},{9,17},{17,25},{2,10},{10,18},{18,26},{... | collective-permute-start | bytes 589832 | tf_op jit(solution)/shard_map/ppermute | solution.py:16
  204.9 2.8 %collective-permute-done.8 = f32[3,1,32,4,128]{4,2,3,1,0:T(8,128)S(1)} collective-permute-done((f32[3,1,32,4,128]{4,2,3,1,0:T(8,128)S(1)}, f32[3,1,32,4,128]{4,2,3,1,0:T(8,128)S(1)}, u32[]{:S(2)}, u32[]{:S(2)}) %collective-permute-start.8) | collective-permute-done | bytes 196640 | tf_op jit(solution)/shard_map/ppermute | solution.py:16
  207.7 4.1 %collective-permute-done.9 = f32[3,1,32,4,128]{4,2,3,1,0:T(8,128)S(1)} collective-permute-done((f32[3,1,32,4,128]{4,2,3,1,0:T(8,128)S(1)}, f32[3,1,32,4,128]{4,2,3,1,0:T(8,128)S(1)}, u32[]{:S(2)}, u32[]{:S(2)}) %collective-permute-start.9) | collective-permute-done | bytes 196640 | tf_op jit(solution)/shard_map/ppermute | solution.py:19
  213.9 3.9 %collective-permute-done.10 = f32[3,34,1,4,128]{4,2,3,1,0:T(1,128)S(1)} collective-permute-done((f32[3,34,1,4,128]{4,2,3,1,0:T(1,128)S(1)}, f32[3,34,1,4,128]{4,2,3,1,0:T(1,128)S(1)}, u32[]{:S(2)}, u32[]{:S(2)}) %collective-permute-start.10) | collective-permute-done | bytes 208928 | tf_op jit(solution)/shard_map/ppermute | solution.py:16
  218.7 9.3 %select_maximum_fusion = f32[3,34,34,6,128]{4,2,3,1,0:T(8,128)} fusion(f32[3,34,1,4,128]{4,2,3,1,0:T(1,128)S(1)} %collective-permute-done.11, f32[3,34,1,4,128]{4,2,3,1,0:T(1,128)S(1)} %collective-permute-done.10, f32[3,1,32,4,128]{4,2,3,1,0:T(8,128)S(1)} %collective-permute-done.9, f32[3,32,32,4,128]{4,2,3,1,0:T(8,128)S(1)} %fusion.8, ...), kind=kLoop, calls=%fused_computation.2 | loop fusion | flops 31961088 | bytes 17756160 | tf_op jit(solution)/shard_map/concatenate | solution.py:20
  227.9 8.8 %slice_bitcast_fusion.2 = (f32[34,34,6,128]{3,1,2,0:T(8,128)S(1)}, f32[34,34,6,128]{3,1,2,0:T(8,128)}, f32[34,34,6,128]{3,1,2,0:T(8,128)}) fusion(f32[3,34,34,6,128]{4,2,3,1,0:T(8,128)} %select_maximum_fusion), kind=kLoop, calls=%fused_computation.17 | loop fusion | bytes 21307392 | tf_op jit(solution)/shard_map/squeeze | solution.py:64
  236.8 16.3 %multiply_add_fusion = (f32[32,32,4,128]{3,1,2,0:T(8,128)S(1)}, f32[32,32,4,128]{3,1,2,0:T(8,128)S(1)}) fusion(f32[32,32,4,128]{3,1,2,0:T(8,128)} %fusion.52, f32[34,34,6,128]{3,1,2,0:T(8,128)} %get-tuple-element.8, f32[32,32,4]{1,2,0:T(4,128)S(1)} %get-tuple-element.44, f32[32,32,4]{1,2,0:T(4,128)S(1)} %get-tuple-element.40, ...), kind=kLoop, calls=%fused_computation.133 | loop fusion | flops 29360128 | bytes 52723712 | tf_op jit(solution)/shard_map/add | solution.py:78
  253.0 3.1 %copy.10 = f32[32,32,4,128]{3,2,1,0:T(4,128)} copy(f32[32,32,4,128]{3,1,2,0:T(8,128)S(1)} %get-tuple-element.4) | data formatting | bytes 4194304
  256.2 3.1 %copy.11 = f32[32,32,4,128]{3,2,1,0:T(4,128)} copy(f32[32,32,4,128]{3,1,2,0:T(8,128)S(1)} %get-tuple-element.5) | data formatting | bytes 4194304
  (37 shorter events, 14.7 us)
Async XLA Ops:
  7.2 62.9 %copy-start = (f32[3,256,256]{2,1,0:T(8,128)S(1)}, f32[3,256,256]{2,1,0:T(8,128)}, u32[]{:S(2)}) copy-start(f32[3,256,256]{2,1,0:T(8,128)} %param.7) | copy-start | bytes 2359300
  7.2 62.9 %all-gather.3.cloned.1.call-start = ((), (), s32[]{:S(2)}) async-start(), calls=%async_computation | async-start | bytes 6291456 | tf_op jit(solution)/shard_map/all_gather | solution.py:56
  10.5 0.9 copy-start.2
  10.5 179.7 %all-gather.5.cloned.1.call-start = ((), (), s32[]{:S(2)}) async-start(), calls=%async_computation.1 | async-start | bytes 6291456 | tf_op jit(solution)/shard_map/all_gather | solution.py:56
  11.4 6.3 %collective-permute-start = (f32[3,1,32,4]{2,3,1,0:T(4,128)S(1)}, f32[3,1,32,4]{2,3,1,0:T(4,128)S(1)}, u32[]{:S(2)}, u32[]{:S(2)}) collective-permute-start(f32[3,1,32,4]{2,3,1,0:T(4,128)S(1)} %get-tuple-element.26), channel_id=1, source_target_pairs={{0,8},{8,16},{16,24},{1,9},{9,17},{17,25},{2,10},{10,18},{18,26},{... | collective-permute-start | bytes 4616 | tf_op jit(solution)/shard_map/ppermute | solution.py:16
  16.3 5.5 %collective-permute-start.1 = (f32[3,1,32,4]{2,3,1,0:T(4,128)S(1)}, f32[3,1,32,4]{2,3,1,0:T(4,128)S(1)}, u32[]{:S(2)}, u32[]{:S(2)}) collective-permute-start(f32[3,1,32,4]{2,3,1,0:T(4,128)S(1)} %get-tuple-element.25), channel_id=1, source_target_pairs={{8,0},{16,8},{24,16},{9,1},{17,9},{25,17},{10,2},{18,10},{26,18},{... | collective-permute-start | bytes 4616 | tf_op jit(solution)/shard_map/ppermute | solution.py:19
  22.0 5.7 %collective-permute-start.2 = (f32[3,34,1,4]{2,3,1,0:T(4,128)S(1)}, f32[3,34,1,4]{2,3,1,0:T(4,128)S(1)}, u32[]{:S(2)}, u32[]{:S(2)}) collective-permute-start(f32[3,34,1,4]{2,3,1,0:T(4,128)S(1)} %get-tuple-element.23), channel_id=1, source_target_pairs={{0,2},{2,4},{4,6},{6,0},{1,3},{3,5},{5,7},{7,1},{8,10},{10,12},{12... | collective-permute-start | bytes 4904 | tf_op jit(solution)/shard_map/ppermute | solution.py:16
  22.1 6.5 %collective-permute-start.3 = (f32[3,34,1,4]{2,3,1,0:T(4,128)S(1)}, f32[3,34,1,4]{2,3,1,0:T(4,128)S(1)}, u32[]{:S(2)}, u32[]{:S(2)}) collective-permute-start(f32[3,34,1,4]{2,3,1,0:T(4,128)S(1)} %get-tuple-element.24), channel_id=1, source_target_pairs={{2,0},{4,2},{6,4},{0,6},{3,1},{5,3},{7,5},{1,7},{10,8},{12,10},{14... | collective-permute-start | bytes 4904 | tf_op jit(solution)/shard_map/ppermute | solution.py:19
  80.0 7.5 %collective-permute-start.4 = (f32[3,1,32,4,128]{4,2,3,1,0:T(8,128)S(1)}, f32[3,1,32,4,128]{4,2,3,1,0:T(8,128)S(1)}, u32[]{:S(2)}, u32[]{:S(2)}) collective-permute-start(f32[3,1,32,4,128]{4,2,3,1,0:T(8,128)S(1)} %get-tuple-element.18), channel_id=1, source_target_pairs={{0,8},{8,16},{16,24},{1,9},{9,17},{17,25},{2,10},{10,18},{18,26},{... | collective-permute-start | bytes 589832 | tf_op jit(solution)/shard_map/ppermute | solution.py:16
  83.4 8.3 %collective-permute-start.5 = (f32[3,1,32,4,128]{4,2,3,1,0:T(8,128)S(1)}, f32[3,1,32,4,128]{4,2,3,1,0:T(8,128)S(1)}, u32[]{:S(2)}, u32[]{:S(2)}) collective-permute-start(f32[3,1,32,4,128]{4,2,3,1,0:T(8,128)S(1)} %get-tuple-element.19), channel_id=1, source_target_pairs={{8,0},{16,8},{24,16},{9,1},{17,9},{25,17},{10,2},{18,10},{26,18},{... | collective-permute-start | bytes 589832 | tf_op jit(solution)/shard_map/ppermute | solution.py:19
  92.0 5.7 %collective-permute-start.6 = (f32[3,34,1,4,128]{4,2,3,1,0:T(1,128)S(1)}, f32[3,34,1,4,128]{4,2,3,1,0:T(1,128)S(1)}, u32[]{:S(2)}, u32[]{:S(2)}) collective-permute-start(f32[3,34,1,4,128]{4,2,3,1,0:T(1,128)S(1)} %get-tuple-element.14), channel_id=1, source_target_pairs={{0,2},{2,4},{4,6},{6,0},{1,3},{3,5},{5,7},{7,1},{8,10},{10,12},{12... | collective-permute-start | bytes 626696 | tf_op jit(solution)/shard_map/ppermute | solution.py:16
  92.0 6.4 %collective-permute-start.7 = (f32[3,34,1,4,128]{4,2,3,1,0:T(1,128)S(1)}, f32[3,34,1,4,128]{4,2,3,1,0:T(1,128)S(1)}, u32[]{:S(2)}, u32[]{:S(2)}) collective-permute-start(f32[3,34,1,4,128]{4,2,3,1,0:T(1,128)S(1)} %get-tuple-element.15), channel_id=1, source_target_pairs={{2,0},{4,2},{6,4},{0,6},{3,1},{5,3},{7,5},{1,7},{10,8},{12,10},{14... | collective-permute-start | bytes 626696 | tf_op jit(solution)/shard_map/ppermute | solution.py:19
  200.2 7.5 %collective-permute-start.8 = (f32[3,1,32,4,128]{4,2,3,1,0:T(8,128)S(1)}, f32[3,1,32,4,128]{4,2,3,1,0:T(8,128)S(1)}, u32[]{:S(2)}, u32[]{:S(2)}) collective-permute-start(f32[3,1,32,4,128]{4,2,3,1,0:T(8,128)S(1)} %get-tuple-element.16), channel_id=1, source_target_pairs={{0,8},{8,16},{16,24},{1,9},{9,17},{17,25},{2,10},{10,18},{18,26},{... | collective-permute-start | bytes 589832 | tf_op jit(solution)/shard_map/ppermute | solution.py:16
  203.6 8.3 %collective-permute-start.9 = (f32[3,1,32,4,128]{4,2,3,1,0:T(8,128)S(1)}, f32[3,1,32,4,128]{4,2,3,1,0:T(8,128)S(1)}, u32[]{:S(2)}, u32[]{:S(2)}) collective-permute-start(f32[3,1,32,4,128]{4,2,3,1,0:T(8,128)S(1)} %get-tuple-element.17), channel_id=1, source_target_pairs={{8,0},{16,8},{24,16},{9,1},{17,9},{25,17},{10,2},{18,10},{26,18},{... | collective-permute-start | bytes 589832 | tf_op jit(solution)/shard_map/ppermute | solution.py:19
  212.2 5.7 %collective-permute-start.10 = (f32[3,34,1,4,128]{4,2,3,1,0:T(1,128)S(1)}, f32[3,34,1,4,128]{4,2,3,1,0:T(1,128)S(1)}, u32[]{:S(2)}, u32[]{:S(2)}) collective-permute-start(f32[3,34,1,4,128]{4,2,3,1,0:T(1,128)S(1)} %get-tuple-element.12), channel_id=1, source_target_pairs={{0,2},{2,4},{4,6},{6,0},{1,3},{3,5},{5,7},{7,1},{8,10},{10,12},{12... | collective-permute-start | bytes 626696 | tf_op jit(solution)/shard_map/ppermute | solution.py:16
  212.2 6.4 %collective-permute-start.11 = (f32[3,34,1,4,128]{4,2,3,1,0:T(1,128)S(1)}, f32[3,34,1,4,128]{4,2,3,1,0:T(1,128)S(1)}, u32[]{:S(2)}, u32[]{:S(2)}) collective-permute-start(f32[3,34,1,4,128]{4,2,3,1,0:T(1,128)S(1)} %get-tuple-element.13), channel_id=1, source_target_pairs={{2,0},{4,2},{6,4},{0,6},{3,1},{5,3},{7,5},{1,7},{10,8},{12,10},{14... | collective-permute-start | bytes 626696 | tf_op jit(solution)/shard_map/ppermute | solution.py:19
  256.2 3.1 %copy-start.1 = (f32[3,256,256]{2,1,0:T(8,128)S(1)}, f32[3,256,256]{2,1,0:T(8,128)}, u32[]{:S(2)}) copy-start(f32[3,256,256]{2,1,0:T(8,128)} %param.7) | copy-start | bytes 2359300
Sparse Core Ops, SparseCore 0:
  10.6 59.4 all-gather.2
  133.9 56.2 all-gather.4
where the time goes:
time: 267 us; the launch traced here: 266 us
  waiting for transfers between devices  129 us (48%)
  other arithmetic  53.7 us (20%)
  local copies, waits for them, and re-layouts  28.3 us (11%)
  starting transfers between devices  21 us (8%)
  matrix products  19.8 us (7%)
  between operations  14.2 us (5%)
    all_gather x2, waiting for transfers between devices, apply_operator(): lax.all_gather(field, 'ma', axis=3, tiled=True)  97.3 us
    dot_general x2, matrix products, apply_operator(): jnp.einsum('xyzj,kij->kxyzi', lax.all_gather(field, 'ma', axis=3, tiled=T...  19.8 us
    concatenate x3, other arithmetic, extended(): block = jnp.concatenate([low, block, high], axis=dim)  18.9 us
    squeeze x2, local copies, waits for them, and re-layouts, apply_operator(): total = stencil(mixed_pad[0], coef_pads[0])  17.6 us
    add x1, other arithmetic, shards(): start_field + step_size * (right_side - apply_operator(start_field, coef_...  17.2 us
    ppermute x6, waiting for transfers between devices, extended(): lax.ppermute(lax.slice_in_dim(block, block.shape[dim] - width, None, axis...  16.8 us
    add x1, other arithmetic, shards(): solution_field = first + step_size * residual  16.3 us
    ppermute x6, waiting for transfers between devices, extended(): lax.ppermute(lax.slice_in_dim(block, 0, width, axis=dim), axis, backward)  14.9 us
  transfers between devices with their start and end apart: 14, of which 13 were waited for; matrix products, arithmetic and copies ran while one was open for 1% of the time, Pallas kernels for 0%

commit v1 on v0

v1 whole, which is shorter than its diff:
```python
import functools

import jax
import jax.numpy as jnp
from jax import lax
from jax.experimental import pallas as pl
from jax.experimental.pallas import tpu as pltpu
from jax.sharding import PartitionSpec as P

step_size = 0.02
lanes = 128
group = 2
pad = 8
vmem_bytes = 28 * 1024 * 1024
f32 = jnp.float32
bf16 = jnp.bfloat16
whole = pl.BlockSpec(memory_space=pltpu.VMEM)
anywhere = pl.BlockSpec(memory_space=pl.ANY)


def call(body, out_shapes, scratch, flops=0, size=0, in_specs=None, out_specs=None, aliases=None, name=None):
    return pl.pallas_call(
        body,
        out_shape=[jax.ShapeDtypeStruct(shape, kind) for shape, kind in out_shapes],
        in_specs=in_specs,
        out_specs=out_specs if out_specs is not None else [whole] * len(out_shapes),
        scratch_shapes=scratch,
        input_output_aliases=aliases or {},
        cost_estimate=pl.CostEstimate(flops=flops, bytes_accessed=size, transcendentals=0),
        compiler_params=pltpu.CompilerParams(vmem_limit_bytes=vmem_bytes),
        name=name,
    )


def sent(array, axis, step, periodic):
    count = lax.axis_size(axis)
    pairs = [(i, (i + step) % count) for i in range(count) if periodic or 0 <= i + step < count]
    return lax.ppermute(array, axis, pairs)


def weights_body(half_ref, couplings_ref, own_hi, own_lo, other_hi, other_lo, turned):
    half = half_ref[0]
    modes = own_hi.shape[1] // 2
    for field in range(3):
        mine = couplings_ref[field, pl.ds(pl.multiple_of(half * modes, modes), modes), :]
        theirs = couplings_ref[field, pl.ds(pl.multiple_of((1 - half) * modes, modes), modes), :]
        turned[:, :modes] = mine.T
        turned[:, modes:] = theirs.T
        own = turned[pl.ds(pl.multiple_of(half * modes, modes), modes), :]
        other = turned[pl.ds(pl.multiple_of((1 - half) * modes, modes), modes), :modes]
        rows = pl.ds(field * modes, modes)
        top = own.astype(bf16)
        own_hi[rows, :] = top
        own_lo[rows, :] = (own - top.astype(f32)).astype(bf16)
        top = other.astype(bf16)
        other_hi[rows, :] = top
        other_lo[rows, :] = (other - top.astype(f32)).astype(bf16)


def neighbours(padded, plane, start, size, depth):
    row = pad + start
    z = lax.broadcasted_iota(jnp.int32, (size, lanes), 0) % depth
    middle = plane + 1
    here = padded[middle, row : row + size, :]
    low_z = jnp.where(z == 0, 0.0, padded[middle, row - 1 : row - 1 + size, :])
    high_z = jnp.where(z == depth - 1, 0.0, padded[middle, row + 1 : row + 1 + size, :])
    return here, (
        padded[plane + 2, row : row + size, :],
        padded[plane, row : row + size, :],
        padded[middle, row + depth : row + depth + size, :],
        padded[middle, row - depth : row - depth + size, :],
        high_z,
        low_z,
    )


def fill_strips(padded, low, high, first, count, depth, source=0):
    rows = padded.shape[1] - 2 * pad

    def one(i, _):
        padded[first + i + 1, pad - depth : pad, :] = low[source + i]
        padded[first + i + 1, pad + rows : pad + rows + depth, :] = high[source + i]
        return 0

    lax.fori_loop(0, count, one, 0)


def faces_body(depth, coef, low_x, high_x, low_y, high_y, faces, padded, sem):
    count, rows = coef.shape[0], coef.shape[1]
    copy = pltpu.make_async_copy(coef, padded.at[pl.ds(1, count), pl.ds(pad, rows), :], sem)
    copy.start()
    padded[0, pad : pad + rows, :] = low_x[...]
    padded[count + 1, pad : pad + rows, :] = high_x[...]
    fill_strips(padded, low_y, high_y, 0, count, depth)
    copy.wait()
    size = 32

    def one(plane, _):
        lane = lax.broadcasted_iota(jnp.int32, (size, lanes), 1)
        for start in range(0, rows, size):
            here, beside = neighbours(padded, plane, start, size, depth)
            chosen = beside[5]
            for direction in range(4, -1, -1):
                chosen = jnp.where(lane < 3 * (direction + 1), beside[direction], chosen)
            faces[plane, start : start + size, :] = 0.5 * (here + chosen)
        return 0

    lax.fori_loop(0, count, one, 0)


def products(padded, faces, plane_of, face_of, step, depth, upper, lower, hi, lo):
    size = 32
    rows = padded.shape[1] - 2 * pad
    for j in range(group):
        plane = plane_of(step * group + j)
        face_plane = face_of(step * group + j)
        for start in range(0, rows, size):
            here, beside = neighbours(padded, plane, start, size, depth)
            face = faces[face_plane, start : start + size, :]
            moved = [here - value for value in beside]
            for field in range(3):
                total = face[:, field : field + 1] * moved[0]
                for direction in range(1, 6):
                    at = 3 * direction + field
                    total = total + face[:, at : at + 1] * moved[direction]
                top = total.astype(bf16)
                where = slice(j * rows + start, j * rows + start + size), slice(field * lanes, (field + 1) * lanes)
                upper[where] = top
                lower[where] = (total - top.astype(f32)).astype(bf16)
    big, small = upper[...], lower[...]
    out = jnp.dot(big, hi[...], preferred_element_type=f32)
    out = out + jnp.dot(big, lo[...], preferred_element_type=f32)
    return out + jnp.dot(small, hi[...], preferred_element_type=f32)


def first_body(depth, begin, count, sent_from, field, right, low_x, high_x, low_y, high_y, faces, hi, lo, rest, part, padded, upper, lower, sem):
    planes, rows = field.shape[0], field.shape[1]
    copy = pltpu.make_async_copy(field, padded.at[pl.ds(1, planes), pl.ds(pad, rows), :], sem)
    copy.start()
    padded[0, pad : pad + rows, :] = low_x[...]
    padded[planes + 1, pad : pad + rows, :] = high_x[...]
    fill_strips(padded, low_y, high_y, 0, planes, depth)
    copy.wait()

    def one(step, _):
        place = lambda i: begin + i
        out = products(padded, faces, place, place, step, depth, upper, lower, hi, lo)
        for j in range(group):
            at = step * group + j
            mine = out[j * rows : (j + 1) * rows]
            rest[at] = right[begin + at] - mine[:, :lanes]

            @pl.when(at >= sent_from)
            def _():
                part[at - sent_from] = mine[:, lanes:]

        return 0

    lax.fori_loop(0, count // group, one, 0)


def middle_body(depth, taken, other, low_y, high_y, faces, rest_a, rest_b, came, hi, lo, residual, low, high, edge, padded, upper, lower, sem):
    held, rows = other.shape[0], other.shape[1]
    copy = pltpu.make_async_copy(other, padded.at[pl.ds(0, held), pl.ds(pad, rows), :], sem)
    copy.start()
    fill_strips(padded, low_y, high_y, -1, held, depth)

    def near(i, _):
        value = rest_a[i] - came[i]
        residual[i] = value
        low[i] = value[:depth]
        high[i] = value[rows - depth :]
        return 0

    lax.fori_loop(0, taken, near, 0)
    edge[...] = residual[0]
    copy.wait()
    count = held - 2

    def one(step, _):
        out = products(padded, faces, lambda i: i, lambda i: taken + i, step, depth, upper, lower, hi, lo)
        for j in range(group):
            at = step * group + j
            value = rest_b[at] - out[j * rows : (j + 1) * rows]
            residual[taken + at] = value
            low[taken + at] = value[:depth]
            high[taken + at] = value[rows - depth :]
        return 0

    lax.fori_loop(0, count // group, one, 0)


def last_rows_body(depth, skip, rest_b, came, residual, low, high, edge):
    rows = came.shape[1]
    count = came.shape[0]

    def one(i, _):
        value = rest_b[skip + i] - came[i]
        residual[i] = value
        low[i] = value[:depth]
        high[i] = value[rows - depth :]
        return 0

    lax.fori_loop(0, count, one, 0)
    edge[...] = residual[count - 1]


def finish(out, residual, start):
    later = residual - step_size * out
    return later, start + step_size * (residual + later)


def second_body(depth, begin, count, residual, start, low_y, high_y, faces, hi, lo, later, fields, part, padded, upper, lower, sem):
    planes, rows = residual.shape[0], residual.shape[1]
    copy = pltpu.make_async_copy(residual, padded.at[pl.ds(1, planes), pl.ds(pad, rows), :], sem)
    copy.start()
    fill_strips(padded, low_y, high_y, 0, planes, depth)
    copy.wait()

    def one(step, _):
        place = lambda i: begin + i
        out = products(padded, faces, place, place, step, depth, upper, lower, hi, lo)
        for j in range(group):
            at = step * group + j
            mine = out[j * rows : (j + 1) * rows]
            here = padded[begin + at + 1, pad : pad + rows, :]
            later[begin + at], fields[begin + at] = finish(mine[:, :lanes], here, start[begin + at])
            part[at] = mine[:, lanes:]
        return 0

    lax.fori_loop(0, count // group, one, 0)


def third_body(depth, first, residual_a, residual_b, start, low_x, high_x, low_a, high_a, low_b, high_b, faces, hi, lo, later_in, fields_in, later, fields, part, padded, upper, lower, staged, sem):
    near, far = residual_a.shape[0], residual_b.shape[0]
    rows = residual_a.shape[1]
    planes = near + far
    copies = [
        pltpu.make_async_copy(residual_a, padded.at[pl.ds(1, near), pl.ds(pad, rows), :], sem.at[0]),
        pltpu.make_async_copy(residual_b, padded.at[pl.ds(1 + near, far), pl.ds(pad, rows), :], sem.at[1]),
    ]
    for copy in copies:
        copy.start()
    padded[0, pad : pad + rows, :] = low_x[...]
    padded[planes + 1, pad : pad + rows, :] = high_x[...]
    fill_strips(padded, low_a, high_a, 0, near, depth)
    fill_strips(padded, low_b, high_b, near, far, depth)
    for copy in copies:
        copy.wait()
    count = planes - first + 1
    place = lambda i: lax.rem(first + i, planes)

    def one(step, _):
        out = products(padded, faces, place, place, step, depth, upper, lower, hi, lo)
        for j in range(group):
            at = step * group + j
            mine = out[j * rows : (j + 1) * rows]
            here = padded[place(at) + 1, pad : pad + rows, :]
            staged[0, at], staged[1, at] = finish(mine[:, :lanes], here, start[place(at)])
            part[at] = mine[:, lanes:]
        return 0

    lax.fori_loop(0, count // group, one, 0)
    outward = []
    for which, target in ((0, later), (1, fields)):
        outward.append(pltpu.make_async_copy(staged.at[which, pl.ds(0, count - 1)], target.at[pl.ds(first, count - 1)], sem.at[2 * which]))
        outward.append(pltpu.make_async_copy(staged.at[which, pl.ds(count - 1, 1)], target.at[pl.ds(0, 1)], sem.at[2 * which + 1]))
    for copy in outward:
        copy.start()
    for copy in outward:
        copy.wait()


def last_body(came, later_in, fields_in, later, fields):
    later[...] = later_in[...] - step_size * came[...]
    fields[...] = fields_in[...] - (step_size * step_size) * came[...]


def add_last(came, later, fields, first):
    count = came.shape[0]
    planes = later.shape[0]
    block = (1,) + later.shape[1:]
    moving = pl.BlockSpec(block, lambda i: (lax.rem(first + i, planes), 0, 0))
    return pl.pallas_call(
        last_body,
        grid=(count,),
        out_shape=[jax.ShapeDtypeStruct(later.shape, f32)] * 2,
        in_specs=[pl.BlockSpec(block, lambda i: (i, 0, 0)), moving, moving],
        out_specs=[moving, moving],
        input_output_aliases={1: 0, 2: 1},
        cost_estimate=pl.CostEstimate(flops=4 * came.size, bytes_accessed=20 * came.size, transcendentals=0),
        name="last",
    )(came, later, fields)


def shards(right_side, start_field, coefficients, couplings):
    nx, ny, depth, modes = start_field.shape
    rows = ny * depth
    flat = (nx, rows, modes)
    start = start_field.reshape(flat)
    right = right_side.reshape(flat)
    begin = (9 * nx) // 32
    end = nx - begin
    taken = begin + 1
    ready = end - 1
    plane = (rows, modes)

    raw = sent(lax.slice_in_dim(start_field, begin, end, axis=0), "ma", 1, True)

    half = lax.axis_index("ma").astype(jnp.int32).reshape(1)
    width = 3 * modes
    own_hi, own_lo, other_hi, other_lo = call(
        weights_body,
        [((width, 2 * modes), bf16)] * 2 + [((width, modes), bf16)] * 2,
        [pltpu.VMEM((2 * modes, 2 * modes), f32)],
        in_specs=[pl.BlockSpec(memory_space=pltpu.SMEM), whole],
        size=couplings.size * 4,
        name="weights",
    )(half, couplings)

    choose = jnp.tile(jnp.eye(3, dtype=f32), (1, 6))
    choose = jnp.pad(choose, ((0, 0), (0, lanes - 18)))
    coef = jnp.einsum("kxyz,kl->xyzl", coefficients, choose, precision=lax.Precision.HIGHEST, preferred_element_type=f32)

    both = jnp.stack([start_field, coef])
    low_x = sent(both[:, nx - 1], "gx", 1, False)
    high_x = sent(both[:, 0], "gx", -1, False)
    low_y = sent(both[:, :, ny - 1], "gy", 1, True)
    high_y = sent(both[:, :, 0], "gy", -1, True)
    low_x, high_x = low_x.reshape((2,) + plane), high_x.reshape((2,) + plane)

    padded = pltpu.VMEM((nx + 2, rows + 2 * pad, lanes), f32)
    products_scratch = [pltpu.VMEM((group * rows, width), bf16)] * 2
    flops_of = lambda count, out: 2 * 3 * count * rows * width * out
    size_of = lambda count: 4 * count * rows * lanes
    (faces,) = call(
        functools.partial(faces_body, depth),
        [(flat, f32)],
        [padded, pltpu.SemaphoreType.DMA],
        in_specs=[anywhere] + [whole] * 4,
        size=2 * size_of(nx),
        name="faces",
    )(coef.reshape(flat), low_x[1], high_x[1], low_y[1], high_y[1])

    def first(begin, count, sent_from, kind):
        return call(
            functools.partial(first_body, depth, begin, count, sent_from),
            [((count,) + plane, f32), ((count - sent_from,) + plane, f32)],
            [padded] + products_scratch + [pltpu.SemaphoreType.DMA],
            in_specs=[anywhere] + [whole] * 8,
            flops=flops_of(count, 2 * modes),
            size=3 * size_of(count),
            name=kind,
        )(start, right, low_x[0], high_x[0], low_y[0], high_y[0], faces, own_hi, own_lo)

    back = (lambda array: array)
    rest_a, part_a = first(0, taken, 0, "first_a")
    came_a = sent(part_a, "ma", 1, True)
    rest_b, part_b = first(taken, nx - taken, ready - taken, "first_b")
    came_b = sent(part_b, "ma", 1, True)

    raw_low = sent(raw[:, ny - 1], "gy", 1, True)
    raw_high = sent(raw[:, 0], "gy", -1, True)
    held = end - begin
    raw = raw.reshape((held,) + plane)
    strip = lambda count: ((count, depth, modes), f32)
    near, low_a, high_a, edge_first = call(
        functools.partial(middle_body, depth, taken),
        [((ready,) + plane, f32), strip(ready), strip(ready), (plane, f32)],
        [pltpu.VMEM((held, rows + 2 * pad, lanes), f32)] + products_scratch + [pltpu.SemaphoreType.DMA],
        in_specs=[anywhere] + [whole] * 8,
        flops=flops_of(held - 2, modes),
        size=3 * size_of(ready),
        name="middle",
    )(raw, raw_low, raw_high, faces, rest_a, rest_b, came_a, other_hi, other_lo)
    next_low_a = sent(high_a, "gy", 1, True)
    next_high_a = sent(low_a, "gy", -1, True)
    next_high_x = sent(edge_first, "gx", -1, False)

    whole_fields = [(flat, f32)] * 2
    count = ready - 2
    later, fields, part_c = call(
        functools.partial(second_body, depth, 1, count),
        whole_fields + [((count,) + plane, f32)],
        [padded] + products_scratch + [pltpu.SemaphoreType.DMA],
        in_specs=[anywhere] + [whole] * 6,
        flops=flops_of(count, 2 * modes),
        size=5 * size_of(count),
        name="second",
    )(near, start, next_low_a, next_high_a, faces, own_hi, own_lo)
    came_c = sent(part_c, "ma", 1, True)

    remaining = nx - ready
    far, low_b, high_b, edge_last = call(
        functools.partial(last_rows_body, depth, ready - taken),
        [((remaining,) + plane, f32), strip(remaining), strip(remaining), (plane, f32)],
        [],
        in_specs=[whole] * 2,
        size=3 * size_of(remaining),
        name="far",
    )(rest_b, came_b)
    next_low_b = sent(high_b, "gy", 1, True)
    next_high_b = sent(low_b, "gy", -1, True)
    next_low_x = sent(edge_last, "gx", 1, False)

    done = ready - 1
    count = nx - done + 1
    later, fields, part_d = call(
        functools.partial(third_body, depth, done),
        whole_fields + [((count,) + plane, f32)],
        [padded] + products_scratch + [pltpu.VMEM((2, count) + plane, f32), pltpu.SemaphoreType.DMA((4,))],
        in_specs=[anywhere] * 2 + [whole] * 10 + [anywhere] * 2,
        out_specs=[anywhere] * 2 + [whole],
        flops=flops_of(count, 2 * modes),
        size=5 * size_of(count),
        aliases={12: 0, 13: 1},
        name="third",
    )(near, far, start, next_low_x, next_high_x, next_low_a, next_high_a, next_low_b, next_high_b, faces, own_hi, own_lo, later, fields)
    came_d = sent(part_d, "ma", 1, True)

    later, fields = add_last(came_c, later, fields, 1)
    later, fields = add_last(came_d, later, fields, done)
    return (fields.reshape(start_field.shape), later.reshape(start_field.shape))


def solution(mesh):
    placed = (P("gx", "gy", None, "ma"), P("gx", "gy", None, "ma"), P(None, "gx", "gy", None), P())
    return jax.shard_map(
        shards,
        mesh=mesh,
        in_specs=placed,
        out_specs=(P("gx", "gy", None, "ma"), P("gx", "gy", None, "ma")),
        check_vma=False,
    )
```

time: 267 us -> 139 us (0.52)
  waiting for transfers between devices: 129 us -> 23.1 us
  Pallas kernels: 0 us -> 72.3 us
  other arithmetic: 53.7 us -> 1.42 us
  matrix products: 19.8 us -> 3.47 us
  local copies, waits for them, and re-layouts: 28.3 us -> 13.3 us
  between operations: 14.2 us -> 0.89 us
    all_gather x2 -> x0, waiting for transfers between devices: 97.3 us -> none  [apply_operator(): lax.all_gather(field, 'ma', axis=3, tiled=True)]
    pallas_call x0 -> x10, Pallas kernels: none -> 72.3 us  [the longest x2 20.6 us: first(): call(functools.partial(first_body, depth, begin, count, sent_from), [((co...]
    add x2 -> x0, other arithmetic: 33.5 us -> none  [the longest x1 17.2 us: shards(): start_field + step_size * (right_side - apply_operator(start_field, coef_...]
    concatenate x3 -> x0, other arithmetic: 18.9 us -> none  [extended(): block = jnp.concatenate([low, block, high], axis=dim)]
    dot_general x2 -> x1, matrix products: 19.8 us -> 3.47 us  [shards(): jnp.einsum('kxyz,kl->xyzl', coefficients, choose, precision=lax.Precision...]
    squeeze x3, local copies, waits for them, and re-layouts: 17.7 us -> 1.77 us  [the longest x1 0.88 us: first(): low_y[0]]
    ppermute x12 -> x17, waiting for transfers between devices: 31.7 us -> 23.1 us  [sent(): return lax.ppermute(array, axis, pairs)]
    unnamed x11 -> x16, local copies, waits for them, and re-layouts: 10.3 us -> 5.02 us
  transfers between devices with their start and end apart: 14 -> 17, of which waited for: 13 -> 8; matrix products, arithmetic and copies ran while one was open for 1% -> 6% of each run, Pallas kernels for 0% -> 47%
where the time goes in v1:
time: 139 us; the launch traced here: 138 us
  Pallas kernels  72.3 us (52%)
  starting transfers between devices  23.1 us (17%)
  waiting for transfers between devices  23.1 us (17%)
  local copies, waits for them, and re-layouts  13.3 us (10%)
  matrix products  3.47 us (2%)
  other arithmetic  1.42 us (1%)
    ppermute x17, waiting for transfers between devices, sent(): return lax.ppermute(array, axis, pairs)  23.1 us
    ppermute x17, starting transfers between devices, sent(): return lax.ppermute(array, axis, pairs)  23.1 us
    pallas_call x2, Pallas kernels, first(): call(functools.partial(first_body, depth, begin, count, sent_from), [((co...  20.6 us
    pallas_call x2, Pallas kernels, add_last(): pl.pallas_call(last_body, grid=(count,), out_shape=[jax.ShapeDtypeStruct(...  18.9 us
    pallas_call x1, Pallas kernels, shards(): call(functools.partial(second_body, depth, 1, count), whole_fields + [((c...  14.7 us
    pallas_call x1, Pallas kernels, shards(): call(functools.partial(third_body, depth, done), whole_fields + [((count,...  9.07 us
    pallas_call x1, Pallas kernels, shards(): call(functools.partial(middle_body, depth, taken), [((ready,) + plane, f3...  7.39 us
    unnamed x16, local copies, waits for them, and re-layouts  5.02 us
  transfers between devices with their start and end apart: 17, of which 8 were waited for; matrix products, arithmetic and copies ran while one was open for 6% of the time, Pallas kernels for 47%

profile of v1, /device:TPU:0, one launch (start us, length us, event | category | flops | bytes accessed | tf_op | source)
XLA Modules:
  0.0 137.6 jit_solution(11435412611759466242)
XLA Ops:
  1.6 3.5 %fusion = f32[128,32,32,4]{0,2,3,1:T(8,128)S(1)} fusion(f32[3,32,32,4]{2,3,1,0:T(4,128)S(1)} %copy-done, f32[3,18]{1,0:T(4,128)S(1)} %tile.10), kind=kOutput, calls=%fused_computation.2 | convolution fusion | flops 18874368 | bytes 2146520 | tf_op jit(solution)/shard_map/kxyz,kl->xyzl/dot_general | solution.py:323
  5.0 1.4 copy.30
  7.9 1.3 collective-permute-start.4
  10.3 3.0 %collective-permute-start = (f32[14,32,4,128]{3,2,0,1:T(4,128)}, f32[14,32,4,128]{3,2,0,1:T(4,128)S(1)}, u32[]{:S(2)}, u32[]{:S(2)}) collective-permute-start(f32[14,32,4,128]{3,2,0,1:T(4,128)} %copy.29), channel_id=1, source_target_pairs={{0,1},{1,0},{2,3},{3,2},{4,5},{5,4},{6,7},{7,6},{8,9},{9,8},{10,11... | collective-permute-start | bytes 2752520 | tf_op jit(solution)/shard_map/ppermute | solution.py:38
  13.3 5.2 %collective-permute-start.3 = (f32[2,32,4,128]{3,2,0,1:T(4,128)S(1)}, f32[2,32,4,128]{3,2,0,1:T(4,128)}, u32[]{:S(2)}, u32[]{:S(2)}) collective-permute-start(f32[2,32,4,128]{3,2,0,1:T(4,128)S(1)} %get-tuple-element.57), channel_id=1, source_target_pairs={{0,8},{8,16},{16,24},{1,9},{9,17},{17,25},{2,10},{10,18},{18,26},{... | collective-permute-start | bytes 393224 | tf_op jit(solution)/shard_map/ppermute | solution.py:38
  19.7 1.8 %copy.20 = f32[32,32,4,128]{3,0,2,1:T(8,128)S(1)} copy(f32[32,32,4,128]{3,2,0,1:T(4,128)} %bitcast.60) | data formatting | bytes 4194304 | tf_op jit(solution)/shard_map/kxyz,kl->xyzl/dot_general | solution.py:323
  28.3 6.6 %first_a.1 = (f32[10,128,128]{2,1,0:T(8,128)S(1)}, f32[10,128,128]{2,1,0:T(8,128)S(1)}) custom-call(f32[32,128,128]{2,1,0:T(8,128)S(1)} %bitcast.45, f32[32,128,128]{2,1,0:T(8,128)S(1)} %bitcast.49, f32[128,128]{1,0:T(8,128)S(1)} %bitcast.54, f32[128,128]{1,0:T(8,128)S(1)} %bitcast.52, f32[32,4,128]{2,1,0:T(4,128)S(1)} %get-tuple-element.64.low_y, ...), custom_call_target="tpu_custom_call" | custom-call | flops 754974720 | bytes 1966080 | tf_op jit(solution)/shard_map/first_a/pallas_call | solution.py:346
  35.1 14.0 %first_b.1 = (f32[22,128,128]{2,1,0:T(8,128)S(1)}, f32[10,128,128]{2,1,0:T(8,128)S(1)}) custom-call(f32[32,128,128]{2,1,0:T(8,128)S(1)} %bitcast.46, f32[32,128,128]{2,1,0:T(8,128)S(1)} %bitcast.50, f32[128,128]{1,0:T(8,128)S(1)} %bitcast.55, f32[128,128]{1,0:T(8,128)S(1)} %bitcast.53, f32[32,4,128]{2,1,0:T(4,128)S(1)} %get-tuple-element.64.low_y, ...), custom_call_target="tpu_custom_call" | custom-call | flops 1660944384 | bytes 4325376 | tf_op jit(solution)/shard_map/first_b/pallas_call | solution.py:346
  49.1 2.0 %collective-permute-start.8 = (f32[10,128,128]{2,1,0:T(8,128)S(1)}, f32[10,128,128]{2,1,0:T(8,128)S(1)}, u32[]{:S(2)}, u32[]{:S(2)}) collective-permute-start(f32[10,128,128]{2,1,0:T(8,128)S(1)} %get-tuple-element.36), channel_id=1, source_target_pairs={{0,1},{1,0},{2,3},{3,2},{4,5},{5,4},{6,7},{7,6},{8,9},{9,8},{10,11... | collective-permute-start | bytes 1966088 | tf_op jit(solution)/shard_map/ppermute | solution.py:38
  53.5 2.0 %collective-permute-done.1.low_y = f32[14,4,128]{2,1,0:T(4,128)S(1)} collective-permute-done((f32[14,4,128]{2,1,0:T(4,128)S(1)}, f32[14,4,128]{2,1,0:T(4,128)S(1)}, u32[]{:S(2)}, u32[]{:S(2)}) %collective-permute-start.1) | collective-permute-done | bytes 28704 | tf_op jit(solution)/shard_map/ppermute | solution.py:38
  55.5 7.4 %middle.1 = (f32[22,128,128]{2,1,0:T(8,128)S(1)}, f32[22,4,128]{2,1,0:T(4,128)S(1)}, f32[22,4,128]{2,1,0:T(4,128)S(1)}, f32[128,128]{1,0:T(8,128)S(1)}) custom-call(f32[14,128,128]{2,1,0:T(8,128)S(1)} %bitcast.51, f32[14,4,128]{2,1,0:T(4,128)S(1)} %collective-permute-done.1.low_y, f32[14,4,128]{2,1,0:T(4,128)S(1)} %collective-permute-done.2.high_y, ...), custom_call_target="tpu_custom_call" | custom-call | flops 452984832 | bytes 4325376 | tf_op jit(solution)/shard_map/middle/pallas_call | solution.py:367
  63.0 1.7 %collective-permute-start.12 = (f32[22,4,128]{2,1,0:T(4,128)S(1)}, f32[22,4,128]{2,1,0:T(4,128)S(1)}, u32[]{:S(2)}, u32[]{:S(2)}) collective-permute-start(f32[22,4,128]{2,1,0:T(4,128)S(1)} %get-tuple-element.41), channel_id=1, source_target_pairs={{0,6},{2,0},{4,2},{6,4},{1,7},{3,1},{5,3},{7,5},{8,14},{10,8},{12,... | collective-permute-start | bytes 135176 | tf_op jit(solution)/shard_map/ppermute | solution.py:38
  64.7 1.7 %collective-permute-done.11.low_y.low_a = f32[22,4,128]{2,1,0:T(4,128)S(1)} collective-permute-done((f32[22,4,128]{2,1,0:T(4,128)S(1)}, f32[22,4,128]{2,1,0:T(4,128)S(1)}, u32[]{:S(2)}, u32[]{:S(2)}) %collective-permute-start.11) | collective-permute-done | bytes 45088 | tf_op jit(solution)/shard_map/ppermute | solution.py:38
  66.4 14.7 %second.1 = (f32[32,128,128]{2,1,0:T(8,128)}, f32[32,128,128]{2,1,0:T(8,128)}, f32[20,128,128]{2,1,0:T(8,128)S(1)}) custom-call(f32[22,128,128]{2,1,0:T(8,128)S(1)} %get-tuple-element.35.residual.residual_a, f32[32,128,128]{2,1,0:T(8,128)S(1)} %bitcast.47, f32[22,4,128]{2,1,0:T(4,128)S(1)} %collective-permute-done.11.low_y.low_a, ...), custom_call_target="tpu_custom_call" | custom-call | flops 1509949440 | bytes 6553600 | tf_op jit(solution)/shard_map/second/pallas_call | solution.py:382
  81.8 2.8 %collective-permute-start.9 = (f32[128,128]{1,0:T(8,128)S(1)}, f32[128,128]{1,0:T(8,128)S(1)}, u32[]{:S(2)}, u32[]{:S(2)}) collective-permute-start(f32[128,128]{1,0:T(8,128)S(1)} %get-tuple-element.38), channel_id=1, source_target_pairs={{0,8},{8,16},{16,24},{1,9},{9,17},{17,25},{2,10},{10,18},{18,26},{... | collective-permute-start | bytes 196616 | tf_op jit(solution)/shard_map/ppermute | solution.py:38
  84.6 1.3 collective-permute-start.10
  87.7 1.5 %collective-permute-done.13.low_b = f32[10,4,128]{2,1,0:T(4,128)S(1)} collective-permute-done((f32[10,4,128]{2,1,0:T(4,128)S(1)}, f32[10,4,128]{2,1,0:T(4,128)S(1)}, u32[]{:S(2)}, u32[]{:S(2)}) %collective-permute-start.13) | collective-permute-done | bytes 20512 | tf_op jit(solution)/shard_map/ppermute | solution.py:38
  89.2 2.2 %collective-permute-done.10.high_x = f32[128,128]{1,0:T(8,128)S(1)} collective-permute-done((f32[128,128]{1,0:T(8,128)S(1)}, f32[128,128]{1,0:T(8,128)S(1)}, u32[]{:S(2)}, u32[]{:S(2)}) %collective-permute-start.10) | collective-permute-done | bytes 65568 | tf_op jit(solution)/shard_map/ppermute | solution.py:38
  91.4 9.1 %third.1 = (f32[32,128,128]{2,1,0:T(8,128)}, f32[32,128,128]{2,1,0:T(8,128)}, f32[12,128,128]{2,1,0:T(8,128)S(1)}) custom-call(f32[22,128,128]{2,1,0:T(8,128)S(1)} %get-tuple-element.35.residual.residual_a, f32[10,128,128]{2,1,0:T(8,128)S(1)} %get-tuple-element.37.residual_b, ...), custom_call_target="tpu_custom_call", output_to_operand_aliasing={{0}: (12, {}), {1}: (13, {})} | custom-call | flops 905969664 | bytes 3932160 | tf_op jit(solution)/shard_map/third/pallas_call | solution.py:408
  100.5 1.9 %collective-permute-start.15 = (f32[12,128,128]{2,1,0:T(8,128)S(1)}, f32[12,128,128]{2,1,0:T(8,128)S(1)}, u32[]{:S(2)}, u32[]{:S(2)}) collective-permute-start(f32[12,128,128]{2,1,0:T(8,128)S(1)} %get-tuple-element.46), channel_id=1, source_target_pairs={{0,1},{1,0},{2,3},{3,2},{4,5},{5,4},{6,7},{7,6},{8,9},{9,8},{10,11... | collective-permute-start | bytes 2359304 | tf_op jit(solution)/shard_map/ppermute | solution.py:38
  102.4 10.2 %collective-permute-done.16.came = f32[20,128,128]{2,1,0:T(8,128)S(1)} collective-permute-done((f32[20,128,128]{2,1,0:T(8,128)S(1)}, f32[20,128,128]{2,1,0:T(8,128)S(1)}, u32[]{:S(2)}, u32[]{:S(2)}) %collective-permute-start.16) | collective-permute-done | bytes 1310752 | tf_op jit(solution)/shard_map/ppermute | solution.py:38
  113.6 11.5 %last.2 = (f32[32,128,128]{2,1,0:T(8,128)}, f32[32,128,128]{2,1,0:T(8,128)}) custom-call(f32[20,128,128]{2,1,0:T(8,128)} %copy-done.5, f32[32,128,128]{2,1,0:T(8,128)} %get-tuple-element.48.later_in, f32[32,128,128]{2,1,0:T(8,128)} %get-tuple-element.49.fields_in), custom_call_target="tpu_custom_call", output_to_operand_aliasing={{0}: (1, {}), {1}: (2, {})} | custom-call | flops 1310720 | bytes 6553600 | tf_op jit(solution)/shard_map/last/pallas_call | solution.py:284
  125.1 4.2 %collective-permute-done.15.came = f32[12,128,128]{2,1,0:T(8,128)S(1)} collective-permute-done((f32[12,128,128]{2,1,0:T(8,128)S(1)}, f32[12,128,128]{2,1,0:T(8,128)S(1)}, u32[]{:S(2)}, u32[]{:S(2)}) %collective-permute-start.15) | collective-permute-done | bytes 786464 | tf_op jit(solution)/shard_map/ppermute | solution.py:38
  130.3 7.4 %last.3 = (f32[32,128,128]{2,1,0:T(8,128)}, f32[32,128,128]{2,1,0:T(8,128)}) custom-call(f32[12,128,128]{2,1,0:T(8,128)} %copy-done.6, f32[32,128,128]{2,1,0:T(8,128)} %get-tuple-element.50.later_in, f32[32,128,128]{2,1,0:T(8,128)} %get-tuple-element.51.fields_in), custom_call_target="tpu_custom_call", output_to_operand_aliasing={{0}: (1, {}), {1}: (2, {})} | custom-call | flops 786432 | bytes 3932160 | tf_op jit(solution)/shard_map/last/pallas_call | solution.py:284
  (53 shorter events, 18.5 us)
Async XLA Ops:
  0.6 0.9 copy-start
  5.0 1.6 %copy-start.1 = (f32[32,32,4,128]{3,2,1,0:T(4,128)S(1)}, f32[32,32,4,128]{3,2,1,0:T(4,128)}, u32[]{:S(2)}) copy-start(f32[32,32,4,128]{3,2,1,0:T(4,128)} %param.5) | copy-start | bytes 6291460
  6.6 11.8 %copy-start.4 = (f32[128,32,32,4]{0,3,1,2:T(4,128)}, f32[128,32,32,4]{0,3,1,2:T(4,128)S(1)}, u32[]{:S(2)}) copy-start(f32[128,32,32,4]{0,3,1,2:T(4,128)S(1)} %copy.30) | copy-start | bytes 6291460
  7.2 2.0 %slice-start = ((f32[32,32,4,128]{3,2,1,0:T(4,128)}), f32[14,32,4,128]{3,2,1,0:T(4,128)S(1)}, s32[]{:S(2)}) async-start(f32[32,32,4,128]{3,2,1,0:T(4,128)} %param.5), calls=%async_computation | async-start | bytes 1835008 | tf_op jit(solution)/shard_map/slice | solution.py:308
  7.9 15.2 %collective-permute-start.4 = (f32[2,32,4,128]{3,2,0,1:T(4,128)}, f32[2,32,4,128]{3,2,0,1:T(4,128)}, u32[]{:S(2)}, u32[]{:S(2)}) collective-permute-start(f32[2,32,4,128]{3,2,0,1:T(4,128)} %get-tuple-element.56), channel_id=1, source_target_pairs={{8,0},{16,8},{24,16},{9,1},{17,9},{25,17},{10,2},{18,10},{26,18},{... | collective-permute-start | bytes 393224 | tf_op jit(solution)/shard_map/ppermute | solution.py:38
  10.3 40.8 %collective-permute-start = (f32[14,32,4,128]{3,2,0,1:T(4,128)}, f32[14,32,4,128]{3,2,0,1:T(4,128)S(1)}, u32[]{:S(2)}, u32[]{:S(2)}) collective-permute-start(f32[14,32,4,128]{3,2,0,1:T(4,128)} %copy.29), channel_id=1, source_target_pairs={{0,1},{1,0},{2,3},{3,2},{4,5},{5,4},{6,7},{7,6},{8,9},{9,8},{10,11... | collective-permute-start | bytes 2752520 | tf_op jit(solution)/shard_map/ppermute | solution.py:38
  13.3 10.7 %collective-permute-start.3 = (f32[2,32,4,128]{3,2,0,1:T(4,128)S(1)}, f32[2,32,4,128]{3,2,0,1:T(4,128)}, u32[]{:S(2)}, u32[]{:S(2)}) collective-permute-start(f32[2,32,4,128]{3,2,0,1:T(4,128)S(1)} %get-tuple-element.57), channel_id=1, source_target_pairs={{0,8},{8,16},{16,24},{1,9},{9,17},{17,25},{2,10},{10,18},{18,26},{... | collective-permute-start | bytes 393224 | tf_op jit(solution)/shard_map/ppermute | solution.py:38
  19.2 5.7 %collective-permute-start.6 = (f32[2,32,4,128]{3,2,1,0:T(4,128)}, f32[2,32,4,128]{3,2,1,0:T(4,128)}, u32[]{:S(2)}, u32[]{:S(2)}) collective-permute-start(f32[2,32,4,128]{3,2,1,0:T(4,128)} %get-tuple-element.54), channel_id=1, source_target_pairs={{0,6},{2,0},{4,2},{6,4},{1,7},{3,1},{5,3},{7,5},{8,14},{10,8},{12,... | collective-permute-start | bytes 393224 | tf_op jit(solution)/shard_map/ppermute | solution.py:38
  19.3 6.5 %collective-permute-start.5 = (f32[2,32,4,128]{3,2,1,0:T(4,128)S(1)}, f32[2,32,4,128]{3,2,1,0:T(4,128)}, u32[]{:S(2)}, u32[]{:S(2)}) collective-permute-start(f32[2,32,4,128]{3,2,1,0:T(4,128)S(1)} %get-tuple-element.55), channel_id=1, source_target_pairs={{0,2},{2,4},{4,6},{6,0},{1,3},{3,5},{5,7},{7,1},{8,10},{10,12},{12... | collective-permute-start | bytes 393224 | tf_op jit(solution)/shard_map/ppermute | solution.py:38
  21.5 1.2 copy-start.3
  26.7 1.6 %copy-start.2 = (f32[32,32,4,128]{3,2,1,0:T(4,128)S(1)}, f32[32,32,4,128]{3,2,1,0:T(4,128)}, u32[]{:S(2)}) copy-start(f32[32,32,4,128]{3,2,1,0:T(4,128)} %param.4) | copy-start | bytes 6291460
  34.9 17.5 %collective-permute-start.7 = (f32[10,128,128]{2,1,0:T(8,128)S(1)}, f32[10,128,128]{2,1,0:T(8,128)S(1)}, u32[]{:S(2)}, u32[]{:S(2)}) collective-permute-start(f32[10,128,128]{2,1,0:T(8,128)S(1)} %get-tuple-element.32), channel_id=1, source_target_pairs={{0,1},{1,0},{2,3},{3,2},{4,5},{5,4},{6,7},{7,6},{8,9},{9,8},{10,11... | collective-permute-start | bytes 1966088 | tf_op jit(solution)/shard_map/ppermute | solution.py:38
  49.1 32.6 %collective-permute-start.8 = (f32[10,128,128]{2,1,0:T(8,128)S(1)}, f32[10,128,128]{2,1,0:T(8,128)S(1)}, u32[]{:S(2)}, u32[]{:S(2)}) collective-permute-start(f32[10,128,128]{2,1,0:T(8,128)S(1)} %get-tuple-element.36), channel_id=1, source_target_pairs={{0,1},{1,0},{2,3},{3,2},{4,5},{5,4},{6,7},{7,6},{8,9},{9,8},{10,11... | collective-permute-start | bytes 1966088 | tf_op jit(solution)/shard_map/ppermute | solution.py:38
  51.1 2.4 %collective-permute-start.2 = (f32[14,4,128]{2,1,0:T(4,128)S(1)}, f32[14,4,128]{2,1,0:T(4,128)S(1)}, u32[]{:S(2)}, u32[]{:S(2)}) collective-permute-start(f32[14,4,128]{2,1,0:T(4,128)S(1)} %get-tuple-element.60), channel_id=1, source_target_pairs={{0,6},{2,0},{4,2},{6,4},{1,7},{3,1},{5,3},{7,5},{8,14},{10,8},{12,... | collective-permute-start | bytes 86024 | tf_op jit(solution)/shard_map/ppermute | solution.py:38
  51.9 3.6 %collective-permute-start.1 = (f32[14,4,128]{2,1,0:T(4,128)S(1)}, f32[14,4,128]{2,1,0:T(4,128)S(1)}, u32[]{:S(2)}, u32[]{:S(2)}) collective-permute-start(f32[14,4,128]{2,1,0:T(4,128)S(1)} %get-tuple-element.61), channel_id=1, source_target_pairs={{0,2},{2,4},{4,6},{6,0},{1,3},{3,5},{5,7},{7,1},{8,10},{10,12},{12... | collective-permute-start | bytes 86024 | tf_op jit(solution)/shard_map/ppermute | solution.py:38
  62.9 3.5 %collective-permute-start.11 = (f32[22,4,128]{2,1,0:T(4,128)S(1)}, f32[22,4,128]{2,1,0:T(4,128)S(1)}, u32[]{:S(2)}, u32[]{:S(2)}) collective-permute-start(f32[22,4,128]{2,1,0:T(4,128)S(1)} %get-tuple-element.40), channel_id=1, source_target_pairs={{0,2},{2,4},{4,6},{6,0},{1,3},{3,5},{5,7},{7,1},{8,10},{10,12},{12... | collective-permute-start | bytes 135176 | tf_op jit(solution)/shard_map/ppermute | solution.py:38
  63.0 3.4 %collective-permute-start.12 = (f32[22,4,128]{2,1,0:T(4,128)S(1)}, f32[22,4,128]{2,1,0:T(4,128)S(1)}, u32[]{:S(2)}, u32[]{:S(2)}) collective-permute-start(f32[22,4,128]{2,1,0:T(4,128)S(1)} %get-tuple-element.41), channel_id=1, source_target_pairs={{0,6},{2,0},{4,2},{6,4},{1,7},{3,1},{5,3},{7,5},{8,14},{10,8},{12,... | collective-permute-start | bytes 135176 | tf_op jit(solution)/shard_map/ppermute | solution.py:38
  81.1 31.4 %collective-permute-start.16 = (f32[20,128,128]{2,1,0:T(8,128)S(1)}, f32[20,128,128]{2,1,0:T(8,128)S(1)}, u32[]{:S(2)}, u32[]{:S(2)}) collective-permute-start(f32[20,128,128]{2,1,0:T(8,128)S(1)} %get-tuple-element.47), channel_id=1, source_target_pairs={{0,1},{1,0},{2,3},{3,2},{4,5},{5,4},{6,7},{7,6},{8,9},{9,8},{10,11... | collective-permute-start | bytes 3932168 | tf_op jit(solution)/shard_map/ppermute | solution.py:38
  81.8 7.4 %collective-permute-start.9 = (f32[128,128]{1,0:T(8,128)S(1)}, f32[128,128]{1,0:T(8,128)S(1)}, u32[]{:S(2)}, u32[]{:S(2)}) collective-permute-start(f32[128,128]{1,0:T(8,128)S(1)} %get-tuple-element.38), channel_id=1, source_target_pairs={{0,8},{8,16},{16,24},{1,9},{9,17},{17,25},{2,10},{10,18},{18,26},{... | collective-permute-start | bytes 196616 | tf_op jit(solution)/shard_map/ppermute | solution.py:38
  84.6 6.8 %collective-permute-start.10 = (f32[128,128]{1,0:T(8,128)S(1)}, f32[128,128]{1,0:T(8,128)S(1)}, u32[]{:S(2)}, u32[]{:S(2)}) collective-permute-start(f32[128,128]{1,0:T(8,128)S(1)} %get-tuple-element.39), channel_id=1, source_target_pairs={{8,0},{16,8},{24,16},{9,1},{17,9},{25,17},{10,2},{18,10},{26,18},{... | collective-permute-start | bytes 196616 | tf_op jit(solution)/shard_map/ppermute | solution.py:38
  85.9 3.3 %collective-permute-start.13 = (f32[10,4,128]{2,1,0:T(4,128)S(1)}, f32[10,4,128]{2,1,0:T(4,128)S(1)}, u32[]{:S(2)}, u32[]{:S(2)}) collective-permute-start(f32[10,4,128]{2,1,0:T(4,128)S(1)} %get-tuple-element.42), channel_id=1, source_target_pairs={{0,2},{2,4},{4,6},{6,0},{1,3},{3,5},{5,7},{7,1},{8,10},{10,12},{12... | collective-permute-start | bytes 61448 | tf_op jit(solution)/shard_map/ppermute | solution.py:38
  87.0 2.2 %collective-permute-start.14 = (f32[10,4,128]{2,1,0:T(4,128)S(1)}, f32[10,4,128]{2,1,0:T(4,128)S(1)}, u32[]{:S(2)}, u32[]{:S(2)}) collective-permute-start(f32[10,4,128]{2,1,0:T(4,128)S(1)} %get-tuple-element.43), channel_id=1, source_target_pairs={{0,6},{2,0},{4,2},{6,4},{1,7},{3,1},{5,3},{7,5},{8,14},{10,8},{12,... | collective-permute-start | bytes 61448 | tf_op jit(solution)/shard_map/ppermute | solution.py:38
  100.5 28.9 %collective-permute-start.15 = (f32[12,128,128]{2,1,0:T(8,128)S(1)}, f32[12,128,128]{2,1,0:T(8,128)S(1)}, u32[]{:S(2)}, u32[]{:S(2)}) collective-permute-start(f32[12,128,128]{2,1,0:T(8,128)S(1)} %get-tuple-element.46), channel_id=1, source_target_pairs={{0,1},{1,0},{2,3},{3,2},{4,5},{5,4},{6,7},{7,6},{8,9},{9,8},{10,11... | collective-permute-start | bytes 2359304 | tf_op jit(solution)/shard_map/ppermute | solution.py:38
  112.5 1.1 copy-start.5
  (1 other events, 0.9 us)

commit v2 on v0

v2 whole, which is shorter than its diff:
```python
import functools

import jax
import jax.numpy as jnp
from jax import lax
from jax.experimental import pallas as pl
from jax.experimental.pallas import tpu as pltpu
from jax.sharding import PartitionSpec as P

step_size = 0.02
lanes = 128
group = 2
pad = 8
vmem_bytes = 12 * 1024 * 1024
f32 = jnp.float32
bf16 = jnp.bfloat16
whole = pl.BlockSpec(memory_space=pltpu.VMEM)
anywhere = pl.BlockSpec(memory_space=pl.ANY)


def call(body, out_shapes, scratch, work=1.0, in_specs=None, out_specs=None, aliases=None, name=None):
    return pl.pallas_call(
        body,
        out_shape=[jax.ShapeDtypeStruct(shape, kind) for shape, kind in out_shapes],
        in_specs=in_specs,
        out_specs=out_specs if out_specs is not None else [whole] * len(out_shapes),
        scratch_shapes=scratch,
        input_output_aliases=aliases or {},
        cost_estimate=pl.CostEstimate(flops=int(work * 1e9), bytes_accessed=int(work * 2e6), transcendentals=0),
        compiler_params=pltpu.CompilerParams(vmem_limit_bytes=vmem_bytes),
        name=name,
    )


def sent(array, axis, step, periodic):
    count = lax.axis_size(axis)
    pairs = [(i, (i + step) % count) for i in range(count) if periodic or 0 <= i + step < count]
    return lax.ppermute(array, axis, pairs)


def weights_body(couplings_ref, own_hi, own_lo, other_hi, other_lo, turned):
    half = lax.axis_index("ma")
    modes = own_hi.shape[1] // 2
    for field in range(3):
        mine = couplings_ref[field, pl.ds(pl.multiple_of(half * modes, modes), modes), :]
        theirs = couplings_ref[field, pl.ds(pl.multiple_of((1 - half) * modes, modes), modes), :]
        turned[:, :modes] = mine.T
        turned[:, modes:] = theirs.T
        own = turned[pl.ds(pl.multiple_of(half * modes, modes), modes), :]
        other = turned[pl.ds(pl.multiple_of((1 - half) * modes, modes), modes), :modes]
        rows = pl.ds(field * modes, modes)
        top = own.astype(bf16)
        own_hi[rows, :] = top
        own_lo[rows, :] = (own - top.astype(f32)).astype(bf16)
        top = other.astype(bf16)
        other_hi[rows, :] = top
        other_lo[rows, :] = (other - top.astype(f32)).astype(bf16)


def layers_body(depth, field, coef, first_x, last_x, first_y, last_y, held, sem):
    planes, rows = field.shape[0], field.shape[1]
    copy = pltpu.make_async_copy(field, held, sem)
    copy.start()
    for out in (first_x, last_x, first_y, last_y):
        out[rows : rows + coef.shape[0]] = coef[...]
        out[rows + coef.shape[0] :] = jnp.zeros((out.shape[0] - rows - coef.shape[0], lanes), f32)
    copy.wait()
    first_x[:rows] = held[0]
    last_x[:rows] = held[planes - 1]
    for plane in range(planes):
        first_y[plane * depth : (plane + 1) * depth] = held[plane, :depth]
        last_y[plane * depth : (plane + 1) * depth] = held[plane, rows - depth :]


def halves_body(coef, halves, square):
    count, rows = coef.shape[0], coef.shape[1]
    square[:count] = 0.5 * coef[...]
    square[count:] = jnp.zeros((lanes - count, rows), f32)
    columns = square[...].T
    planes = count // 3
    for plane in range(planes):
        for field in range(3):
            at = field * planes + plane
            halves[field, plane + 1, pad : pad + rows, :] = jnp.broadcast_to(columns[:, at : at + 1], (rows, lanes))


def around(ref, middle, row, size, depth):
    z = lax.broadcasted_iota(jnp.int32, (size, lanes), 0) % depth
    low = jnp.where(z != 0, ref[middle, row - 1 : row - 1 + size, :], 0.0)
    high = jnp.where(z != depth - 1, ref[middle, row + 1 : row + 1 + size, :], 0.0)
    beside = ref[middle, row - depth : row - depth + size, :] + ref[middle, row + depth : row + depth + size, :]
    return (ref[middle - 1, row : row + size, :] + ref[middle + 1, row : row + size, :]) + (beside + (low + high))


def diagonal_body(depth, low_x, high_x, low_y, high_y, halves_in, halves, diagonal):
    planes, rows = diagonal.shape[1], diagonal.shape[2]
    spread = lambda column, height: jnp.broadcast_to(column, (height, lanes))
    before = (0.5 * low_x[rows:]).T
    after = (0.5 * high_x[rows:]).T
    for field in range(3):
        at = field * planes + planes - 1
        halves[field, 0, pad : pad + rows, :] = spread(before[:, at : at + 1], rows)
        at = field * planes
        halves[field, planes + 1, pad : pad + rows, :] = spread(after[:, at : at + 1], rows)
    below = (0.5 * low_y[rows:]).T[rows - depth :]
    above = (0.5 * high_y[rows:]).T[:depth]
    for plane in range(planes):
        for field in range(3):
            at = field * planes + plane
            halves[field, plane + 1, pad - depth : pad, :] = spread(below[:, at : at + 1], depth)
            halves[field, plane + 1, pad + rows : pad + rows + depth, :] = spread(above[:, at : at + 1], depth)
    size = 32

    def one(plane, _):
        for start in range(0, rows, size):
            row = pad + start
            for field in range(3):
                here = halves[field, plane + 1, row : row + size, :]
                diagonal[field, plane, start : start + size, :] = 6.0 * here + around(halves.at[field], plane + 1, row, size, depth)
        return 0

    lax.fori_loop(0, planes, one, 0)


def weigh(padded, halves, weighed, local, first, count):
    size = (padded.shape[1]) // 3

    def one(i, _):
        for start in range(0, padded.shape[1], size):
            value = padded[local + i, start : start + size, :]
            for field in range(3):
                weighed[field, local + i, start : start + size, :] = halves[field, first + i, start : start + size, :] * value
        return 0

    lax.fori_loop(0, count, one, 0)


def stencil(padded, halves, diagonal, weighed, middle, plane, at, depth, upper, lower):
    size = 32
    rows = padded.shape[1] - 2 * pad
    for start in range(0, rows, size):
        row = pad + start
        here = padded[middle, row : row + size, :]
        total = around(padded, middle, row, size, depth)
        for field in range(3):
            value = diagonal[field, plane, start : start + size, :] * here - halves[field, plane + 1, row : row + size, :] * total
            value = value - around(weighed.at[field], middle, row, size, depth)
            where = slice(at + start, at + start + size), slice(field * lanes, (field + 1) * lanes)
            top = value.astype(bf16)
            upper[where] = top
            lower[where] = (value - top.astype(f32)).astype(bf16)


def operate(depth, count, place, scratch, halves, diagonal, hi, lo, emit):
    padded, weighed, upper_a, lower_a, upper_b, lower_b = scratch
    rows = padded.shape[1] - 2 * pad

    def fill(at, upper, lower):
        for j in range(group):
            middle, plane = place(at + j)
            stencil(padded, halves, diagonal, weighed, middle, plane, j * rows, depth, upper, lower)

    def flush(at, upper, lower):
        big, small = upper[...], lower[...]
        out = jnp.dot(big, hi[...], preferred_element_type=f32)
        out = out + jnp.dot(big, lo[...], preferred_element_type=f32)
        out = out + jnp.dot(small, hi[...], preferred_element_type=f32)
        for j in range(group):
            emit(at + j, out[j * rows : (j + 1) * rows])

    groups = count // group
    fill(0, upper_a, lower_a)

    def one(i, _):
        at = 2 * group * i
        flush(at, upper_a, lower_a)
        fill(at + group, upper_b, lower_b)
        flush(at + group, upper_b, lower_b)
        fill(at + 2 * group, upper_a, lower_a)
        return 0

    lax.fori_loop(0, (groups - 1) // 2, one, 0)
    if groups % 2:
        flush(count - group, upper_a, lower_a)
    else:
        at = count - 2 * group
        flush(at, upper_a, lower_a)
        fill(at + group, upper_b, lower_b)
        flush(at + group, upper_b, lower_b)


def strips(padded, local, count, depth, low, high, source, stacked):
    rows = padded.shape[1] - 2 * pad
    for i in range(count):
        at = slice((source + i) * depth, (source + i + 1) * depth) if stacked else source + i
        padded[local + i, pad - depth : pad, :] = low[at]
        padded[local + i, pad + rows : pad + rows + depth, :] = high[at]


def loads(pieces, padded, sem):
    rows = padded.shape[1] - 2 * pad
    copies = []
    for number, (source, start, count, local) in enumerate(pieces):
        target = padded.at[pl.ds(local, count), pl.ds(pad, rows), :]
        copies.append(pltpu.make_async_copy(source.at[pl.ds(start, count)], target, sem.at[number]))
        copies[-1].start()
    return copies


def scratch_for(locals_, rows, width):
    padded = pltpu.VMEM((locals_, rows + 2 * pad, lanes), f32)
    weighed = pltpu.VMEM((3, locals_, rows + 2 * pad, lanes), f32)
    return [padded, weighed] + [pltpu.VMEM((group * rows, width), bf16)] * 4 + [pltpu.SemaphoreType.DMA((4,))]


def first_body(depth, begin, count, sent_from, field, right, low_x, high_x, low_y, high_y, halves, diagonal, hi, lo, rest, part, *scratch):
    padded, weighed, sem = scratch[0], scratch[1], scratch[-1]
    planes, rows = field.shape[0], field.shape[1]
    low, high = max(begin - 1, 0), min(begin + count + 1, planes)
    copies = loads([(field, low, high - low, low - begin + 1)], padded, sem)
    if begin == 0:
        padded[0, pad : pad + rows, :] = low_x[:rows]
    if begin + count == planes:
        padded[count + 1, pad : pad + rows, :] = high_x[:rows]
    strips(padded, 1, count, depth, low_y, high_y, begin, True)
    for copy in copies:
        copy.wait()
    weigh(padded, halves, weighed, 0, begin, count + 2)

    def emit(at, out):
        rest[at] = right[begin + at] - out[:, :lanes]

        @pl.when(at >= sent_from)
        def _():
            part[at - sent_from] = out[:, lanes:]

    operate(depth, count, lambda i: (i + 1, begin + i), scratch[:-1], halves, diagonal, hi, lo, emit)


def sides_body(depth, planes, first, last):
    rows = planes.shape[1]
    first[...] = planes[:, :depth, :]
    last[...] = planes[:, rows - depth :, :]


def middle_body(depth, taken, other, low_y, high_y, halves, diagonal, rest, hi, lo, residual, low, high, *scratch):
    padded, weighed, sem = scratch[0], scratch[1], scratch[-1]
    held, rows = other.shape[0], other.shape[1]
    count = held - 2
    copies = loads([(other, 0, held, 0)], padded, sem)
    strips(padded, 1, count, depth, low_y, high_y, 1, False)
    for copy in copies:
        copy.wait()
    weigh(padded, halves, weighed, 0, taken, held)

    def emit(at, out):
        value = rest[at] - out
        residual[taken + at] = value
        low[taken + at] = value[:depth]
        high[taken + at] = value[rows - depth :]

    operate(depth, count, lambda i: (i + 1, taken + i), scratch[:-1], halves, diagonal, hi, lo, emit)


def near_body(depth, rest, came, residual_in, low_in, high_in, residual, low, high, edge):
    count, rows = came.shape[0], came.shape[1]

    def one(i, _):
        value = rest[i] - came[i]
        residual[i] = value
        low[i] = value[:depth]
        high[i] = value[rows - depth :]
        return 0

    lax.fori_loop(0, count, one, 0)
    edge[...] = residual[0]


def far_body(depth, skip, rest, came, residual, low, high, edge):
    count, rows = came.shape[0], came.shape[1]

    def one(i, _):
        value = rest[skip + i] - came[i]
        residual[i] = value
        low[i] = value[:depth]
        high[i] = value[rows - depth :]
        return 0

    lax.fori_loop(0, count, one, 0)
    edge[...] = residual[count - 1]


def finish(out, residual, start):
    later = residual - step_size * out
    return later, start + step_size * (residual + later)


def second_body(depth, begin, count, residual, start, low_y, high_y, halves, diagonal, hi, lo, later, fields, part, *scratch):
    padded, weighed, sem = scratch[0], scratch[1], scratch[-1]
    rows = residual.shape[1]
    copies = loads([(residual, begin - 1, count + 2, 0)], padded, sem)
    strips(padded, 1, count, depth, low_y, high_y, begin, False)
    for copy in copies:
        copy.wait()
    weigh(padded, halves, weighed, 0, begin, count + 2)

    def emit(at, out):
        here = padded[at + 1, pad : pad + rows, :]
        later[at], fields[at] = finish(out[:, :lanes], here, start[begin + at])
        part[at] = out[:, lanes:]

    operate(depth, count, lambda i: (i + 1, begin + i), scratch[:-1], halves, diagonal, hi, lo, emit)


def third_body(depth, first, near, far, start, low_x, high_x, low_a, high_a, low_b, high_b, halves, diagonal, hi, lo, later, fields, part, *scratch):
    padded, weighed, sem = scratch[0], scratch[1], scratch[-1]
    ready, remaining = near.shape[0], far.shape[0]
    rows = near.shape[1]
    planes = ready + remaining
    run = planes - first
    copies = loads([(near, first - 1, ready - first + 1, 0), (far, 0, remaining, ready - first + 1), (near, 0, 2, run + 3)], padded, sem)
    padded[run + 1, pad : pad + rows, :] = high_x[...]
    padded[run + 2, pad : pad + rows, :] = low_x[...]
    strips(padded, 1, ready - first, depth, low_a, high_a, first, False)
    strips(padded, 1 + ready - first, remaining, depth, low_b, high_b, 0, False)
    strips(padded, run + 3, 1, depth, low_a, high_a, 0, False)
    for copy in copies:
        copy.wait()
    weigh(padded, halves, weighed, 0, first, run + 2)
    weigh(padded, halves, weighed, run + 2, 0, 3)

    def place(i):
        wrapped = jnp.where(i >= run, 1, 0)
        return i + 1 + 2 * wrapped, first + i - planes * wrapped

    def emit(at, out):
        middle, plane = place(at)
        here = padded[middle, pad : pad + rows, :]
        later[at], fields[at] = finish(out[:, :lanes], here, start[plane])
        part[at] = out[:, lanes:]

    operate(depth, run + 1, place, scratch[:-1], halves, diagonal, hi, lo, emit)


def last_body(first, later_part, fields_part, came, *refs):
    later, fields, staged, sem = refs[-4:]
    count = came.shape[0]
    planes = later.shape[0]
    piece = 4
    copies = []
    for begin in range(0, count, piece):
        for at in range(begin, begin + piece):
            staged[0, at] = later_part[at] - step_size * came[at]
            staged[1, at] = fields_part[at] - (step_size * step_size) * came[at]
        end = begin + piece
        wrap = max(begin, min(end, planes - first))
        for which, target in ((0, later), (1, fields)):
            for low, high in ((begin, wrap), (wrap, end)):
                if high > low:
                    goal = (first + low) % planes
                    copy = pltpu.make_async_copy(
                        staged.at[which, pl.ds(low, high - low)], target.at[pl.ds(goal, high - low)], sem.at[len(copies)]
                    )
                    copy.start()
                    copies.append(copy)
    for copy in copies:
        copy.wait()


def add_last(first, shape, later_part, fields_part, came, before):
    count = came.shape[0]
    return call(
        functools.partial(last_body, first),
        [(shape, f32)] * 2,
        [pltpu.VMEM((2,) + came.shape, f32), pltpu.SemaphoreType.DMA((count + 4,))],
        in_specs=[whole] * 3 + [anywhere] * len(before),
        out_specs=[anywhere] * 2,
        aliases={3: 0, 4: 1} if before else {},
        work=0.2,
        name="last",
    )(later_part, fields_part, came, *before)


def shards(right_side, start_field, coefficients, couplings):
    nx, ny, depth, modes = start_field.shape
    rows = ny * depth
    plane = (rows, modes)
    flat = (nx,) + plane
    start = start_field.reshape(flat)
    right = right_side.reshape(flat)
    begin = (9 * nx) // 32
    end = nx - begin
    held = end - begin
    taken = begin + 1
    ready = end - 1
    done = ready - 1
    width = 3 * modes

    raw = sent(lax.slice_in_dim(start, begin, end, axis=0), "ma", 1, True)

    coef = coefficients.reshape(3 * nx, rows)
    layer = ((rows + lanes, lanes), f32)
    first_x, last_x, first_y, last_y = call(
        functools.partial(layers_body, depth),
        [layer] * 4,
        [pltpu.VMEM(flat, f32), pltpu.SemaphoreType.DMA],
        in_specs=[anywhere, whole],
        name="layers",
    )(start, coef)
    low_y = sent(last_y, "gy", 1, True)
    high_y = sent(first_y, "gy", -1, True)
    low_x = sent(last_x, "gx", 1, False)
    high_x = sent(first_x, "gx", -1, False)

    own_hi, own_lo, other_hi, other_lo = call(
        weights_body,
        [((width, 2 * modes), bf16)] * 2 + [((width, modes), bf16)] * 2,
        [pltpu.VMEM((2 * modes, 2 * modes), f32)],
        in_specs=[whole],
        name="weights",
    )(couplings)

    halves_shape = (3, nx + 2, rows + 2 * pad, lanes)
    (halves,) = call(halves_body, [(halves_shape, f32)], [pltpu.VMEM((lanes, rows), f32)], in_specs=[whole], name="halves")(coef)
    halves, diagonal = call(
        functools.partial(diagonal_body, depth),
        [(halves_shape, f32), ((3,) + flat, f32)],
        [],
        in_specs=[whole] * 5,
        aliases={4: 0},
        name="diagonal",
    )(low_x, high_x, low_y, high_y, halves)

    def first(begin, count, sent_from, name):
        return call(
            functools.partial(first_body, depth, begin, count, sent_from),
            [((count,) + plane, f32), ((count - sent_from,) + plane, f32)],
            scratch_for(count + 2, rows, width),
            in_specs=[anywhere] + [whole] * 9,
            work=count / 10,
            name=name,
        )(start, right, low_x, high_x, low_y, high_y, halves, diagonal, own_hi, own_lo)

    rest_a, part_a = first(0, taken, 0, "first_a")
    came_a = sent(part_a, "ma", 1, True)
    rest_b, part_b = first(taken, nx - taken, ready - taken, "first_b")
    came_b = sent(part_b, "ma", 1, True)

    strip = lambda count: ((count, depth, modes), f32)
    raw_first, raw_last = call(
        functools.partial(sides_body, depth), [strip(held)] * 2, [], in_specs=[whole], work=0.1, name="sides"
    )(raw)
    raw_low = sent(raw_last, "gy", 1, True)
    raw_high = sent(raw_first, "gy", -1, True)
    near_shapes = [((ready,) + plane, f32), strip(ready), strip(ready)]
    near, low_a, high_a = call(
        functools.partial(middle_body, depth, taken),
        near_shapes,
        scratch_for(held, rows, width),
        in_specs=[anywhere] + [whole] * 7,
        work=(held - 2) / 12,
        name="middle",
    )(raw, raw_low, raw_high, halves, diagonal, rest_b, other_hi, other_lo)
    near, low_a, high_a, edge_first = call(
        functools.partial(near_body, depth),
        near_shapes + [(plane, f32)],
        [],
        in_specs=[whole] * 5,
        aliases={2: 0, 3: 1, 4: 2},
        work=0.2,
        name="near",
    )(rest_a, came_a, near, low_a, high_a)
    next_low_a = sent(high_a, "gy", 1, True)
    next_high_a = sent(low_a, "gy", -1, True)
    next_high_x = sent(edge_first, "gx", -1, False)

    count = ready - 2
    later_c, fields_c, part_c = call(
        functools.partial(second_body, depth, 1, count),
        [((count,) + plane, f32)] * 3,
        scratch_for(count + 2, rows, width),
        in_specs=[anywhere] + [whole] * 7,
        work=count / 10,
        name="second",
    )(near, start, next_low_a, next_high_a, halves, diagonal, own_hi, own_lo)
    came_c = sent(part_c, "ma", 1, True)

    remaining = nx - ready
    far, low_b, high_b, edge_last = call(
        functools.partial(far_body, depth, ready - taken),
        [((remaining,) + plane, f32), strip(remaining), strip(remaining), (plane, f32)],
        [],
        in_specs=[whole] * 2,
        work=0.2,
        name="far",
    )(rest_b, came_b)
    next_low_b = sent(high_b, "gy", 1, True)
    next_high_b = sent(low_b, "gy", -1, True)
    next_low_x = sent(edge_last, "gx", 1, False)

    count = nx - done + 1
    later_d, fields_d, part_d = call(
        functools.partial(third_body, depth, done),
        [((count,) + plane, f32)] * 3,
        scratch_for(count + 4, rows, width),
        in_specs=[anywhere] * 2 + [whole] * 11,
        work=count / 10,
        name="third",
    )(near, far, start, next_low_x, next_high_x, next_low_a, next_high_a, next_low_b, next_high_b, halves, diagonal, own_hi, own_lo)
    came_d = sent(part_d, "ma", 1, True)

    outs = add_last(1, flat, later_c, fields_c, came_c, ())
    later, fields = add_last(done, flat, later_d, fields_d, came_d, outs)
    return (fields.reshape(start_field.shape), later.reshape(start_field.shape))


def solution(mesh):
    placed = (P("gx", "gy", None, "ma"), P("gx", "gy", None, "ma"), P(None, "gx", "gy", None), P())
    return jax.shard_map(
        shards,
        mesh=mesh,
        in_specs=placed,
        out_specs=(P("gx", "gy", None, "ma"), P("gx", "gy", None, "ma")),
        check_vma=False,
    )
```

time: 267 us -> 103 us (0.39)
  waiting for transfers between devices: 129 us -> 40.6 us
  other arithmetic: 53.7 us -> 0 us
  Pallas kernels: 0 us -> 34 us
  local copies, waits for them, and re-layouts: 28.3 us -> 3.68 us
  matrix products: 19.8 us -> 0 us
  between operations: 14.2 us -> 0.87 us
    all_gather x2 -> x0, waiting for transfers between devices: 97.3 us -> none  [apply_operator(): lax.all_gather(field, 'ma', axis=3, tiled=True)]
    pallas_call x0 -> x14, Pallas kernels: none -> 34 us  [the longest x2 13.2 us: first(): call(functools.partial(first_body, depth, begin, count, sent_from), [((co...]
    add x2 -> x0, other arithmetic: 33.5 us -> none  [the longest x1 17.2 us: shards(): start_field + step_size * (right_side - apply_operator(start_field, coef_...]
    dot_general x2 -> x0, matrix products: 19.8 us -> none  [apply_operator(): jnp.einsum('xyzj,kij->kxyzi', lax.all_gather(field, 'ma', axis=3, tiled=T...]
    concatenate x3 -> x0, other arithmetic: 18.9 us -> none  [extended(): block = jnp.concatenate([low, block, high], axis=dim)]
    squeeze x3 -> x0, local copies, waits for them, and re-layouts: 17.7 us -> none  [the longest x2 17.6 us: apply_operator(): total = stencil(mixed_pad[0], coef_pads[0])]
    unnamed x11 -> x7, local copies, waits for them, and re-layouts: 10.3 us -> 1.13 us
    ppermute x12 -> x17, waiting for transfers between devices: 31.7 us -> 40.6 us  [sent(): return lax.ppermute(array, axis, pairs)]
  transfers between devices with their start and end apart: 14 -> 17, of which waited for: 13 -> 8; matrix products, arithmetic and copies ran while one was open for 1% -> 1% of each run, Pallas kernels for 0% -> 32%
where the time goes in v2:
time: 103 us; the launch traced here: 102 us
  waiting for transfers between devices  40.6 us (39%)
  Pallas kernels  34 us (33%)
  starting transfers between devices  23.3 us (23%)
  local copies, waits for them, and re-layouts  3.68 us (4%)
    ppermute x17, waiting for transfers between devices, sent(): return lax.ppermute(array, axis, pairs)  40.6 us
    ppermute x17, starting transfers between devices, sent(): return lax.ppermute(array, axis, pairs)  23.3 us
    pallas_call x2, Pallas kernels, first(): call(functools.partial(first_body, depth, begin, count, sent_from), [((co...  13.2 us
    pallas_call x1, Pallas kernels, shards(): call(functools.partial(second_body, depth, 1, count), [((count,) + plane,...  5.61 us
    pallas_call x1, Pallas kernels, shards(): call(functools.partial(third_body, depth, done), [((count,) + plane, f32)...  3.59 us
    pallas_call x1, Pallas kernels, shards(): call(functools.partial(middle_body, depth, taken), near_shapes, scratch_f...  3.15 us
    pallas_call x2, Pallas kernels, add_last(): call(functools.partial(last_body, first), [(shape, f32)] * 2, [pltpu.VMEM...  3.07 us
    pallas_call x1, Pallas kernels, shards(): call(functools.partial(diagonal_body, depth), [(halves_shape, f32), ((3,)...  2.67 us
  transfers between devices with their start and end apart: 17, of which 8 were waited for; matrix products, arithmetic and copies ran while one was open for 1% of the time, Pallas kernels for 32%

profile of v2, /device:TPU:0, one launch (start us, length us, event | category | flops | bytes accessed | tf_op | source)
XLA Modules:
  0.0 102.4 jit_solution(14132057001748800077)
XLA Ops:
  0.6 2.3 %slice.6 = f32[14,32,4,128]{3,2,1,0:T(4,128)} slice(f32[32,32,4,128]{3,2,1,0:T(4,128)} %param.5), slice={[9:23], [0:32], [0:4], [0:128]} | slice | bytes 1835008 | tf_op jit(solution)/shard_map/slice | solution.py:399
  3.0 3.0 %collective-permute-start.5 = (f32[14,128,128]{2,1,0:T(8,128)}, f32[14,128,128]{2,1,0:T(8,128)S(1)}, u32[]{:S(2)}, u32[]{:S(2)}) collective-permute-start(f32[14,128,128]{2,1,0:T(8,128)} %bitcast.2), channel_id=1, source_target_pairs={{0,1},{1,0},{2,3},{3,2},{4,5},{5,4},{6,7},{7,6},{8,9},{9,8},{10,11... | collective-permute-start | bytes 2752520 | tf_op jit(solution)/shard_map/ppermute | solution.py:38
  7.5 3.5 %collective-permute-start = (f32[256,128]{1,0:T(8,128)S(1)}, f32[256,128]{1,0:T(8,128)S(1)}, u32[]{:S(2)}, u32[]{:S(2)}) collective-permute-start(f32[256,128]{1,0:T(8,128)S(1)} %get-tuple-element.39), channel_id=1, source_target_pairs={{0,8},{8,16},{16,24},{1,9},{9,17},{17,25},{2,10},{10,18},{18,26},{... | collective-permute-start | bytes 393224 | tf_op jit(solution)/shard_map/ppermute | solution.py:38
  12.4 1.7 %collective-permute-start.3 = (f32[256,128]{1,0:T(8,128)S(1)}, f32[256,128]{1,0:T(8,128)S(1)}, u32[]{:S(2)}, u32[]{:S(2)}) collective-permute-start(f32[256,128]{1,0:T(8,128)S(1)} %get-tuple-element.42), channel_id=1, source_target_pairs={{0,6},{2,0},{4,2},{6,4},{1,7},{3,1},{5,3},{7,5},{8,14},{10,8},{12,... | collective-permute-start | bytes 393224 | tf_op jit(solution)/shard_map/ppermute | solution.py:38
  14.1 1.9 %halves.1.halves_in = f32[3,34,144,128]{3,2,1,0:T(8,128)S(1)} custom-call(f32[96,128]{1,0:T(8,128)S(1)} %copy.14.coef), custom_call_target="tpu_custom_call" | custom-call | flops 1000000000 | bytes 2000000 | tf_op jit(solution)/shard_map/halves/pallas_call | solution.py:424
  16.5 1.4 %collective-permute-done.1.high_x = f32[256,128]{1,0:T(8,128)S(1)} collective-permute-done((f32[256,128]{1,0:T(8,128)S(1)}, f32[256,128]{1,0:T(8,128)S(1)}, u32[]{:S(2)}, u32[]{:S(2)}) %collective-permute-start.1) | collective-permute-done | bytes 131104 | tf_op jit(solution)/shard_map/ppermute | solution.py:38
  17.9 2.7 %diagonal.1 = (f32[3,34,144,128]{3,2,1,0:T(8,128)S(1)}, f32[3,32,128,128]{3,2,1,0:T(8,128)S(1)}) custom-call(f32[256,128]{1,0:T(8,128)S(1)} %collective-permute-done.low_x, f32[256,128]{1,0:T(8,128)S(1)} %collective-permute-done.1.high_x, f32[256,128]{1,0:T(8,128)S(1)} %collective-permute-done.2.low_y, ...), custom_call_target="tpu_custom_call", output_to_operand_aliasing={{0}: (4, {})} | custom-call | flops 1000000000 | bytes 2000000 | tf_op jit(solution)/shard_map/diagonal/pallas_call | solution.py:425
  20.6 4.1 %first_a.1 = (f32[10,128,128]{2,1,0:T(8,128)S(1)}, f32[10,128,128]{2,1,0:T(8,128)S(1)}) custom-call(f32[32,128,128]{2,1,0:T(8,128)S(1)} %bitcast.8, f32[32,128,128]{2,1,0:T(8,128)S(1)} %bitcast.12, f32[256,128]{1,0:T(8,128)S(1)} %collective-permute-done.low_x, f32[256,128]{1,0:T(8,128)S(1)} %collective-permute-done.1.high_x, ...), custom_call_target="tpu_custom_call" | custom-call | flops 1000000000 | bytes 2000000 | tf_op jit(solution)/shard_map/first_a/pallas_call | solution.py:435
  26.6 1.7 %collective-permute-start.7 = (f32[14,4,128]{2,1,0:T(4,128)S(1)}, f32[14,4,128]{2,1,0:T(4,128)S(1)}, u32[]{:S(2)}, u32[]{:S(2)}) collective-permute-start(f32[14,4,128]{2,1,0:T(4,128)S(1)} %get-tuple-element.50), channel_id=1, source_target_pairs={{0,6},{2,0},{4,2},{6,4},{1,7},{3,1},{5,3},{7,5},{8,14},{10,8},{12,... | collective-permute-start | bytes 86024 | tf_op jit(solution)/shard_map/ppermute | solution.py:38
  28.3 9.1 %first_b.1 = (f32[22,128,128]{2,1,0:T(8,128)S(1)}, f32[10,128,128]{2,1,0:T(8,128)S(1)}) custom-call(f32[32,128,128]{2,1,0:T(8,128)S(1)} %bitcast.9, f32[32,128,128]{2,1,0:T(8,128)S(1)} %bitcast.13, f32[256,128]{1,0:T(8,128)S(1)} %collective-permute-done.low_x, f32[256,128]{1,0:T(8,128)S(1)} %collective-permute-done.1.high_x, ...), custom_call_target="tpu_custom_call" | custom-call | flops 2200000000 | bytes 4400000 | tf_op jit(solution)/shard_map/first_b/pallas_call | solution.py:435
  37.4 1.8 %collective-permute-start.8 = (f32[10,128,128]{2,1,0:T(8,128)S(1)}, f32[10,128,128]{2,1,0:T(8,128)S(1)}, u32[]{:S(2)}, u32[]{:S(2)}) collective-permute-start(f32[10,128,128]{2,1,0:T(8,128)S(1)} %get-tuple-element.58), channel_id=1, source_target_pairs={{0,1},{1,0},{2,3},{3,2},{4,5},{5,4},{6,7},{7,6},{8,9},{9,8},{10,11... | collective-permute-start | bytes 1966088 | tf_op jit(solution)/shard_map/ppermute | solution.py:38
  39.2 3.1 %middle.1 = (f32[22,128,128]{2,1,0:T(8,128)S(1)}, f32[22,4,128]{2,1,0:T(4,128)S(1)}, f32[22,4,128]{2,1,0:T(4,128)S(1)}) custom-call(f32[14,128,128]{2,1,0:T(8,128)S(1)} %collective-permute-done.5.planes.other, f32[14,4,128]{2,1,0:T(4,128)S(1)} %collective-permute-done.6.low_y, f32[14,4,128]{2,1,0:T(4,128)S(1)} %collective-permute-done.7.high_y, ...), custom_call_target="tpu_custom_call" | custom-call | flops 1000000000 | bytes 2000000 | tf_op jit(solution)/shard_map/middle/pallas_call | solution.py:456
  42.5 1.7 %collective-permute-start.12 = (f32[22,4,128]{2,1,0:T(4,128)S(1)}, f32[22,4,128]{2,1,0:T(4,128)S(1)}, u32[]{:S(2)}, u32[]{:S(2)}) collective-permute-start(f32[22,4,128]{2,1,0:T(4,128)S(1)} %get-tuple-element.63), channel_id=1, source_target_pairs={{0,6},{2,0},{4,2},{6,4},{1,7},{3,1},{5,3},{7,5},{8,14},{10,8},{12,... | collective-permute-start | bytes 135176 | tf_op jit(solution)/shard_map/ppermute | solution.py:38
  44.3 1.7 %collective-permute-done.11.low_a.low_y = f32[22,4,128]{2,1,0:T(4,128)S(1)} collective-permute-done((f32[22,4,128]{2,1,0:T(4,128)S(1)}, f32[22,4,128]{2,1,0:T(4,128)S(1)}, u32[]{:S(2)}, u32[]{:S(2)}) %collective-permute-start.11) | collective-permute-done | bytes 45088 | tf_op jit(solution)/shard_map/ppermute | solution.py:38
  46.0 5.6 %second.1 = (f32[20,128,128]{2,1,0:T(8,128)S(1)}, f32[20,128,128]{2,1,0:T(8,128)S(1)}, f32[20,128,128]{2,1,0:T(8,128)S(1)}) custom-call(f32[22,128,128]{2,1,0:T(8,128)S(1)} %get-tuple-element.57.near.residual, f32[32,128,128]{2,1,0:T(8,128)S(1)} %bitcast.10, f32[22,4,128]{2,1,0:T(4,128)S(1)} %collective-permute-done.11.low_a.low_y, ...), custom_call_target="tpu_custom_call" | custom-call | flops 2000000000 | bytes 4000000 | tf_op jit(solution)/shard_map/second/pallas_call | solution.py:478
  52.2 4.0 %collective-permute-done.8.came = f32[10,128,128]{2,1,0:T(8,128)S(1)} collective-permute-done((f32[10,128,128]{2,1,0:T(8,128)S(1)}, f32[10,128,128]{2,1,0:T(8,128)S(1)}, u32[]{:S(2)}, u32[]{:S(2)}) %collective-permute-start.8) | collective-permute-done | bytes 655392 | tf_op jit(solution)/shard_map/ppermute | solution.py:38
  56.3 3.6 %collective-permute-start.9 = (f32[128,128]{1,0:T(8,128)S(1)}, f32[128,128]{1,0:T(8,128)S(1)}, u32[]{:S(2)}, u32[]{:S(2)}) collective-permute-start(f32[128,128]{1,0:T(8,128)S(1)} %get-tuple-element.60), channel_id=1, source_target_pairs={{0,8},{8,16},{16,24},{1,9},{9,17},{17,25},{2,10},{10,18},{18,26},{... | collective-permute-start | bytes 196616 | tf_op jit(solution)/shard_map/ppermute | solution.py:38
  63.0 1.5 %collective-permute-done.13.low_b = f32[10,4,128]{2,1,0:T(4,128)S(1)} collective-permute-done((f32[10,4,128]{2,1,0:T(4,128)S(1)}, f32[10,4,128]{2,1,0:T(4,128)S(1)}, u32[]{:S(2)}, u32[]{:S(2)}) %collective-permute-start.13) | collective-permute-done | bytes 20512 | tf_op jit(solution)/shard_map/ppermute | solution.py:38
  64.5 2.0 %collective-permute-done.10.high_x = f32[128,128]{1,0:T(8,128)S(1)} collective-permute-done((f32[128,128]{1,0:T(8,128)S(1)}, f32[128,128]{1,0:T(8,128)S(1)}, u32[]{:S(2)}, u32[]{:S(2)}) %collective-permute-start.10) | collective-permute-done | bytes 65568 | tf_op jit(solution)/shard_map/ppermute | solution.py:38
  66.5 3.6 %third.1 = (f32[12,128,128]{2,1,0:T(8,128)S(1)}, f32[12,128,128]{2,1,0:T(8,128)S(1)}, f32[12,128,128]{2,1,0:T(8,128)S(1)}) custom-call(f32[22,128,128]{2,1,0:T(8,128)S(1)} %get-tuple-element.57.near.residual, f32[10,128,128]{2,1,0:T(8,128)S(1)} %get-tuple-element.59.far, f32[32,128,128]{2,1,0:T(8,128)S(1)} %bitcast.11, ...), custom_call_target="tpu_custom_call" | custom-call | flops 1200000000 | bytes 2400000 | tf_op jit(solution)/shard_map/third/pallas_call | solution.py:502
  70.7 13.6 %collective-permute-done.16.came = f32[20,128,128]{2,1,0:T(8,128)S(1)} collective-permute-done((f32[20,128,128]{2,1,0:T(8,128)S(1)}, f32[20,128,128]{2,1,0:T(8,128)S(1)}, u32[]{:S(2)}, u32[]{:S(2)}) %collective-permute-start.16) | collective-permute-done | bytes 1310752 | tf_op jit(solution)/shard_map/ppermute | solution.py:38
  84.3 1.8 %last.2 = (f32[32,128,128]{2,1,0:T(8,128)}, f32[32,128,128]{2,1,0:T(8,128)}) custom-call(f32[20,128,128]{2,1,0:T(8,128)S(1)} %get-tuple-element.69.later_part, f32[20,128,128]{2,1,0:T(8,128)S(1)} %get-tuple-element.70.fields_part, f32[20,128,128]{2,1,0:T(8,128)S(1)} %collective-permute-done.16.came), custom_call_target="tpu_custom_call" | custom-call | flops 200000000 | bytes 400000 | tf_op jit(solution)/shard_map/last/pallas_call | solution.py:372
  86.0 15.1 %collective-permute-done.15.came = f32[12,128,128]{2,1,0:T(8,128)S(1)} collective-permute-done((f32[12,128,128]{2,1,0:T(8,128)S(1)}, f32[12,128,128]{2,1,0:T(8,128)S(1)}, u32[]{:S(2)}, u32[]{:S(2)}) %collective-permute-start.15) | collective-permute-done | bytes 786464 | tf_op jit(solution)/shard_map/ppermute | solution.py:38
  101.1 1.3 %last.3 = (f32[32,128,128]{2,1,0:T(8,128)}, f32[32,128,128]{2,1,0:T(8,128)}) custom-call(f32[12,128,128]{2,1,0:T(8,128)S(1)} %get-tuple-element.66.later_part, f32[12,128,128]{2,1,0:T(8,128)S(1)} %get-tuple-element.67.fields_part, f32[12,128,128]{2,1,0:T(8,128)S(1)} %collective-permute-done.15.came, ...), custom_call_target="tpu_custom_call", output_to_operand_aliasing={{0}: (3, {}), {1}: (4, {})} | custom-call | flops 200000000 | bytes 400000 | tf_op jit(solution)/shard_map/last/pallas_call | solution.py:372
  (34 shorter events, 9.7 us)
Async XLA Ops:
  0.6 6.7 %copy-start = (f32[32,32,4,128]{3,2,1,0:T(4,128)S(1)}, f32[32,32,4,128]{3,2,1,0:T(4,128)}, u32[]{:S(2)}) copy-start(f32[32,32,4,128]{3,2,1,0:T(4,128)} %param.5) | copy-start | bytes 6291460
  3.0 23.5 %collective-permute-start.5 = (f32[14,128,128]{2,1,0:T(8,128)}, f32[14,128,128]{2,1,0:T(8,128)S(1)}, u32[]{:S(2)}, u32[]{:S(2)}) collective-permute-start(f32[14,128,128]{2,1,0:T(8,128)} %bitcast.2), channel_id=1, source_target_pairs={{0,1},{1,0},{2,3},{3,2},{4,5},{5,4},{6,7},{7,6},{8,9},{9,8},{10,11... | collective-permute-start | bytes 2752520 | tf_op jit(solution)/shard_map/ppermute | solution.py:38
  7.5 9.0 %collective-permute-start = (f32[256,128]{1,0:T(8,128)S(1)}, f32[256,128]{1,0:T(8,128)S(1)}, u32[]{:S(2)}, u32[]{:S(2)}) collective-permute-start(f32[256,128]{1,0:T(8,128)S(1)} %get-tuple-element.39), channel_id=1, source_target_pairs={{0,8},{8,16},{16,24},{1,9},{9,17},{17,25},{2,10},{10,18},{18,26},{... | collective-permute-start | bytes 393224 | tf_op jit(solution)/shard_map/ppermute | solution.py:38
  11.0 6.9 %collective-permute-start.1 = (f32[256,128]{1,0:T(8,128)S(1)}, f32[256,128]{1,0:T(8,128)S(1)}, u32[]{:S(2)}, u32[]{:S(2)}) collective-permute-start(f32[256,128]{1,0:T(8,128)S(1)} %get-tuple-element.40), channel_id=1, source_target_pairs={{8,0},{16,8},{24,16},{9,1},{17,9},{25,17},{10,2},{18,10},{26,18},{... | collective-permute-start | bytes 393224 | tf_op jit(solution)/shard_map/ppermute | solution.py:38
  12.3 5.6 %collective-permute-start.2 = (f32[256,128]{1,0:T(8,128)S(1)}, f32[256,128]{1,0:T(8,128)S(1)}, u32[]{:S(2)}, u32[]{:S(2)}) collective-permute-start(f32[256,128]{1,0:T(8,128)S(1)} %get-tuple-element.41), channel_id=1, source_target_pairs={{0,2},{2,4},{4,6},{6,0},{1,3},{3,5},{5,7},{7,1},{8,10},{10,12},{12... | collective-permute-start | bytes 393224 | tf_op jit(solution)/shard_map/ppermute | solution.py:38
  12.4 3.7 %copy-start.2 = (f32[3,256,256]{2,1,0:T(8,128)S(1)}, f32[3,256,256]{2,1,0:T(8,128)}, u32[]{:S(2)}) copy-start(f32[3,256,256]{2,1,0:T(8,128)} %couplings_ref.1) | copy-start | bytes 2359300
  12.4 5.5 %collective-permute-start.3 = (f32[256,128]{1,0:T(8,128)S(1)}, f32[256,128]{1,0:T(8,128)S(1)}, u32[]{:S(2)}, u32[]{:S(2)}) collective-permute-start(f32[256,128]{1,0:T(8,128)S(1)} %get-tuple-element.42), channel_id=1, source_target_pairs={{0,6},{2,0},{4,2},{6,4},{1,7},{3,1},{5,3},{7,5},{8,14},{10,8},{12,... | collective-permute-start | bytes 393224 | tf_op jit(solution)/shard_map/ppermute | solution.py:38
  16.5 4.1 %copy-start.1 = (f32[32,32,4,128]{3,2,1,0:T(4,128)S(1)}, f32[32,32,4,128]{3,2,1,0:T(4,128)}, u32[]{:S(2)}) copy-start(f32[32,32,4,128]{3,2,1,0:T(4,128)} %param.4) | copy-start | bytes 6291460
  24.7 17.7 %collective-permute-start.4 = (f32[10,128,128]{2,1,0:T(8,128)S(1)}, f32[10,128,128]{2,1,0:T(8,128)S(1)}, u32[]{:S(2)}, u32[]{:S(2)}) collective-permute-start(f32[10,128,128]{2,1,0:T(8,128)S(1)} %get-tuple-element.48), channel_id=1, source_target_pairs={{0,1},{1,0},{2,3},{3,2},{4,5},{5,4},{6,7},{7,6},{8,9},{9,8},{10,11... | collective-permute-start | bytes 1966088 | tf_op jit(solution)/shard_map/ppermute | solution.py:38
  26.5 12.7 %collective-permute-start.6 = (f32[14,4,128]{2,1,0:T(4,128)S(1)}, f32[14,4,128]{2,1,0:T(4,128)S(1)}, u32[]{:S(2)}, u32[]{:S(2)}) collective-permute-start(f32[14,4,128]{2,1,0:T(4,128)S(1)} %get-tuple-element.49), channel_id=1, source_target_pairs={{0,2},{2,4},{4,6},{6,0},{1,3},{3,5},{5,7},{7,1},{8,10},{10,12},{12... | collective-permute-start | bytes 86024 | tf_op jit(solution)/shard_map/ppermute | solution.py:38
  26.6 12.6 %collective-permute-start.7 = (f32[14,4,128]{2,1,0:T(4,128)S(1)}, f32[14,4,128]{2,1,0:T(4,128)S(1)}, u32[]{:S(2)}, u32[]{:S(2)}) collective-permute-start(f32[14,4,128]{2,1,0:T(4,128)S(1)} %get-tuple-element.50), channel_id=1, source_target_pairs={{0,6},{2,0},{4,2},{6,4},{1,7},{3,1},{5,3},{7,5},{8,14},{10,8},{12,... | collective-permute-start | bytes 86024 | tf_op jit(solution)/shard_map/ppermute | solution.py:38
  37.4 18.8 %collective-permute-start.8 = (f32[10,128,128]{2,1,0:T(8,128)S(1)}, f32[10,128,128]{2,1,0:T(8,128)S(1)}, u32[]{:S(2)}, u32[]{:S(2)}) collective-permute-start(f32[10,128,128]{2,1,0:T(8,128)S(1)} %get-tuple-element.58), channel_id=1, source_target_pairs={{0,1},{1,0},{2,3},{3,2},{4,5},{5,4},{6,7},{7,6},{8,9},{9,8},{10,11... | collective-permute-start | bytes 1966088 | tf_op jit(solution)/shard_map/ppermute | solution.py:38
  42.5 3.5 %collective-permute-start.11 = (f32[22,4,128]{2,1,0:T(4,128)S(1)}, f32[22,4,128]{2,1,0:T(4,128)S(1)}, u32[]{:S(2)}, u32[]{:S(2)}) collective-permute-start(f32[22,4,128]{2,1,0:T(4,128)S(1)} %get-tuple-element.62), channel_id=1, source_target_pairs={{0,2},{2,4},{4,6},{6,0},{1,3},{3,5},{5,7},{7,1},{8,10},{10,12},{12... | collective-permute-start | bytes 135176 | tf_op jit(solution)/shard_map/ppermute | solution.py:38
  42.5 3.5 %collective-permute-start.12 = (f32[22,4,128]{2,1,0:T(4,128)S(1)}, f32[22,4,128]{2,1,0:T(4,128)S(1)}, u32[]{:S(2)}, u32[]{:S(2)}) collective-permute-start(f32[22,4,128]{2,1,0:T(4,128)S(1)} %get-tuple-element.63), channel_id=1, source_target_pairs={{0,6},{2,0},{4,2},{6,4},{1,7},{3,1},{5,3},{7,5},{8,14},{10,8},{12,... | collective-permute-start | bytes 135176 | tf_op jit(solution)/shard_map/ppermute | solution.py:38
  51.6 32.6 %collective-permute-start.16 = (f32[20,128,128]{2,1,0:T(8,128)S(1)}, f32[20,128,128]{2,1,0:T(8,128)S(1)}, u32[]{:S(2)}, u32[]{:S(2)}) collective-permute-start(f32[20,128,128]{2,1,0:T(8,128)S(1)} %get-tuple-element.71), channel_id=1, source_target_pairs={{0,1},{1,0},{2,3},{3,2},{4,5},{5,4},{6,7},{7,6},{8,9},{9,8},{10,11... | collective-permute-start | bytes 3932168 | tf_op jit(solution)/shard_map/ppermute | solution.py:38
  56.3 8.2 %collective-permute-start.9 = (f32[128,128]{1,0:T(8,128)S(1)}, f32[128,128]{1,0:T(8,128)S(1)}, u32[]{:S(2)}, u32[]{:S(2)}) collective-permute-start(f32[128,128]{1,0:T(8,128)S(1)} %get-tuple-element.60), channel_id=1, source_target_pairs={{0,8},{8,16},{16,24},{1,9},{9,17},{17,25},{2,10},{10,18},{18,26},{... | collective-permute-start | bytes 196616 | tf_op jit(solution)/shard_map/ppermute | solution.py:38
  59.9 6.6 %collective-permute-start.10 = (f32[128,128]{1,0:T(8,128)S(1)}, f32[128,128]{1,0:T(8,128)S(1)}, u32[]{:S(2)}, u32[]{:S(2)}) collective-permute-start(f32[128,128]{1,0:T(8,128)S(1)} %get-tuple-element.61), channel_id=1, source_target_pairs={{8,0},{16,8},{24,16},{9,1},{17,9},{25,17},{10,2},{18,10},{26,18},{... | collective-permute-start | bytes 196616 | tf_op jit(solution)/shard_map/ppermute | solution.py:38
  61.2 3.3 %collective-permute-start.13 = (f32[10,4,128]{2,1,0:T(4,128)S(1)}, f32[10,4,128]{2,1,0:T(4,128)S(1)}, u32[]{:S(2)}, u32[]{:S(2)}) collective-permute-start(f32[10,4,128]{2,1,0:T(4,128)S(1)} %get-tuple-element.64), channel_id=1, source_target_pairs={{0,2},{2,4},{4,6},{6,0},{1,3},{3,5},{5,7},{7,1},{8,10},{10,12},{12... | collective-permute-start | bytes 61448 | tf_op jit(solution)/shard_map/ppermute | solution.py:38
  62.0 2.5 %collective-permute-start.14 = (f32[10,4,128]{2,1,0:T(4,128)S(1)}, f32[10,4,128]{2,1,0:T(4,128)S(1)}, u32[]{:S(2)}, u32[]{:S(2)}) collective-permute-start(f32[10,4,128]{2,1,0:T(4,128)S(1)} %get-tuple-element.65), channel_id=1, source_target_pairs={{0,6},{2,0},{4,2},{6,4},{1,7},{3,1},{5,3},{7,5},{8,14},{10,8},{12,... | collective-permute-start | bytes 61448 | tf_op jit(solution)/shard_map/ppermute | solution.py:38
  70.1 31.0 %collective-permute-start.15 = (f32[12,128,128]{2,1,0:T(8,128)S(1)}, f32[12,128,128]{2,1,0:T(8,128)S(1)}, u32[]{:S(2)}, u32[]{:S(2)}) collective-permute-start(f32[12,128,128]{2,1,0:T(8,128)S(1)} %get-tuple-element.68), channel_id=1, source_target_pairs={{0,1},{1,0},{2,3},{3,2},{4,5},{5,4},{6,7},{7,6},{8,9},{9,8},{10,11... | collective-permute-start | bytes 2359304 | tf_op jit(solution)/shard_map/ppermute | solution.py:38

commit v3 on v2

--- a/solution.py
+++ b/solution.py
@@ -18,7 +18,7 @@
 anywhere = pl.BlockSpec(memory_space=pl.ANY)
 
 
-def call(body, out_shapes, scratch, work=1.0, in_specs=None, out_specs=None, aliases=None, name=None):
+def call(body, out_shapes, scratch, work=1.0, vmem=vmem_bytes, in_specs=None, out_specs=None, aliases=None, name=None):
     return pl.pallas_call(
         body,
         out_shape=[jax.ShapeDtypeStruct(shape, kind) for shape, kind in out_shapes],
@@ -27,7 +27,7 @@
         scratch_shapes=scratch,
         input_output_aliases=aliases or {},
         cost_estimate=pl.CostEstimate(flops=int(work * 1e9), bytes_accessed=int(work * 2e6), transcendentals=0),
-        compiler_params=pltpu.CompilerParams(vmem_limit_bytes=vmem_bytes),
+        compiler_params=pltpu.CompilerParams(vmem_limit_bytes=vmem),
         name=name,
     )
 
@@ -55,6 +55,12 @@
         top = other.astype(bf16)
         other_hi[rows, :] = top
         other_lo[rows, :] = (other - top.astype(f32)).astype(bf16)
+
+
+def chosen_body(begin, field, out, sem):
+    copy = pltpu.make_async_copy(field.at[pl.ds(begin, out.shape[0])], out, sem)
+    copy.start()
+    copy.wait()
 
 
 def layers_body(depth, field, coef, first_x, last_x, first_y, last_y, held, sem):
@@ -168,25 +174,24 @@
         for j in range(group):
             emit(at + j, out[j * rows : (j + 1) * rows])
 
-    groups = count // group
+    groups = -(-count // group)
+    begin = lambda number: jnp.minimum(number * group, count - group)
     fill(0, upper_a, lower_a)
 
     def one(i, _):
-        at = 2 * group * i
-        flush(at, upper_a, lower_a)
-        fill(at + group, upper_b, lower_b)
-        flush(at + group, upper_b, lower_b)
-        fill(at + 2 * group, upper_a, lower_a)
+        flush(begin(2 * i), upper_a, lower_a)
+        fill(begin(2 * i + 1), upper_b, lower_b)
+        flush(begin(2 * i + 1), upper_b, lower_b)
+        fill(begin(2 * i + 2), upper_a, lower_a)
         return 0
 
     lax.fori_loop(0, (groups - 1) // 2, one, 0)
     if groups % 2:
         flush(count - group, upper_a, lower_a)
     else:
-        at = count - 2 * group
-        flush(at, upper_a, lower_a)
-        fill(at + group, upper_b, lower_b)
-        flush(at + group, upper_b, lower_b)
+        flush(begin(groups - 2), upper_a, lower_a)
+        fill(count - group, upper_b, lower_b)
+        flush(count - group, upper_b, lower_b)
 
 
 def strips(padded, local, count, depth, low, high, source, stacked):
@@ -276,7 +281,7 @@
     edge[...] = residual[0]
 
 
-def far_body(depth, skip, rest, came, residual, low, high, edge):
+def far_body(depth, skip, rest, came, after, residual, low, high, edge):
     count, rows = came.shape[0], came.shape[1]
 
     def one(i, _):
@@ -312,7 +317,10 @@
     operate(depth, count, lambda i: (i + 1, begin + i), scratch[:-1], halves, diagonal, hi, lo, emit)
 
 
-def third_body(depth, first, near, far, start, low_x, high_x, low_a, high_a, low_b, high_b, halves, diagonal, hi, lo, later, fields, part, *scratch):
+def third_body(depth, first, near, far, start, low_x, high_x, low_a, high_a, low_b, high_b, halves, diagonal, hi, lo, *refs):
+    later, fields, part, final_later, final_fields, final_part = refs[:6]
+    scratch = refs[6:]
+    split = part.shape[0]
     padded, weighed, sem = scratch[0], scratch[1], scratch[-1]
     ready, remaining = near.shape[0], far.shape[0]
     rows = near.shape[1]
@@ -336,8 +344,15 @@
     def emit(at, out):
         middle, plane = place(at)
         here = padded[middle, pad : pad + rows, :]
-        later[at], fields[at] = finish(out[:, :lanes], here, start[plane])
-        part[at] = out[:, lanes:]
+        one, two = finish(out[:, :lanes], here, start[plane])
+
+        @pl.when(at < split)
+        def _():
+            later[at], fields[at], part[at] = one, two, out[:, lanes:]
+
+        @pl.when(at >= split)
+        def _():
+            final_later[at - split], final_fields[at - split], final_part[at - split] = one, two, out[:, lanes:]
 
     operate(depth, run + 1, place, scratch[:-1], halves, diagonal, hi, lo, emit)
 
@@ -346,13 +361,13 @@
     later, fields, staged, sem = refs[-4:]
     count = came.shape[0]
     planes = later.shape[0]
-    piece = 4
+    piece = 2
     copies = []
     for begin in range(0, count, piece):
-        for at in range(begin, begin + piece):
+        end = min(begin + piece, count)
+        for at in range(begin, end):
             staged[0, at] = later_part[at] - step_size * came[at]
             staged[1, at] = fields_part[at] - (step_size * step_size) * came[at]
-        end = begin + piece
         wrap = max(begin, min(end, planes - first))
         for which, target in ((0, later), (1, fields)):
             for low, high in ((begin, wrap), (wrap, end)):
@@ -372,7 +387,7 @@
     return call(
         functools.partial(last_body, first),
         [(shape, f32)] * 2,
-        [pltpu.VMEM((2,) + came.shape, f32), pltpu.SemaphoreType.DMA((count + 4,))],
+        [pltpu.VMEM((2,) + came.shape, f32), pltpu.SemaphoreType.DMA((2 * count + 4,))],
         in_specs=[whole] * 3 + [anywhere] * len(before),
         out_specs=[anywhere] * 2,
         aliases={3: 0, 4: 1} if before else {},
@@ -388,7 +403,7 @@
     flat = (nx,) + plane
     start = start_field.reshape(flat)
     right = right_side.reshape(flat)
-    begin = (9 * nx) // 32
+    begin = nx // 4
     end = nx - begin
     held = end - begin
     taken = begin + 1
@@ -396,7 +411,16 @@
     done = ready - 1
     width = 3 * modes
 
-    raw = sent(lax.slice_in_dim(start, begin, end, axis=0), "ma", 1, True)
+    (chosen,) = call(
+        functools.partial(chosen_body, begin),
+        [((held,) + plane, f32)],
+        [pltpu.SemaphoreType.DMA],
+        in_specs=[pl.BlockSpec(memory_space=pltpu.HBM)],
+        out_specs=[anywhere],
+        vmem=60 * 1024 * 1024,
+        name="chosen",
+    )(start)
+    raw = sent(chosen, "ma", 1, True)
 
     coef = coefficients.reshape(3 * nx, rows)
     layer = ((rows + lanes, lanes), f32)
@@ -490,27 +514,30 @@
         functools.partial(far_body, depth, ready - taken),
         [((remaining,) + plane, f32), strip(remaining), strip(remaining), (plane, f32)],
         [],
-        in_specs=[whole] * 2,
+        in_specs=[whole] * 2 + [anywhere],
         work=0.2,
         name="far",
-    )(rest_b, came_b)
+    )(rest_b, came_b, part_c)
     next_low_b = sent(high_b, "gy", 1, True)
     next_high_b = sent(low_b, "gy", -1, True)
     next_low_x = sent(edge_last, "gx", 1, False)
 
     count = nx - done + 1
-    later_d, fields_d, part_d = call(
+    final = 4
+    later_d, fields_d, part_d, later_e, fields_e, part_e = call(
         functools.partial(third_body, depth, done),
-        [((count,) + plane, f32)] * 3,
+        [((count - final,) + plane, f32)] * 3 + [((final,) + plane, f32)] * 3,
         scratch_for(count + 4, rows, width),
         in_specs=[anywhere] * 2 + [whole] * 11,
-        work=count / 10,
+        work=6.0,
         name="third",
     )(near, far, start, next_low_x, next_high_x, next_low_a, next_high_a, next_low_b, next_high_b, halves, diagonal, own_hi, own_lo)
     came_d = sent(part_d, "ma", 1, True)
+    came_e = sent(part_e, "ma", 1, True)
 
     outs = add_last(1, flat, later_c, fields_c, came_c, ())
-    later, fields = add_last(done, flat, later_d, fields_d, came_d, outs)
+    outs = add_last(done, flat, later_d, fields_d, came_d, outs)
+    later, fields = add_last(done + count - final, flat, later_e, fields_e, came_e, outs)
     return (fields.reshape(start_field.shape), later.reshape(start_field.shape))
 
 

time: 103 us -> 137 us (1.33)
  Pallas kernels: 34 us -> 70.5 us
  waiting for transfers between devices: 40.6 us -> 37.8 us
  starting transfers between devices: 23.3 us -> 25.7 us
  local copies, waits for them, and re-layouts: 3.68 us -> 1.36 us
    pallas_call x1 -> x2, Pallas kernels: 3.59 us -> 37.7 us  [the longest x1 32.9 us: shards(): call(functools.partial(chosen_body, begin), [((held,) + plane, f32)], [pl...]
    ppermute x17 -> x18, waiting for transfers between devices: 40.6 us -> 37.8 us  [sent(): return lax.ppermute(array, axis, pairs)]
    ppermute x17 -> x18, starting transfers between devices: 23.3 us -> 25.7 us  [sent(): return lax.ppermute(array, axis, pairs)]
    slice x1 -> x0, local copies, waits for them, and re-layouts: 2.32 us -> none  [shards(): raw = sent(lax.slice_in_dim(start, begin, end, axis=0), 'ma', 1, True)]
    pallas_call x2 -> x3, Pallas kernels: 3.07 us -> 3.95 us  [add_last(): call(functools.partial(last_body, first), [(shape, f32)] * 2, [pltpu.VMEM...]
  transfers between devices with their start and end apart: 17 -> 18, of which waited for: 8 -> 7; matrix products, arithmetic and copies ran while one was open for 1% -> 1% of each run, Pallas kernels for 32% -> 27%
where the time goes in v3:
time: 137 us; the launch traced here: 136 us
  Pallas kernels  70.5 us (51%)
  waiting for transfers between devices  37.8 us (28%)
  starting transfers between devices  25.7 us (19%)
    ppermute x18, waiting for transfers between devices, sent(): return lax.ppermute(array, axis, pairs)  37.8 us
    pallas_call x1, Pallas kernels, shards(): call(functools.partial(chosen_body, begin), [((held,) + plane, f32)], [pl...  32.9 us
    ppermute x18, starting transfers between devices, sent(): return lax.ppermute(array, axis, pairs)  25.7 us
    pallas_call x2, Pallas kernels, first(): call(functools.partial(first_body, depth, begin, count, sent_from), [((co...  13.7 us
    pallas_call x1, Pallas kernels, shards(): call(functools.partial(second_body, depth, 1, count), [((count,) + plane,...  6.33 us
    pallas_call x1, Pallas kernels, shards(): call(functools.partial(third_body, depth, done), [((count - final,) + pla...  4.79 us
    pallas_call x3, Pallas kernels, add_last(): call(functools.partial(last_body, first), [(shape, f32)] * 2, [pltpu.VMEM...  3.95 us
    pallas_call x1, Pallas kernels, shards(): call(functools.partial(middle_body, depth, taken), near_shapes, scratch_f...  3.4 us
  transfers between devices with their start and end apart: 18, of which 7 were waited for; matrix products, arithmetic and copies ran while one was open for 1% of the time, Pallas kernels for 27%

profile of v3, /device:TPU:0, one launch (start us, length us, event | category | flops | bytes accessed | tf_op | source)
XLA Modules:
  0.0 136.4 jit_solution(11669562015218283941)
XLA Ops:
  0.6 32.9 %chosen.1 = f32[16,128,128]{2,1,0:T(8,128)} custom-call(f32[32,128,128]{2,1,0:T(8,128)} %bitcast.6), custom_call_target="tpu_custom_call" | custom-call | flops 1000000000 | bytes 2000000 | tf_op jit(solution)/shard_map/chosen/pallas_call | solution.py:414
  33.5 3.0 %collective-permute-start.5 = (f32[16,128,128]{2,1,0:T(8,128)}, f32[16,128,128]{2,1,0:T(8,128)S(1)}, u32[]{:S(2)}, u32[]{:S(2)}) collective-permute-start(f32[16,128,128]{2,1,0:T(8,128)} %chosen.1), channel_id=1, source_target_pairs={{0,1},{1,0},{2,3},{3,2},{4,5},{5,4},{6,7},{7,6},{8,9},{9,8},{10,11... | collective-permute-start | bytes 3145736 | tf_op jit(solution)/shard_map/ppermute | solution.py:38
  38.1 3.5 %collective-permute-start = (f32[256,128]{1,0:T(8,128)S(1)}, f32[256,128]{1,0:T(8,128)S(1)}, u32[]{:S(2)}, u32[]{:S(2)}) collective-permute-start(f32[256,128]{1,0:T(8,128)S(1)} %get-tuple-element.44), channel_id=1, source_target_pairs={{0,8},{8,16},{16,24},{1,9},{9,17},{17,25},{2,10},{10,18},{18,26},{... | collective-permute-start | bytes 393224 | tf_op jit(solution)/shard_map/ppermute | solution.py:38
  43.0 1.7 %collective-permute-start.3 = (f32[256,128]{1,0:T(8,128)S(1)}, f32[256,128]{1,0:T(8,128)S(1)}, u32[]{:S(2)}, u32[]{:S(2)}) collective-permute-start(f32[256,128]{1,0:T(8,128)S(1)} %get-tuple-element.47), channel_id=1, source_target_pairs={{0,6},{2,0},{4,2},{6,4},{1,7},{3,1},{5,3},{7,5},{8,14},{10,8},{12,... | collective-permute-start | bytes 393224 | tf_op jit(solution)/shard_map/ppermute | solution.py:38
  44.7 1.9 %halves.1.halves_in = f32[3,34,144,128]{3,2,1,0:T(8,128)S(1)} custom-call(f32[96,128]{1,0:T(8,128)S(1)} %copy.16.coef), custom_call_target="tpu_custom_call" | custom-call | flops 1000000000 | bytes 2000000 | tf_op jit(solution)/shard_map/halves/pallas_call | solution.py:448
  48.5 2.7 %diagonal.1 = (f32[3,34,144,128]{3,2,1,0:T(8,128)S(1)}, f32[3,32,128,128]{3,2,1,0:T(8,128)S(1)}) custom-call(f32[256,128]{1,0:T(8,128)S(1)} %collective-permute-done.low_x, f32[256,128]{1,0:T(8,128)S(1)} %collective-permute-done.1.high_x, f32[256,128]{1,0:T(8,128)S(1)} %collective-permute-done.2.low_y, ...), custom_call_target="tpu_custom_call", output_to_operand_aliasing={{0}: (4, {})} | custom-call | flops 1000000000 | bytes 2000000 | tf_op jit(solution)/shard_map/diagonal/pallas_call | solution.py:449
  51.2 4.1 %first_a.1 = (f32[9,128,128]{2,1,0:T(8,128)S(1)}, f32[9,128,128]{2,1,0:T(8,128)S(1)}) custom-call(f32[32,128,128]{2,1,0:T(8,128)S(1)} %bitcast.8, f32[32,128,128]{2,1,0:T(8,128)S(1)} %bitcast.12, f32[256,128]{1,0:T(8,128)S(1)} %collective-permute-done.low_x, f32[256,128]{1,0:T(8,128)S(1)} %collective-permute-done.1.high_x, ...), custom_call_target="tpu_custom_call" | custom-call | flops 900000000 | bytes 1800000 | tf_op jit(solution)/shard_map/first_a/pallas_call | solution.py:459
  55.8 4.9 %collective-permute-done.5.planes.other = f32[16,128,128]{2,1,0:T(8,128)S(1)} collective-permute-done((f32[16,128,128]{2,1,0:T(8,128)}, f32[16,128,128]{2,1,0:T(8,128)S(1)}, u32[]{:S(2)}, u32[]{:S(2)}) %collective-permute-start.5) | collective-permute-done | bytes 1048608 | tf_op jit(solution)/shard_map/ppermute | solution.py:38
  60.8 1.7 %collective-permute-start.7 = (f32[16,4,128]{2,1,0:T(4,128)S(1)}, f32[16,4,128]{2,1,0:T(4,128)S(1)}, u32[]{:S(2)}, u32[]{:S(2)}) collective-permute-start(f32[16,4,128]{2,1,0:T(4,128)S(1)} %get-tuple-element.55), channel_id=1, source_target_pairs={{0,6},{2,0},{4,2},{6,4},{1,7},{3,1},{5,3},{7,5},{8,14},{10,8},{12,... | collective-permute-start | bytes 98312 | tf_op jit(solution)/shard_map/ppermute | solution.py:38
  62.6 9.6 %first_b.1 = (f32[23,128,128]{2,1,0:T(8,128)S(1)}, f32[9,128,128]{2,1,0:T(8,128)S(1)}) custom-call(f32[32,128,128]{2,1,0:T(8,128)S(1)} %bitcast.9, f32[32,128,128]{2,1,0:T(8,128)S(1)} %bitcast.13, f32[256,128]{1,0:T(8,128)S(1)} %collective-permute-done.low_x, f32[256,128]{1,0:T(8,128)S(1)} %collective-permute-done.1.high_x, ...), custom_call_target="tpu_custom_call" | custom-call | flops 2300000000 | bytes 4600000 | tf_op jit(solution)/shard_map/first_b/pallas_call | solution.py:459
  72.2 2.1 %collective-permute-start.8 = (f32[9,128,128]{2,1,0:T(8,128)S(1)}, f32[9,128,128]{2,1,0:T(8,128)S(1)}, u32[]{:S(2)}, u32[]{:S(2)}) collective-permute-start(f32[9,128,128]{2,1,0:T(8,128)S(1)} %get-tuple-element.63), channel_id=1, source_target_pairs={{0,1},{1,0},{2,3},{3,2},{4,5},{5,4},{6,7},{7,6},{8,9},{9,8},{10,11... | collective-permute-start | bytes 1769480 | tf_op jit(solution)/shard_map/ppermute | solution.py:38
  74.3 3.4 %middle.1 = (f32[23,128,128]{2,1,0:T(8,128)S(1)}, f32[23,4,128]{2,1,0:T(4,128)S(1)}, f32[23,4,128]{2,1,0:T(4,128)S(1)}) custom-call(f32[16,128,128]{2,1,0:T(8,128)S(1)} %collective-permute-done.5.planes.other, f32[16,4,128]{2,1,0:T(4,128)S(1)} %collective-permute-done.6.low_y, f32[16,4,128]{2,1,0:T(4,128)S(1)} %collective-permute-done.7.high_y, ...), custom_call_target="tpu_custom_call" | custom-call | flops 1166666624 | bytes 2333333 | tf_op jit(solution)/shard_map/middle/pallas_call | solution.py:480
  77.9 1.7 %collective-permute-start.10 = (f32[23,4,128]{2,1,0:T(4,128)S(1)}, f32[23,4,128]{2,1,0:T(4,128)S(1)}, u32[]{:S(2)}, u32[]{:S(2)}) collective-permute-start(f32[23,4,128]{2,1,0:T(4,128)S(1)} %get-tuple-element.65), channel_id=1, source_target_pairs={{0,6},{2,0},{4,2},{6,4},{1,7},{3,1},{5,3},{7,5},{8,14},{10,8},{12,... | collective-permute-start | bytes 141320 | tf_op jit(solution)/shard_map/ppermute | solution.py:38
  79.6 1.7 %collective-permute-done.9.low_y.low_a = f32[23,4,128]{2,1,0:T(4,128)S(1)} collective-permute-done((f32[23,4,128]{2,1,0:T(4,128)S(1)}, f32[23,4,128]{2,1,0:T(4,128)S(1)}, u32[]{:S(2)}, u32[]{:S(2)}) %collective-permute-start.9) | collective-permute-done | bytes 47136 | tf_op jit(solution)/shard_map/ppermute | solution.py:38
  81.4 6.3 %second.1 = (f32[21,128,128]{2,1,0:T(8,128)S(1)}, f32[21,128,128]{2,1,0:T(8,128)S(1)}, f32[21,128,128]{2,1,0:T(8,128)S(1)}) custom-call(f32[23,128,128]{2,1,0:T(8,128)S(1)} %get-tuple-element.62.residual.near, f32[32,128,128]{2,1,0:T(8,128)S(1)} %bitcast.10, f32[23,4,128]{2,1,0:T(4,128)S(1)} %collective-permute-done.9.low_y.low_a, ...), custom_call_target="tpu_custom_call" | custom-call | flops 2100000000 | bytes 4200000 | tf_op jit(solution)/shard_map/second/pallas_call | solution.py:502
  89.2 4.5 %collective-permute-start.11 = (f32[128,128]{1,0:T(8,128)S(1)}, f32[128,128]{1,0:T(8,128)S(1)}, u32[]{:S(2)}, u32[]{:S(2)}) collective-permute-start(f32[128,128]{1,0:T(8,128)S(1)} %get-tuple-element.68), channel_id=1, source_target_pairs={{0,8},{8,16},{16,24},{1,9},{9,17},{17,25},{2,10},{10,18},{18,26},{... | collective-permute-start | bytes 196616 | tf_op jit(solution)/shard_map/ppermute | solution.py:38
  93.8 1.6 %collective-permute-start.13 = (f32[9,4,128]{2,1,0:T(4,128)S(1)}, f32[9,4,128]{2,1,0:T(4,128)S(1)}, u32[]{:S(2)}, u32[]{:S(2)}) collective-permute-start(f32[9,4,128]{2,1,0:T(4,128)S(1)} %get-tuple-element.70), channel_id=1, source_target_pairs={{0,2},{2,4},{4,6},{6,0},{1,3},{3,5},{5,7},{7,1},{8,10},{10,12},{12... | collective-permute-start | bytes 55304 | tf_op jit(solution)/shard_map/ppermute | solution.py:38
  95.6 1.4 %collective-permute-done.13.low_b = f32[9,4,128]{2,1,0:T(4,128)S(1)} collective-permute-done((f32[9,4,128]{2,1,0:T(4,128)S(1)}, f32[9,4,128]{2,1,0:T(4,128)S(1)}, u32[]{:S(2)}, u32[]{:S(2)}) %collective-permute-start.13) | collective-permute-done | bytes 18464 | tf_op jit(solution)/shard_map/ppermute | solution.py:38
  97.0 4.8 %third.1 = (f32[7,128,128]{2,1,0:T(8,128)S(1)}, f32[7,128,128]{2,1,0:T(8,128)S(1)}, f32[7,128,128]{2,1,0:T(8,128)S(1)}, f32[4,128,128]{2,1,0:T(8,128)S(1)}, f32[...) custom-call(f32[23,128,128]{2,1,0:T(8,128)S(1)} %get-tuple-element.62.residual.near, ...), custom_call_target="tpu_custom_call" | custom-call | flops 6000000000 | bytes 12000000 | tf_op jit(solution)/shard_map/third/pallas_call | solution.py:527
  101.8 2.1 %collective-permute-start.16 = (f32[7,128,128]{2,1,0:T(8,128)S(1)}, f32[7,128,128]{2,1,0:T(8,128)S(1)}, u32[]{:S(2)}, u32[]{:S(2)}) collective-permute-start(f32[7,128,128]{2,1,0:T(8,128)S(1)} %get-tuple-element.77), channel_id=1, source_target_pairs={{0,1},{1,0},{2,3},{3,2},{4,5},{5,4},{6,7},{7,6},{8,9},{9,8},{10,11... | collective-permute-start | bytes 1376264 | tf_op jit(solution)/shard_map/ppermute | solution.py:38
  104.0 15.9 %collective-permute-done.17.came = f32[21,128,128]{2,1,0:T(8,128)S(1)} collective-permute-done((f32[21,128,128]{2,1,0:T(8,128)S(1)}, f32[21,128,128]{2,1,0:T(8,128)S(1)}, u32[]{:S(2)}, u32[]{:S(2)}) %collective-permute-start.17) | collective-permute-done | bytes 1376288 | tf_op jit(solution)/shard_map/ppermute | solution.py:38
  119.9 1.9 %last.3 = (f32[32,128,128]{2,1,0:T(8,128)}, f32[32,128,128]{2,1,0:T(8,128)}) custom-call(f32[21,128,128]{2,1,0:T(8,128)S(1)} %get-tuple-element.78.later_part, f32[21,128,128]{2,1,0:T(8,128)S(1)} %get-tuple-element.79.fields_part, f32[21,128,128]{2,1,0:T(8,128)S(1)} %collective-permute-done.17.came), custom_call_target="tpu_custom_call" | custom-call | flops 200000000 | bytes 400000 | tf_op jit(solution)/shard_map/last/pallas_call | solution.py:387
  121.9 7.9 %collective-permute-done.16.came = f32[7,128,128]{2,1,0:T(8,128)S(1)} collective-permute-done((f32[7,128,128]{2,1,0:T(8,128)S(1)}, f32[7,128,128]{2,1,0:T(8,128)S(1)}, u32[]{:S(2)}, u32[]{:S(2)}) %collective-permute-start.16) | collective-permute-done | bytes 458784 | tf_op jit(solution)/shard_map/ppermute | solution.py:38
  130.8 4.5 %collective-permute-done.15.came = f32[4,128,128]{2,1,0:T(8,128)S(1)} collective-permute-done((f32[4,128,128]{2,1,0:T(8,128)S(1)}, f32[4,128,128]{2,1,0:T(8,128)S(1)}, u32[]{:S(2)}, u32[]{:S(2)}) %collective-permute-start.15) | collective-permute-done | bytes 262176 | tf_op jit(solution)/shard_map/ppermute | solution.py:38
  (37 shorter events, 9.3 us)
Async XLA Ops:
  0.6 37.3 %copy-start = (f32[32,32,4,128]{3,2,1,0:T(4,128)S(1)}, f32[32,32,4,128]{3,2,1,0:T(4,128)}, u32[]{:S(2)}) copy-start(f32[32,32,4,128]{3,2,1,0:T(4,128)} %param.5) | copy-start | bytes 6291460
  33.5 27.2 %collective-permute-start.5 = (f32[16,128,128]{2,1,0:T(8,128)}, f32[16,128,128]{2,1,0:T(8,128)S(1)}, u32[]{:S(2)}, u32[]{:S(2)}) collective-permute-start(f32[16,128,128]{2,1,0:T(8,128)} %chosen.1), channel_id=1, source_target_pairs={{0,1},{1,0},{2,3},{3,2},{4,5},{5,4},{6,7},{7,6},{8,9},{9,8},{10,11... | collective-permute-start | bytes 3145736 | tf_op jit(solution)/shard_map/ppermute | solution.py:38
  38.1 9.0 %collective-permute-start = (f32[256,128]{1,0:T(8,128)S(1)}, f32[256,128]{1,0:T(8,128)S(1)}, u32[]{:S(2)}, u32[]{:S(2)}) collective-permute-start(f32[256,128]{1,0:T(8,128)S(1)} %get-tuple-element.44), channel_id=1, source_target_pairs={{0,8},{8,16},{16,24},{1,9},{9,17},{17,25},{2,10},{10,18},{18,26},{... | collective-permute-start | bytes 393224 | tf_op jit(solution)/shard_map/ppermute | solution.py:38
  41.6 6.9 %collective-permute-start.1 = (f32[256,128]{1,0:T(8,128)S(1)}, f32[256,128]{1,0:T(8,128)S(1)}, u32[]{:S(2)}, u32[]{:S(2)}) collective-permute-start(f32[256,128]{1,0:T(8,128)S(1)} %get-tuple-element.45), channel_id=1, source_target_pairs={{8,0},{16,8},{24,16},{9,1},{17,9},{25,17},{10,2},{18,10},{26,18},{... | collective-permute-start | bytes 393224 | tf_op jit(solution)/shard_map/ppermute | solution.py:38
  42.9 5.6 %collective-permute-start.2 = (f32[256,128]{1,0:T(8,128)S(1)}, f32[256,128]{1,0:T(8,128)S(1)}, u32[]{:S(2)}, u32[]{:S(2)}) collective-permute-start(f32[256,128]{1,0:T(8,128)S(1)} %get-tuple-element.46), channel_id=1, source_target_pairs={{0,2},{2,4},{4,6},{6,0},{1,3},{3,5},{5,7},{7,1},{8,10},{10,12},{12... | collective-permute-start | bytes 393224 | tf_op jit(solution)/shard_map/ppermute | solution.py:38
  43.0 3.7 %copy-start.2 = (f32[3,256,256]{2,1,0:T(8,128)S(1)}, f32[3,256,256]{2,1,0:T(8,128)}, u32[]{:S(2)}) copy-start(f32[3,256,256]{2,1,0:T(8,128)} %couplings_ref.1) | copy-start | bytes 2359300
  43.0 5.5 %collective-permute-start.3 = (f32[256,128]{1,0:T(8,128)S(1)}, f32[256,128]{1,0:T(8,128)S(1)}, u32[]{:S(2)}, u32[]{:S(2)}) collective-permute-start(f32[256,128]{1,0:T(8,128)S(1)} %get-tuple-element.47), channel_id=1, source_target_pairs={{0,6},{2,0},{4,2},{6,4},{1,7},{3,1},{5,3},{7,5},{8,14},{10,8},{12,... | collective-permute-start | bytes 393224 | tf_op jit(solution)/shard_map/ppermute | solution.py:38
  47.1 4.1 %copy-start.1 = (f32[32,32,4,128]{3,2,1,0:T(4,128)S(1)}, f32[32,32,4,128]{3,2,1,0:T(4,128)}, u32[]{:S(2)}) copy-start(f32[32,32,4,128]{3,2,1,0:T(4,128)} %param.4) | copy-start | bytes 6291460
  55.3 22.4 %collective-permute-start.4 = (f32[9,128,128]{2,1,0:T(8,128)S(1)}, f32[9,128,128]{2,1,0:T(8,128)S(1)}, u32[]{:S(2)}, u32[]{:S(2)}) collective-permute-start(f32[9,128,128]{2,1,0:T(8,128)S(1)} %get-tuple-element.53), channel_id=1, source_target_pairs={{0,1},{1,0},{2,3},{3,2},{4,5},{5,4},{6,7},{7,6},{8,9},{9,8},{10,11... | collective-permute-start | bytes 1769480 | tf_op jit(solution)/shard_map/ppermute | solution.py:38
  60.8 13.5 %collective-permute-start.6 = (f32[16,4,128]{2,1,0:T(4,128)S(1)}, f32[16,4,128]{2,1,0:T(4,128)S(1)}, u32[]{:S(2)}, u32[]{:S(2)}) collective-permute-start(f32[16,4,128]{2,1,0:T(4,128)S(1)} %get-tuple-element.54), channel_id=1, source_target_pairs={{0,2},{2,4},{4,6},{6,0},{1,3},{3,5},{5,7},{7,1},{8,10},{10,12},{12... | collective-permute-start | bytes 98312 | tf_op jit(solution)/shard_map/ppermute | solution.py:38
  60.8 13.5 %collective-permute-start.7 = (f32[16,4,128]{2,1,0:T(4,128)S(1)}, f32[16,4,128]{2,1,0:T(4,128)S(1)}, u32[]{:S(2)}, u32[]{:S(2)}) collective-permute-start(f32[16,4,128]{2,1,0:T(4,128)S(1)} %get-tuple-element.55), channel_id=1, source_target_pairs={{0,6},{2,0},{4,2},{6,4},{1,7},{3,1},{5,3},{7,5},{8,14},{10,8},{12,... | collective-permute-start | bytes 98312 | tf_op jit(solution)/shard_map/ppermute | solution.py:38
  72.2 16.9 %collective-permute-start.8 = (f32[9,128,128]{2,1,0:T(8,128)S(1)}, f32[9,128,128]{2,1,0:T(8,128)S(1)}, u32[]{:S(2)}, u32[]{:S(2)}) collective-permute-start(f32[9,128,128]{2,1,0:T(8,128)S(1)} %get-tuple-element.63), channel_id=1, source_target_pairs={{0,1},{1,0},{2,3},{3,2},{4,5},{5,4},{6,7},{7,6},{8,9},{9,8},{10,11... | collective-permute-start | bytes 1769480 | tf_op jit(solution)/shard_map/ppermute | solution.py:38
  77.8 3.5 %collective-permute-start.9 = (f32[23,4,128]{2,1,0:T(4,128)S(1)}, f32[23,4,128]{2,1,0:T(4,128)S(1)}, u32[]{:S(2)}, u32[]{:S(2)}) collective-permute-start(f32[23,4,128]{2,1,0:T(4,128)S(1)} %get-tuple-element.64), channel_id=1, source_target_pairs={{0,2},{2,4},{4,6},{6,0},{1,3},{3,5},{5,7},{7,1},{8,10},{10,12},{12... | collective-permute-start | bytes 141320 | tf_op jit(solution)/shard_map/ppermute | solution.py:38
  77.9 3.5 %collective-permute-start.10 = (f32[23,4,128]{2,1,0:T(4,128)S(1)}, f32[23,4,128]{2,1,0:T(4,128)S(1)}, u32[]{:S(2)}, u32[]{:S(2)}) collective-permute-start(f32[23,4,128]{2,1,0:T(4,128)S(1)} %get-tuple-element.65), channel_id=1, source_target_pairs={{0,6},{2,0},{4,2},{6,4},{1,7},{3,1},{5,3},{7,5},{8,14},{10,8},{12,... | collective-permute-start | bytes 141320 | tf_op jit(solution)/shard_map/ppermute | solution.py:38
  87.7 32.2 %collective-permute-start.17 = (f32[21,128,128]{2,1,0:T(8,128)S(1)}, f32[21,128,128]{2,1,0:T(8,128)S(1)}, u32[]{:S(2)}, u32[]{:S(2)}) collective-permute-start(f32[21,128,128]{2,1,0:T(8,128)S(1)} %get-tuple-element.66.after), channel_id=1, source_target_pairs={{0,1},{1,0},{2,3},{3,2},{4,5},{5,4},{6,7},{7,6},{8,9},{9,8},{10,11... | collective-permute-start | bytes 4128776 | tf_op jit(solution)/shard_map/ppermute | solution.py:38
  87.8 7.8 %collective-permute-start.12 = (f32[128,128]{1,0:T(8,128)S(1)}, f32[128,128]{1,0:T(8,128)S(1)}, u32[]{:S(2)}, u32[]{:S(2)}) collective-permute-start(f32[128,128]{1,0:T(8,128)S(1)} %get-tuple-element.69), channel_id=1, source_target_pairs={{8,0},{16,8},{24,16},{9,1},{17,9},{25,17},{10,2},{18,10},{26,18},{... | collective-permute-start | bytes 196616 | tf_op jit(solution)/shard_map/ppermute | solution.py:38
  89.2 7.8 %collective-permute-start.11 = (f32[128,128]{1,0:T(8,128)S(1)}, f32[128,128]{1,0:T(8,128)S(1)}, u32[]{:S(2)}, u32[]{:S(2)}) collective-permute-start(f32[128,128]{1,0:T(8,128)S(1)} %get-tuple-element.68), channel_id=1, source_target_pairs={{0,8},{8,16},{16,24},{1,9},{9,17},{17,25},{2,10},{10,18},{18,26},{... | collective-permute-start | bytes 196616 | tf_op jit(solution)/shard_map/ppermute | solution.py:38
  93.8 3.2 %collective-permute-start.13 = (f32[9,4,128]{2,1,0:T(4,128)S(1)}, f32[9,4,128]{2,1,0:T(4,128)S(1)}, u32[]{:S(2)}, u32[]{:S(2)}) collective-permute-start(f32[9,4,128]{2,1,0:T(4,128)S(1)} %get-tuple-element.70), channel_id=1, source_target_pairs={{0,2},{2,4},{4,6},{6,0},{1,3},{3,5},{5,7},{7,1},{8,10},{10,12},{12... | collective-permute-start | bytes 55304 | tf_op jit(solution)/shard_map/ppermute | solution.py:38
  95.4 1.7 %collective-permute-start.14 = (f32[9,4,128]{2,1,0:T(4,128)S(1)}, f32[9,4,128]{2,1,0:T(4,128)S(1)}, u32[]{:S(2)}, u32[]{:S(2)}) collective-permute-start(f32[9,4,128]{2,1,0:T(4,128)S(1)} %get-tuple-element.71), channel_id=1, source_target_pairs={{0,6},{2,0},{4,2},{6,4},{1,7},{3,1},{5,3},{7,5},{8,14},{10,8},{12,... | collective-permute-start | bytes 55304 | tf_op jit(solution)/shard_map/ppermute | solution.py:38
  101.8 27.9 %collective-permute-start.16 = (f32[7,128,128]{2,1,0:T(8,128)S(1)}, f32[7,128,128]{2,1,0:T(8,128)S(1)}, u32[]{:S(2)}, u32[]{:S(2)}) collective-permute-start(f32[7,128,128]{2,1,0:T(8,128)S(1)} %get-tuple-element.77), channel_id=1, source_target_pairs={{0,1},{1,0},{2,3},{3,2},{4,5},{5,4},{6,7},{7,6},{8,9},{9,8},{10,11... | collective-permute-start | bytes 1376264 | tf_op jit(solution)/shard_map/ppermute | solution.py:38
  103.9 31.5 %collective-permute-start.15 = (f32[4,128,128]{2,1,0:T(8,128)S(1)}, f32[4,128,128]{2,1,0:T(8,128)S(1)}, u32[]{:S(2)}, u32[]{:S(2)}) collective-permute-start(f32[4,128,128]{2,1,0:T(8,128)S(1)} %get-tuple-element.74), channel_id=1, source_target_pairs={{0,1},{1,0},{2,3},{3,2},{4,5},{5,4},{6,7},{7,6},{8,9},{9,8},{10,11... | collective-permute-start | bytes 786440 | tf_op jit(solution)/shard_map/ppermute | solution.py:38

commit v4 on v3

--- a/solution.py
+++ b/solution.py
@@ -218,7 +218,8 @@
     return [padded, weighed] + [pltpu.VMEM((group * rows, width), bf16)] * 4 + [pltpu.SemaphoreType.DMA((4,))]
 
 
-def first_body(depth, begin, count, sent_from, field, right, low_x, high_x, low_y, high_y, halves, diagonal, hi, lo, rest, part, *scratch):
+def first_body(depth, begin, count, sends, field, right, low_x, high_x, low_y, high_y, halves, diagonal, hi, lo, rest, *refs):
+    scratch = refs[1:] if sends else refs
     padded, weighed, sem = scratch[0], scratch[1], scratch[-1]
     planes, rows = field.shape[0], field.shape[1]
     low, high = max(begin - 1, 0), min(begin + count + 1, planes)
@@ -234,12 +235,11 @@
 
     def emit(at, out):
         rest[at] = right[begin + at] - out[:, :lanes]
-
-        @pl.when(at >= sent_from)
-        def _():
-            part[at - sent_from] = out[:, lanes:]
-
-    operate(depth, count, lambda i: (i + 1, begin + i), scratch[:-1], halves, diagonal, hi, lo, emit)
+        if sends:
+            refs[0][at] = out[:, lanes:]
+
+    used = pl.ds(0, 2 * lanes if sends else lanes)
+    operate(depth, count, lambda i: (i + 1, begin + i), scratch[:-1], halves, diagonal, hi.at[:, used], lo.at[:, used], emit)
 
 
 def sides_body(depth, planes, first, last):
@@ -281,11 +281,11 @@
     edge[...] = residual[0]
 
 
-def far_body(depth, skip, rest, came, after, residual, low, high, edge):
+def far_body(depth, rest, came, after, residual, low, high, edge):
     count, rows = came.shape[0], came.shape[1]
 
     def one(i, _):
-        value = rest[skip + i] - came[i]
+        value = rest[i] - came[i]
         residual[i] = value
         low[i] = value[:depth]
         high[i] = value[rows - depth :]
@@ -404,7 +404,7 @@
     start = start_field.reshape(flat)
     right = right_side.reshape(flat)
     begin = nx // 4
-    end = nx - begin
+    end = nx - begin - nx // 32
     held = end - begin
     taken = begin + 1
     ready = end - 1
@@ -416,7 +416,6 @@
         [((held,) + plane, f32)],
         [pltpu.SemaphoreType.DMA],
         in_specs=[pl.BlockSpec(memory_space=pltpu.HBM)],
-        out_specs=[anywhere],
         vmem=60 * 1024 * 1024,
         name="chosen",
     )(start)
@@ -455,20 +454,21 @@
         name="diagonal",
     )(low_x, high_x, low_y, high_y, halves)
 
-    def first(begin, count, sent_from, name):
+    def first(begin, count, sends, name):
         return call(
-            functools.partial(first_body, depth, begin, count, sent_from),
-            [((count,) + plane, f32), ((count - sent_from,) + plane, f32)],
+            functools.partial(first_body, depth, begin, count, sends),
+            [((count,) + plane, f32)] * (2 if sends else 1),
             scratch_for(count + 2, rows, width),
             in_specs=[anywhere] + [whole] * 9,
             work=count / 10,
             name=name,
         )(start, right, low_x, high_x, low_y, high_y, halves, diagonal, own_hi, own_lo)
 
-    rest_a, part_a = first(0, taken, 0, "first_a")
+    rest_a, part_a = first(0, taken, True, "first_a")
     came_a = sent(part_a, "ma", 1, True)
-    rest_b, part_b = first(taken, nx - taken, ready - taken, "first_b")
+    rest_b, part_b = first(ready, nx - ready, True, "first_b")
     came_b = sent(part_b, "ma", 1, True)
+    (rest_c,) = first(taken, ready - taken, False, "first_c")
 
     strip = lambda count: ((count, depth, modes), f32)
     raw_first, raw_last = call(
@@ -484,7 +484,7 @@
         in_specs=[anywhere] + [whole] * 7,
         work=(held - 2) / 12,
         name="middle",
-    )(raw, raw_low, raw_high, halves, diagonal, rest_b, other_hi, other_lo)
+    )(raw, raw_low, raw_high, halves, diagonal, rest_c, other_hi, other_lo)
     near, low_a, high_a, edge_first = call(
         functools.partial(near_body, depth),
         near_shapes + [(plane, f32)],
@@ -511,7 +511,7 @@
 
     remaining = nx - ready
     far, low_b, high_b, edge_last = call(
-        functools.partial(far_body, depth, ready - taken),
+        functools.partial(far_body, depth),
         [((remaining,) + plane, f32), strip(remaining), strip(remaining), (plane, f32)],
         [],
         in_specs=[whole] * 2 + [anywhere],

time: 137 us -> 100 us (0.73)
  Pallas kernels: 70.5 us -> 36 us
  waiting for transfers between devices: 37.8 us -> 35.2 us
    pallas_call x1, Pallas kernels: 32.9 us -> 2.3 us  [shards(): call(functools.partial(chosen_body, begin), [((held,) + plane, f32)], [pl...]
    pallas_call x3 -> x4, Pallas kernels: 13.8 us -> 9.91 us  [the longest x3 9.81 us: first(): call(functools.partial(first_body, depth, begin, count, sends), [((count,...]
    ppermute x18, waiting for transfers between devices: 37.8 us -> 35.2 us  [sent(): return lax.ppermute(array, axis, pairs)]
  transfers between devices with their start and end apart: 18 -> 18, of which waited for: 7 -> 9; matrix products, arithmetic and copies ran while one was open for 1% -> 0% of each run, Pallas kernels for 27% -> 33%
where the time goes in v4:
time: 100 us; the launch traced here: 99.4 us
  Pallas kernels  36 us (36%)
  waiting for transfers between devices  35.2 us (35%)
  starting transfers between devices  26.6 us (27%)
  between operations  1.07 us (1%)
    ppermute x18, waiting for transfers between devices, sent(): return lax.ppermute(array, axis, pairs)  35.2 us
    ppermute x18, starting transfers between devices, sent(): return lax.ppermute(array, axis, pairs)  26.6 us
    pallas_call x3, Pallas kernels, first(): call(functools.partial(first_body, depth, begin, count, sends), [((count,...  9.81 us
    pallas_call x1, Pallas kernels, shards(): call(functools.partial(second_body, depth, 1, count), [((count,) + plane,...  5.66 us
    pallas_call x1, Pallas kernels, shards(): call(functools.partial(third_body, depth, done), [((count - final,) + pla...  4.91 us
    pallas_call x1, Pallas kernels, shards(): call(functools.partial(middle_body, depth, taken), near_shapes, scratch_f...  3.98 us
    pallas_call x3, Pallas kernels, add_last(): call(functools.partial(last_body, first), [(shape, f32)] * 2, [pltpu.VMEM...  3.96 us
    pallas_call x1, Pallas kernels, shards(): call(functools.partial(diagonal_body, depth), [(halves_shape, f32), ((3,)...  2.67 us
  transfers between devices with their start and end apart: 18, of which 9 were waited for; matrix products, arithmetic and copies ran while one was open for 0% of the time, Pallas kernels for 33%

profile of v4, /device:TPU:0, one launch (start us, length us, event | category | flops | bytes accessed | tf_op | source)
XLA Modules:
  0.0 99.4 jit_solution(8623549893761442426)
XLA Ops:
  0.6 2.3 %chosen.1 = f32[15,128,128]{2,1,0:T(8,128)} custom-call(f32[32,128,128]{2,1,0:T(8,128)} %bitcast.6), custom_call_target="tpu_custom_call" | custom-call | flops 1000000000 | bytes 2000000 | tf_op jit(solution)/shard_map/chosen/pallas_call | solution.py:414
  3.0 3.0 %collective-permute-start.5 = (f32[15,128,128]{2,1,0:T(8,128)}, f32[15,128,128]{2,1,0:T(8,128)S(1)}, u32[]{:S(2)}, u32[]{:S(2)}) collective-permute-start(f32[15,128,128]{2,1,0:T(8,128)} %chosen.1), channel_id=1, source_target_pairs={{0,1},{1,0},{2,3},{3,2},{4,5},{5,4},{6,7},{7,6},{8,9},{9,8},{10,11... | collective-permute-start | bytes 2949128 | tf_op jit(solution)/shard_map/ppermute | solution.py:38
  6.7 3.5 %collective-permute-start = (f32[256,128]{1,0:T(8,128)S(1)}, f32[256,128]{1,0:T(8,128)S(1)}, u32[]{:S(2)}, u32[]{:S(2)}) collective-permute-start(f32[256,128]{1,0:T(8,128)S(1)} %get-tuple-element.44), channel_id=1, source_target_pairs={{0,8},{8,16},{16,24},{1,9},{9,17},{17,25},{2,10},{10,18},{18,26},{... | collective-permute-start | bytes 393224 | tf_op jit(solution)/shard_map/ppermute | solution.py:38
  11.5 1.7 %collective-permute-start.3 = (f32[256,128]{1,0:T(8,128)S(1)}, f32[256,128]{1,0:T(8,128)S(1)}, u32[]{:S(2)}, u32[]{:S(2)}) collective-permute-start(f32[256,128]{1,0:T(8,128)S(1)} %get-tuple-element.47), channel_id=1, source_target_pairs={{0,6},{2,0},{4,2},{6,4},{1,7},{3,1},{5,3},{7,5},{8,14},{10,8},{12,... | collective-permute-start | bytes 393224 | tf_op jit(solution)/shard_map/ppermute | solution.py:38
  13.3 1.9 %halves.1.halves_in = f32[3,34,144,128]{3,2,1,0:T(8,128)S(1)} custom-call(f32[96,128]{1,0:T(8,128)S(1)} %copy.16.coef), custom_call_target="tpu_custom_call" | custom-call | flops 1000000000 | bytes 2000000 | tf_op jit(solution)/shard_map/halves/pallas_call | solution.py:447
  17.0 2.7 %diagonal.1 = (f32[3,34,144,128]{3,2,1,0:T(8,128)S(1)}, f32[3,32,128,128]{3,2,1,0:T(8,128)S(1)}) custom-call(f32[256,128]{1,0:T(8,128)S(1)} %collective-permute-done.low_x, f32[256,128]{1,0:T(8,128)S(1)} %collective-permute-done.1.high_x, f32[256,128]{1,0:T(8,128)S(1)} %collective-permute-done.2.low_y, ...), custom_call_target="tpu_custom_call", output_to_operand_aliasing={{0}: (4, {})} | custom-call | flops 1000000000 | bytes 2000000 | tf_op jit(solution)/shard_map/diagonal/pallas_call | solution.py:448
  19.7 3.0 %first_a.1 = (f32[9,128,128]{2,1,0:T(8,128)S(1)}, f32[9,128,128]{2,1,0:T(8,128)S(1)}) custom-call(f32[32,128,128]{2,1,0:T(8,128)S(1)} %bitcast.8, f32[32,128,128]{2,1,0:T(8,128)S(1)} %bitcast.13, f32[256,128]{1,0:T(8,128)S(1)} %collective-permute-done.low_x, f32[256,128]{1,0:T(8,128)S(1)} %collective-permute-done.1.high_x, ...), custom_call_target="tpu_custom_call" | custom-call | flops 900000000 | bytes 1800000 | tf_op jit(solution)/shard_map/first_a/pallas_call | solution.py:458
  23.3 2.9 %first_b.1 = (f32[10,128,128]{2,1,0:T(8,128)S(1)}, f32[10,128,128]{2,1,0:T(8,128)S(1)}) custom-call(f32[32,128,128]{2,1,0:T(8,128)S(1)} %bitcast.9, f32[32,128,128]{2,1,0:T(8,128)S(1)} %bitcast.14, f32[256,128]{1,0:T(8,128)S(1)} %collective-permute-done.low_x, f32[256,128]{1,0:T(8,128)S(1)} %collective-permute-done.1.high_x, ...), custom_call_target="tpu_custom_call" | custom-call | flops 1000000000 | bytes 2000000 | tf_op jit(solution)/shard_map/first_b/pallas_call | solution.py:458
  26.2 1.6 %collective-permute-start.8 = (f32[10,128,128]{2,1,0:T(8,128)S(1)}, f32[10,128,128]{2,1,0:T(8,128)S(1)}, u32[]{:S(2)}, u32[]{:S(2)}) collective-permute-start(f32[10,128,128]{2,1,0:T(8,128)S(1)} %get-tuple-element.63), channel_id=1, source_target_pairs={{0,1},{1,0},{2,3},{3,2},{4,5},{5,4},{6,7},{7,6},{8,9},{9,8},{10,11... | collective-permute-start | bytes 1966088 | tf_op jit(solution)/shard_map/ppermute | solution.py:38
  28.9 1.7 %collective-permute-start.7 = (f32[15,4,128]{2,1,0:T(4,128)S(1)}, f32[15,4,128]{2,1,0:T(4,128)S(1)}, u32[]{:S(2)}, u32[]{:S(2)}) collective-permute-start(f32[15,4,128]{2,1,0:T(4,128)S(1)} %get-tuple-element.55), channel_id=1, source_target_pairs={{0,6},{2,0},{4,2},{6,4},{1,7},{3,1},{5,3},{7,5},{8,14},{10,8},{12,... | collective-permute-start | bytes 92168 | tf_op jit(solution)/shard_map/ppermute | solution.py:38
  30.6 3.9 %first_c.1.rest = f32[13,128,128]{2,1,0:T(8,128)S(1)} custom-call(f32[32,128,128]{2,1,0:T(8,128)S(1)} %bitcast.10, f32[32,128,128]{2,1,0:T(8,128)S(1)} %bitcast.15, f32[256,128]{1,0:T(8,128)S(1)} %collective-permute-done.low_x, f32[256,128]{1,0:T(8,128)S(1)} %collective-permute-done.1.high_x, f32[256,128]{1,0:T(8,128)S(1)} %collective-permute-done.2.low_y, ...), custom_call_target="tpu_custom_call" | custom-call | flops 1300000000 | bytes 2600000 | tf_op jit(solution)/shard_map/first_c/pallas_call | solution.py:458
  34.5 4.0 %middle.1 = (f32[22,128,128]{2,1,0:T(8,128)S(1)}, f32[22,4,128]{2,1,0:T(4,128)S(1)}, f32[22,4,128]{2,1,0:T(4,128)S(1)}) custom-call(f32[15,128,128]{2,1,0:T(8,128)S(1)} %collective-permute-done.5.planes.other, f32[15,4,128]{2,1,0:T(4,128)S(1)} %collective-permute-done.6.low_y, f32[15,4,128]{2,1,0:T(4,128)S(1)} %collective-permute-done.7.high_y, ...), custom_call_target="tpu_custom_call" | custom-call | flops 1083333376 | bytes 2166666 | tf_op jit(solution)/shard_map/middle/pallas_call | solution.py:480
  38.5 2.9 %collective-permute-done.4.came = f32[9,128,128]{2,1,0:T(8,128)S(1)} collective-permute-done((f32[9,128,128]{2,1,0:T(8,128)S(1)}, f32[9,128,128]{2,1,0:T(8,128)S(1)}, u32[]{:S(2)}, u32[]{:S(2)}) %collective-permute-start.4) | collective-permute-done | bytes 589856 | tf_op jit(solution)/shard_map/ppermute | solution.py:38
  41.6 1.7 %collective-permute-start.10 = (f32[22,4,128]{2,1,0:T(4,128)S(1)}, f32[22,4,128]{2,1,0:T(4,128)S(1)}, u32[]{:S(2)}, u32[]{:S(2)}) collective-permute-start(f32[22,4,128]{2,1,0:T(4,128)S(1)} %get-tuple-element.65), channel_id=1, source_target_pairs={{0,6},{2,0},{4,2},{6,4},{1,7},{3,1},{5,3},{7,5},{8,14},{10,8},{12,... | collective-permute-start | bytes 135176 | tf_op jit(solution)/shard_map/ppermute | solution.py:38
  43.3 1.7 %collective-permute-done.9.low_y.low_a = f32[22,4,128]{2,1,0:T(4,128)S(1)} collective-permute-done((f32[22,4,128]{2,1,0:T(4,128)S(1)}, f32[22,4,128]{2,1,0:T(4,128)S(1)}, u32[]{:S(2)}, u32[]{:S(2)}) %collective-permute-start.9) | collective-permute-done | bytes 45088 | tf_op jit(solution)/shard_map/ppermute | solution.py:38
  45.1 5.7 %second.1 = (f32[20,128,128]{2,1,0:T(8,128)S(1)}, f32[20,128,128]{2,1,0:T(8,128)S(1)}, f32[20,128,128]{2,1,0:T(8,128)S(1)}) custom-call(f32[22,128,128]{2,1,0:T(8,128)S(1)} %get-tuple-element.61.residual.near, f32[32,128,128]{2,1,0:T(8,128)S(1)} %bitcast.11, f32[22,4,128]{2,1,0:T(4,128)S(1)} %collective-permute-done.9.low_y.low_a, ...), custom_call_target="tpu_custom_call" | custom-call | flops 2000000000 | bytes 4000000 | tf_op jit(solution)/shard_map/second/pallas_call | solution.py:502
  50.7 2.1 %collective-permute-start.17 = (f32[20,128,128]{2,1,0:T(8,128)S(1)}, f32[20,128,128]{2,1,0:T(8,128)S(1)}, u32[]{:S(2)}, u32[]{:S(2)}) collective-permute-start(f32[20,128,128]{2,1,0:T(8,128)S(1)} %get-tuple-element.66.after), channel_id=1, source_target_pairs={{0,1},{1,0},{2,3},{3,2},{4,5},{5,4},{6,7},{7,6},{8,9},{9,8},{10,11... | collective-permute-start | bytes 3932168 | tf_op jit(solution)/shard_map/ppermute | solution.py:38
  54.8 4.1 %collective-permute-start.11 = (f32[128,128]{1,0:T(8,128)S(1)}, f32[128,128]{1,0:T(8,128)S(1)}, u32[]{:S(2)}, u32[]{:S(2)}) collective-permute-start(f32[128,128]{1,0:T(8,128)S(1)} %get-tuple-element.68), channel_id=1, source_target_pairs={{0,8},{8,16},{16,24},{1,9},{9,17},{17,25},{2,10},{10,18},{18,26},{... | collective-permute-start | bytes 196616 | tf_op jit(solution)/shard_map/ppermute | solution.py:38
  60.6 1.5 %collective-permute-done.13.low_b = f32[10,4,128]{2,1,0:T(4,128)S(1)} collective-permute-done((f32[10,4,128]{2,1,0:T(4,128)S(1)}, f32[10,4,128]{2,1,0:T(4,128)S(1)}, u32[]{:S(2)}, u32[]{:S(2)}) %collective-permute-start.13) | collective-permute-done | bytes 20512 | tf_op jit(solution)/shard_map/ppermute | solution.py:38
  62.1 4.9 %third.1 = (f32[8,128,128]{2,1,0:T(8,128)S(1)}, f32[8,128,128]{2,1,0:T(8,128)S(1)}, f32[8,128,128]{2,1,0:T(8,128)S(1)}, f32[4,128,128]{2,1,0:T(8,128)S(1)}, f32[...) custom-call(f32[22,128,128]{2,1,0:T(8,128)S(1)} %get-tuple-element.61.residual.near, ...), custom_call_target="tpu_custom_call" | custom-call | flops 6000000000 | bytes 12000000 | tf_op jit(solution)/shard_map/third/pallas_call | solution.py:527
  69.1 12.4 %collective-permute-done.17.came = f32[20,128,128]{2,1,0:T(8,128)S(1)} collective-permute-done((f32[20,128,128]{2,1,0:T(8,128)S(1)}, f32[20,128,128]{2,1,0:T(8,128)S(1)}, u32[]{:S(2)}, u32[]{:S(2)}) %collective-permute-start.17) | collective-permute-done | bytes 1310752 | tf_op jit(solution)/shard_map/ppermute | solution.py:38
  81.5 1.9 %last.3 = (f32[32,128,128]{2,1,0:T(8,128)}, f32[32,128,128]{2,1,0:T(8,128)}) custom-call(f32[20,128,128]{2,1,0:T(8,128)S(1)} %get-tuple-element.78.later_part, f32[20,128,128]{2,1,0:T(8,128)S(1)} %get-tuple-element.79.fields_part, f32[20,128,128]{2,1,0:T(8,128)S(1)} %collective-permute-done.17.came), custom_call_target="tpu_custom_call" | custom-call | flops 200000000 | bytes 400000 | tf_op jit(solution)/shard_map/last/pallas_call | solution.py:387
  83.4 9.3 %collective-permute-done.16.came = f32[8,128,128]{2,1,0:T(8,128)S(1)} collective-permute-done((f32[8,128,128]{2,1,0:T(8,128)S(1)}, f32[8,128,128]{2,1,0:T(8,128)S(1)}, u32[]{:S(2)}, u32[]{:S(2)}) %collective-permute-start.16) | collective-permute-done | bytes 524320 | tf_op jit(solution)/shard_map/ppermute | solution.py:38
  93.9 4.4 %collective-permute-done.15.came = f32[4,128,128]{2,1,0:T(8,128)S(1)} collective-permute-done((f32[4,128,128]{2,1,0:T(8,128)S(1)}, f32[4,128,128]{2,1,0:T(8,128)S(1)}, u32[]{:S(2)}, u32[]{:S(2)}) %collective-permute-start.15) | collective-permute-done | bytes 262176 | tf_op jit(solution)/shard_map/ppermute | solution.py:38
  (40 shorter events, 13.5 us)
Async XLA Ops:
  0.6 5.4 %copy-start.3 = (f32[3,32,32,4]{2,3,1,0:T(4,128)S(1)}, f32[3,32,32,4]{2,3,1,0:T(4,128)}, u32[]{:S(2)}) copy-start(f32[3,32,32,4]{2,3,1,0:T(4,128)} %param.6) | copy-start | bytes 147460
  0.6 5.8 %copy-start = (f32[32,32,4,128]{3,2,1,0:T(4,128)S(1)}, f32[32,32,4,128]{3,2,1,0:T(4,128)}, u32[]{:S(2)}) copy-start(f32[32,32,4,128]{3,2,1,0:T(4,128)} %param.5) | copy-start | bytes 6291460
  3.0 25.8 %collective-permute-start.5 = (f32[15,128,128]{2,1,0:T(8,128)}, f32[15,128,128]{2,1,0:T(8,128)S(1)}, u32[]{:S(2)}, u32[]{:S(2)}) collective-permute-start(f32[15,128,128]{2,1,0:T(8,128)} %chosen.1), channel_id=1, source_target_pairs={{0,1},{1,0},{2,3},{3,2},{4,5},{5,4},{6,7},{7,6},{8,9},{9,8},{10,11... | collective-permute-start | bytes 2949128 | tf_op jit(solution)/shard_map/ppermute | solution.py:38
  6.7 9.0 %collective-permute-start = (f32[256,128]{1,0:T(8,128)S(1)}, f32[256,128]{1,0:T(8,128)S(1)}, u32[]{:S(2)}, u32[]{:S(2)}) collective-permute-start(f32[256,128]{1,0:T(8,128)S(1)} %get-tuple-element.44), channel_id=1, source_target_pairs={{0,8},{8,16},{16,24},{1,9},{9,17},{17,25},{2,10},{10,18},{18,26},{... | collective-permute-start | bytes 393224 | tf_op jit(solution)/shard_map/ppermute | solution.py:38
  10.2 6.9 %collective-permute-start.1 = (f32[256,128]{1,0:T(8,128)S(1)}, f32[256,128]{1,0:T(8,128)S(1)}, u32[]{:S(2)}, u32[]{:S(2)}) collective-permute-start(f32[256,128]{1,0:T(8,128)S(1)} %get-tuple-element.45), channel_id=1, source_target_pairs={{8,0},{16,8},{24,16},{9,1},{17,9},{25,17},{10,2},{18,10},{26,18},{... | collective-permute-start | bytes 393224 | tf_op jit(solution)/shard_map/ppermute | solution.py:38
  11.5 5.6 %collective-permute-start.2 = (f32[256,128]{1,0:T(8,128)S(1)}, f32[256,128]{1,0:T(8,128)S(1)}, u32[]{:S(2)}, u32[]{:S(2)}) collective-permute-start(f32[256,128]{1,0:T(8,128)S(1)} %get-tuple-element.46), channel_id=1, source_target_pairs={{0,2},{2,4},{4,6},{6,0},{1,3},{3,5},{5,7},{7,1},{8,10},{10,12},{12... | collective-permute-start | bytes 393224 | tf_op jit(solution)/shard_map/ppermute | solution.py:38
  11.5 3.7 %copy-start.2 = (f32[3,256,256]{2,1,0:T(8,128)S(1)}, f32[3,256,256]{2,1,0:T(8,128)}, u32[]{:S(2)}) copy-start(f32[3,256,256]{2,1,0:T(8,128)} %couplings_ref.1) | copy-start | bytes 2359300
  11.5 5.5 %collective-permute-start.3 = (f32[256,128]{1,0:T(8,128)S(1)}, f32[256,128]{1,0:T(8,128)S(1)}, u32[]{:S(2)}, u32[]{:S(2)}) collective-permute-start(f32[256,128]{1,0:T(8,128)S(1)} %get-tuple-element.47), channel_id=1, source_target_pairs={{0,6},{2,0},{4,2},{6,4},{1,7},{3,1},{5,3},{7,5},{8,14},{10,8},{12,... | collective-permute-start | bytes 393224 | tf_op jit(solution)/shard_map/ppermute | solution.py:38
  15.6 4.1 %copy-start.1 = (f32[32,32,4,128]{3,2,1,0:T(4,128)S(1)}, f32[32,32,4,128]{3,2,1,0:T(4,128)}, u32[]{:S(2)}) copy-start(f32[32,32,4,128]{3,2,1,0:T(4,128)} %param.4) | copy-start | bytes 6291460
  22.7 18.7 %collective-permute-start.4 = (f32[9,128,128]{2,1,0:T(8,128)S(1)}, f32[9,128,128]{2,1,0:T(8,128)S(1)}, u32[]{:S(2)}, u32[]{:S(2)}) collective-permute-start(f32[9,128,128]{2,1,0:T(8,128)S(1)} %get-tuple-element.53), channel_id=1, source_target_pairs={{0,1},{1,0},{2,3},{3,2},{4,5},{5,4},{6,7},{7,6},{8,9},{9,8},{10,11... | collective-permute-start | bytes 1769480 | tf_op jit(solution)/shard_map/ppermute | solution.py:38
  26.2 28.5 %collective-permute-start.8 = (f32[10,128,128]{2,1,0:T(8,128)S(1)}, f32[10,128,128]{2,1,0:T(8,128)S(1)}, u32[]{:S(2)}, u32[]{:S(2)}) collective-permute-start(f32[10,128,128]{2,1,0:T(8,128)S(1)} %get-tuple-element.63), channel_id=1, source_target_pairs={{0,1},{1,0},{2,3},{3,2},{4,5},{5,4},{6,7},{7,6},{8,9},{9,8},{10,11... | collective-permute-start | bytes 1966088 | tf_op jit(solution)/shard_map/ppermute | solution.py:38
  28.8 5.7 %collective-permute-start.6 = (f32[15,4,128]{2,1,0:T(4,128)S(1)}, f32[15,4,128]{2,1,0:T(4,128)S(1)}, u32[]{:S(2)}, u32[]{:S(2)}) collective-permute-start(f32[15,4,128]{2,1,0:T(4,128)S(1)} %get-tuple-element.54), channel_id=1, source_target_pairs={{0,2},{2,4},{4,6},{6,0},{1,3},{3,5},{5,7},{7,1},{8,10},{10,12},{12... | collective-permute-start | bytes 92168 | tf_op jit(solution)/shard_map/ppermute | solution.py:38
  28.9 5.7 %collective-permute-start.7 = (f32[15,4,128]{2,1,0:T(4,128)S(1)}, f32[15,4,128]{2,1,0:T(4,128)S(1)}, u32[]{:S(2)}, u32[]{:S(2)}) collective-permute-start(f32[15,4,128]{2,1,0:T(4,128)S(1)} %get-tuple-element.55), channel_id=1, source_target_pairs={{0,6},{2,0},{4,2},{6,4},{1,7},{3,1},{5,3},{7,5},{8,14},{10,8},{12,... | collective-permute-start | bytes 92168 | tf_op jit(solution)/shard_map/ppermute | solution.py:38
  41.5 3.5 %collective-permute-start.9 = (f32[22,4,128]{2,1,0:T(4,128)S(1)}, f32[22,4,128]{2,1,0:T(4,128)S(1)}, u32[]{:S(2)}, u32[]{:S(2)}) collective-permute-start(f32[22,4,128]{2,1,0:T(4,128)S(1)} %get-tuple-element.64), channel_id=1, source_target_pairs={{0,2},{2,4},{4,6},{6,0},{1,3},{3,5},{5,7},{7,1},{8,10},{10,12},{12... | collective-permute-start | bytes 135176 | tf_op jit(solution)/shard_map/ppermute | solution.py:38
  41.6 3.5 %collective-permute-start.10 = (f32[22,4,128]{2,1,0:T(4,128)S(1)}, f32[22,4,128]{2,1,0:T(4,128)S(1)}, u32[]{:S(2)}, u32[]{:S(2)}) collective-permute-start(f32[22,4,128]{2,1,0:T(4,128)S(1)} %get-tuple-element.65), channel_id=1, source_target_pairs={{0,6},{2,0},{4,2},{6,4},{1,7},{3,1},{5,3},{7,5},{8,14},{10,8},{12,... | collective-permute-start | bytes 135176 | tf_op jit(solution)/shard_map/ppermute | solution.py:38
  50.7 30.7 %collective-permute-start.17 = (f32[20,128,128]{2,1,0:T(8,128)S(1)}, f32[20,128,128]{2,1,0:T(8,128)S(1)}, u32[]{:S(2)}, u32[]{:S(2)}) collective-permute-start(f32[20,128,128]{2,1,0:T(8,128)S(1)} %get-tuple-element.66.after), channel_id=1, source_target_pairs={{0,1},{1,0},{2,3},{3,2},{4,5},{5,4},{6,7},{7,6},{8,9},{9,8},{10,11... | collective-permute-start | bytes 3932168 | tf_op jit(solution)/shard_map/ppermute | solution.py:38
  52.8 9.3 %collective-permute-start.12 = (f32[128,128]{1,0:T(8,128)S(1)}, f32[128,128]{1,0:T(8,128)S(1)}, u32[]{:S(2)}, u32[]{:S(2)}) collective-permute-start(f32[128,128]{1,0:T(8,128)S(1)} %get-tuple-element.69), channel_id=1, source_target_pairs={{8,0},{16,8},{24,16},{9,1},{17,9},{25,17},{10,2},{18,10},{26,18},{... | collective-permute-start | bytes 196616 | tf_op jit(solution)/shard_map/ppermute | solution.py:38
  54.8 7.4 %collective-permute-start.11 = (f32[128,128]{1,0:T(8,128)S(1)}, f32[128,128]{1,0:T(8,128)S(1)}, u32[]{:S(2)}, u32[]{:S(2)}) collective-permute-start(f32[128,128]{1,0:T(8,128)S(1)} %get-tuple-element.68), channel_id=1, source_target_pairs={{0,8},{8,16},{16,24},{1,9},{9,17},{17,25},{2,10},{10,18},{18,26},{... | collective-permute-start | bytes 196616 | tf_op jit(solution)/shard_map/ppermute | solution.py:38
  58.8 3.3 %collective-permute-start.13 = (f32[10,4,128]{2,1,0:T(4,128)S(1)}, f32[10,4,128]{2,1,0:T(4,128)S(1)}, u32[]{:S(2)}, u32[]{:S(2)}) collective-permute-start(f32[10,4,128]{2,1,0:T(4,128)S(1)} %get-tuple-element.70), channel_id=1, source_target_pairs={{0,2},{2,4},{4,6},{6,0},{1,3},{3,5},{5,7},{7,1},{8,10},{10,12},{12... | collective-permute-start | bytes 61448 | tf_op jit(solution)/shard_map/ppermute | solution.py:38
  59.9 2.2 %collective-permute-start.14 = (f32[10,4,128]{2,1,0:T(4,128)S(1)}, f32[10,4,128]{2,1,0:T(4,128)S(1)}, u32[]{:S(2)}, u32[]{:S(2)}) collective-permute-start(f32[10,4,128]{2,1,0:T(4,128)S(1)} %get-tuple-element.71), channel_id=1, source_target_pairs={{0,6},{2,0},{4,2},{6,4},{1,7},{3,1},{5,3},{7,5},{8,14},{10,8},{12,... | collective-permute-start | bytes 61448 | tf_op jit(solution)/shard_map/ppermute | solution.py:38
  67.0 25.7 %collective-permute-start.16 = (f32[8,128,128]{2,1,0:T(8,128)S(1)}, f32[8,128,128]{2,1,0:T(8,128)S(1)}, u32[]{:S(2)}, u32[]{:S(2)}) collective-permute-start(f32[8,128,128]{2,1,0:T(8,128)S(1)} %get-tuple-element.77), channel_id=1, source_target_pairs={{0,1},{1,0},{2,3},{3,2},{4,5},{5,4},{6,7},{7,6},{8,9},{9,8},{10,11... | collective-permute-start | bytes 1572872 | tf_op jit(solution)/shard_map/ppermute | solution.py:38
  68.3 30.1 %collective-permute-start.15 = (f32[4,128,128]{2,1,0:T(8,128)S(1)}, f32[4,128,128]{2,1,0:T(8,128)S(1)}, u32[]{:S(2)}, u32[]{:S(2)}) collective-permute-start(f32[4,128,128]{2,1,0:T(8,128)S(1)} %get-tuple-element.74), channel_id=1, source_target_pairs={{0,1},{1,0},{2,3},{3,2},{4,5},{5,4},{6,7},{7,6},{8,9},{9,8},{10,11... | collective-permute-start | bytes 786440 | tf_op jit(solution)/shard_map/ppermute | solution.py:38

commit v5 on v4

--- a/solution.py
+++ b/solution.py
@@ -12,6 +12,7 @@
 group = 2
 pad = 8
 vmem_bytes = 12 * 1024 * 1024
+most_bytes = 60 * 1024 * 1024
 f32 = jnp.float32
 bf16 = jnp.bfloat16
 whole = pl.BlockSpec(memory_space=pltpu.VMEM)
@@ -26,7 +27,7 @@
         out_specs=out_specs if out_specs is not None else [whole] * len(out_shapes),
         scratch_shapes=scratch,
         input_output_aliases=aliases or {},
-        cost_estimate=pl.CostEstimate(flops=int(work * 1e9), bytes_accessed=int(work * 2e6), transcendentals=0),
+        cost_estimate=pl.CostEstimate(flops=int(work * 1e6), bytes_accessed=int(work * 2e3), transcendentals=0),
         compiler_params=pltpu.CompilerParams(vmem_limit_bytes=vmem),
         name=name,
     )
@@ -57,7 +58,8 @@
         other_lo[rows, :] = (other - top.astype(f32)).astype(bf16)
 
 
-def chosen_body(begin, field, out, sem):
+def chosen_body(begin, field, *refs):
+    out, sem = refs[-2:]
     copy = pltpu.make_async_copy(field.at[pl.ds(begin, out.shape[0])], out, sem)
     copy.start()
     copy.wait()
@@ -202,159 +204,126 @@
         padded[local + i, pad + rows : pad + rows + depth, :] = high[at]
 
 
-def loads(pieces, padded, sem):
-    rows = padded.shape[1] - 2 * pad
-    copies = []
-    for number, (source, start, count, local) in enumerate(pieces):
-        target = padded.at[pl.ds(local, count), pl.ds(pad, rows), :]
-        copies.append(pltpu.make_async_copy(source.at[pl.ds(start, count)], target, sem.at[number]))
-        copies[-1].start()
-    return copies
-
-
 def scratch_for(locals_, rows, width):
     padded = pltpu.VMEM((locals_, rows + 2 * pad, lanes), f32)
     weighed = pltpu.VMEM((3, locals_, rows + 2 * pad, lanes), f32)
-    return [padded, weighed] + [pltpu.VMEM((group * rows, width), bf16)] * 4 + [pltpu.SemaphoreType.DMA((4,))]
-
-
-def first_body(depth, begin, count, sends, field, right, low_x, high_x, low_y, high_y, halves, diagonal, hi, lo, rest, *refs):
-    scratch = refs[1:] if sends else refs
+    return [padded, weighed] + [pltpu.VMEM((group * rows, width), bf16)] * 4 + [pltpu.SemaphoreType.DMA((8,))]
+
+
+class Run:
+    def __init__(self, local, plane, count):
+        self.local, self.plane, self.count = local, plane, count
+
+
+def planes_body(depth, names, outs, pieces, edges, layers, runs, sends, emit, *refs):
+    named = dict(zip(names + outs, refs))
+    scratch = refs[len(names) + len(outs) :]
     padded, weighed, sem = scratch[0], scratch[1], scratch[-1]
-    planes, rows = field.shape[0], field.shape[1]
-    low, high = max(begin - 1, 0), min(begin + count + 1, planes)
-    copies = loads([(field, low, high - low, low - begin + 1)], padded, sem)
-    if begin == 0:
-        padded[0, pad : pad + rows, :] = low_x[:rows]
-    if begin + count == planes:
-        padded[count + 1, pad : pad + rows, :] = high_x[:rows]
-    strips(padded, 1, count, depth, low_y, high_y, begin, True)
+    rows = padded.shape[1] - 2 * pad
+    halves, diagonal = named["halves"], named["diagonal"]
+    copies = []
+    for number, (source, first, count, local) in enumerate(pieces):
+        target = padded.at[pl.ds(local, count), pl.ds(pad, rows), :]
+        copies.append(pltpu.make_async_copy(named[source].at[pl.ds(first, count)], target, sem.at[number]))
+        copies[-1].start()
+    for source, local in edges:
+        padded[local, pad : pad + rows, :] = named[source][:rows]
+    for low, high, first, count, local, stacked in layers:
+        strips(padded, local, count, depth, named[low], named[high], first, stacked)
     for copy in copies:
         copy.wait()
-    weigh(padded, halves, weighed, 0, begin, count + 2)
-
-    def emit(at, out):
-        rest[at] = right[begin + at] - out[:, :lanes]
-        if sends:
-            refs[0][at] = out[:, lanes:]
+    for run in runs:
+        weigh(padded, halves, weighed, run.local - 1, run.plane, run.count + 2)
+    total = sum(run.count for run in runs)
+
+    def place(i):
+        local, plane = i + runs[0].local, i + runs[0].plane
+        if len(runs) > 1:
+            later = i >= runs[0].count
+            local = jnp.where(later, i - runs[0].count + runs[1].local, local)
+            plane = jnp.where(later, i - runs[0].count + runs[1].plane, plane)
+        return local, plane
+
+    def put(i, out):
+        local, plane = place(i)
+        emit(named, i, plane, out, padded, local, rows)
 
     used = pl.ds(0, 2 * lanes if sends else lanes)
-    operate(depth, count, lambda i: (i + 1, begin + i), scratch[:-1], halves, diagonal, hi.at[:, used], lo.at[:, used], emit)
-
-
-def sides_body(depth, planes, first, last):
+    operate(depth, total, place, scratch[:-1], halves, diagonal, named["hi"].at[:, used], named["lo"].at[:, used], put)
+
+
+def own_emit(named, i, plane, out, padded, local, rows):
+    named["rest"][i] = named["right"][plane] - out
+
+
+def middle_emit(depth, named, i, plane, out, padded, local, rows):
+    value = named["rest"][i] - out
+    named["residual"][i] = value
+    named["low"][i] = value[:depth]
+    named["high"][i] = value[rows - depth :]
+    if "last" in named:
+
+        @pl.when(i == 0)
+        def _():
+            named["last"][...] = value
+
+        @pl.when(i == 1)
+        def _():
+            named["first"][...] = value
+
+
+def second_emit(split, named, i, plane, out, padded, local, rows):
+    here = padded[local, pad : pad + rows, :]
+    later = here - step_size * out[:, :lanes]
+    fields = named["start"][plane] + step_size * (here + later)
+    values = (later, fields, out[:, lanes:])
+    if split is None:
+        for name, value in zip(("later", "fields", "part"), values):
+            named[name][i] = value
+    else:
+
+        @pl.when(i < split)
+        def _():
+            for name, value in zip(("later", "fields", "part"), values):
+                named[name][i] = value
+
+        @pl.when(i >= split)
+        def _():
+            for name, value in zip(("later2", "fields2", "part2"), values):
+                named[name][i - split] = value
+
+
+def over_planes(name, depth, width, operands, outs, pieces, edges, layers, runs, sends, emit, work, ties=()):
+    locals_ = max(run.local + run.count + 1 for run in runs)
+    operands = dict(operands)
+    copied = {piece[0] for piece in pieces} - {edge[0] for edge in edges}
+    names = list(operands) + ["tie" + str(number) for number in range(len(ties))]
+    rows = operands["diagonal"].shape[2]
+    return call(
+        functools.partial(planes_body, depth, tuple(names), tuple(outs), pieces, edges, layers, runs, sends, emit),
+        [(shape, f32) for shape in outs.values()],
+        scratch_for(locals_, rows, width),
+        in_specs=[anywhere if key in copied or key.startswith("tie") else whole for key in names],
+        work=work,
+        name=name,
+    )(*operands.values(), *ties)
+
+
+def sides_body(depth, *refs):
+    first, last = refs[-2:]
+    planes = refs[0]
     rows = planes.shape[1]
     first[...] = planes[:, :depth, :]
     last[...] = planes[:, rows - depth :, :]
 
 
-def middle_body(depth, taken, other, low_y, high_y, halves, diagonal, rest, hi, lo, residual, low, high, *scratch):
-    padded, weighed, sem = scratch[0], scratch[1], scratch[-1]
-    held, rows = other.shape[0], other.shape[1]
-    count = held - 2
-    copies = loads([(other, 0, held, 0)], padded, sem)
-    strips(padded, 1, count, depth, low_y, high_y, 1, False)
-    for copy in copies:
-        copy.wait()
-    weigh(padded, halves, weighed, 0, taken, held)
-
-    def emit(at, out):
-        value = rest[at] - out
-        residual[taken + at] = value
-        low[taken + at] = value[:depth]
-        high[taken + at] = value[rows - depth :]
-
-    operate(depth, count, lambda i: (i + 1, taken + i), scratch[:-1], halves, diagonal, hi, lo, emit)
-
-
-def near_body(depth, rest, came, residual_in, low_in, high_in, residual, low, high, edge):
-    count, rows = came.shape[0], came.shape[1]
-
-    def one(i, _):
-        value = rest[i] - came[i]
-        residual[i] = value
-        low[i] = value[:depth]
-        high[i] = value[rows - depth :]
-        return 0
-
-    lax.fori_loop(0, count, one, 0)
-    edge[...] = residual[0]
-
-
-def far_body(depth, rest, came, after, residual, low, high, edge):
-    count, rows = came.shape[0], came.shape[1]
-
-    def one(i, _):
-        value = rest[i] - came[i]
-        residual[i] = value
-        low[i] = value[:depth]
-        high[i] = value[rows - depth :]
-        return 0
-
-    lax.fori_loop(0, count, one, 0)
-    edge[...] = residual[count - 1]
-
-
-def finish(out, residual, start):
-    later = residual - step_size * out
-    return later, start + step_size * (residual + later)
-
-
-def second_body(depth, begin, count, residual, start, low_y, high_y, halves, diagonal, hi, lo, later, fields, part, *scratch):
-    padded, weighed, sem = scratch[0], scratch[1], scratch[-1]
-    rows = residual.shape[1]
-    copies = loads([(residual, begin - 1, count + 2, 0)], padded, sem)
-    strips(padded, 1, count, depth, low_y, high_y, begin, False)
-    for copy in copies:
-        copy.wait()
-    weigh(padded, halves, weighed, 0, begin, count + 2)
-
-    def emit(at, out):
-        here = padded[at + 1, pad : pad + rows, :]
-        later[at], fields[at] = finish(out[:, :lanes], here, start[begin + at])
-        part[at] = out[:, lanes:]
-
-    operate(depth, count, lambda i: (i + 1, begin + i), scratch[:-1], halves, diagonal, hi, lo, emit)
-
-
-def third_body(depth, first, near, far, start, low_x, high_x, low_a, high_a, low_b, high_b, halves, diagonal, hi, lo, *refs):
-    later, fields, part, final_later, final_fields, final_part = refs[:6]
-    scratch = refs[6:]
-    split = part.shape[0]
-    padded, weighed, sem = scratch[0], scratch[1], scratch[-1]
-    ready, remaining = near.shape[0], far.shape[0]
-    rows = near.shape[1]
-    planes = ready + remaining
-    run = planes - first
-    copies = loads([(near, first - 1, ready - first + 1, 0), (far, 0, remaining, ready - first + 1), (near, 0, 2, run + 3)], padded, sem)
-    padded[run + 1, pad : pad + rows, :] = high_x[...]
-    padded[run + 2, pad : pad + rows, :] = low_x[...]
-    strips(padded, 1, ready - first, depth, low_a, high_a, first, False)
-    strips(padded, 1 + ready - first, remaining, depth, low_b, high_b, 0, False)
-    strips(padded, run + 3, 1, depth, low_a, high_a, 0, False)
-    for copy in copies:
-        copy.wait()
-    weigh(padded, halves, weighed, 0, first, run + 2)
-    weigh(padded, halves, weighed, run + 2, 0, 3)
-
-    def place(i):
-        wrapped = jnp.where(i >= run, 1, 0)
-        return i + 1 + 2 * wrapped, first + i - planes * wrapped
-
-    def emit(at, out):
-        middle, plane = place(at)
-        here = padded[middle, pad : pad + rows, :]
-        one, two = finish(out[:, :lanes], here, start[plane])
-
-        @pl.when(at < split)
-        def _():
-            later[at], fields[at], part[at] = one, two, out[:, lanes:]
-
-        @pl.when(at >= split)
-        def _():
-            final_later[at - split], final_fields[at - split], final_part[at - split] = one, two, out[:, lanes:]
-
-    operate(depth, run + 1, place, scratch[:-1], halves, diagonal, hi, lo, emit)
+def sides_and_plane_body(depth, which, *refs):
+    first, last, plane = refs[-3:]
+    planes = refs[0]
+    rows = planes.shape[1]
+    first[...] = planes[:, :depth, :]
+    last[...] = planes[:, rows - depth :, :]
+    plane[...] = planes[which]
 
 
 def last_body(first, later_part, fields_part, came, *refs):
@@ -403,23 +372,22 @@
     flat = (nx,) + plane
     start = start_field.reshape(flat)
     right = right_side.reshape(flat)
-    begin = nx // 4
-    end = nx - begin - nx // 32
-    held = end - begin
-    taken = begin + 1
-    ready = end - 1
-    done = ready - 1
+    low, high = nx // 4, (11 * nx) // 16
     width = 3 * modes
-
-    (chosen,) = call(
-        functools.partial(chosen_body, begin),
-        [((held,) + plane, f32)],
-        [pltpu.SemaphoreType.DMA],
-        in_specs=[pl.BlockSpec(memory_space=pltpu.HBM)],
-        vmem=60 * 1024 * 1024,
-        name="chosen",
-    )(start)
-    raw = sent(chosen, "ma", 1, True)
+    strip = lambda count: ((count, depth, modes), f32)
+
+    def chosen(begin, count, name, *ties):
+        (out,) = call(
+            functools.partial(chosen_body, begin),
+            [((count,) + plane, f32)],
+            [pltpu.SemaphoreType.DMA],
+            in_specs=[anywhere] * (1 + len(ties)),
+            vmem=vmem_bytes if ties else most_bytes,
+            name=name,
+        )(start, *ties)
+        return sent(out, "ma", 1, True)
+
+    raw_1 = chosen(low, high - low, "chosen_1")
 
     coef = coefficients.reshape(3 * nx, rows)
     layer = ((rows + lanes, lanes), f32)
@@ -428,6 +396,7 @@
         [layer] * 4,
         [pltpu.VMEM(flat, f32), pltpu.SemaphoreType.DMA],
         in_specs=[anywhere, whole],
+        vmem=most_bytes,
         name="layers",
     )(start, coef)
     low_y = sent(last_y, "gy", 1, True)
@@ -453,91 +422,191 @@
         aliases={4: 0},
         name="diagonal",
     )(low_x, high_x, low_y, high_y, halves)
-
-    def first(begin, count, sends, name):
+    shared = {"halves": halves, "diagonal": diagonal}
+    mine = {**shared, "hi": own_hi, "lo": own_lo}
+    theirs = {**shared, "hi": other_hi, "lo": other_lo}
+    raw_2 = chosen(high, nx - high, "chosen_2", own_hi, diagonal)
+
+    n1, n2, n3 = high - low - 2, nx - high, low + 2
+    ring = [Run(1, nx - 1, 1), Run(4, 0, low + 1)]
+
+    def own(name, count, pieces, edges, layers, runs, ties=()):
+        operands = {**mine, "start": start, "right": right, "low_y": low_y, "high_y": high_y, "low_x": low_x, "high_x": high_x}
+        outs = {"rest": (count,) + plane}
+        return over_planes(name, depth, width, operands, outs, pieces, edges, layers, runs, False, own_emit, count / 10, ties)[0]
+
+    rest_1 = own(
+        "own_1", n1, [("start", low, n1 + 2, 0)], [], [("low_y", "high_y", low + 1, n1, 1, True)], [Run(1, low + 1, n1)]
+    )
+    raw_3 = chosen(0, low, "chosen_3", rest_1)
+
+    def sides(chunk, which, name, *ties):
+        count = chunk.shape[0]
+        body = functools.partial(sides_body, depth) if which is None else functools.partial(sides_and_plane_body, depth, which)
         return call(
-            functools.partial(first_body, depth, begin, count, sends),
-            [((count,) + plane, f32)] * (2 if sends else 1),
-            scratch_for(count + 2, rows, width),
-            in_specs=[anywhere] + [whole] * 9,
-            work=count / 10,
+            body,
+            [strip(count)] * 2 + ([] if which is None else [(plane, f32)]),
+            [],
+            in_specs=[whole] + [anywhere] * len(ties),
+            work=0.1,
             name=name,
-        )(start, right, low_x, high_x, low_y, high_y, halves, diagonal, own_hi, own_lo)
-
-    rest_a, part_a = first(0, taken, True, "first_a")
-    came_a = sent(part_a, "ma", 1, True)
-    rest_b, part_b = first(ready, nx - ready, True, "first_b")
-    came_b = sent(part_b, "ma", 1, True)
-    (rest_c,) = first(taken, ready - taken, False, "first_c")
-
-    strip = lambda count: ((count, depth, modes), f32)
-    raw_first, raw_last = call(
-        functools.partial(sides_body, depth), [strip(held)] * 2, [], in_specs=[whole], work=0.1, name="sides"
-    )(raw)
-    raw_low = sent(raw_last, "gy", 1, True)
-    raw_high = sent(raw_first, "gy", -1, True)
-    near_shapes = [((ready,) + plane, f32), strip(ready), strip(ready)]
-    near, low_a, high_a = call(
-        functools.partial(middle_body, depth, taken),
-        near_shapes,
-        scratch_for(held, rows, width),
-        in_specs=[anywhere] + [whole] * 7,
-        work=(held - 2) / 12,
-        name="middle",
-    )(raw, raw_low, raw_high, halves, diagonal, rest_c, other_hi, other_lo)
-    near, low_a, high_a, edge_first = call(
-        functools.partial(near_body, depth),
-        near_shapes + [(plane, f32)],
+        )(chunk, *ties)
+
+    def exchanged(first, last):
+        return sent(last, "gy", 1, True), sent(first, "gy", -1, True)
+
+    def middle(name, count, operands, pieces, edges, layers, runs, with_edges, ties=()):
+        outs = {"residual": (count,) + plane, "low": (count, depth, modes), "high": (count, depth, modes)}
+        if with_edges:
+            outs.update({"last": plane, "first": plane})
+        emit = functools.partial(middle_emit, depth)
+        return over_planes(name, depth, width, {**theirs, **operands}, outs, pieces, edges, layers, runs, False, emit, count / 10, ties)
+
+    def second(name, counts, operands, pieces, edges, layers, runs, ties=(), work=1.0):
+        outs = {}
+        for number, count in enumerate(counts):
+            mark = "" if number == 0 else "2"
+            outs.update({key + mark: (count,) + plane for key in ("later", "fields", "part")})
+        emit = functools.partial(second_emit, counts[0] if len(counts) > 1 else None)
+        operands = {**mine, "start": start, **operands}
+        return over_planes(name, depth, width, operands, outs, pieces, edges, layers, runs, True, emit, work, ties)
+
+    raw_low_1, raw_high_1 = exchanged(*sides(raw_1, None, "sides_1"))
+    residual_1, first_1, last_1 = middle(
+        "middle_1",
+        n1,
+        {"rest": rest_1, "raw_1": raw_1, "low_1": raw_low_1, "high_1": raw_high_1},
+        [("raw_1", 0, n1 + 2, 0)],
         [],
-        in_specs=[whole] * 5,
-        aliases={2: 0, 3: 1, 4: 2},
-        work=0.2,
-        name="near",
-    )(rest_a, came_a, near, low_a, high_a)
-    next_low_a = sent(high_a, "gy", 1, True)
-    next_high_a = sent(low_a, "gy", -1, True)
+        [("low_1", "high_1", 1, n1, 1, False)],
+        [Run(1, low + 1, n1)],
+        False,
+    )
+    low_1, high_1 = exchanged(first_1, last_1)
+    rest_2 = own(
+        "own_2",
+        n2,
+        [("start", high - 2, n2 + 2, 0)],
+        [],
+        [("low_y", "high_y", high - 1, n2, 1, True)],
+        [Run(1, high - 1, n2)],
+        (first_1,),
+    )
+    later_1, fields_1, part_1 = second(
+        "second_1",
+        [n1 - 2],
+        {"residual_1": residual_1, "low_1": low_1, "high_1": high_1},
+        [("residual_1", 0, n1, 0)],
+        [],
+        [("low_1", "high_1", 1, n1 - 2, 1, False)],
+        [Run(1, low + 2, n1 - 2)],
+        (rest_2,),
+    )
+    came_1 = sent(part_1, "ma", 1, True)
+
+    sides_2 = sides(raw_2, nx - high - 1, "sides_2", part_1)
+    raw_low_2, raw_high_2 = exchanged(sides_2[0], sides_2[1])
+    raw_low_x = sent(sides_2[2], "gx", 1, False)
+    rest_3 = own(
+        "own_3",
+        n3,
+        [("start", nx - 2, 2, 0), ("start", 0, low + 2, 4)],
+        [("high_x", 2), ("low_x", 3)],
+        [("low_y", "high_y", nx - 1, 1, 1, True), ("low_y", "high_y", 0, low + 1, 4, True)],
+        ring,
+        (sides_2[0],),
+    )
+    residual_2, first_2, last_2 = middle(
+        "middle_2",
+        n2,
+        {"rest": rest_2, "raw_1": raw_1, "raw_2": raw_2, "low_1": raw_low_1, "high_1": raw_high_1, "low_2": raw_low_2, "high_2": raw_high_2},
+        [("raw_1", high - low - 2, 2, 0), ("raw_2", 0, n2, 2)],
+        [],
+        [("low_1", "high_1", high - low - 1, 1, 1, False), ("low_2", "high_2", 0, n2 - 1, 2, False)],
+        [Run(1, high - 1, n2)],
+        False,
+        (rest_3,),
+    )
+    low_2, high_2 = exchanged(first_2, last_2)
+
+    sides_3 = sides(raw_3, 0, "sides_3", first_2)
+    raw_low_3, raw_high_3 = exchanged(sides_3[0], sides_3[1])
+    raw_high_x = sent(sides_3[2], "gx", -1, False)
+    later_2, fields_2, part_2 = second(
+        "second_2",
+        [n2],
+        {"residual_1": residual_1, "residual_2": residual_2, "low_1": low_1, "high_1": high_1, "low_2": low_2, "high_2": high_2},
+        [("residual_1", n1 - 2, 2, 0), ("residual_2", 0, n2, 2)],
+        [],
+        [("low_1", "high_1", n1 - 1, 1, 1, False), ("low_2", "high_2", 0, n2 - 1, 2, False)],
+        [Run(1, high - 2, n2)],
+        (sides_3[0], raw_low_x),
+    )
+    came_2 = sent(part_2, "ma", 1, True)
+    residual_3, first_3, last_3, edge_last, edge_first = middle(
+        "middle_3",
+        n3,
+        {
+            "rest": rest_3,
+            "raw_1": raw_1,
+            "raw_2": raw_2,
+            "raw_3": raw_3,
+            "low_x": raw_low_x,
+            "high_x": raw_high_x,
+            "low_1": raw_low_1,
+            "high_1": raw_high_1,
+            "low_2": raw_low_2,
+            "high_2": raw_high_2,
+            "low_3": raw_low_3,
+            "high_3": raw_high_3,
+        },
+        [("raw_2", n2 - 2, 2, 0), ("raw_3", 0, low, 4), ("raw_1", 0, 2, 4 + low)],
+        [("high_x", 2), ("low_x", 3)],
+        [("low_2", "high_2", n2 - 1, 1, 1, False), ("low_3", "high_3", 0, low, 4, False), ("low_1", "high_1", 0, 1, 4 + low, False)],
+        ring,
+        True,
+        (part_2,),
+    )
+    low_3, high_3 = exchanged(first_3, last_3)
+    next_low_x = sent(edge_last, "gx", 1, False)
     next_high_x = sent(edge_first, "gx", -1, False)
-
-    count = ready - 2
-    later_c, fields_c, part_c = call(
-        functools.partial(second_body, depth, 1, count),
-        [((count,) + plane, f32)] * 3,
-        scratch_for(count + 2, rows, width),
-        in_specs=[anywhere] + [whole] * 7,
-        work=count / 10,
-        name="second",
-    )(near, start, next_low_a, next_high_a, halves, diagonal, own_hi, own_lo)
-    came_c = sent(part_c, "ma", 1, True)
-
-    remaining = nx - ready
-    far, low_b, high_b, edge_last = call(
-        functools.partial(far_body, depth),
-        [((remaining,) + plane, f32), strip(remaining), strip(remaining), (plane, f32)],
-        [],
-        in_specs=[whole] * 2 + [anywhere],
-        work=0.2,
-        name="far",
-    )(rest_b, came_b, part_c)
-    next_low_b = sent(high_b, "gy", 1, True)
-    next_high_b = sent(low_b, "gy", -1, True)
-    next_low_x = sent(edge_last, "gx", 1, False)
-
-    count = nx - done + 1
     final = 4
-    later_d, fields_d, part_d, later_e, fields_e, part_e = call(
-        functools.partial(third_body, depth, done),
-        [((count - final,) + plane, f32)] * 3 + [((final,) + plane, f32)] * 3,
-        scratch_for(count + 4, rows, width),
-        in_specs=[anywhere] * 2 + [whole] * 11,
-        work=6.0,
-        name="third",
-    )(near, far, start, next_low_x, next_high_x, next_low_a, next_high_a, next_low_b, next_high_b, halves, diagonal, own_hi, own_lo)
-    came_d = sent(part_d, "ma", 1, True)
-    came_e = sent(part_e, "ma", 1, True)
-
-    outs = add_last(1, flat, later_c, fields_c, came_c, ())
-    outs = add_last(done, flat, later_d, fields_d, came_d, outs)
-    later, fields = add_last(done + count - final, flat, later_e, fields_e, came_e, outs)
+    count = low + 4
+    later_3, fields_3, part_3, later_4, fields_4, part_4 = second(
+        "second_3",
+        [count - final, final],
+        {
+            "residual_1": residual_1,
+            "residual_2": residual_2,
+            "residual_3": residual_3,
+            "low_x": next_low_x,
+            "high_x": next_high_x,
+            "low_1": low_1,
+            "high_1": high_1,
+            "low_2": low_2,
+            "high_2": high_2,
+            "low_3": low_3,
+            "high_3": high_3,
+        },
+        [("residual_2", n2 - 2, 2, 0), ("residual_3", 0, 1, 2), ("residual_3", 1, low + 1, 5), ("residual_1", 0, 2, 6 + low)],
+        [("high_x", 3), ("low_x", 4)],
+        [
+            ("low_2", "high_2", n2 - 1, 1, 1, False),
+            ("low_3", "high_3", 0, 1, 2, False),
+            ("low_3", "high_3", 1, low + 1, 5, False),
+            ("low_1", "high_1", 0, 1, 6 + low, False),
+        ],
+        [Run(1, nx - 2, 2), Run(5, 0, low + 2)],
+        (came_1,),
+        1.0,
+    )
+    came_3 = sent(part_3, "ma", 1, True)
+    came_4 = sent(part_4, "ma", 1, True)
+
+    outs = add_last(low + 2, flat, later_1, fields_1, came_1, ())
+    outs = add_last(high - 2, flat, later_2, fields_2, came_2, outs)
+    outs = add_last(nx - 2, flat, later_3, fields_3, came_3, outs)
+    later, fields = add_last(low + 2 - final, flat, later_4, fields_4, came_4, outs)
     return (fields.reshape(start_field.shape), later.reshape(start_field.shape))
 
 

time: 100 us -> 106 us (1.060)
  waiting for transfers between devices: 35.2 us -> 23 us
  starting transfers between devices: 26.6 us -> 37.3 us
  Pallas kernels: 36 us -> 43.1 us
    ppermute x18 -> x27, waiting for transfers between devices: 35.2 us -> 23 us  [sent(): return lax.ppermute(array, axis, pairs)]
    ppermute x18 -> x27, starting transfers between devices: 26.6 us -> 37.3 us  [sent(): return lax.ppermute(array, axis, pairs)]
    pallas_call x10 -> x15, Pallas kernels: 26.9 us -> 30.2 us  [the longest x9 27.7 us: over_planes(): call(functools.partial(planes_body, depth, tuple(names), tuple(outs), pie...]
    pallas_call x1, Pallas kernels: 0.2 us -> 3.25 us  [shards(): call(functools.partial(layers_body, depth), [layer] * 4, [pltpu.VMEM(flat...]
    pallas_call x3 -> x4, Pallas kernels: 3.96 us -> 4.65 us  [add_last(): call(functools.partial(last_body, first), [(shape, f32)] * 2, [pltpu.VMEM...]
  transfers between devices with their start and end apart: 18 -> 27, of which waited for: 9 -> 9; matrix products, arithmetic and copies ran while one was open for 0% -> 1% of each run, Pallas kernels for 33% -> 38%
where the time goes in v5:
time: 106 us
  Pallas kernels  43.1 us (41%)
  starting transfers between devices  37.3 us (35%)
  waiting for transfers between devices  23 us (22%)
  between operations  1.16 us (1%)
  local copies, waits for them, and re-layouts  1.08 us (1%)
    ppermute x27, starting transfers between devices, sent(): return lax.ppermute(array, axis, pairs)  37.3 us
    pallas_call x9, Pallas kernels, over_planes(): call(functools.partial(planes_body, depth, tuple(names), tuple(outs), pie...  27.7 us
    ppermute x27, waiting for transfers between devices, sent(): return lax.ppermute(array, axis, pairs)  23 us
    pallas_call x4, Pallas kernels, add_last(): call(functools.partial(last_body, first), [(shape, f32)] * 2, [pltpu.VMEM...  4.65 us
    pallas_call x1, Pallas kernels, shards(): call(functools.partial(layers_body, depth), [layer] * 4, [pltpu.VMEM(flat...  3.25 us
    pallas_call x1, Pallas kernels, shards(): call(functools.partial(diagonal_body, depth), [(halves_shape, f32), ((3,)...  2.67 us
    pallas_call x3, Pallas kernels, chosen(): call(functools.partial(chosen_body, begin), [((count,) + plane, f32)], [p...  2.41 us
  transfers between devices with their start and end apart: 27, of which 9 were waited for; matrix products, arithmetic and copies ran while one was open for 1% of the time, Pallas kernels for 38%

profile of v5, /device:TPU:0, one launch (start us, length us, event | category | flops | bytes accessed | tf_op | source)
XLA Modules:
  0.0 105.6 jit_solution(11858107645313694535)
XLA Ops:
  0.6 2.2 %chosen_1.1 = f32[14,128,128]{2,1,0:T(8,128)} custom-call(f32[32,128,128]{2,1,0:T(8,128)} %bitcast.6), custom_call_target="tpu_custom_call" | custom-call | flops 1000000 | bytes 2000 | tf_op jit(solution)/shard_map/chosen_1/pallas_call | solution.py:380
  2.8 3.0 %collective-permute-start.4 = (f32[14,128,128]{2,1,0:T(8,128)}, f32[14,128,128]{2,1,0:T(8,128)S(1)}, u32[]{:S(2)}, u32[]{:S(2)}) collective-permute-start(f32[14,128,128]{2,1,0:T(8,128)} %chosen_1.1), channel_id=1, source_target_pairs={{0,1},{1,0},{2,3},{3,2},{4,5},{5,4},{6,7},{7,6},{8,9},{9,8},{10,11... | collective-permute-start | bytes 2752520 | tf_op jit(solution)/shard_map/ppermute | solution.py:39
  6.9 3.2 %layers.1 = (f32[256,128]{1,0:T(8,128)}, f32[256,128]{1,0:T(8,128)}, f32[256,128]{1,0:T(8,128)}, f32[256,128]{1,0:T(8,128)}) custom-call(f32[32,128,128]{2,1,0:T(8,128)} %bitcast.7, f32[96,128]{1,0:T(8,128)} %copy.15.coef), custom_call_target="tpu_custom_call" | custom-call | flops 1000000 | bytes 2000 | tf_op jit(solution)/shard_map/layers/pallas_call | solution.py:394
  10.2 3.5 %collective-permute-start = (f32[256,128]{1,0:T(8,128)}, f32[256,128]{1,0:T(8,128)S(1)}, u32[]{:S(2)}, u32[]{:S(2)}) collective-permute-start(f32[256,128]{1,0:T(8,128)} %get-tuple-element.51), channel_id=1, source_target_pairs={{0,8},{8,16},{16,24},{1,9},{9,17},{17,25},{2,10},{10,18},{18,26},{... | collective-permute-start | bytes 393224 | tf_op jit(solution)/shard_map/ppermute | solution.py:39
  15.0 1.7 %collective-permute-start.3 = (f32[256,128]{1,0:T(8,128)}, f32[256,128]{1,0:T(8,128)S(1)}, u32[]{:S(2)}, u32[]{:S(2)}) collective-permute-start(f32[256,128]{1,0:T(8,128)} %get-tuple-element.54), channel_id=1, source_target_pairs={{0,6},{2,0},{4,2},{6,4},{1,7},{3,1},{5,3},{7,5},{8,14},{10,8},{12,... | collective-permute-start | bytes 393224 | tf_op jit(solution)/shard_map/ppermute | solution.py:39
  16.8 1.9 %halves.1.halves_in = f32[3,34,144,128]{3,2,1,0:T(8,128)S(1)} custom-call(f32[96,128]{1,0:T(8,128)S(1)} %copy-done.3), custom_call_target="tpu_custom_call" | custom-call | flops 1000000 | bytes 2000 | tf_op jit(solution)/shard_map/halves/pallas_call | solution.py:416
  20.7 2.7 %diagonal.1 = (f32[3,34,144,128]{3,2,1,0:T(8,128)S(1)}, f32[3,32,128,128]{3,2,1,0:T(8,128)S(1)}) custom-call(f32[256,128]{1,0:T(8,128)S(1)} %collective-permute-done.low_x.refs_8_, f32[256,128]{1,0:T(8,128)S(1)} %collective-permute-done.1.high_x.refs_9_, f32[256,128]{1,0:T(8,128)S(1)} %collective-permute-done.2.low_y.refs_6_, ...), custom_call_target="tpu_custom_call", output_to_operand_aliasing={{0}: (4, {})} | custom-call | flops 1000000 | bytes 2000 | tf_op jit(solution)/shard_map/diagonal/pallas_call | solution.py:417
  24.2 2.2 %collective-permute-done.4.refs_0_.refs_5_ = f32[14,128,128]{2,1,0:T(8,128)S(1)} collective-permute-done((f32[14,128,128]{2,1,0:T(8,128)}, f32[14,128,128]{2,1,0:T(8,128)S(1)}, u32[]{:S(2)}, u32[]{:S(2)}) %collective-permute-start.4) | collective-permute-done | bytes 917536 | tf_op jit(solution)/shard_map/ppermute | solution.py:39
  26.5 1.7 %collective-permute-start.6 = (f32[14,4,128]{2,1,0:T(4,128)S(1)}, f32[14,4,128]{2,1,0:T(4,128)S(1)}, u32[]{:S(2)}, u32[]{:S(2)}) collective-permute-start(f32[14,4,128]{2,1,0:T(4,128)S(1)} %get-tuple-element.62), channel_id=1, source_target_pairs={{0,6},{2,0},{4,2},{6,4},{1,7},{3,1},{5,3},{7,5},{8,14},{10,8},{12,... | collective-permute-start | bytes 86024 | tf_op jit(solution)/shard_map/ppermute | solution.py:39
  28.2 2.8 %own_1.1.refs_4_.refs_0_ = f32[12,128,128]{2,1,0:T(8,128)S(1)} custom-call(f32[3,34,144,128]{3,2,1,0:T(8,128)S(1)} %get-tuple-element.55.refs_0_, f32[3,32,128,128]{3,2,1,0:T(8,128)S(1)} %get-tuple-element.56.refs_1_, bf16[384,256]{1,0:T(8,128)(2,1)S(1)} %get-tuple-element.57.refs_2_.refs_0_, bf16[384,256]{1,0:T(8,128)(2,1)S(1)} %get-tuple-element.58.refs_3_, ...), custom_call_target="tpu_custom_call" | custom-call | flops 1200000 | bytes 2400 | tf_op jit(solution)/shard_map/own_1/pallas_call | solution.py:302
  31.1 3.0 %middle_1.1 = (f32[12,128,128]{2,1,0:T(8,128)S(1)}, f32[12,4,128]{2,1,0:T(4,128)S(1)}, f32[12,4,128]{2,1,0:T(4,128)S(1)}) custom-call(f32[3,34,144,128]{3,2,1,0:T(8,128)S(1)} %get-tuple-element.55.refs_0_, f32[3,32,128,128]{3,2,1,0:T(8,128)S(1)} %get-tuple-element.56.refs_1_, bf16[384,128]{1,0:T(8,128)(2,1)S(1)} %get-tuple-element.59.refs_2_, ...), custom_call_target="tpu_custom_call" | custom-call | flops 1200000 | bytes 2400 | tf_op jit(solution)/shard_map/middle_1/pallas_call | solution.py:302
  35.9 2.3 %collective-permute-start.12 = (f32[8,128,128]{2,1,0:T(8,128)S(1)}, f32[8,128,128]{2,1,0:T(8,128)S(1)}, u32[]{:S(2)}, u32[]{:S(2)}) collective-permute-start(f32[8,128,128]{2,1,0:T(8,128)S(1)} %chosen_3.1), channel_id=1, source_target_pairs={{0,1},{1,0},{2,3},{3,2},{4,5},{5,4},{6,7},{7,6},{8,9},{9,8},{10,11... | collective-permute-start | bytes 1572872 | tf_op jit(solution)/shard_map/ppermute | solution.py:39
  38.2 2.5 %own_2.1.refs_8_.refs_4_ = f32[10,128,128]{2,1,0:T(8,128)S(1)} custom-call(f32[3,34,144,128]{3,2,1,0:T(8,128)S(1)} %get-tuple-element.55.refs_0_, f32[3,32,128,128]{3,2,1,0:T(8,128)S(1)} %get-tuple-element.56.refs_1_, bf16[384,256]{1,0:T(8,128)(2,1)S(1)} %get-tuple-element.57.refs_2_.refs_0_, bf16[384,256]{1,0:T(8,128)(2,1)S(1)} %get-tuple-element.58.refs_3_, ...), custom_call_target="tpu_custom_call" | custom-call | flops 1000000 | bytes 2000 | tf_op jit(solution)/shard_map/own_2/pallas_call | solution.py:302
  40.7 2.7 %second_1.1 = (f32[10,128,128]{2,1,0:T(8,128)S(1)}, f32[10,128,128]{2,1,0:T(8,128)S(1)}, f32[10,128,128]{2,1,0:T(8,128)S(1)}) custom-call(f32[3,34,144,128]{3,2,1,0:T(8,128)S(1)} %get-tuple-element.55.refs_0_, f32[3,32,128,128]{3,2,1,0:T(8,128)S(1)} %get-tuple-element.56.refs_1_, bf16[384,256]{1,0:T(8,128)(2,1)S(1)} %get-tuple-element.57.refs_2_.refs_0_, ...), custom_call_target="tpu_custom_call" | custom-call | flops 1000000 | bytes 2000 | tf_op jit(solution)/shard_map/second_1/pallas_call | solution.py:302
  43.6 3.5 %collective-permute-start.13 = (f32[128,128]{1,0:T(8,128)S(1)}, f32[128,128]{1,0:T(8,128)S(1)}, u32[]{:S(2)}, u32[]{:S(2)}) collective-permute-start(f32[128,128]{1,0:T(8,128)S(1)} %get-tuple-element.70), channel_id=1, source_target_pairs={{0,8},{8,16},{16,24},{1,9},{9,17},{17,25},{2,10},{10,18},{18,26},{... | collective-permute-start | bytes 196616 | tf_op jit(solution)/shard_map/ppermute | solution.py:39
  47.1 1.7 %collective-permute-start.11 = (f32[10,4,128]{2,1,0:T(4,128)S(1)}, f32[10,4,128]{2,1,0:T(4,128)S(1)}, u32[]{:S(2)}, u32[]{:S(2)}) collective-permute-start(f32[10,4,128]{2,1,0:T(4,128)S(1)} %get-tuple-element.68.refs_10_), channel_id=1, source_target_pairs={{0,6},{2,0},{4,2},{6,4},{1,7},{3,1},{5,3},{7,5},{8,14},{10,8},{12,... | collective-permute-start | bytes 61448 | tf_op jit(solution)/shard_map/ppermute | solution.py:39
  48.9 2.9 %own_3.1.refs_11_.refs_4_ = f32[10,128,128]{2,1,0:T(8,128)S(1)} custom-call(f32[3,34,144,128]{3,2,1,0:T(8,128)S(1)} %get-tuple-element.55.refs_0_, f32[3,32,128,128]{3,2,1,0:T(8,128)S(1)} %get-tuple-element.56.refs_1_, bf16[384,256]{1,0:T(8,128)(2,1)S(1)} %get-tuple-element.57.refs_2_.refs_0_, bf16[384,256]{1,0:T(8,128)(2,1)S(1)} %get-tuple-element.58.refs_3_, ...), custom_call_target="tpu_custom_call" | custom-call | flops 1000000 | bytes 2000 | tf_op jit(solution)/shard_map/own_3/pallas_call | solution.py:302
  51.8 2.7 %middle_2.1 = (f32[10,128,128]{2,1,0:T(8,128)S(1)}, f32[10,4,128]{2,1,0:T(4,128)S(1)}, f32[10,4,128]{2,1,0:T(4,128)S(1)}) custom-call(f32[3,34,144,128]{3,2,1,0:T(8,128)S(1)} %get-tuple-element.55.refs_0_, f32[3,32,128,128]{3,2,1,0:T(8,128)S(1)} %get-tuple-element.56.refs_1_, bf16[384,128]{1,0:T(8,128)(2,1)S(1)} %get-tuple-element.59.refs_2_, ...), custom_call_target="tpu_custom_call" | custom-call | flops 1000000 | bytes 2000 | tf_op jit(solution)/shard_map/middle_2/pallas_call | solution.py:302
  57.8 2.8 %second_2.1 = (f32[10,128,128]{2,1,0:T(8,128)S(1)}, f32[10,128,128]{2,1,0:T(8,128)S(1)}, f32[10,128,128]{2,1,0:T(8,128)S(1)}) custom-call(f32[3,34,144,128]{3,2,1,0:T(8,128)S(1)} %get-tuple-element.55.refs_0_, f32[3,32,128,128]{3,2,1,0:T(8,128)S(1)} %get-tuple-element.56.refs_1_, bf16[384,256]{1,0:T(8,128)(2,1)S(1)} %get-tuple-element.57.refs_2_.refs_0_, ...), custom_call_target="tpu_custom_call" | custom-call | flops 1000000 | bytes 2000 | tf_op jit(solution)/shard_map/second_2/pallas_call | solution.py:302
  65.3 3.4 %middle_3.1 = (f32[10,128,128]{2,1,0:T(8,128)S(1)}, f32[10,4,128]{2,1,0:T(4,128)S(1)}, f32[10,4,128]{2,1,0:T(4,128)S(1)}, f32[128,128]{1,0:T(8,128)S(1)}, f32[128,128]{1,0:T(8,128)S(1)}) custom-call(f32[3,34,144,128]{3,2,1,0:T(8,128)S(1)} %get-tuple-element.55.refs_0_, f32[3,32,128,128]{3,2,1,0:T(8,128)S(1)} %get-tuple-element.56.refs_1_, ...), custom_call_target="tpu_custom_call" | custom-call | flops 1000000 | bytes 2000 | tf_op jit(solution)/shard_map/middle_3/pallas_call | solution.py:302
  68.8 4.4 %collective-permute-start.19 = (f32[128,128]{1,0:T(8,128)S(1)}, f32[128,128]{1,0:T(8,128)S(1)}, u32[]{:S(2)}, u32[]{:S(2)}) collective-permute-start(f32[128,128]{1,0:T(8,128)S(1)} %get-tuple-element.78), channel_id=1, source_target_pairs={{0,8},{8,16},{16,24},{1,9},{9,17},{17,25},{2,10},{10,18},{18,26},{... | collective-permute-start | bytes 196616 | tf_op jit(solution)/shard_map/ppermute | solution.py:39
  79.5 4.9 %second_3.1 = (f32[8,128,128]{2,1,0:T(8,128)S(1)}, f32[8,128,128]{2,1,0:T(8,128)S(1)}, f32[8,128,128]{2,1,0:T(8,128)S(1)}, f32[4,128,128]{2,1,0:T(8,128)S(1)}, f...) custom-call(f32[3,34,144,128]{3,2,1,0:T(8,128)S(1)} %get-tuple-element.55.refs_0_, ...), custom_call_target="tpu_custom_call" | custom-call | flops 1000000 | bytes 2000 | tf_op jit(solution)/shard_map/second_3/pallas_call | solution.py:302
  89.1 9.8 %collective-permute-done.25.came = f32[8,128,128]{2,1,0:T(8,128)S(1)} collective-permute-done((f32[8,128,128]{2,1,0:T(8,128)S(1)}, f32[8,128,128]{2,1,0:T(8,128)S(1)}, u32[]{:S(2)}, u32[]{:S(2)}) %collective-permute-start.25) | collective-permute-done | bytes 524320 | tf_op jit(solution)/shard_map/ppermute | solution.py:39
  100.1 4.5 %collective-permute-done.24.came = f32[4,128,128]{2,1,0:T(8,128)S(1)} collective-permute-done((f32[4,128,128]{2,1,0:T(8,128)S(1)}, f32[4,128,128]{2,1,0:T(8,128)S(1)}, u32[]{:S(2)}, u32[]{:S(2)}) %collective-permute-start.24) | collective-permute-done | bytes 262176 | tf_op jit(solution)/shard_map/ppermute | solution.py:39
  (66 shorter events, 28.4 us)
Async XLA Ops:
  2.8 23.6 %collective-permute-start.4 = (f32[14,128,128]{2,1,0:T(8,128)}, f32[14,128,128]{2,1,0:T(8,128)S(1)}, u32[]{:S(2)}, u32[]{:S(2)}) collective-permute-start(f32[14,128,128]{2,1,0:T(8,128)} %chosen_1.1), channel_id=1, source_target_pairs={{0,1},{1,0},{2,3},{3,2},{4,5},{5,4},{6,7},{7,6},{8,9},{9,8},{10,11... | collective-permute-start | bytes 2752520 | tf_op jit(solution)/shard_map/ppermute | solution.py:39
  10.2 9.0 %collective-permute-start = (f32[256,128]{1,0:T(8,128)}, f32[256,128]{1,0:T(8,128)S(1)}, u32[]{:S(2)}, u32[]{:S(2)}) collective-permute-start(f32[256,128]{1,0:T(8,128)} %get-tuple-element.51), channel_id=1, source_target_pairs={{0,8},{8,16},{16,24},{1,9},{9,17},{17,25},{2,10},{10,18},{18,26},{... | collective-permute-start | bytes 393224 | tf_op jit(solution)/shard_map/ppermute | solution.py:39
  13.6 7.1 %collective-permute-start.1 = (f32[256,128]{1,0:T(8,128)}, f32[256,128]{1,0:T(8,128)S(1)}, u32[]{:S(2)}, u32[]{:S(2)}) collective-permute-start(f32[256,128]{1,0:T(8,128)} %get-tuple-element.52), channel_id=1, source_target_pairs={{8,0},{16,8},{24,16},{9,1},{17,9},{25,17},{10,2},{18,10},{26,18},{... | collective-permute-start | bytes 393224 | tf_op jit(solution)/shard_map/ppermute | solution.py:39
  14.9 5.8 %collective-permute-start.2 = (f32[256,128]{1,0:T(8,128)}, f32[256,128]{1,0:T(8,128)S(1)}, u32[]{:S(2)}, u32[]{:S(2)}) collective-permute-start(f32[256,128]{1,0:T(8,128)} %get-tuple-element.53), channel_id=1, source_target_pairs={{0,2},{2,4},{4,6},{6,0},{1,3},{3,5},{5,7},{7,1},{8,10},{10,12},{12... | collective-permute-start | bytes 393224 | tf_op jit(solution)/shard_map/ppermute | solution.py:39
  15.0 5.7 %collective-permute-start.3 = (f32[256,128]{1,0:T(8,128)}, f32[256,128]{1,0:T(8,128)S(1)}, u32[]{:S(2)}, u32[]{:S(2)}) collective-permute-start(f32[256,128]{1,0:T(8,128)} %get-tuple-element.54), channel_id=1, source_target_pairs={{0,6},{2,0},{4,2},{6,4},{1,7},{3,1},{5,3},{7,5},{8,14},{10,8},{12,... | collective-permute-start | bytes 393224 | tf_op jit(solution)/shard_map/ppermute | solution.py:39
  23.6 19.9 %collective-permute-start.7 = (f32[10,128,128]{2,1,0:T(8,128)S(1)}, f32[10,128,128]{2,1,0:T(8,128)S(1)}, u32[]{:S(2)}, u32[]{:S(2)}) collective-permute-start(f32[10,128,128]{2,1,0:T(8,128)S(1)} %chosen_2.1), channel_id=1, source_target_pairs={{0,1},{1,0},{2,3},{3,2},{4,5},{5,4},{6,7},{7,6},{8,9},{9,8},{10,11... | collective-permute-start | bytes 1966088 | tf_op jit(solution)/shard_map/ppermute | solution.py:39
  26.4 4.7 %collective-permute-start.5 = (f32[14,4,128]{2,1,0:T(4,128)S(1)}, f32[14,4,128]{2,1,0:T(4,128)S(1)}, u32[]{:S(2)}, u32[]{:S(2)}) collective-permute-start(f32[14,4,128]{2,1,0:T(4,128)S(1)} %get-tuple-element.61), channel_id=1, source_target_pairs={{0,2},{2,4},{4,6},{6,0},{1,3},{3,5},{5,7},{7,1},{8,10},{10,12},{12... | collective-permute-start | bytes 86024 | tf_op jit(solution)/shard_map/ppermute | solution.py:39
  26.5 4.6 %collective-permute-start.6 = (f32[14,4,128]{2,1,0:T(4,128)S(1)}, f32[14,4,128]{2,1,0:T(4,128)S(1)}, u32[]{:S(2)}, u32[]{:S(2)}) collective-permute-start(f32[14,4,128]{2,1,0:T(4,128)S(1)} %get-tuple-element.62), channel_id=1, source_target_pairs={{0,6},{2,0},{4,2},{6,4},{1,7},{3,1},{5,3},{7,5},{8,14},{10,8},{12,... | collective-permute-start | bytes 86024 | tf_op jit(solution)/shard_map/ppermute | solution.py:39
  34.1 6.6 %collective-permute-start.8 = (f32[12,4,128]{2,1,0:T(4,128)S(1)}, f32[12,4,128]{2,1,0:T(4,128)S(1)}, u32[]{:S(2)}, u32[]{:S(2)}) collective-permute-start(f32[12,4,128]{2,1,0:T(4,128)S(1)} %get-tuple-element.65), channel_id=1, source_target_pairs={{0,2},{2,4},{4,6},{6,0},{1,3},{3,5},{5,7},{7,1},{8,10},{10,12},{12... | collective-permute-start | bytes 73736 | tf_op jit(solution)/shard_map/ppermute | solution.py:39
  34.9 5.8 %collective-permute-start.9 = (f32[12,4,128]{2,1,0:T(4,128)S(1)}, f32[12,4,128]{2,1,0:T(4,128)S(1)}, u32[]{:S(2)}, u32[]{:S(2)}) collective-permute-start(f32[12,4,128]{2,1,0:T(4,128)S(1)} %get-tuple-element.64.refs_10_), channel_id=1, source_target_pairs={{0,6},{2,0},{4,2},{6,4},{1,7},{3,1},{5,3},{7,5},{8,14},{10,8},{12,... | collective-permute-start | bytes 73736 | tf_op jit(solution)/shard_map/ppermute | solution.py:39
  35.9 20.4 %collective-permute-start.12 = (f32[8,128,128]{2,1,0:T(8,128)S(1)}, f32[8,128,128]{2,1,0:T(8,128)S(1)}, u32[]{:S(2)}, u32[]{:S(2)}) collective-permute-start(f32[8,128,128]{2,1,0:T(8,128)S(1)} %chosen_3.1), channel_id=1, source_target_pairs={{0,1},{1,0},{2,3},{3,2},{4,5},{5,4},{6,7},{7,6},{8,9},{9,8},{10,11... | collective-permute-start | bytes 1572872 | tf_op jit(solution)/shard_map/ppermute | solution.py:39
  43.4 36.0 %collective-permute-start.23 = (f32[10,128,128]{2,1,0:T(8,128)S(1)}, f32[10,128,128]{2,1,0:T(8,128)S(1)}, u32[]{:S(2)}, u32[]{:S(2)}) collective-permute-start(f32[10,128,128]{2,1,0:T(8,128)S(1)} %get-tuple-element.66.refs_1_), channel_id=1, source_target_pairs={{0,1},{1,0},{2,3},{3,2},{4,5},{5,4},{6,7},{7,6},{8,9},{9,8},{10,11... | collective-permute-start | bytes 1966088 | tf_op jit(solution)/shard_map/ppermute | solution.py:39
  43.6 14.2 %collective-permute-start.13 = (f32[128,128]{1,0:T(8,128)S(1)}, f32[128,128]{1,0:T(8,128)S(1)}, u32[]{:S(2)}, u32[]{:S(2)}) collective-permute-start(f32[128,128]{1,0:T(8,128)S(1)} %get-tuple-element.70), channel_id=1, source_target_pairs={{0,8},{8,16},{16,24},{1,9},{9,17},{17,25},{2,10},{10,18},{18,26},{... | collective-permute-start | bytes 196616 | tf_op jit(solution)/shard_map/ppermute | solution.py:39
  47.1 4.7 %collective-permute-start.10 = (f32[10,4,128]{2,1,0:T(4,128)S(1)}, f32[10,4,128]{2,1,0:T(4,128)S(1)}, u32[]{:S(2)}, u32[]{:S(2)}) collective-permute-start(f32[10,4,128]{2,1,0:T(4,128)S(1)} %get-tuple-element.67), channel_id=1, source_target_pairs={{0,2},{2,4},{4,6},{6,0},{1,3},{3,5},{5,7},{7,1},{8,10},{10,12},{12... | collective-permute-start | bytes 61448 | tf_op jit(solution)/shard_map/ppermute | solution.py:39
  47.1 4.7 %collective-permute-start.11 = (f32[10,4,128]{2,1,0:T(4,128)S(1)}, f32[10,4,128]{2,1,0:T(4,128)S(1)}, u32[]{:S(2)}, u32[]{:S(2)}) collective-permute-start(f32[10,4,128]{2,1,0:T(4,128)S(1)} %get-tuple-element.68.refs_10_), channel_id=1, source_target_pairs={{0,6},{2,0},{4,2},{6,4},{1,7},{3,1},{5,3},{7,5},{8,14},{10,8},{12,... | collective-permute-start | bytes 61448 | tf_op jit(solution)/shard_map/ppermute | solution.py:39
  54.5 3.3 %collective-permute-start.17 = (f32[10,4,128]{2,1,0:T(4,128)S(1)}, f32[10,4,128]{2,1,0:T(4,128)S(1)}, u32[]{:S(2)}, u32[]{:S(2)}) collective-permute-start(f32[10,4,128]{2,1,0:T(4,128)S(1)} %get-tuple-element.75), channel_id=1, source_target_pairs={{0,2},{2,4},{4,6},{6,0},{1,3},{3,5},{5,7},{7,1},{8,10},{10,12},{12... | collective-permute-start | bytes 61448 | tf_op jit(solution)/shard_map/ppermute | solution.py:39
  56.3 9.0 %collective-permute-start.14 = (f32[128,128]{1,0:T(8,128)S(1)}, f32[128,128]{1,0:T(8,128)S(1)}, u32[]{:S(2)}, u32[]{:S(2)}) collective-permute-start(f32[128,128]{1,0:T(8,128)S(1)} %get-tuple-element.72), channel_id=1, source_target_pairs={{8,0},{16,8},{24,16},{9,1},{17,9},{25,17},{10,2},{18,10},{26,18},{... | collective-permute-start | bytes 196616 | tf_op jit(solution)/shard_map/ppermute | solution.py:39
  60.5 27.2 %collective-permute-start.26 = (f32[10,128,128]{2,1,0:T(8,128)S(1)}, f32[10,128,128]{2,1,0:T(8,128)S(1)}, u32[]{:S(2)}, u32[]{:S(2)}) collective-permute-start(f32[10,128,128]{2,1,0:T(8,128)S(1)} %get-tuple-element.76.refs_16_), channel_id=1, source_target_pairs={{0,1},{1,0},{2,3},{3,2},{4,5},{5,4},{6,7},{7,6},{8,9},{9,8},{10,11... | collective-permute-start | bytes 1966088 | tf_op jit(solution)/shard_map/ppermute | solution.py:39
  62.1 3.2 %collective-permute-start.15 = (f32[8,4,128]{2,1,0:T(4,128)S(1)}, f32[8,4,128]{2,1,0:T(4,128)S(1)}, u32[]{:S(2)}, u32[]{:S(2)}) collective-permute-start(f32[8,4,128]{2,1,0:T(4,128)S(1)} %get-tuple-element.73), channel_id=1, source_target_pairs={{0,2},{2,4},{4,6},{6,0},{1,3},{3,5},{5,7},{7,1},{8,10},{10,12},{12... | collective-permute-start | bytes 49160 | tf_op jit(solution)/shard_map/ppermute | solution.py:39
  68.8 10.5 %collective-permute-start.19 = (f32[128,128]{1,0:T(8,128)S(1)}, f32[128,128]{1,0:T(8,128)S(1)}, u32[]{:S(2)}, u32[]{:S(2)}) collective-permute-start(f32[128,128]{1,0:T(8,128)S(1)} %get-tuple-element.78), channel_id=1, source_target_pairs={{0,8},{8,16},{16,24},{1,9},{9,17},{17,25},{2,10},{10,18},{18,26},{... | collective-permute-start | bytes 196616 | tf_op jit(solution)/shard_map/ppermute | solution.py:39
  73.2 6.3 %collective-permute-start.20 = (f32[128,128]{1,0:T(8,128)S(1)}, f32[128,128]{1,0:T(8,128)S(1)}, u32[]{:S(2)}, u32[]{:S(2)}) collective-permute-start(f32[128,128]{1,0:T(8,128)S(1)} %get-tuple-element.79), channel_id=1, source_target_pairs={{8,0},{16,8},{24,16},{9,1},{17,9},{25,17},{10,2},{18,10},{26,18},{... | collective-permute-start | bytes 196616 | tf_op jit(solution)/shard_map/ppermute | solution.py:39
  74.5 3.3 %collective-permute-start.21 = (f32[10,4,128]{2,1,0:T(4,128)S(1)}, f32[10,4,128]{2,1,0:T(4,128)S(1)}, u32[]{:S(2)}, u32[]{:S(2)}) collective-permute-start(f32[10,4,128]{2,1,0:T(4,128)S(1)} %get-tuple-element.80), channel_id=1, source_target_pairs={{0,2},{2,4},{4,6},{6,0},{1,3},{3,5},{5,7},{7,1},{8,10},{10,12},{12... | collective-permute-start | bytes 61448 | tf_op jit(solution)/shard_map/ppermute | solution.py:39
  84.4 14.5 %collective-permute-start.25 = (f32[8,128,128]{2,1,0:T(8,128)S(1)}, f32[8,128,128]{2,1,0:T(8,128)S(1)}, u32[]{:S(2)}, u32[]{:S(2)}) collective-permute-start(f32[8,128,128]{2,1,0:T(8,128)S(1)} %get-tuple-element.87), channel_id=1, source_target_pairs={{0,1},{1,0},{2,3},{3,2},{4,5},{5,4},{6,7},{7,6},{8,9},{9,8},{10,11... | collective-permute-start | bytes 1572872 | tf_op jit(solution)/shard_map/ppermute | solution.py:39
  85.0 19.6 %collective-permute-start.24 = (f32[4,128,128]{2,1,0:T(8,128)S(1)}, f32[4,128,128]{2,1,0:T(8,128)S(1)}, u32[]{:S(2)}, u32[]{:S(2)}) collective-permute-start(f32[4,128,128]{2,1,0:T(8,128)S(1)} %get-tuple-element.84), channel_id=1, source_target_pairs={{0,1},{1,0},{2,3},{3,2},{4,5},{5,4},{6,7},{7,6},{8,9},{9,8},{10,11... | collective-permute-start | bytes 786440 | tf_op jit(solution)/shard_map/ppermute | solution.py:39
  (8 other events, 33.7 us)

commit v6 on v5

--- a/solution.py
+++ b/solution.py
@@ -59,20 +59,36 @@
 
 
 def chosen_body(begin, field, *refs):
-    out, sem = refs[-2:]
-    copy = pltpu.make_async_copy(field.at[pl.ds(begin, out.shape[0])], out, sem)
-    copy.start()
-    copy.wait()
+    out, held, sem = refs[-3:]
+    count = out.shape[0]
+    piece = 2
+    inward, outward = [], []
+    for number, at in enumerate(range(0, count, piece)):
+        here = pl.ds(at, piece)
+        inward.append(pltpu.make_async_copy(field.at[pl.ds(begin + at, piece)], held.at[here], sem.at[0, number]))
+        outward.append(pltpu.make_async_copy(held.at[here], out.at[here], sem.at[1, number]))
+        inward[-1].start()
+    for first, then in zip(inward, outward):
+        first.wait()
+        then.start()
+    for copy in outward:
+        copy.wait()
 
 
 def layers_body(depth, field, coef, first_x, last_x, first_y, last_y, held, sem):
     planes, rows = field.shape[0], field.shape[1]
-    copy = pltpu.make_async_copy(field, held, sem)
-    copy.start()
+    pieces = sem.shape[0]
+    size = planes // pieces
+    copies = []
+    for number in range(pieces):
+        here = pl.ds(number * size, size)
+        copies.append(pltpu.make_async_copy(field.at[here], held.at[here], sem.at[number]))
+        copies[-1].start()
     for out in (first_x, last_x, first_y, last_y):
         out[rows : rows + coef.shape[0]] = coef[...]
         out[rows + coef.shape[0] :] = jnp.zeros((out.shape[0] - rows - coef.shape[0], lanes), f32)
-    copy.wait()
+    for copy in copies:
+        copy.wait()
     first_x[:rows] = held[0]
     last_x[:rows] = held[planes - 1]
     for plane in range(planes):
@@ -191,7 +207,7 @@
     if groups % 2:
         flush(count - group, upper_a, lower_a)
     else:
-        flush(begin(groups - 2), upper_a, lower_a)
+        flush((groups - 2) * group, upper_a, lower_a)
         fill(count - group, upper_b, lower_b)
         flush(count - group, upper_b, lower_b)
 
@@ -238,6 +254,9 @@
 
     def place(i):
         local, plane = i + runs[0].local, i + runs[0].plane
+        if len(runs) > 1 and isinstance(i, int):
+            run = runs[0] if i < runs[0].count else runs[1]
+            return i - (0 if i < runs[0].count else runs[0].count) + run.local, i - (0 if i < runs[0].count else runs[0].count) + run.plane
         if len(runs) > 1:
             later = i >= runs[0].count
             local = jnp.where(later, i - runs[0].count + runs[1].local, local)
@@ -250,6 +269,9 @@
 
     used = pl.ds(0, 2 * lanes if sends else lanes)
     operate(depth, total, place, scratch[:-1], halves, diagonal, named["hi"].at[:, used], named["lo"].at[:, used], put)
+    if "last" in named:
+        named["last"][...] = named["residual"][0]
+        named["first"][...] = named["residual"][1]
 
 
 def own_emit(named, i, plane, out, padded, local, rows):
@@ -261,15 +283,6 @@
     named["residual"][i] = value
     named["low"][i] = value[:depth]
     named["high"][i] = value[rows - depth :]
-    if "last" in named:
-
-        @pl.when(i == 0)
-        def _():
-            named["last"][...] = value
-
-        @pl.when(i == 1)
-        def _():
-            named["first"][...] = value
 
 
 def second_emit(split, named, i, plane, out, padded, local, rows):
@@ -277,20 +290,11 @@
     later = here - step_size * out[:, :lanes]
     fields = named["start"][plane] + step_size * (here + later)
     values = (later, fields, out[:, lanes:])
-    if split is None:
-        for name, value in zip(("later", "fields", "part"), values):
-            named[name][i] = value
+    named["later"][i], named["fields"][i] = later, fields
+    if split is not None and isinstance(i, int) and i >= split:
+        named["part2"][i - split] = out[:, lanes:]
     else:
-
-        @pl.when(i < split)
-        def _():
-            for name, value in zip(("later", "fields", "part"), values):
-                named[name][i] = value
-
-        @pl.when(i >= split)
-        def _():
-            for name, value in zip(("later2", "fields2", "part2"), values):
-                named[name][i - split] = value
+        named["part"][i] = out[:, lanes:]
 
 
 def over_planes(name, depth, width, operands, outs, pieces, edges, layers, runs, sends, emit, work, ties=()):
@@ -317,6 +321,11 @@
     last[...] = planes[:, rows - depth :, :]
 
 
+def handed_body(first, last, tie, first_out, last_out):
+    first_out[...] = first[...]
+    last_out[...] = last[...]
+
+
 def sides_and_plane_body(depth, which, *refs):
     first, last, plane = refs[-3:]
     planes = refs[0]
@@ -326,7 +335,7 @@
     plane[...] = planes[which]
 
 
-def last_body(first, later_part, fields_part, came, *refs):
+def last_body(first, skip, later_part, fields_part, came, *refs):
     later, fields, staged, sem = refs[-4:]
     count = came.shape[0]
     planes = later.shape[0]
@@ -335,8 +344,8 @@
     for begin in range(0, count, piece):
         end = min(begin + piece, count)
         for at in range(begin, end):
-            staged[0, at] = later_part[at] - step_size * came[at]
-            staged[1, at] = fields_part[at] - (step_size * step_size) * came[at]
+            staged[0, at] = later_part[skip + at] - step_size * came[at]
+            staged[1, at] = fields_part[skip + at] - (step_size * step_size) * came[at]
         wrap = max(begin, min(end, planes - first))
         for which, target in ((0, later), (1, fields)):
             for low, high in ((begin, wrap), (wrap, end)):
@@ -351,10 +360,10 @@
         copy.wait()
 
 
-def add_last(first, shape, later_part, fields_part, came, before):
+def add_last(first, shape, later_part, fields_part, came, before, skip=0):
     count = came.shape[0]
     return call(
-        functools.partial(last_body, first),
+        functools.partial(last_body, first, skip),
         [(shape, f32)] * 2,
         [pltpu.VMEM((2,) + came.shape, f32), pltpu.SemaphoreType.DMA((2 * count + 4,))],
         in_specs=[whole] * 3 + [anywhere] * len(before),
@@ -372,7 +381,7 @@
     flat = (nx,) + plane
     start = start_field.reshape(flat)
     right = right_side.reshape(flat)
-    low, high = nx // 4, (11 * nx) // 16
+    low, high = (3 * nx) // 16, (5 * nx) // 8
     width = 3 * modes
     strip = lambda count: ((count, depth, modes), f32)
 
@@ -380,8 +389,9 @@
         (out,) = call(
             functools.partial(chosen_body, begin),
             [((count,) + plane, f32)],
-            [pltpu.SemaphoreType.DMA],
+            [pltpu.VMEM((count,) + plane, f32), pltpu.SemaphoreType.DMA((2, count))],
             in_specs=[anywhere] * (1 + len(ties)),
+            out_specs=[anywhere],
             vmem=vmem_bytes if ties else most_bytes,
             name=name,
         )(start, *ties)
@@ -394,7 +404,7 @@
     first_x, last_x, first_y, last_y = call(
         functools.partial(layers_body, depth),
         [layer] * 4,
-        [pltpu.VMEM(flat, f32), pltpu.SemaphoreType.DMA],
+        [pltpu.VMEM(flat, f32), pltpu.SemaphoreType.DMA((8,))],
         in_specs=[anywhere, whole],
         vmem=most_bytes,
         name="layers",
@@ -463,15 +473,25 @@
         return over_planes(name, depth, width, {**theirs, **operands}, outs, pieces, edges, layers, runs, False, emit, count / 10, ties)
 
     def second(name, counts, operands, pieces, edges, layers, runs, ties=(), work=1.0):
-        outs = {}
-        for number, count in enumerate(counts):
-            mark = "" if number == 0 else "2"
-            outs.update({key + mark: (count,) + plane for key in ("later", "fields", "part")})
+        outs = {key: (sum(counts),) + plane for key in ("later", "fields")}
+        outs["part"] = (counts[0],) + plane
+        if len(counts) > 1:
+            outs["part2"] = (counts[1],) + plane
         emit = functools.partial(second_emit, counts[0] if len(counts) > 1 else None)
         operands = {**mine, "start": start, **operands}
         return over_planes(name, depth, width, operands, outs, pieces, edges, layers, runs, True, emit, work, ties)
 
-    raw_low_1, raw_high_1 = exchanged(*sides(raw_1, None, "sides_1"))
+    sides_1 = sides(raw_1, None, "sides_1", rest_1)
+    raw_low_1, raw_high_1 = exchanged(*sides_1)
+    rest_2 = own(
+        "own_2",
+        n2,
+        [("start", high - 2, n2 + 2, 0)],
+        [],
+        [("low_y", "high_y", high - 1, n2, 1, True)],
+        [Run(1, high - 1, n2)],
+        (sides_1[0],),
+    )
     residual_1, first_1, last_1 = middle(
         "middle_1",
         n1,
@@ -481,15 +501,16 @@
         [("low_1", "high_1", 1, n1, 1, False)],
         [Run(1, low + 1, n1)],
         False,
+        (rest_2,),
     )
     low_1, high_1 = exchanged(first_1, last_1)
-    rest_2 = own(
-        "own_2",
-        n2,
-        [("start", high - 2, n2 + 2, 0)],
-        [],
-        [("low_y", "high_y", high - 1, n2, 1, True)],
-        [Run(1, high - 1, n2)],
+    rest_3 = own(
+        "own_3",
+        n3,
+        [("start", nx - 2, 2, 0), ("start", 0, low + 2, 4)],
+        [("high_x", 2), ("low_x", 3)],
+        [("low_y", "high_y", nx - 1, 1, 1, True), ("low_y", "high_y", 0, low + 1, 4, True)],
+        ring,
         (first_1,),
     )
     later_1, fields_1, part_1 = second(
@@ -500,22 +521,13 @@
         [],
         [("low_1", "high_1", 1, n1 - 2, 1, False)],
         [Run(1, low + 2, n1 - 2)],
-        (rest_2,),
+        (rest_3,),
     )
     came_1 = sent(part_1, "ma", 1, True)
 
     sides_2 = sides(raw_2, nx - high - 1, "sides_2", part_1)
     raw_low_2, raw_high_2 = exchanged(sides_2[0], sides_2[1])
     raw_low_x = sent(sides_2[2], "gx", 1, False)
-    rest_3 = own(
-        "own_3",
-        n3,
-        [("start", nx - 2, 2, 0), ("start", 0, low + 2, 4)],
-        [("high_x", 2), ("low_x", 3)],
-        [("low_y", "high_y", nx - 1, 1, 1, True), ("low_y", "high_y", 0, low + 1, 4, True)],
-        ring,
-        (sides_2[0],),
-    )
     residual_2, first_2, last_2 = middle(
         "middle_2",
         n2,
@@ -525,7 +537,6 @@
         [("low_1", "high_1", high - low - 1, 1, 1, False), ("low_2", "high_2", 0, n2 - 1, 2, False)],
         [Run(1, high - 1, n2)],
         False,
-        (rest_3,),
     )
     low_2, high_2 = exchanged(first_2, last_2)
 
@@ -567,12 +578,21 @@
         True,
         (part_2,),
     )
-    low_3, high_3 = exchanged(first_3, last_3)
     next_low_x = sent(edge_last, "gx", 1, False)
     next_high_x = sent(edge_first, "gx", -1, False)
-    final = 4
+    low_3, high_3 = exchanged(
+        *call(
+            handed_body,
+            [strip(n3)] * 2,
+            [],
+            in_specs=[whole] * 2 + [anywhere],
+            work=0.1,
+            name="handed",
+        )(first_3, last_3, came_1)
+    )
+    final = 2 * group if -(-(low + 4) // group) % 2 == 0 else group
     count = low + 4
-    later_3, fields_3, part_3, later_4, fields_4, part_4 = second(
+    later_3, fields_3, part_3, part_4 = second(
         "second_3",
         [count - final, final],
         {
@@ -606,7 +626,7 @@
     outs = add_last(low + 2, flat, later_1, fields_1, came_1, ())
     outs = add_last(high - 2, flat, later_2, fields_2, came_2, outs)
     outs = add_last(nx - 2, flat, later_3, fields_3, came_3, outs)
-    later, fields = add_last(low + 2 - final, flat, later_4, fields_4, came_4, outs)
+    later, fields = add_last(low + 2 - final, flat, later_3, fields_3, came_4, outs, count - final)
     return (fields.reshape(start_field.shape), later.reshape(start_field.shape))
 
 

time: 106 us -> 114 us (1.075)
  waiting for transfers between devices: 23 us -> 30 us
    ppermute x27, waiting for transfers between devices: 23 us -> 30 us  [sent(): return lax.ppermute(array, axis, pairs)]
    pallas_call x3, Pallas kernels: 2.41 us -> 5.54 us  [chosen(): call(functools.partial(chosen_body, begin), [((count,) + plane, f32)], [p...]
    pallas_call x9, Pallas kernels: 27.7 us -> 25.2 us  [over_planes(): call(functools.partial(planes_body, depth, tuple(names), tuple(outs), pie...]
    pallas_call x4 -> x5, Pallas kernels: 4.65 us -> 4.66 us  [the longest x4 4.65 us: add_last(): call(functools.partial(last_body, first, skip), [(shape, f32)] * 2, [pltp...]
  transfers between devices with their start and end apart: 27 -> 27, of which waited for: 9 -> 8; matrix products, arithmetic and copies ran while one was open for 1% -> 1% of each run, Pallas kernels for 38% -> 36%
where the time goes in v6:
time: 114 us
  Pallas kernels  43.7 us (38%)
  starting transfers between devices  37.7 us (33%)
  waiting for transfers between devices  30 us (26%)
  between operations  1.19 us (1%)
    ppermute x27, starting transfers between devices, sent(): return lax.ppermute(array, axis, pairs)  37.7 us
    ppermute x27, waiting for transfers between devices, sent(): return lax.ppermute(array, axis, pairs)  30 us
    pallas_call x9, Pallas kernels, over_planes(): call(functools.partial(planes_body, depth, tuple(names), tuple(outs), pie...  25.2 us
    pallas_call x3, Pallas kernels, chosen(): call(functools.partial(chosen_body, begin), [((count,) + plane, f32)], [p...  5.54 us
    pallas_call x4, Pallas kernels, add_last(): call(functools.partial(last_body, first, skip), [(shape, f32)] * 2, [pltp...  4.65 us
    pallas_call x1, Pallas kernels, shards(): call(functools.partial(layers_body, depth), [layer] * 4, [pltpu.VMEM(flat...  3.23 us
    pallas_call x1, Pallas kernels, shards(): call(functools.partial(diagonal_body, depth), [(halves_shape, f32), ((3,)...  2.67 us
  transfers between devices with their start and end apart: 27, of which 8 were waited for; matrix products, arithmetic and copies ran while one was open for 1% of the time, Pallas kernels for 36%

profile of v6, /device:TPU:0, one launch (start us, length us, event | category | flops | bytes accessed | tf_op | source)
XLA Modules:
  0.0 113.6 jit_solution(7451227572598354299)
XLA Ops:
  0.6 2.2 %chosen_1.1 = f32[14,128,128]{2,1,0:T(8,128)} custom-call(f32[32,128,128]{2,1,0:T(8,128)} %bitcast.6), custom_call_target="tpu_custom_call" | custom-call | flops 1000000 | bytes 2000 | tf_op jit(solution)/shard_map/chosen_1/pallas_call | solution.py:389
  2.8 3.0 %collective-permute-start.4 = (f32[14,128,128]{2,1,0:T(8,128)}, f32[14,128,128]{2,1,0:T(8,128)S(1)}, u32[]{:S(2)}, u32[]{:S(2)}) collective-permute-start(f32[14,128,128]{2,1,0:T(8,128)} %chosen_1.1), channel_id=1, source_target_pairs={{0,1},{1,0},{2,3},{3,2},{4,5},{5,4},{6,7},{7,6},{8,9},{9,8},{10,11... | collective-permute-start | bytes 2752520 | tf_op jit(solution)/shard_map/ppermute | solution.py:39
  6.9 3.2 %layers.1 = (f32[256,128]{1,0:T(8,128)}, f32[256,128]{1,0:T(8,128)}, f32[256,128]{1,0:T(8,128)}, f32[256,128]{1,0:T(8,128)}) custom-call(f32[32,128,128]{2,1,0:T(8,128)} %bitcast.7, f32[96,128]{1,0:T(8,128)} %copy.15.coef), custom_call_target="tpu_custom_call" | custom-call | flops 1000000 | bytes 2000 | tf_op jit(solution)/shard_map/layers/pallas_call | solution.py:404
  10.2 3.5 %collective-permute-start = (f32[256,128]{1,0:T(8,128)}, f32[256,128]{1,0:T(8,128)S(1)}, u32[]{:S(2)}, u32[]{:S(2)}) collective-permute-start(f32[256,128]{1,0:T(8,128)} %get-tuple-element.51), channel_id=1, source_target_pairs={{0,8},{8,16},{16,24},{1,9},{9,17},{17,25},{2,10},{10,18},{18,26},{... | collective-permute-start | bytes 393224 | tf_op jit(solution)/shard_map/ppermute | solution.py:39
  16.8 1.9 %halves.1.halves_in = f32[3,34,144,128]{3,2,1,0:T(8,128)S(1)} custom-call(f32[96,128]{1,0:T(8,128)S(1)} %copy-done.3), custom_call_target="tpu_custom_call" | custom-call | flops 1000000 | bytes 2000 | tf_op jit(solution)/shard_map/halves/pallas_call | solution.py:426
  20.7 2.7 %diagonal.1 = (f32[3,34,144,128]{3,2,1,0:T(8,128)S(1)}, f32[3,32,128,128]{3,2,1,0:T(8,128)S(1)}) custom-call(f32[256,128]{1,0:T(8,128)S(1)} %collective-permute-done.low_x.refs_8_, f32[256,128]{1,0:T(8,128)S(1)} %collective-permute-done.1.high_x.refs_9_, f32[256,128]{1,0:T(8,128)S(1)} %collective-permute-done.2.low_y.refs_6_, ...), custom_call_target="tpu_custom_call", output_to_operand_aliasing={{0}: (4, {})} | custom-call | flops 1000000 | bytes 2000 | tf_op jit(solution)/shard_map/diagonal/pallas_call | solution.py:427
  23.4 2.3 %chosen_2.1 = f32[12,128,128]{2,1,0:T(8,128)S(1)} custom-call(f32[32,128,128]{2,1,0:T(8,128)S(1)} %bitcast.8, bf16[384,256]{1,0:T(8,128)(2,1)S(1)} %get-tuple-element.57.refs_2_.refs_0_, f32[3,32,128,128]{3,2,1,0:T(8,128)S(1)} %get-tuple-element.56.refs_1_), custom_call_target="tpu_custom_call" | custom-call | flops 1000000 | bytes 2000 | tf_op jit(solution)/shard_map/chosen_2/pallas_call | solution.py:389
  26.3 2.9 %own_1.1.refs_1_.refs_4_.refs_0_ = f32[12,128,128]{2,1,0:T(8,128)S(1)} custom-call(f32[3,34,144,128]{3,2,1,0:T(8,128)S(1)} %get-tuple-element.55.refs_0_, f32[3,32,128,128]{3,2,1,0:T(8,128)S(1)} %get-tuple-element.56.refs_1_, bf16[384,256]{1,0:T(8,128)(2,1)S(1)} %get-tuple-element.57.refs_2_.refs_0_, bf16[384,256]{1,0:T(8,128)(2,1)S(1)} %get-tuple-element.58.refs_3_, ...), custom_call_target="tpu_custom_call" | custom-call | flops 1200000 | bytes 2400 | tf_op jit(solution)/shard_map/own_1/pallas_call | solution.py:306
  31.0 2.9 %own_2.1.refs_8_.refs_4_ = f32[12,128,128]{2,1,0:T(8,128)S(1)} custom-call(f32[3,34,144,128]{3,2,1,0:T(8,128)S(1)} %get-tuple-element.55.refs_0_, f32[3,32,128,128]{3,2,1,0:T(8,128)S(1)} %get-tuple-element.56.refs_1_, bf16[384,256]{1,0:T(8,128)(2,1)S(1)} %get-tuple-element.57.refs_2_.refs_0_, bf16[384,256]{1,0:T(8,128)(2,1)S(1)} %get-tuple-element.58.refs_3_, ...), custom_call_target="tpu_custom_call" | custom-call | flops 1200000 | bytes 2400 | tf_op jit(solution)/shard_map/own_2/pallas_call | solution.py:306
  33.9 2.9 %middle_1.1 = (f32[12,128,128]{2,1,0:T(8,128)S(1)}, f32[12,4,128]{2,1,0:T(4,128)S(1)}, f32[12,4,128]{2,1,0:T(4,128)S(1)}) custom-call(f32[3,34,144,128]{3,2,1,0:T(8,128)S(1)} %get-tuple-element.55.refs_0_, f32[3,32,128,128]{3,2,1,0:T(8,128)S(1)} %get-tuple-element.56.refs_1_, bf16[384,128]{1,0:T(8,128)(2,1)S(1)} %get-tuple-element.59.refs_2_, ...), custom_call_target="tpu_custom_call" | custom-call | flops 1200000 | bytes 2400 | tf_op jit(solution)/shard_map/middle_1/pallas_call | solution.py:306
  38.6 2.1 %own_3.1.refs_8_.refs_4_ = f32[8,128,128]{2,1,0:T(8,128)S(1)} custom-call(f32[3,34,144,128]{3,2,1,0:T(8,128)S(1)} %get-tuple-element.55.refs_0_, f32[3,32,128,128]{3,2,1,0:T(8,128)S(1)} %get-tuple-element.56.refs_1_, bf16[384,256]{1,0:T(8,128)(2,1)S(1)} %get-tuple-element.57.refs_2_.refs_0_, bf16[384,256]{1,0:T(8,128)(2,1)S(1)} %get-tuple-element.58.refs_3_, ...), custom_call_target="tpu_custom_call" | custom-call | flops 800000 | bytes 1600 | tf_op jit(solution)/shard_map/own_3/pallas_call | solution.py:306
  40.8 2.7 %second_1.1 = (f32[10,128,128]{2,1,0:T(8,128)S(1)}, f32[10,128,128]{2,1,0:T(8,128)S(1)}, f32[10,128,128]{2,1,0:T(8,128)S(1)}) custom-call(f32[3,34,144,128]{3,2,1,0:T(8,128)S(1)} %get-tuple-element.55.refs_0_, f32[3,32,128,128]{3,2,1,0:T(8,128)S(1)} %get-tuple-element.56.refs_1_, bf16[384,256]{1,0:T(8,128)(2,1)S(1)} %get-tuple-element.57.refs_2_.refs_0_, ...), custom_call_target="tpu_custom_call" | custom-call | flops 1000000 | bytes 2000 | tf_op jit(solution)/shard_map/second_1/pallas_call | solution.py:306
  46.8 4.1 %collective-permute-start.13 = (f32[128,128]{1,0:T(8,128)S(1)}, f32[128,128]{1,0:T(8,128)S(1)}, u32[]{:S(2)}, u32[]{:S(2)}) collective-permute-start(f32[128,128]{1,0:T(8,128)S(1)} %get-tuple-element.70), channel_id=1, source_target_pairs={{0,8},{8,16},{16,24},{1,9},{9,17},{17,25},{2,10},{10,18},{18,26},{... | collective-permute-start | bytes 196616 | tf_op jit(solution)/shard_map/ppermute | solution.py:39
  54.1 3.0 %middle_2.1 = (f32[12,128,128]{2,1,0:T(8,128)S(1)}, f32[12,4,128]{2,1,0:T(4,128)S(1)}, f32[12,4,128]{2,1,0:T(4,128)S(1)}) custom-call(f32[3,34,144,128]{3,2,1,0:T(8,128)S(1)} %get-tuple-element.55.refs_0_, f32[3,32,128,128]{3,2,1,0:T(8,128)S(1)} %get-tuple-element.56.refs_1_, bf16[384,128]{1,0:T(8,128)(2,1)S(1)} %get-tuple-element.59.refs_2_, ...), custom_call_target="tpu_custom_call" | custom-call | flops 1200000 | bytes 2400 | tf_op jit(solution)/shard_map/middle_2/pallas_call | solution.py:306
  57.1 1.9 %collective-permute-start.17 = (f32[12,4,128]{2,1,0:T(4,128)S(1)}, f32[12,4,128]{2,1,0:T(4,128)S(1)}, u32[]{:S(2)}, u32[]{:S(2)}) collective-permute-start(f32[12,4,128]{2,1,0:T(4,128)S(1)} %get-tuple-element.75), channel_id=1, source_target_pairs={{0,2},{2,4},{4,6},{6,0},{1,3},{3,5},{5,7},{7,1},{8,10},{10,12},{12... | collective-permute-start | bytes 73736 | tf_op jit(solution)/shard_map/ppermute | solution.py:39
  59.3 9.9 %collective-permute-done.12.refs_0_.refs_7_ = f32[6,128,128]{2,1,0:T(8,128)S(1)} collective-permute-done((f32[6,128,128]{2,1,0:T(8,128)S(1)}, f32[6,128,128]{2,1,0:T(8,128)S(1)}, u32[]{:S(2)}, u32[]{:S(2)}) %collective-permute-start.12) | collective-permute-done | bytes 393248 | tf_op jit(solution)/shard_map/ppermute | solution.py:39
  69.3 3.2 %second_2.1 = (f32[12,128,128]{2,1,0:T(8,128)S(1)}, f32[12,128,128]{2,1,0:T(8,128)S(1)}, f32[12,128,128]{2,1,0:T(8,128)S(1)}) custom-call(f32[3,34,144,128]{3,2,1,0:T(8,128)S(1)} %get-tuple-element.55.refs_0_, f32[3,32,128,128]{3,2,1,0:T(8,128)S(1)} %get-tuple-element.56.refs_1_, bf16[384,256]{1,0:T(8,128)(2,1)S(1)} %get-tuple-element.57.refs_2_.refs_0_, ...), custom_call_target="tpu_custom_call" | custom-call | flops 1000000 | bytes 2000 | tf_op jit(solution)/shard_map/second_2/pallas_call | solution.py:306
  75.4 1.7 %collective-permute-start.16 = (f32[6,4,128]{2,1,0:T(4,128)S(1)}, f32[6,4,128]{2,1,0:T(4,128)S(1)}, u32[]{:S(2)}, u32[]{:S(2)}) collective-permute-start(f32[6,4,128]{2,1,0:T(4,128)S(1)} %get-tuple-element.74.refs_11_), channel_id=1, source_target_pairs={{0,6},{2,0},{4,2},{6,4},{1,7},{3,1},{5,3},{7,5},{8,14},{10,8},{12,... | collective-permute-start | bytes 36872 | tf_op jit(solution)/shard_map/ppermute | solution.py:39
  78.5 1.9 %collective-permute-done.14.refs_9_ = f32[128,128]{1,0:T(8,128)S(1)} collective-permute-done((f32[128,128]{1,0:T(8,128)S(1)}, f32[128,128]{1,0:T(8,128)S(1)}, u32[]{:S(2)}, u32[]{:S(2)}) %collective-permute-start.14) | collective-permute-done | bytes 65568 | tf_op jit(solution)/shard_map/ppermute | solution.py:39
  80.4 2.3 %middle_3.1 = (f32[8,128,128]{2,1,0:T(8,128)S(1)}, f32[8,4,128]{2,1,0:T(4,128)S(1)}, f32[8,4,128]{2,1,0:T(4,128)S(1)}, f32[128,128]{1,0:T(8,128)S(1)}, f32[128,128]{1,0:T(8,128)S(1)}) custom-call(f32[3,34,144,128]{3,2,1,0:T(8,128)S(1)} %get-tuple-element.55.refs_0_, f32[3,32,128,128]{3,2,1,0:T(8,128)S(1)} %get-tuple-element.56.refs_1_, ...), custom_call_target="tpu_custom_call" | custom-call | flops 800000 | bytes 1600 | tf_op jit(solution)/shard_map/middle_3/pallas_call | solution.py:306
  82.7 3.9 %collective-permute-start.19 = (f32[128,128]{1,0:T(8,128)S(1)}, f32[128,128]{1,0:T(8,128)S(1)}, u32[]{:S(2)}, u32[]{:S(2)}) collective-permute-start(f32[128,128]{1,0:T(8,128)S(1)} %get-tuple-element.78), channel_id=1, source_target_pairs={{0,8},{8,16},{16,24},{1,9},{9,17},{17,25},{2,10},{10,18},{18,26},{... | collective-permute-start | bytes 196616 | tf_op jit(solution)/shard_map/ppermute | solution.py:39
  89.7 3.2 %collective-permute-done.20.refs_9_ = f32[128,128]{1,0:T(8,128)S(1)} collective-permute-done((f32[128,128]{1,0:T(8,128)S(1)}, f32[128,128]{1,0:T(8,128)S(1)}, u32[]{:S(2)}, u32[]{:S(2)}) %collective-permute-start.20) | collective-permute-done | bytes 65568 | tf_op jit(solution)/shard_map/ppermute | solution.py:39
  93.0 3.3 %second_3.1 = (f32[10,128,128]{2,1,0:T(8,128)S(1)}, f32[10,128,128]{2,1,0:T(8,128)S(1)}, f32[8,128,128]{2,1,0:T(8,128)S(1)}, f32[2,128,128]{2,1,0:T(8,128)S(1)}) custom-call(f32[3,34,144,128]{3,2,1,0:T(8,128)S(1)} %get-tuple-element.55.refs_0_, f32[3,32,128,128]{3,2,1,0:T(8,128)S(1)} %get-tuple-element.56.refs_1_, ...), custom_call_target="tpu_custom_call" | custom-call | flops 1000000 | bytes 2000 | tf_op jit(solution)/shard_map/second_3/pallas_call | solution.py:306
  101.1 10.1 %collective-permute-done.25.came = f32[8,128,128]{2,1,0:T(8,128)S(1)} collective-permute-done((f32[8,128,128]{2,1,0:T(8,128)S(1)}, f32[8,128,128]{2,1,0:T(8,128)S(1)}, u32[]{:S(2)}, u32[]{:S(2)}) %collective-permute-start.25) | collective-permute-done | bytes 524320 | tf_op jit(solution)/shard_map/ppermute | solution.py:39
  (67 shorter events, 31.7 us)
Async XLA Ops:
  2.8 26.3 %collective-permute-start.4 = (f32[14,128,128]{2,1,0:T(8,128)}, f32[14,128,128]{2,1,0:T(8,128)S(1)}, u32[]{:S(2)}, u32[]{:S(2)}) collective-permute-start(f32[14,128,128]{2,1,0:T(8,128)} %chosen_1.1), channel_id=1, source_target_pairs={{0,1},{1,0},{2,3},{3,2},{4,5},{5,4},{6,7},{7,6},{8,9},{9,8},{10,11... | collective-permute-start | bytes 2752520 | tf_op jit(solution)/shard_map/ppermute | solution.py:39
  10.2 9.0 %collective-permute-start = (f32[256,128]{1,0:T(8,128)}, f32[256,128]{1,0:T(8,128)S(1)}, u32[]{:S(2)}, u32[]{:S(2)}) collective-permute-start(f32[256,128]{1,0:T(8,128)} %get-tuple-element.51), channel_id=1, source_target_pairs={{0,8},{8,16},{16,24},{1,9},{9,17},{17,25},{2,10},{10,18},{18,26},{... | collective-permute-start | bytes 393224 | tf_op jit(solution)/shard_map/ppermute | solution.py:39
  13.7 7.1 %collective-permute-start.1 = (f32[256,128]{1,0:T(8,128)}, f32[256,128]{1,0:T(8,128)S(1)}, u32[]{:S(2)}, u32[]{:S(2)}) collective-permute-start(f32[256,128]{1,0:T(8,128)} %get-tuple-element.52), channel_id=1, source_target_pairs={{8,0},{16,8},{24,16},{9,1},{17,9},{25,17},{10,2},{18,10},{26,18},{... | collective-permute-start | bytes 393224 | tf_op jit(solution)/shard_map/ppermute | solution.py:39
  15.0 5.8 %collective-permute-start.2 = (f32[256,128]{1,0:T(8,128)}, f32[256,128]{1,0:T(8,128)S(1)}, u32[]{:S(2)}, u32[]{:S(2)}) collective-permute-start(f32[256,128]{1,0:T(8,128)} %get-tuple-element.53), channel_id=1, source_target_pairs={{0,2},{2,4},{4,6},{6,0},{1,3},{3,5},{5,7},{7,1},{8,10},{10,12},{12... | collective-permute-start | bytes 393224 | tf_op jit(solution)/shard_map/ppermute | solution.py:39
  15.0 5.7 %collective-permute-start.3 = (f32[256,128]{1,0:T(8,128)}, f32[256,128]{1,0:T(8,128)S(1)}, u32[]{:S(2)}, u32[]{:S(2)}) collective-permute-start(f32[256,128]{1,0:T(8,128)} %get-tuple-element.54), channel_id=1, source_target_pairs={{0,6},{2,0},{4,2},{6,4},{1,7},{3,1},{5,3},{7,5},{8,14},{10,8},{12,... | collective-permute-start | bytes 393224 | tf_op jit(solution)/shard_map/ppermute | solution.py:39
  25.7 21.0 %collective-permute-start.7 = (f32[12,128,128]{2,1,0:T(8,128)S(1)}, f32[12,128,128]{2,1,0:T(8,128)S(1)}, u32[]{:S(2)}, u32[]{:S(2)}) collective-permute-start(f32[12,128,128]{2,1,0:T(8,128)S(1)} %chosen_2.1), channel_id=1, source_target_pairs={{0,1},{1,0},{2,3},{3,2},{4,5},{5,4},{6,7},{7,6},{8,9},{9,8},{10,11... | collective-permute-start | bytes 2359304 | tf_op jit(solution)/shard_map/ppermute | solution.py:39
  29.2 4.7 %collective-permute-start.5 = (f32[14,4,128]{2,1,0:T(4,128)S(1)}, f32[14,4,128]{2,1,0:T(4,128)S(1)}, u32[]{:S(2)}, u32[]{:S(2)}) collective-permute-start(f32[14,4,128]{2,1,0:T(4,128)S(1)} %get-tuple-element.61), channel_id=1, source_target_pairs={{0,2},{2,4},{4,6},{6,0},{1,3},{3,5},{5,7},{7,1},{8,10},{10,12},{12... | collective-permute-start | bytes 86024 | tf_op jit(solution)/shard_map/ppermute | solution.py:39
  29.7 4.1 %collective-permute-start.6 = (f32[14,4,128]{2,1,0:T(4,128)S(1)}, f32[14,4,128]{2,1,0:T(4,128)S(1)}, u32[]{:S(2)}, u32[]{:S(2)}) collective-permute-start(f32[14,4,128]{2,1,0:T(4,128)S(1)} %get-tuple-element.62.refs_10_), channel_id=1, source_target_pairs={{0,6},{2,0},{4,2},{6,4},{1,7},{3,1},{5,3},{7,5},{8,14},{10,8},{12,... | collective-permute-start | bytes 86024 | tf_op jit(solution)/shard_map/ppermute | solution.py:39
  36.8 3.9 %collective-permute-start.8 = (f32[12,4,128]{2,1,0:T(4,128)S(1)}, f32[12,4,128]{2,1,0:T(4,128)S(1)}, u32[]{:S(2)}, u32[]{:S(2)}) collective-permute-start(f32[12,4,128]{2,1,0:T(4,128)S(1)} %get-tuple-element.64), channel_id=1, source_target_pairs={{0,2},{2,4},{4,6},{6,0},{1,3},{3,5},{5,7},{7,1},{8,10},{10,12},{12... | collective-permute-start | bytes 73736 | tf_op jit(solution)/shard_map/ppermute | solution.py:39
  37.5 3.3 %collective-permute-start.9 = (f32[12,4,128]{2,1,0:T(4,128)S(1)}, f32[12,4,128]{2,1,0:T(4,128)S(1)}, u32[]{:S(2)}, u32[]{:S(2)}) collective-permute-start(f32[12,4,128]{2,1,0:T(4,128)S(1)} %get-tuple-element.65.refs_10_), channel_id=1, source_target_pairs={{0,6},{2,0},{4,2},{6,4},{1,7},{3,1},{5,3},{7,5},{8,14},{10,8},{12,... | collective-permute-start | bytes 73736 | tf_op jit(solution)/shard_map/ppermute | solution.py:39
  43.5 44.4 %collective-permute-start.21 = (f32[10,128,128]{2,1,0:T(8,128)S(1)}, f32[10,128,128]{2,1,0:T(8,128)S(1)}, u32[]{:S(2)}, u32[]{:S(2)}) collective-permute-start(f32[10,128,128]{2,1,0:T(8,128)S(1)} %get-tuple-element.66.refs_1_), channel_id=1, source_target_pairs={{0,1},{1,0},{2,3},{3,2},{4,5},{5,4},{6,7},{7,6},{8,9},{9,8},{10,11... | collective-permute-start | bytes 1966088 | tf_op jit(solution)/shard_map/ppermute | solution.py:39
  46.2 23.1 %collective-permute-start.12 = (f32[6,128,128]{2,1,0:T(8,128)S(1)}, f32[6,128,128]{2,1,0:T(8,128)S(1)}, u32[]{:S(2)}, u32[]{:S(2)}) collective-permute-start(f32[6,128,128]{2,1,0:T(8,128)S(1)} %chosen_3.1), channel_id=1, source_target_pairs={{0,1},{1,0},{2,3},{3,2},{4,5},{5,4},{6,7},{7,6},{8,9},{9,8},{10,11... | collective-permute-start | bytes 1179656 | tf_op jit(solution)/shard_map/ppermute | solution.py:39
  46.8 22.5 %collective-permute-start.13 = (f32[128,128]{1,0:T(8,128)S(1)}, f32[128,128]{1,0:T(8,128)S(1)}, u32[]{:S(2)}, u32[]{:S(2)}) collective-permute-start(f32[128,128]{1,0:T(8,128)S(1)} %get-tuple-element.70), channel_id=1, source_target_pairs={{0,8},{8,16},{16,24},{1,9},{9,17},{17,25},{2,10},{10,18},{18,26},{... | collective-permute-start | bytes 196616 | tf_op jit(solution)/shard_map/ppermute | solution.py:39
  50.8 3.3 %collective-permute-start.10 = (f32[12,4,128]{2,1,0:T(4,128)S(1)}, f32[12,4,128]{2,1,0:T(4,128)S(1)}, u32[]{:S(2)}, u32[]{:S(2)}) collective-permute-start(f32[12,4,128]{2,1,0:T(4,128)S(1)} %get-tuple-element.67), channel_id=1, source_target_pairs={{0,2},{2,4},{4,6},{6,0},{1,3},{3,5},{5,7},{7,1},{8,10},{10,12},{12... | collective-permute-start | bytes 73736 | tf_op jit(solution)/shard_map/ppermute | solution.py:39
  57.1 12.1 %collective-permute-start.17 = (f32[12,4,128]{2,1,0:T(4,128)S(1)}, f32[12,4,128]{2,1,0:T(4,128)S(1)}, u32[]{:S(2)}, u32[]{:S(2)}) collective-permute-start(f32[12,4,128]{2,1,0:T(4,128)S(1)} %get-tuple-element.75), channel_id=1, source_target_pairs={{0,2},{2,4},{4,6},{6,0},{1,3},{3,5},{5,7},{7,1},{8,10},{10,12},{12... | collective-permute-start | bytes 73736 | tf_op jit(solution)/shard_map/ppermute | solution.py:39
  59.0 10.2 %collective-permute-start.18 = (f32[12,4,128]{2,1,0:T(4,128)S(1)}, f32[12,4,128]{2,1,0:T(4,128)S(1)}, u32[]{:S(2)}, u32[]{:S(2)}) collective-permute-start(f32[12,4,128]{2,1,0:T(4,128)S(1)} %get-tuple-element.71.refs_1_), channel_id=1, source_target_pairs={{0,6},{2,0},{4,2},{6,4},{1,7},{3,1},{5,3},{7,5},{8,14},{10,8},{12,... | collective-permute-start | bytes 73736 | tf_op jit(solution)/shard_map/ppermute | solution.py:39
  72.4 27.2 %collective-permute-start.26 = (f32[12,128,128]{2,1,0:T(8,128)S(1)}, f32[12,128,128]{2,1,0:T(8,128)S(1)}, u32[]{:S(2)}, u32[]{:S(2)}) collective-permute-start(f32[12,128,128]{2,1,0:T(8,128)S(1)} %get-tuple-element.76.refs_16_), channel_id=1, source_target_pairs={{0,1},{1,0},{2,3},{3,2},{4,5},{5,4},{6,7},{7,6},{8,9},{9,8},{10,11... | collective-permute-start | bytes 2359304 | tf_op jit(solution)/shard_map/ppermute | solution.py:39
  74.0 6.4 %collective-permute-start.14 = (f32[128,128]{1,0:T(8,128)S(1)}, f32[128,128]{1,0:T(8,128)S(1)}, u32[]{:S(2)}, u32[]{:S(2)}) collective-permute-start(f32[128,128]{1,0:T(8,128)S(1)} %get-tuple-element.72), channel_id=1, source_target_pairs={{8,0},{16,8},{24,16},{9,1},{17,9},{25,17},{10,2},{18,10},{26,18},{... | collective-permute-start | bytes 196616 | tf_op jit(solution)/shard_map/ppermute | solution.py:39
  82.7 7.1 %collective-permute-start.19 = (f32[128,128]{1,0:T(8,128)S(1)}, f32[128,128]{1,0:T(8,128)S(1)}, u32[]{:S(2)}, u32[]{:S(2)}) collective-permute-start(f32[128,128]{1,0:T(8,128)S(1)} %get-tuple-element.78), channel_id=1, source_target_pairs={{0,8},{8,16},{16,24},{1,9},{9,17},{17,25},{2,10},{10,18},{18,26},{... | collective-permute-start | bytes 196616 | tf_op jit(solution)/shard_map/ppermute | solution.py:39
  86.6 6.3 %collective-permute-start.20 = (f32[128,128]{1,0:T(8,128)S(1)}, f32[128,128]{1,0:T(8,128)S(1)}, u32[]{:S(2)}, u32[]{:S(2)}) collective-permute-start(f32[128,128]{1,0:T(8,128)S(1)} %get-tuple-element.79), channel_id=1, source_target_pairs={{8,0},{16,8},{24,16},{9,1},{17,9},{25,17},{10,2},{18,10},{26,18},{... | collective-permute-start | bytes 196616 | tf_op jit(solution)/shard_map/ppermute | solution.py:39
  87.9 5.0 %collective-permute-start.22 = (f32[8,4,128]{2,1,0:T(4,128)S(1)}, f32[8,4,128]{2,1,0:T(4,128)S(1)}, u32[]{:S(2)}, u32[]{:S(2)}) collective-permute-start(f32[8,4,128]{2,1,0:T(4,128)S(1)} %get-tuple-element.82), channel_id=1, source_target_pairs={{0,2},{2,4},{4,6},{6,0},{1,3},{3,5},{5,7},{7,1},{8,10},{10,12},{12... | collective-permute-start | bytes 49160 | tf_op jit(solution)/shard_map/ppermute | solution.py:39
  88.1 4.8 %collective-permute-start.23 = (f32[8,4,128]{2,1,0:T(4,128)S(1)}, f32[8,4,128]{2,1,0:T(4,128)S(1)}, u32[]{:S(2)}, u32[]{:S(2)}) collective-permute-start(f32[8,4,128]{2,1,0:T(4,128)S(1)} %get-tuple-element.83), channel_id=1, source_target_pairs={{0,6},{2,0},{4,2},{6,4},{1,7},{3,1},{5,3},{7,5},{8,14},{10,8},{12,... | collective-permute-start | bytes 49160 | tf_op jit(solution)/shard_map/ppermute | solution.py:39
  96.3 14.9 %collective-permute-start.25 = (f32[8,128,128]{2,1,0:T(8,128)S(1)}, f32[8,128,128]{2,1,0:T(8,128)S(1)}, u32[]{:S(2)}, u32[]{:S(2)}) collective-permute-start(f32[8,128,128]{2,1,0:T(8,128)S(1)} %get-tuple-element.87), channel_id=1, source_target_pairs={{0,1},{1,0},{2,3},{3,2},{4,5},{5,4},{6,7},{7,6},{8,9},{9,8},{10,11... | collective-permute-start | bytes 1572872 | tf_op jit(solution)/shard_map/ppermute | solution.py:39
  96.8 15.8 %collective-permute-start.24 = (f32[2,128,128]{2,1,0:T(8,128)S(1)}, f32[2,128,128]{2,1,0:T(8,128)S(1)}, u32[]{:S(2)}, u32[]{:S(2)}) collective-permute-start(f32[2,128,128]{2,1,0:T(8,128)S(1)} %get-tuple-element.86), channel_id=1, source_target_pairs={{0,1},{1,0},{2,3},{3,2},{4,5},{5,4},{6,7},{7,6},{8,9},{9,8},{10,11... | collective-permute-start | bytes 393224 | tf_op jit(solution)/shard_map/ppermute | solution.py:39
  (8 other events, 35.1 us)

commit v7 on v6

--- a/solution.py
+++ b/solution.py
@@ -27,7 +27,7 @@
         out_specs=out_specs if out_specs is not None else [whole] * len(out_shapes),
         scratch_shapes=scratch,
         input_output_aliases=aliases or {},
-        cost_estimate=pl.CostEstimate(flops=int(work * 1e6), bytes_accessed=int(work * 2e3), transcendentals=0),
+        cost_estimate=pl.CostEstimate(flops=int(work * 1e9), bytes_accessed=int(work * 2e6), transcendentals=0),
         compiler_params=pltpu.CompilerParams(vmem_limit_bytes=vmem),
         name=name,
     )
@@ -59,20 +59,10 @@
 
 
 def chosen_body(begin, field, *refs):
-    out, held, sem = refs[-3:]
-    count = out.shape[0]
-    piece = 2
-    inward, outward = [], []
-    for number, at in enumerate(range(0, count, piece)):
-        here = pl.ds(at, piece)
-        inward.append(pltpu.make_async_copy(field.at[pl.ds(begin + at, piece)], held.at[here], sem.at[0, number]))
-        outward.append(pltpu.make_async_copy(held.at[here], out.at[here], sem.at[1, number]))
-        inward[-1].start()
-    for first, then in zip(inward, outward):
-        first.wait()
-        then.start()
-    for copy in outward:
-        copy.wait()
+    out, sem = refs[-2:]
+    copy = pltpu.make_async_copy(field.at[pl.ds(begin, out.shape[0])], out, sem)
+    copy.start()
+    copy.wait()
 
 
 def layers_body(depth, field, coef, first_x, last_x, first_y, last_y, held, sem):
@@ -389,10 +379,9 @@
         (out,) = call(
             functools.partial(chosen_body, begin),
             [((count,) + plane, f32)],
-            [pltpu.VMEM((count,) + plane, f32), pltpu.SemaphoreType.DMA((2, count))],
+            [pltpu.SemaphoreType.DMA],
             in_specs=[anywhere] * (1 + len(ties)),
-            out_specs=[anywhere],
-            vmem=vmem_bytes if ties else most_bytes,
+            vmem=vmem_bytes,
             name=name,
         )(start, *ties)
         return sent(out, "ma", 1, True)
@@ -406,7 +395,6 @@
         [layer] * 4,
         [pltpu.VMEM(flat, f32), pltpu.SemaphoreType.DMA((8,))],
         in_specs=[anywhere, whole],
-        vmem=most_bytes,
         name="layers",
     )(start, coef)
     low_y = sent(last_y, "gy", 1, True)

time: 114 us -> 99.8 us (0.88)
  waiting for transfers between devices: 30 us -> 20.3 us
  Pallas kernels: 43.7 us -> 36.5 us
  local copies, waits for them, and re-layouts: 1.08 us -> 2.97 us
    ppermute x27, waiting for transfers between devices: 30 us -> 20.3 us  [sent(): return lax.ppermute(array, axis, pairs)]
    pallas_call x3, Pallas kernels: 5.54 us -> 1.41 us  [chosen(): call(functools.partial(chosen_body, begin), [((count,) + plane, f32)], [p...]
    pallas_call x1, Pallas kernels: 3.23 us -> 0.28 us  [shards(): call(functools.partial(layers_body, depth), [layer] * 4, [pltpu.VMEM(flat...]
    unnamed x11, local copies, waits for them, and re-layouts: 0.23 us -> 2.74 us
  transfers between devices with their start and end apart: 27 -> 27, of which waited for: 8 -> 8; matrix products, arithmetic and copies ran while one was open for 1% -> 0% of each run, Pallas kernels for 36% -> 35%
where the time goes in v7:
time: 99.8 us; the launch traced here: 99.5 us
  starting transfers between devices  38.5 us (39%)
  Pallas kernels  36.5 us (37%)
  waiting for transfers between devices  20.3 us (20%)
  local copies, waits for them, and re-layouts  2.97 us (3%)
  between operations  1.18 us (1%)
    ppermute x27, starting transfers between devices, sent(): return lax.ppermute(array, axis, pairs)  38.5 us
    pallas_call x9, Pallas kernels, over_planes(): call(functools.partial(planes_body, depth, tuple(names), tuple(outs), pie...  25.1 us
    ppermute x27, waiting for transfers between devices, sent(): return lax.ppermute(array, axis, pairs)  20.3 us
    pallas_call x4, Pallas kernels, add_last(): call(functools.partial(last_body, first, skip), [(shape, f32)] * 2, [pltp...  4.65 us
    unnamed x11, local copies, waits for them, and re-layouts  2.74 us
    pallas_call x1, Pallas kernels, shards(): call(functools.partial(diagonal_body, depth), [(halves_shape, f32), ((3,)...  2.67 us
  transfers between devices with their start and end apart: 27, of which 8 were waited for; matrix products, arithmetic and copies ran while one was open for 0% of the time, Pallas kernels for 35%

profile of v7, /device:TPU:0, one launch (start us, length us, event | category | flops | bytes accessed | tf_op | source)
XLA Modules:
  0.0 99.5 jit_solution(2916626712856137803)
XLA Ops:
  3.4 3.0 %collective-permute-start.4 = (f32[14,128,128]{2,1,0:T(8,128)}, f32[14,128,128]{2,1,0:T(8,128)S(1)}, u32[]{:S(2)}, u32[]{:S(2)}) collective-permute-start(f32[14,128,128]{2,1,0:T(8,128)} %chosen_1.1), channel_id=1, source_target_pairs={{0,1},{1,0},{2,3},{3,2},{4,5},{5,4},{6,7},{7,6},{8,9},{9,8},{10,11... | collective-permute-start | bytes 2752520 | tf_op jit(solution)/shard_map/ppermute | solution.py:39
  7.2 3.5 %collective-permute-start = (f32[256,128]{1,0:T(8,128)S(1)}, f32[256,128]{1,0:T(8,128)S(1)}, u32[]{:S(2)}, u32[]{:S(2)}) collective-permute-start(f32[256,128]{1,0:T(8,128)S(1)} %get-tuple-element.51), channel_id=1, source_target_pairs={{0,8},{8,16},{16,24},{1,9},{9,17},{17,25},{2,10},{10,18},{18,26},{... | collective-permute-start | bytes 393224 | tf_op jit(solution)/shard_map/ppermute | solution.py:39
  12.0 1.7 %collective-permute-start.3 = (f32[256,128]{1,0:T(8,128)S(1)}, f32[256,128]{1,0:T(8,128)S(1)}, u32[]{:S(2)}, u32[]{:S(2)}) collective-permute-start(f32[256,128]{1,0:T(8,128)S(1)} %get-tuple-element.54), channel_id=1, source_target_pairs={{0,6},{2,0},{4,2},{6,4},{1,7},{3,1},{5,3},{7,5},{8,14},{10,8},{12,... | collective-permute-start | bytes 393224 | tf_op jit(solution)/shard_map/ppermute | solution.py:39
  13.8 1.9 %halves.1.halves_in = f32[3,34,144,128]{3,2,1,0:T(8,128)S(1)} custom-call(f32[96,128]{1,0:T(8,128)S(1)} %copy.15.coef), custom_call_target="tpu_custom_call" | custom-call | flops 1000000000 | bytes 2000000 | tf_op jit(solution)/shard_map/halves/pallas_call | solution.py:414
  17.5 2.7 %diagonal.1 = (f32[3,34,144,128]{3,2,1,0:T(8,128)S(1)}, f32[3,32,128,128]{3,2,1,0:T(8,128)S(1)}) custom-call(f32[256,128]{1,0:T(8,128)S(1)} %collective-permute-done.low_x.refs_8_, f32[256,128]{1,0:T(8,128)S(1)} %collective-permute-done.1.high_x.refs_9_, f32[256,128]{1,0:T(8,128)S(1)} %collective-permute-done.2.low_y.refs_6_, ...), custom_call_target="tpu_custom_call", output_to_operand_aliasing={{0}: (4, {})} | custom-call | flops 1000000000 | bytes 2000000 | tf_op jit(solution)/shard_map/diagonal/pallas_call | solution.py:415
  21.8 2.9 %own_1.1.refs_1_.refs_4_.refs_0_ = f32[12,128,128]{2,1,0:T(8,128)S(1)} custom-call(f32[3,34,144,128]{3,2,1,0:T(8,128)S(1)} %get-tuple-element.55.refs_0_, f32[3,32,128,128]{3,2,1,0:T(8,128)S(1)} %get-tuple-element.56.refs_1_, bf16[384,256]{1,0:T(8,128)(2,1)S(1)} %get-tuple-element.57.refs_2_.refs_0_, bf16[384,256]{1,0:T(8,128)(2,1)S(1)} %get-tuple-element.58.refs_3_, ...), custom_call_target="tpu_custom_call" | custom-call | flops 1200000000 | bytes 2400000 | tf_op jit(solution)/shard_map/own_1/pallas_call | solution.py:296
  25.6 2.2 %collective-permute-done.4.refs_0_.refs_5_ = f32[14,128,128]{2,1,0:T(8,128)S(1)} collective-permute-done((f32[14,128,128]{2,1,0:T(8,128)}, f32[14,128,128]{2,1,0:T(8,128)S(1)}, u32[]{:S(2)}, u32[]{:S(2)}) %collective-permute-start.4) | collective-permute-done | bytes 917536 | tf_op jit(solution)/shard_map/ppermute | solution.py:39
  27.9 1.7 %collective-permute-start.6 = (f32[14,4,128]{2,1,0:T(4,128)S(1)}, f32[14,4,128]{2,1,0:T(4,128)S(1)}, u32[]{:S(2)}, u32[]{:S(2)}) collective-permute-start(f32[14,4,128]{2,1,0:T(4,128)S(1)} %get-tuple-element.62.refs_10_), channel_id=1, source_target_pairs={{0,6},{2,0},{4,2},{6,4},{1,7},{3,1},{5,3},{7,5},{8,14},{10,8},{12,... | collective-permute-start | bytes 86024 | tf_op jit(solution)/shard_map/ppermute | solution.py:39
  29.6 2.9 %own_2.1.refs_8_.refs_4_ = f32[12,128,128]{2,1,0:T(8,128)S(1)} custom-call(f32[3,34,144,128]{3,2,1,0:T(8,128)S(1)} %get-tuple-element.55.refs_0_, f32[3,32,128,128]{3,2,1,0:T(8,128)S(1)} %get-tuple-element.56.refs_1_, bf16[384,256]{1,0:T(8,128)(2,1)S(1)} %get-tuple-element.57.refs_2_.refs_0_, bf16[384,256]{1,0:T(8,128)(2,1)S(1)} %get-tuple-element.58.refs_3_, ...), custom_call_target="tpu_custom_call" | custom-call | flops 1200000000 | bytes 2400000 | tf_op jit(solution)/shard_map/own_2/pallas_call | solution.py:296
  32.5 2.8 %middle_1.1 = (f32[12,128,128]{2,1,0:T(8,128)S(1)}, f32[12,4,128]{2,1,0:T(4,128)S(1)}, f32[12,4,128]{2,1,0:T(4,128)S(1)}) custom-call(f32[3,34,144,128]{3,2,1,0:T(8,128)S(1)} %get-tuple-element.55.refs_0_, f32[3,32,128,128]{3,2,1,0:T(8,128)S(1)} %get-tuple-element.56.refs_1_, bf16[384,128]{1,0:T(8,128)(2,1)S(1)} %get-tuple-element.59.refs_2_, ...), custom_call_target="tpu_custom_call" | custom-call | flops 1200000000 | bytes 2400000 | tf_op jit(solution)/shard_map/middle_1/pallas_call | solution.py:296
  37.2 2.1 %own_3.1.refs_8_.refs_4_ = f32[8,128,128]{2,1,0:T(8,128)S(1)} custom-call(f32[3,34,144,128]{3,2,1,0:T(8,128)S(1)} %get-tuple-element.55.refs_0_, f32[3,32,128,128]{3,2,1,0:T(8,128)S(1)} %get-tuple-element.56.refs_1_, bf16[384,256]{1,0:T(8,128)(2,1)S(1)} %get-tuple-element.57.refs_2_.refs_0_, bf16[384,256]{1,0:T(8,128)(2,1)S(1)} %get-tuple-element.58.refs_3_, ...), custom_call_target="tpu_custom_call" | custom-call | flops 800000000 | bytes 1600000 | tf_op jit(solution)/shard_map/own_3/pallas_call | solution.py:296
  39.3 2.7 %second_1.1 = (f32[10,128,128]{2,1,0:T(8,128)S(1)}, f32[10,128,128]{2,1,0:T(8,128)S(1)}, f32[10,128,128]{2,1,0:T(8,128)S(1)}) custom-call(f32[3,34,144,128]{3,2,1,0:T(8,128)S(1)} %get-tuple-element.55.refs_0_, f32[3,32,128,128]{3,2,1,0:T(8,128)S(1)} %get-tuple-element.56.refs_1_, bf16[384,256]{1,0:T(8,128)(2,1)S(1)} %get-tuple-element.57.refs_2_.refs_0_, ...), custom_call_target="tpu_custom_call" | custom-call | flops 1000000000 | bytes 2000000 | tf_op jit(solution)/shard_map/second_1/pallas_call | solution.py:296
  42.1 2.1 %collective-permute-start.21 = (f32[10,128,128]{2,1,0:T(8,128)S(1)}, f32[10,128,128]{2,1,0:T(8,128)S(1)}, u32[]{:S(2)}, u32[]{:S(2)}) collective-permute-start(f32[10,128,128]{2,1,0:T(8,128)S(1)} %get-tuple-element.66.refs_1_), channel_id=1, source_target_pairs={{0,1},{1,0},{2,3},{3,2},{4,5},{5,4},{6,7},{7,6},{8,9},{9,8},{10,11... | collective-permute-start | bytes 1966088 | tf_op jit(solution)/shard_map/ppermute | solution.py:39
  46.7 4.0 %collective-permute-start.13 = (f32[128,128]{1,0:T(8,128)S(1)}, f32[128,128]{1,0:T(8,128)S(1)}, u32[]{:S(2)}, u32[]{:S(2)}) collective-permute-start(f32[128,128]{1,0:T(8,128)S(1)} %get-tuple-element.70), channel_id=1, source_target_pairs={{0,8},{8,16},{16,24},{1,9},{9,17},{17,25},{2,10},{10,18},{18,26},{... | collective-permute-start | bytes 196616 | tf_op jit(solution)/shard_map/ppermute | solution.py:39
  50.7 2.9 %middle_2.1 = (f32[12,128,128]{2,1,0:T(8,128)S(1)}, f32[12,4,128]{2,1,0:T(4,128)S(1)}, f32[12,4,128]{2,1,0:T(4,128)S(1)}) custom-call(f32[3,34,144,128]{3,2,1,0:T(8,128)S(1)} %get-tuple-element.55.refs_0_, f32[3,32,128,128]{3,2,1,0:T(8,128)S(1)} %get-tuple-element.56.refs_1_, bf16[384,128]{1,0:T(8,128)(2,1)S(1)} %get-tuple-element.59.refs_2_, ...), custom_call_target="tpu_custom_call" | custom-call | flops 1200000000 | bytes 2400000 | tf_op jit(solution)/shard_map/middle_2/pallas_call | solution.py:296
  53.7 1.7 %collective-permute-start.18 = (f32[12,4,128]{2,1,0:T(4,128)S(1)}, f32[12,4,128]{2,1,0:T(4,128)S(1)}, u32[]{:S(2)}, u32[]{:S(2)}) collective-permute-start(f32[12,4,128]{2,1,0:T(4,128)S(1)} %get-tuple-element.71.refs_1_), channel_id=1, source_target_pairs={{0,6},{2,0},{4,2},{6,4},{1,7},{3,1},{5,3},{7,5},{8,14},{10,8},{12,... | collective-permute-start | bytes 73736 | tf_op jit(solution)/shard_map/ppermute | solution.py:39
  56.9 3.2 %second_2.1 = (f32[12,128,128]{2,1,0:T(8,128)S(1)}, f32[12,128,128]{2,1,0:T(8,128)S(1)}, f32[12,128,128]{2,1,0:T(8,128)S(1)}) custom-call(f32[3,34,144,128]{3,2,1,0:T(8,128)S(1)} %get-tuple-element.55.refs_0_, f32[3,32,128,128]{3,2,1,0:T(8,128)S(1)} %get-tuple-element.56.refs_1_, bf16[384,256]{1,0:T(8,128)(2,1)S(1)} %get-tuple-element.57.refs_2_.refs_0_, ...), custom_call_target="tpu_custom_call" | custom-call | flops 1000000000 | bytes 2000000 | tf_op jit(solution)/shard_map/second_2/pallas_call | solution.py:296
  61.7 1.6 %collective-permute-start.15 = (f32[6,4,128]{2,1,0:T(4,128)S(1)}, f32[6,4,128]{2,1,0:T(4,128)S(1)}, u32[]{:S(2)}, u32[]{:S(2)}) collective-permute-start(f32[6,4,128]{2,1,0:T(4,128)S(1)} %get-tuple-element.73), channel_id=1, source_target_pairs={{0,2},{2,4},{4,6},{6,0},{1,3},{3,5},{5,7},{7,1},{8,10},{10,12},{12... | collective-permute-start | bytes 36872 | tf_op jit(solution)/shard_map/ppermute | solution.py:39
  64.9 2.2 %middle_3.1 = (f32[8,128,128]{2,1,0:T(8,128)S(1)}, f32[8,4,128]{2,1,0:T(4,128)S(1)}, f32[8,4,128]{2,1,0:T(4,128)S(1)}, f32[128,128]{1,0:T(8,128)S(1)}, f32[128,128]{1,0:T(8,128)S(1)}) custom-call(f32[3,34,144,128]{3,2,1,0:T(8,128)S(1)} %get-tuple-element.55.refs_0_, f32[3,32,128,128]{3,2,1,0:T(8,128)S(1)} %get-tuple-element.56.refs_1_, ...), custom_call_target="tpu_custom_call" | custom-call | flops 800000000 | bytes 1600000 | tf_op jit(solution)/shard_map/middle_3/pallas_call | solution.py:296
  67.1 4.4 %collective-permute-start.19 = (f32[128,128]{1,0:T(8,128)S(1)}, f32[128,128]{1,0:T(8,128)S(1)}, u32[]{:S(2)}, u32[]{:S(2)}) collective-permute-start(f32[128,128]{1,0:T(8,128)S(1)} %get-tuple-element.78), channel_id=1, source_target_pairs={{0,8},{8,16},{16,24},{1,9},{9,17},{17,25},{2,10},{10,18},{18,26},{... | collective-permute-start | bytes 196616 | tf_op jit(solution)/shard_map/ppermute | solution.py:39
  72.8 1.6 %collective-permute-start.22 = (f32[8,4,128]{2,1,0:T(4,128)S(1)}, f32[8,4,128]{2,1,0:T(4,128)S(1)}, u32[]{:S(2)}, u32[]{:S(2)}) collective-permute-start(f32[8,4,128]{2,1,0:T(4,128)S(1)} %get-tuple-element.82), channel_id=1, source_target_pairs={{0,2},{2,4},{4,6},{6,0},{1,3},{3,5},{5,7},{7,1},{8,10},{10,12},{12... | collective-permute-start | bytes 49160 | tf_op jit(solution)/shard_map/ppermute | solution.py:39
  74.7 3.1 %collective-permute-done.20.refs_9_ = f32[128,128]{1,0:T(8,128)S(1)} collective-permute-done((f32[128,128]{1,0:T(8,128)S(1)}, f32[128,128]{1,0:T(8,128)S(1)}, u32[]{:S(2)}, u32[]{:S(2)}) %collective-permute-start.20) | collective-permute-done | bytes 65568 | tf_op jit(solution)/shard_map/ppermute | solution.py:39
  77.8 3.3 %second_3.1 = (f32[10,128,128]{2,1,0:T(8,128)S(1)}, f32[10,128,128]{2,1,0:T(8,128)S(1)}, f32[8,128,128]{2,1,0:T(8,128)S(1)}, f32[2,128,128]{2,1,0:T(8,128)S(1)}) custom-call(f32[3,34,144,128]{3,2,1,0:T(8,128)S(1)} %get-tuple-element.55.refs_0_, f32[3,32,128,128]{3,2,1,0:T(8,128)S(1)} %get-tuple-element.56.refs_1_, ...), custom_call_target="tpu_custom_call" | custom-call | flops 1000000000 | bytes 2000000 | tf_op jit(solution)/shard_map/second_3/pallas_call | solution.py:296
  85.9 10.0 %collective-permute-done.25.came = f32[8,128,128]{2,1,0:T(8,128)S(1)} collective-permute-done((f32[8,128,128]{2,1,0:T(8,128)S(1)}, f32[8,128,128]{2,1,0:T(8,128)S(1)}, u32[]{:S(2)}, u32[]{:S(2)}) %collective-permute-start.25) | collective-permute-done | bytes 524320 | tf_op jit(solution)/shard_map/ppermute | solution.py:39
  (67 shorter events, 27.7 us)
Async XLA Ops:
  3.4 24.4 %collective-permute-start.4 = (f32[14,128,128]{2,1,0:T(8,128)}, f32[14,128,128]{2,1,0:T(8,128)S(1)}, u32[]{:S(2)}, u32[]{:S(2)}) collective-permute-start(f32[14,128,128]{2,1,0:T(8,128)} %chosen_1.1), channel_id=1, source_target_pairs={{0,1},{1,0},{2,3},{3,2},{4,5},{5,4},{6,7},{7,6},{8,9},{9,8},{10,11... | collective-permute-start | bytes 2752520 | tf_op jit(solution)/shard_map/ppermute | solution.py:39
  7.2 9.0 %collective-permute-start = (f32[256,128]{1,0:T(8,128)S(1)}, f32[256,128]{1,0:T(8,128)S(1)}, u32[]{:S(2)}, u32[]{:S(2)}) collective-permute-start(f32[256,128]{1,0:T(8,128)S(1)} %get-tuple-element.51), channel_id=1, source_target_pairs={{0,8},{8,16},{16,24},{1,9},{9,17},{17,25},{2,10},{10,18},{18,26},{... | collective-permute-start | bytes 393224 | tf_op jit(solution)/shard_map/ppermute | solution.py:39
  10.7 6.9 %collective-permute-start.1 = (f32[256,128]{1,0:T(8,128)S(1)}, f32[256,128]{1,0:T(8,128)S(1)}, u32[]{:S(2)}, u32[]{:S(2)}) collective-permute-start(f32[256,128]{1,0:T(8,128)S(1)} %get-tuple-element.52), channel_id=1, source_target_pairs={{8,0},{16,8},{24,16},{9,1},{17,9},{25,17},{10,2},{18,10},{26,18},{... | collective-permute-start | bytes 393224 | tf_op jit(solution)/shard_map/ppermute | solution.py:39
  12.0 5.6 %collective-permute-start.2 = (f32[256,128]{1,0:T(8,128)S(1)}, f32[256,128]{1,0:T(8,128)S(1)}, u32[]{:S(2)}, u32[]{:S(2)}) collective-permute-start(f32[256,128]{1,0:T(8,128)S(1)} %get-tuple-element.53), channel_id=1, source_target_pairs={{0,2},{2,4},{4,6},{6,0},{1,3},{3,5},{5,7},{7,1},{8,10},{10,12},{12... | collective-permute-start | bytes 393224 | tf_op jit(solution)/shard_map/ppermute | solution.py:39
  12.0 5.5 %collective-permute-start.3 = (f32[256,128]{1,0:T(8,128)S(1)}, f32[256,128]{1,0:T(8,128)S(1)}, u32[]{:S(2)}, u32[]{:S(2)}) collective-permute-start(f32[256,128]{1,0:T(8,128)S(1)} %get-tuple-element.54), channel_id=1, source_target_pairs={{0,6},{2,0},{4,2},{6,4},{1,7},{3,1},{5,3},{7,5},{8,14},{10,8},{12,... | collective-permute-start | bytes 393224 | tf_op jit(solution)/shard_map/ppermute | solution.py:39
  20.3 24.4 %collective-permute-start.7 = (f32[12,128,128]{2,1,0:T(8,128)S(1)}, f32[12,128,128]{2,1,0:T(8,128)S(1)}, u32[]{:S(2)}, u32[]{:S(2)}) collective-permute-start(f32[12,128,128]{2,1,0:T(8,128)S(1)} %chosen_2.1), channel_id=1, source_target_pairs={{0,1},{1,0},{2,3},{3,2},{4,5},{5,4},{6,7},{7,6},{8,9},{9,8},{10,11... | collective-permute-start | bytes 2359304 | tf_op jit(solution)/shard_map/ppermute | solution.py:39
  24.9 30.5 %collective-permute-start.12 = (f32[6,128,128]{2,1,0:T(8,128)S(1)}, f32[6,128,128]{2,1,0:T(8,128)S(1)}, u32[]{:S(2)}, u32[]{:S(2)}) collective-permute-start(f32[6,128,128]{2,1,0:T(8,128)S(1)} %chosen_3.1), channel_id=1, source_target_pairs={{0,1},{1,0},{2,3},{3,2},{4,5},{5,4},{6,7},{7,6},{8,9},{9,8},{10,11... | collective-permute-start | bytes 1179656 | tf_op jit(solution)/shard_map/ppermute | solution.py:39
  27.8 4.7 %collective-permute-start.5 = (f32[14,4,128]{2,1,0:T(4,128)S(1)}, f32[14,4,128]{2,1,0:T(4,128)S(1)}, u32[]{:S(2)}, u32[]{:S(2)}) collective-permute-start(f32[14,4,128]{2,1,0:T(4,128)S(1)} %get-tuple-element.61), channel_id=1, source_target_pairs={{0,2},{2,4},{4,6},{6,0},{1,3},{3,5},{5,7},{7,1},{8,10},{10,12},{12... | collective-permute-start | bytes 86024 | tf_op jit(solution)/shard_map/ppermute | solution.py:39
  27.9 4.7 %collective-permute-start.6 = (f32[14,4,128]{2,1,0:T(4,128)S(1)}, f32[14,4,128]{2,1,0:T(4,128)S(1)}, u32[]{:S(2)}, u32[]{:S(2)}) collective-permute-start(f32[14,4,128]{2,1,0:T(4,128)S(1)} %get-tuple-element.62.refs_10_), channel_id=1, source_target_pairs={{0,6},{2,0},{4,2},{6,4},{1,7},{3,1},{5,3},{7,5},{8,14},{10,8},{12,... | collective-permute-start | bytes 86024 | tf_op jit(solution)/shard_map/ppermute | solution.py:39
  35.4 3.9 %collective-permute-start.8 = (f32[12,4,128]{2,1,0:T(4,128)S(1)}, f32[12,4,128]{2,1,0:T(4,128)S(1)}, u32[]{:S(2)}, u32[]{:S(2)}) collective-permute-start(f32[12,4,128]{2,1,0:T(4,128)S(1)} %get-tuple-element.64), channel_id=1, source_target_pairs={{0,2},{2,4},{4,6},{6,0},{1,3},{3,5},{5,7},{7,1},{8,10},{10,12},{12... | collective-permute-start | bytes 73736 | tf_op jit(solution)/shard_map/ppermute | solution.py:39
  42.1 30.7 %collective-permute-start.21 = (f32[10,128,128]{2,1,0:T(8,128)S(1)}, f32[10,128,128]{2,1,0:T(8,128)S(1)}, u32[]{:S(2)}, u32[]{:S(2)}) collective-permute-start(f32[10,128,128]{2,1,0:T(8,128)S(1)} %get-tuple-element.66.refs_1_), channel_id=1, source_target_pairs={{0,1},{1,0},{2,3},{3,2},{4,5},{5,4},{6,7},{7,6},{8,9},{9,8},{10,11... | collective-permute-start | bytes 1966088 | tf_op jit(solution)/shard_map/ppermute | solution.py:39
  44.7 6.0 %collective-permute-start.10 = (f32[12,4,128]{2,1,0:T(4,128)S(1)}, f32[12,4,128]{2,1,0:T(4,128)S(1)}, u32[]{:S(2)}, u32[]{:S(2)}) collective-permute-start(f32[12,4,128]{2,1,0:T(4,128)S(1)} %get-tuple-element.67), channel_id=1, source_target_pairs={{0,2},{2,4},{4,6},{6,0},{1,3},{3,5},{5,7},{7,1},{8,10},{10,12},{12... | collective-permute-start | bytes 73736 | tf_op jit(solution)/shard_map/ppermute | solution.py:39
  45.4 5.3 %collective-permute-start.11 = (f32[12,4,128]{2,1,0:T(4,128)S(1)}, f32[12,4,128]{2,1,0:T(4,128)S(1)}, u32[]{:S(2)}, u32[]{:S(2)}) collective-permute-start(f32[12,4,128]{2,1,0:T(4,128)S(1)} %get-tuple-element.68), channel_id=1, source_target_pairs={{0,6},{2,0},{4,2},{6,4},{1,7},{3,1},{5,3},{7,5},{8,14},{10,8},{12,... | collective-permute-start | bytes 73736 | tf_op jit(solution)/shard_map/ppermute | solution.py:39
  46.7 10.3 %collective-permute-start.13 = (f32[128,128]{1,0:T(8,128)S(1)}, f32[128,128]{1,0:T(8,128)S(1)}, u32[]{:S(2)}, u32[]{:S(2)}) collective-permute-start(f32[128,128]{1,0:T(8,128)S(1)} %get-tuple-element.70), channel_id=1, source_target_pairs={{0,8},{8,16},{16,24},{1,9},{9,17},{17,25},{2,10},{10,18},{18,26},{... | collective-permute-start | bytes 196616 | tf_op jit(solution)/shard_map/ppermute | solution.py:39
  53.6 3.3 %collective-permute-start.17 = (f32[12,4,128]{2,1,0:T(4,128)S(1)}, f32[12,4,128]{2,1,0:T(4,128)S(1)}, u32[]{:S(2)}, u32[]{:S(2)}) collective-permute-start(f32[12,4,128]{2,1,0:T(4,128)S(1)} %get-tuple-element.75), channel_id=1, source_target_pairs={{0,2},{2,4},{4,6},{6,0},{1,3},{3,5},{5,7},{7,1},{8,10},{10,12},{12... | collective-permute-start | bytes 73736 | tf_op jit(solution)/shard_map/ppermute | solution.py:39
  53.7 3.3 %collective-permute-start.18 = (f32[12,4,128]{2,1,0:T(4,128)S(1)}, f32[12,4,128]{2,1,0:T(4,128)S(1)}, u32[]{:S(2)}, u32[]{:S(2)}) collective-permute-start(f32[12,4,128]{2,1,0:T(4,128)S(1)} %get-tuple-element.71.refs_1_), channel_id=1, source_target_pairs={{0,6},{2,0},{4,2},{6,4},{1,7},{3,1},{5,3},{7,5},{8,14},{10,8},{12,... | collective-permute-start | bytes 73736 | tf_op jit(solution)/shard_map/ppermute | solution.py:39
  55.4 9.4 %collective-permute-start.14 = (f32[128,128]{1,0:T(8,128)S(1)}, f32[128,128]{1,0:T(8,128)S(1)}, u32[]{:S(2)}, u32[]{:S(2)}) collective-permute-start(f32[128,128]{1,0:T(8,128)S(1)} %get-tuple-element.72), channel_id=1, source_target_pairs={{8,0},{16,8},{24,16},{9,1},{17,9},{25,17},{10,2},{18,10},{26,18},{... | collective-permute-start | bytes 196616 | tf_op jit(solution)/shard_map/ppermute | solution.py:39
  60.1 24.4 %collective-permute-start.26 = (f32[12,128,128]{2,1,0:T(8,128)S(1)}, f32[12,128,128]{2,1,0:T(8,128)S(1)}, u32[]{:S(2)}, u32[]{:S(2)}) collective-permute-start(f32[12,128,128]{2,1,0:T(8,128)S(1)} %get-tuple-element.76.refs_16_), channel_id=1, source_target_pairs={{0,1},{1,0},{2,3},{3,2},{4,5},{5,4},{6,7},{7,6},{8,9},{9,8},{10,11... | collective-permute-start | bytes 2359304 | tf_op jit(solution)/shard_map/ppermute | solution.py:39
  67.1 7.6 %collective-permute-start.19 = (f32[128,128]{1,0:T(8,128)S(1)}, f32[128,128]{1,0:T(8,128)S(1)}, u32[]{:S(2)}, u32[]{:S(2)}) collective-permute-start(f32[128,128]{1,0:T(8,128)S(1)} %get-tuple-element.78), channel_id=1, source_target_pairs={{0,8},{8,16},{16,24},{1,9},{9,17},{17,25},{2,10},{10,18},{18,26},{... | collective-permute-start | bytes 196616 | tf_op jit(solution)/shard_map/ppermute | solution.py:39
  71.5 6.3 %collective-permute-start.20 = (f32[128,128]{1,0:T(8,128)S(1)}, f32[128,128]{1,0:T(8,128)S(1)}, u32[]{:S(2)}, u32[]{:S(2)}) collective-permute-start(f32[128,128]{1,0:T(8,128)S(1)} %get-tuple-element.79), channel_id=1, source_target_pairs={{8,0},{16,8},{24,16},{9,1},{17,9},{25,17},{10,2},{18,10},{26,18},{... | collective-permute-start | bytes 196616 | tf_op jit(solution)/shard_map/ppermute | solution.py:39
  72.8 5.0 %collective-permute-start.22 = (f32[8,4,128]{2,1,0:T(4,128)S(1)}, f32[8,4,128]{2,1,0:T(4,128)S(1)}, u32[]{:S(2)}, u32[]{:S(2)}) collective-permute-start(f32[8,4,128]{2,1,0:T(4,128)S(1)} %get-tuple-element.82), channel_id=1, source_target_pairs={{0,2},{2,4},{4,6},{6,0},{1,3},{3,5},{5,7},{7,1},{8,10},{10,12},{12... | collective-permute-start | bytes 49160 | tf_op jit(solution)/shard_map/ppermute | solution.py:39
  74.5 3.3 %collective-permute-start.23 = (f32[8,4,128]{2,1,0:T(4,128)S(1)}, f32[8,4,128]{2,1,0:T(4,128)S(1)}, u32[]{:S(2)}, u32[]{:S(2)}) collective-permute-start(f32[8,4,128]{2,1,0:T(4,128)S(1)} %get-tuple-element.83), channel_id=1, source_target_pairs={{0,6},{2,0},{4,2},{6,4},{1,7},{3,1},{5,3},{7,5},{8,14},{10,8},{12,... | collective-permute-start | bytes 49160 | tf_op jit(solution)/shard_map/ppermute | solution.py:39
  81.1 14.9 %collective-permute-start.25 = (f32[8,128,128]{2,1,0:T(8,128)S(1)}, f32[8,128,128]{2,1,0:T(8,128)S(1)}, u32[]{:S(2)}, u32[]{:S(2)}) collective-permute-start(f32[8,128,128]{2,1,0:T(8,128)S(1)} %get-tuple-element.87), channel_id=1, source_target_pairs={{0,1},{1,0},{2,3},{3,2},{4,5},{5,4},{6,7},{7,6},{8,9},{9,8},{10,11... | collective-permute-start | bytes 1572872 | tf_op jit(solution)/shard_map/ppermute | solution.py:39
  81.7 16.8 %collective-permute-start.24 = (f32[2,128,128]{2,1,0:T(8,128)S(1)}, f32[2,128,128]{2,1,0:T(8,128)S(1)}, u32[]{:S(2)}, u32[]{:S(2)}) collective-permute-start(f32[2,128,128]{2,1,0:T(8,128)S(1)} %get-tuple-element.86), channel_id=1, source_target_pairs={{0,1},{1,0},{2,3},{3,2},{4,5},{5,4},{6,7},{7,6},{8,9},{9,8},{10,11... | collective-permute-start | bytes 393224 | tf_op jit(solution)/shard_map/ppermute | solution.py:39
  (8 other events, 23.2 us)

commit v8 on v7

--- a/solution.py
+++ b/solution.py
@@ -12,7 +12,7 @@
 group = 2
 pad = 8
 vmem_bytes = 12 * 1024 * 1024
-most_bytes = 60 * 1024 * 1024
+first_bytes = 60 * 1024 * 1024
 f32 = jnp.float32
 bf16 = jnp.bfloat16
 whole = pl.BlockSpec(memory_space=pltpu.VMEM)
@@ -381,7 +381,7 @@
             [((count,) + plane, f32)],
             [pltpu.SemaphoreType.DMA],
             in_specs=[anywhere] * (1 + len(ties)),
-            vmem=vmem_bytes,
+            vmem=vmem_bytes if ties else first_bytes,
             name=name,
         )(start, *ties)
         return sent(out, "ma", 1, True)
@@ -540,6 +540,7 @@
         [("low_1", "high_1", n1 - 1, 1, 1, False), ("low_2", "high_2", 0, n2 - 1, 2, False)],
         [Run(1, high - 2, n2)],
         (sides_3[0], raw_low_x),
+        4.0,
     )
     came_2 = sent(part_2, "ma", 1, True)
     residual_3, first_3, last_3, edge_last, edge_first = middle(
@@ -606,7 +607,7 @@
         ],
         [Run(1, nx - 2, 2), Run(5, 0, low + 2)],
         (came_1,),
-        1.0,
+        2.0,
     )
     came_3 = sent(part_3, "ma", 1, True)
     came_4 = sent(part_4, "ma", 1, True)

time: 99.8 us -> 98 us (0.982)
  local copies, waits for them, and re-layouts: 2.97 us -> 1.38 us
  starting transfers between devices: 38.5 us -> 37 us
  Pallas kernels: 36.5 us -> 37.7 us
    unnamed x11 -> x9, local copies, waits for them, and re-layouts: 2.74 us -> 1.16 us
    ppermute x27, starting transfers between devices: 38.5 us -> 37 us  [sent(): return lax.ppermute(array, axis, pairs)]
    pallas_call x3, Pallas kernels: 1.41 us -> 2.52 us  [chosen(): call(functools.partial(chosen_body, begin), [((count,) + plane, f32)], [p...]
where the time goes in v8:
time: 98 us; the launch traced here: 97.7 us
  Pallas kernels  37.7 us (38%)
  starting transfers between devices  37 us (38%)
  waiting for transfers between devices  20.4 us (21%)
  local copies, waits for them, and re-layouts  1.38 us (1%)
  between operations  1.19 us (1%)
    ppermute x27, starting transfers between devices, sent(): return lax.ppermute(array, axis, pairs)  37 us
    pallas_call x9, Pallas kernels, over_planes(): call(functools.partial(planes_body, depth, tuple(names), tuple(outs), pie...  25.1 us
    ppermute x27, waiting for transfers between devices, sent(): return lax.ppermute(array, axis, pairs)  20.4 us
    pallas_call x4, Pallas kernels, add_last(): call(functools.partial(last_body, first, skip), [(shape, f32)] * 2, [pltp...  4.65 us
    pallas_call x1, Pallas kernels, shards(): call(functools.partial(diagonal_body, depth), [(halves_shape, f32), ((3,)...  2.67 us
    pallas_call x3, Pallas kernels, chosen(): call(functools.partial(chosen_body, begin), [((count,) + plane, f32)], [p...  2.52 us
  transfers between devices with their start and end apart: 27, of which 8 were waited for; matrix products, arithmetic and copies ran while one was open for 0% of the time, Pallas kernels for 35%

profile of v8, /device:TPU:0, one launch (start us, length us, event | category | flops | bytes accessed | tf_op | source)
XLA Modules:
  0.0 97.7 jit_solution(1679997526999774317)
XLA Ops:
  0.6 2.3 %chosen_1.1 = f32[14,128,128]{2,1,0:T(8,128)} custom-call(f32[32,128,128]{2,1,0:T(8,128)} %bitcast.6), custom_call_target="tpu_custom_call" | custom-call | flops 1000000000 | bytes 2000000 | tf_op jit(solution)/shard_map/chosen_1/pallas_call | solution.py:379
  2.9 3.0 %collective-permute-start.4 = (f32[14,128,128]{2,1,0:T(8,128)}, f32[14,128,128]{2,1,0:T(8,128)S(1)}, u32[]{:S(2)}, u32[]{:S(2)}) collective-permute-start(f32[14,128,128]{2,1,0:T(8,128)} %chosen_1.1), channel_id=1, source_target_pairs={{0,1},{1,0},{2,3},{3,2},{4,5},{5,4},{6,7},{7,6},{8,9},{9,8},{10,11... | collective-permute-start | bytes 2752520 | tf_op jit(solution)/shard_map/ppermute | solution.py:39
  6.7 3.5 %collective-permute-start = (f32[256,128]{1,0:T(8,128)S(1)}, f32[256,128]{1,0:T(8,128)S(1)}, u32[]{:S(2)}, u32[]{:S(2)}) collective-permute-start(f32[256,128]{1,0:T(8,128)S(1)} %get-tuple-element.51), channel_id=1, source_target_pairs={{0,8},{8,16},{16,24},{1,9},{9,17},{17,25},{2,10},{10,18},{18,26},{... | collective-permute-start | bytes 393224 | tf_op jit(solution)/shard_map/ppermute | solution.py:39
  11.6 1.7 %collective-permute-start.3 = (f32[256,128]{1,0:T(8,128)S(1)}, f32[256,128]{1,0:T(8,128)S(1)}, u32[]{:S(2)}, u32[]{:S(2)}) collective-permute-start(f32[256,128]{1,0:T(8,128)S(1)} %get-tuple-element.54), channel_id=1, source_target_pairs={{0,6},{2,0},{4,2},{6,4},{1,7},{3,1},{5,3},{7,5},{8,14},{10,8},{12,... | collective-permute-start | bytes 393224 | tf_op jit(solution)/shard_map/ppermute | solution.py:39
  13.3 1.9 %halves.1.halves_in = f32[3,34,144,128]{3,2,1,0:T(8,128)S(1)} custom-call(f32[96,128]{1,0:T(8,128)S(1)} %copy.15.coef), custom_call_target="tpu_custom_call" | custom-call | flops 1000000000 | bytes 2000000 | tf_op jit(solution)/shard_map/halves/pallas_call | solution.py:414
  17.1 2.7 %diagonal.1 = (f32[3,34,144,128]{3,2,1,0:T(8,128)S(1)}, f32[3,32,128,128]{3,2,1,0:T(8,128)S(1)}) custom-call(f32[256,128]{1,0:T(8,128)S(1)} %collective-permute-done.low_x.refs_8_, f32[256,128]{1,0:T(8,128)S(1)} %collective-permute-done.1.high_x.refs_9_, f32[256,128]{1,0:T(8,128)S(1)} %collective-permute-done.2.low_y.refs_6_, ...), custom_call_target="tpu_custom_call", output_to_operand_aliasing={{0}: (4, {})} | custom-call | flops 1000000000 | bytes 2000000 | tf_op jit(solution)/shard_map/diagonal/pallas_call | solution.py:415
  21.3 2.9 %own_1.1.refs_1_.refs_4_.refs_0_ = f32[12,128,128]{2,1,0:T(8,128)S(1)} custom-call(f32[3,34,144,128]{3,2,1,0:T(8,128)S(1)} %get-tuple-element.55.refs_0_, f32[3,32,128,128]{3,2,1,0:T(8,128)S(1)} %get-tuple-element.56.refs_1_, bf16[384,256]{1,0:T(8,128)(2,1)S(1)} %get-tuple-element.57.refs_2_.refs_0_, bf16[384,256]{1,0:T(8,128)(2,1)S(1)} %get-tuple-element.58.refs_3_, ...), custom_call_target="tpu_custom_call" | custom-call | flops 1200000000 | bytes 2400000 | tf_op jit(solution)/shard_map/own_1/pallas_call | solution.py:296
  25.1 2.2 %collective-permute-done.4.refs_0_.refs_5_ = f32[14,128,128]{2,1,0:T(8,128)S(1)} collective-permute-done((f32[14,128,128]{2,1,0:T(8,128)}, f32[14,128,128]{2,1,0:T(8,128)S(1)}, u32[]{:S(2)}, u32[]{:S(2)}) %collective-permute-start.4) | collective-permute-done | bytes 917536 | tf_op jit(solution)/shard_map/ppermute | solution.py:39
  27.4 1.7 %collective-permute-start.6 = (f32[14,4,128]{2,1,0:T(4,128)S(1)}, f32[14,4,128]{2,1,0:T(4,128)S(1)}, u32[]{:S(2)}, u32[]{:S(2)}) collective-permute-start(f32[14,4,128]{2,1,0:T(4,128)S(1)} %get-tuple-element.62.refs_10_), channel_id=1, source_target_pairs={{0,6},{2,0},{4,2},{6,4},{1,7},{3,1},{5,3},{7,5},{8,14},{10,8},{12,... | collective-permute-start | bytes 86024 | tf_op jit(solution)/shard_map/ppermute | solution.py:39
  29.2 2.9 %own_2.1.refs_8_.refs_4_ = f32[12,128,128]{2,1,0:T(8,128)S(1)} custom-call(f32[3,34,144,128]{3,2,1,0:T(8,128)S(1)} %get-tuple-element.55.refs_0_, f32[3,32,128,128]{3,2,1,0:T(8,128)S(1)} %get-tuple-element.56.refs_1_, bf16[384,256]{1,0:T(8,128)(2,1)S(1)} %get-tuple-element.57.refs_2_.refs_0_, bf16[384,256]{1,0:T(8,128)(2,1)S(1)} %get-tuple-element.58.refs_3_, ...), custom_call_target="tpu_custom_call" | custom-call | flops 1200000000 | bytes 2400000 | tf_op jit(solution)/shard_map/own_2/pallas_call | solution.py:296
  32.1 2.8 %middle_1.1 = (f32[12,128,128]{2,1,0:T(8,128)S(1)}, f32[12,4,128]{2,1,0:T(4,128)S(1)}, f32[12,4,128]{2,1,0:T(4,128)S(1)}) custom-call(f32[3,34,144,128]{3,2,1,0:T(8,128)S(1)} %get-tuple-element.55.refs_0_, f32[3,32,128,128]{3,2,1,0:T(8,128)S(1)} %get-tuple-element.56.refs_1_, bf16[384,128]{1,0:T(8,128)(2,1)S(1)} %get-tuple-element.59.refs_2_, ...), custom_call_target="tpu_custom_call" | custom-call | flops 1200000000 | bytes 2400000 | tf_op jit(solution)/shard_map/middle_1/pallas_call | solution.py:296
  36.7 2.1 %own_3.1.refs_8_.refs_4_ = f32[8,128,128]{2,1,0:T(8,128)S(1)} custom-call(f32[3,34,144,128]{3,2,1,0:T(8,128)S(1)} %get-tuple-element.55.refs_0_, f32[3,32,128,128]{3,2,1,0:T(8,128)S(1)} %get-tuple-element.56.refs_1_, bf16[384,256]{1,0:T(8,128)(2,1)S(1)} %get-tuple-element.57.refs_2_.refs_0_, bf16[384,256]{1,0:T(8,128)(2,1)S(1)} %get-tuple-element.58.refs_3_, ...), custom_call_target="tpu_custom_call" | custom-call | flops 800000000 | bytes 1600000 | tf_op jit(solution)/shard_map/own_3/pallas_call | solution.py:296
  38.9 2.7 %second_1.1 = (f32[10,128,128]{2,1,0:T(8,128)S(1)}, f32[10,128,128]{2,1,0:T(8,128)S(1)}, f32[10,128,128]{2,1,0:T(8,128)S(1)}) custom-call(f32[3,34,144,128]{3,2,1,0:T(8,128)S(1)} %get-tuple-element.55.refs_0_, f32[3,32,128,128]{3,2,1,0:T(8,128)S(1)} %get-tuple-element.56.refs_1_, bf16[384,256]{1,0:T(8,128)(2,1)S(1)} %get-tuple-element.57.refs_2_.refs_0_, ...), custom_call_target="tpu_custom_call" | custom-call | flops 1000000000 | bytes 2000000 | tf_op jit(solution)/shard_map/second_1/pallas_call | solution.py:296
  41.6 2.1 %collective-permute-start.21 = (f32[10,128,128]{2,1,0:T(8,128)S(1)}, f32[10,128,128]{2,1,0:T(8,128)S(1)}, u32[]{:S(2)}, u32[]{:S(2)}) collective-permute-start(f32[10,128,128]{2,1,0:T(8,128)S(1)} %get-tuple-element.66.refs_1_), channel_id=1, source_target_pairs={{0,1},{1,0},{2,3},{3,2},{4,5},{5,4},{6,7},{7,6},{8,9},{9,8},{10,11... | collective-permute-start | bytes 1966088 | tf_op jit(solution)/shard_map/ppermute | solution.py:39
  46.0 4.0 %collective-permute-start.13 = (f32[128,128]{1,0:T(8,128)S(1)}, f32[128,128]{1,0:T(8,128)S(1)}, u32[]{:S(2)}, u32[]{:S(2)}) collective-permute-start(f32[128,128]{1,0:T(8,128)S(1)} %get-tuple-element.70), channel_id=1, source_target_pairs={{0,8},{8,16},{16,24},{1,9},{9,17},{17,25},{2,10},{10,18},{18,26},{... | collective-permute-start | bytes 196616 | tf_op jit(solution)/shard_map/ppermute | solution.py:39
  50.0 2.9 %middle_2.1 = (f32[12,128,128]{2,1,0:T(8,128)S(1)}, f32[12,4,128]{2,1,0:T(4,128)S(1)}, f32[12,4,128]{2,1,0:T(4,128)S(1)}) custom-call(f32[3,34,144,128]{3,2,1,0:T(8,128)S(1)} %get-tuple-element.55.refs_0_, f32[3,32,128,128]{3,2,1,0:T(8,128)S(1)} %get-tuple-element.56.refs_1_, bf16[384,128]{1,0:T(8,128)(2,1)S(1)} %get-tuple-element.59.refs_2_, ...), custom_call_target="tpu_custom_call" | custom-call | flops 1200000000 | bytes 2400000 | tf_op jit(solution)/shard_map/middle_2/pallas_call | solution.py:296
  53.0 1.7 %collective-permute-start.18 = (f32[12,4,128]{2,1,0:T(4,128)S(1)}, f32[12,4,128]{2,1,0:T(4,128)S(1)}, u32[]{:S(2)}, u32[]{:S(2)}) collective-permute-start(f32[12,4,128]{2,1,0:T(4,128)S(1)} %get-tuple-element.71.refs_1_), channel_id=1, source_target_pairs={{0,6},{2,0},{4,2},{6,4},{1,7},{3,1},{5,3},{7,5},{8,14},{10,8},{12,... | collective-permute-start | bytes 73736 | tf_op jit(solution)/shard_map/ppermute | solution.py:39
  57.9 3.2 %second_2.1 = (f32[12,128,128]{2,1,0:T(8,128)S(1)}, f32[12,128,128]{2,1,0:T(8,128)S(1)}, f32[12,128,128]{2,1,0:T(8,128)S(1)}) custom-call(f32[3,34,144,128]{3,2,1,0:T(8,128)S(1)} %get-tuple-element.55.refs_0_, f32[3,32,128,128]{3,2,1,0:T(8,128)S(1)} %get-tuple-element.56.refs_1_, bf16[384,256]{1,0:T(8,128)(2,1)S(1)} %get-tuple-element.57.refs_2_.refs_0_, ...), custom_call_target="tpu_custom_call" | custom-call | flops 4000000000 | bytes 8000000 | tf_op jit(solution)/shard_map/second_2/pallas_call | solution.py:296
  61.1 1.6 %collective-permute-start.26 = (f32[12,128,128]{2,1,0:T(8,128)S(1)}, f32[12,128,128]{2,1,0:T(8,128)S(1)}, u32[]{:S(2)}, u32[]{:S(2)}) collective-permute-start(f32[12,128,128]{2,1,0:T(8,128)S(1)} %get-tuple-element.76.refs_16_), channel_id=1, source_target_pairs={{0,1},{1,0},{2,3},{3,2},{4,5},{5,4},{6,7},{7,6},{8,9},{9,8},{10,11... | collective-permute-start | bytes 2359304 | tf_op jit(solution)/shard_map/ppermute | solution.py:39
  62.7 2.2 %middle_3.1 = (f32[8,128,128]{2,1,0:T(8,128)S(1)}, f32[8,4,128]{2,1,0:T(4,128)S(1)}, f32[8,4,128]{2,1,0:T(4,128)S(1)}, f32[128,128]{1,0:T(8,128)S(1)}, f32[128,128]{1,0:T(8,128)S(1)}) custom-call(f32[3,34,144,128]{3,2,1,0:T(8,128)S(1)} %get-tuple-element.55.refs_0_, f32[3,32,128,128]{3,2,1,0:T(8,128)S(1)} %get-tuple-element.56.refs_1_, ...), custom_call_target="tpu_custom_call" | custom-call | flops 800000000 | bytes 1600000 | tf_op jit(solution)/shard_map/middle_3/pallas_call | solution.py:296
  65.0 4.5 %collective-permute-start.19 = (f32[128,128]{1,0:T(8,128)S(1)}, f32[128,128]{1,0:T(8,128)S(1)}, u32[]{:S(2)}, u32[]{:S(2)}) collective-permute-start(f32[128,128]{1,0:T(8,128)S(1)} %get-tuple-element.78), channel_id=1, source_target_pairs={{0,8},{8,16},{16,24},{1,9},{9,17},{17,25},{2,10},{10,18},{18,26},{... | collective-permute-start | bytes 196616 | tf_op jit(solution)/shard_map/ppermute | solution.py:39
  72.6 3.6 %collective-permute-done.20.refs_9_ = f32[128,128]{1,0:T(8,128)S(1)} collective-permute-done((f32[128,128]{1,0:T(8,128)S(1)}, f32[128,128]{1,0:T(8,128)S(1)}, u32[]{:S(2)}, u32[]{:S(2)}) %collective-permute-start.20) | collective-permute-done | bytes 65568 | tf_op jit(solution)/shard_map/ppermute | solution.py:39
  76.3 3.3 %second_3.1 = (f32[10,128,128]{2,1,0:T(8,128)S(1)}, f32[10,128,128]{2,1,0:T(8,128)S(1)}, f32[8,128,128]{2,1,0:T(8,128)S(1)}, f32[2,128,128]{2,1,0:T(8,128)S(1)}) custom-call(f32[3,34,144,128]{3,2,1,0:T(8,128)S(1)} %get-tuple-element.55.refs_0_, f32[3,32,128,128]{3,2,1,0:T(8,128)S(1)} %get-tuple-element.56.refs_1_, ...), custom_call_target="tpu_custom_call" | custom-call | flops 2000000000 | bytes 4000000 | tf_op jit(solution)/shard_map/second_3/pallas_call | solution.py:296
  84.4 10.1 %collective-permute-done.25.came = f32[8,128,128]{2,1,0:T(8,128)S(1)} collective-permute-done((f32[8,128,128]{2,1,0:T(8,128)S(1)}, f32[8,128,128]{2,1,0:T(8,128)S(1)}, u32[]{:S(2)}, u32[]{:S(2)}) %collective-permute-start.25) | collective-permute-done | bytes 524320 | tf_op jit(solution)/shard_map/ppermute | solution.py:39
  (65 shorter events, 24.5 us)
Async XLA Ops:
  2.9 24.4 %collective-permute-start.4 = (f32[14,128,128]{2,1,0:T(8,128)}, f32[14,128,128]{2,1,0:T(8,128)S(1)}, u32[]{:S(2)}, u32[]{:S(2)}) collective-permute-start(f32[14,128,128]{2,1,0:T(8,128)} %chosen_1.1), channel_id=1, source_target_pairs={{0,1},{1,0},{2,3},{3,2},{4,5},{5,4},{6,7},{7,6},{8,9},{9,8},{10,11... | collective-permute-start | bytes 2752520 | tf_op jit(solution)/shard_map/ppermute | solution.py:39
  6.7 9.0 %collective-permute-start = (f32[256,128]{1,0:T(8,128)S(1)}, f32[256,128]{1,0:T(8,128)S(1)}, u32[]{:S(2)}, u32[]{:S(2)}) collective-permute-start(f32[256,128]{1,0:T(8,128)S(1)} %get-tuple-element.51), channel_id=1, source_target_pairs={{0,8},{8,16},{16,24},{1,9},{9,17},{17,25},{2,10},{10,18},{18,26},{... | collective-permute-start | bytes 393224 | tf_op jit(solution)/shard_map/ppermute | solution.py:39
  10.2 6.9 %collective-permute-start.1 = (f32[256,128]{1,0:T(8,128)S(1)}, f32[256,128]{1,0:T(8,128)S(1)}, u32[]{:S(2)}, u32[]{:S(2)}) collective-permute-start(f32[256,128]{1,0:T(8,128)S(1)} %get-tuple-element.52), channel_id=1, source_target_pairs={{8,0},{16,8},{24,16},{9,1},{17,9},{25,17},{10,2},{18,10},{26,18},{... | collective-permute-start | bytes 393224 | tf_op jit(solution)/shard_map/ppermute | solution.py:39
  11.5 5.6 %collective-permute-start.2 = (f32[256,128]{1,0:T(8,128)S(1)}, f32[256,128]{1,0:T(8,128)S(1)}, u32[]{:S(2)}, u32[]{:S(2)}) collective-permute-start(f32[256,128]{1,0:T(8,128)S(1)} %get-tuple-element.53), channel_id=1, source_target_pairs={{0,2},{2,4},{4,6},{6,0},{1,3},{3,5},{5,7},{7,1},{8,10},{10,12},{12... | collective-permute-start | bytes 393224 | tf_op jit(solution)/shard_map/ppermute | solution.py:39
  11.6 5.5 %collective-permute-start.3 = (f32[256,128]{1,0:T(8,128)S(1)}, f32[256,128]{1,0:T(8,128)S(1)}, u32[]{:S(2)}, u32[]{:S(2)}) collective-permute-start(f32[256,128]{1,0:T(8,128)S(1)} %get-tuple-element.54), channel_id=1, source_target_pairs={{0,6},{2,0},{4,2},{6,4},{1,7},{3,1},{5,3},{7,5},{8,14},{10,8},{12,... | collective-permute-start | bytes 393224 | tf_op jit(solution)/shard_map/ppermute | solution.py:39
  19.8 24.4 %collective-permute-start.7 = (f32[12,128,128]{2,1,0:T(8,128)S(1)}, f32[12,128,128]{2,1,0:T(8,128)S(1)}, u32[]{:S(2)}, u32[]{:S(2)}) collective-permute-start(f32[12,128,128]{2,1,0:T(8,128)S(1)} %chosen_2.1), channel_id=1, source_target_pairs={{0,1},{1,0},{2,3},{3,2},{4,5},{5,4},{6,7},{7,6},{8,9},{9,8},{10,11... | collective-permute-start | bytes 2359304 | tf_op jit(solution)/shard_map/ppermute | solution.py:39
  24.4 30.3 %collective-permute-start.12 = (f32[6,128,128]{2,1,0:T(8,128)S(1)}, f32[6,128,128]{2,1,0:T(8,128)S(1)}, u32[]{:S(2)}, u32[]{:S(2)}) collective-permute-start(f32[6,128,128]{2,1,0:T(8,128)S(1)} %chosen_3.1), channel_id=1, source_target_pairs={{0,1},{1,0},{2,3},{3,2},{4,5},{5,4},{6,7},{7,6},{8,9},{9,8},{10,11... | collective-permute-start | bytes 1179656 | tf_op jit(solution)/shard_map/ppermute | solution.py:39
  27.4 4.7 %collective-permute-start.5 = (f32[14,4,128]{2,1,0:T(4,128)S(1)}, f32[14,4,128]{2,1,0:T(4,128)S(1)}, u32[]{:S(2)}, u32[]{:S(2)}) collective-permute-start(f32[14,4,128]{2,1,0:T(4,128)S(1)} %get-tuple-element.61), channel_id=1, source_target_pairs={{0,2},{2,4},{4,6},{6,0},{1,3},{3,5},{5,7},{7,1},{8,10},{10,12},{12... | collective-permute-start | bytes 86024 | tf_op jit(solution)/shard_map/ppermute | solution.py:39
  27.4 4.7 %collective-permute-start.6 = (f32[14,4,128]{2,1,0:T(4,128)S(1)}, f32[14,4,128]{2,1,0:T(4,128)S(1)}, u32[]{:S(2)}, u32[]{:S(2)}) collective-permute-start(f32[14,4,128]{2,1,0:T(4,128)S(1)} %get-tuple-element.62.refs_10_), channel_id=1, source_target_pairs={{0,6},{2,0},{4,2},{6,4},{1,7},{3,1},{5,3},{7,5},{8,14},{10,8},{12,... | collective-permute-start | bytes 86024 | tf_op jit(solution)/shard_map/ppermute | solution.py:39
  34.9 3.9 %collective-permute-start.8 = (f32[12,4,128]{2,1,0:T(4,128)S(1)}, f32[12,4,128]{2,1,0:T(4,128)S(1)}, u32[]{:S(2)}, u32[]{:S(2)}) collective-permute-start(f32[12,4,128]{2,1,0:T(4,128)S(1)} %get-tuple-element.64), channel_id=1, source_target_pairs={{0,2},{2,4},{4,6},{6,0},{1,3},{3,5},{5,7},{7,1},{8,10},{10,12},{12... | collective-permute-start | bytes 73736 | tf_op jit(solution)/shard_map/ppermute | solution.py:39
  41.6 29.2 %collective-permute-start.21 = (f32[10,128,128]{2,1,0:T(8,128)S(1)}, f32[10,128,128]{2,1,0:T(8,128)S(1)}, u32[]{:S(2)}, u32[]{:S(2)}) collective-permute-start(f32[10,128,128]{2,1,0:T(8,128)S(1)} %get-tuple-element.66.refs_1_), channel_id=1, source_target_pairs={{0,1},{1,0},{2,3},{3,2},{4,5},{5,4},{6,7},{7,6},{8,9},{9,8},{10,11... | collective-permute-start | bytes 1966088 | tf_op jit(solution)/shard_map/ppermute | solution.py:39
  44.2 5.8 %collective-permute-start.10 = (f32[12,4,128]{2,1,0:T(4,128)S(1)}, f32[12,4,128]{2,1,0:T(4,128)S(1)}, u32[]{:S(2)}, u32[]{:S(2)}) collective-permute-start(f32[12,4,128]{2,1,0:T(4,128)S(1)} %get-tuple-element.67), channel_id=1, source_target_pairs={{0,2},{2,4},{4,6},{6,0},{1,3},{3,5},{5,7},{7,1},{8,10},{10,12},{12... | collective-permute-start | bytes 73736 | tf_op jit(solution)/shard_map/ppermute | solution.py:39
  44.8 5.3 %collective-permute-start.11 = (f32[12,4,128]{2,1,0:T(4,128)S(1)}, f32[12,4,128]{2,1,0:T(4,128)S(1)}, u32[]{:S(2)}, u32[]{:S(2)}) collective-permute-start(f32[12,4,128]{2,1,0:T(4,128)S(1)} %get-tuple-element.68), channel_id=1, source_target_pairs={{0,6},{2,0},{4,2},{6,4},{1,7},{3,1},{5,3},{7,5},{8,14},{10,8},{12,... | collective-permute-start | bytes 73736 | tf_op jit(solution)/shard_map/ppermute | solution.py:39
  46.0 11.9 %collective-permute-start.13 = (f32[128,128]{1,0:T(8,128)S(1)}, f32[128,128]{1,0:T(8,128)S(1)}, u32[]{:S(2)}, u32[]{:S(2)}) collective-permute-start(f32[128,128]{1,0:T(8,128)S(1)} %get-tuple-element.70), channel_id=1, source_target_pairs={{0,8},{8,16},{16,24},{1,9},{9,17},{17,25},{2,10},{10,18},{18,26},{... | collective-permute-start | bytes 196616 | tf_op jit(solution)/shard_map/ppermute | solution.py:39
  54.8 7.9 %collective-permute-start.15 = (f32[6,4,128]{2,1,0:T(4,128)S(1)}, f32[6,4,128]{2,1,0:T(4,128)S(1)}, u32[]{:S(2)}, u32[]{:S(2)}) collective-permute-start(f32[6,4,128]{2,1,0:T(4,128)S(1)} %get-tuple-element.73), channel_id=1, source_target_pairs={{0,2},{2,4},{4,6},{6,0},{1,3},{3,5},{5,7},{7,1},{8,10},{10,12},{12... | collective-permute-start | bytes 36872 | tf_op jit(solution)/shard_map/ppermute | solution.py:39
  56.3 6.4 %collective-permute-start.16 = (f32[6,4,128]{2,1,0:T(4,128)S(1)}, f32[6,4,128]{2,1,0:T(4,128)S(1)}, u32[]{:S(2)}, u32[]{:S(2)}) collective-permute-start(f32[6,4,128]{2,1,0:T(4,128)S(1)} %get-tuple-element.74.refs_11_), channel_id=1, source_target_pairs={{0,6},{2,0},{4,2},{6,4},{1,7},{3,1},{5,3},{7,5},{8,14},{10,8},{12,... | collective-permute-start | bytes 36872 | tf_op jit(solution)/shard_map/ppermute | solution.py:39
  56.6 6.1 %collective-permute-start.14 = (f32[128,128]{1,0:T(8,128)S(1)}, f32[128,128]{1,0:T(8,128)S(1)}, u32[]{:S(2)}, u32[]{:S(2)}) collective-permute-start(f32[128,128]{1,0:T(8,128)S(1)} %get-tuple-element.72), channel_id=1, source_target_pairs={{8,0},{16,8},{24,16},{9,1},{17,9},{25,17},{10,2},{18,10},{26,18},{... | collective-permute-start | bytes 196616 | tf_op jit(solution)/shard_map/ppermute | solution.py:39
  61.1 21.9 %collective-permute-start.26 = (f32[12,128,128]{2,1,0:T(8,128)S(1)}, f32[12,128,128]{2,1,0:T(8,128)S(1)}, u32[]{:S(2)}, u32[]{:S(2)}) collective-permute-start(f32[12,128,128]{2,1,0:T(8,128)S(1)} %get-tuple-element.76.refs_16_), channel_id=1, source_target_pairs={{0,1},{1,0},{2,3},{3,2},{4,5},{5,4},{6,7},{7,6},{8,9},{9,8},{10,11... | collective-permute-start | bytes 2359304 | tf_op jit(solution)/shard_map/ppermute | solution.py:39
  65.0 7.6 %collective-permute-start.19 = (f32[128,128]{1,0:T(8,128)S(1)}, f32[128,128]{1,0:T(8,128)S(1)}, u32[]{:S(2)}, u32[]{:S(2)}) collective-permute-start(f32[128,128]{1,0:T(8,128)S(1)} %get-tuple-element.78), channel_id=1, source_target_pairs={{0,8},{8,16},{16,24},{1,9},{9,17},{17,25},{2,10},{10,18},{18,26},{... | collective-permute-start | bytes 196616 | tf_op jit(solution)/shard_map/ppermute | solution.py:39
  69.5 6.8 %collective-permute-start.20 = (f32[128,128]{1,0:T(8,128)S(1)}, f32[128,128]{1,0:T(8,128)S(1)}, u32[]{:S(2)}, u32[]{:S(2)}) collective-permute-start(f32[128,128]{1,0:T(8,128)S(1)} %get-tuple-element.79), channel_id=1, source_target_pairs={{8,0},{16,8},{24,16},{9,1},{17,9},{25,17},{10,2},{18,10},{26,18},{... | collective-permute-start | bytes 196616 | tf_op jit(solution)/shard_map/ppermute | solution.py:39
  70.8 5.4 %collective-permute-start.22 = (f32[8,4,128]{2,1,0:T(4,128)S(1)}, f32[8,4,128]{2,1,0:T(4,128)S(1)}, u32[]{:S(2)}, u32[]{:S(2)}) collective-permute-start(f32[8,4,128]{2,1,0:T(4,128)S(1)} %get-tuple-element.82), channel_id=1, source_target_pairs={{0,2},{2,4},{4,6},{6,0},{1,3},{3,5},{5,7},{7,1},{8,10},{10,12},{12... | collective-permute-start | bytes 49160 | tf_op jit(solution)/shard_map/ppermute | solution.py:39
  71.8 4.5 %collective-permute-start.23 = (f32[8,4,128]{2,1,0:T(4,128)S(1)}, f32[8,4,128]{2,1,0:T(4,128)S(1)}, u32[]{:S(2)}, u32[]{:S(2)}) collective-permute-start(f32[8,4,128]{2,1,0:T(4,128)S(1)} %get-tuple-element.83), channel_id=1, source_target_pairs={{0,6},{2,0},{4,2},{6,4},{1,7},{3,1},{5,3},{7,5},{8,14},{10,8},{12,... | collective-permute-start | bytes 49160 | tf_op jit(solution)/shard_map/ppermute | solution.py:39
  79.6 14.9 %collective-permute-start.25 = (f32[8,128,128]{2,1,0:T(8,128)S(1)}, f32[8,128,128]{2,1,0:T(8,128)S(1)}, u32[]{:S(2)}, u32[]{:S(2)}) collective-permute-start(f32[8,128,128]{2,1,0:T(8,128)S(1)} %get-tuple-element.87), channel_id=1, source_target_pairs={{0,1},{1,0},{2,3},{3,2},{4,5},{5,4},{6,7},{7,6},{8,9},{9,8},{10,11... | collective-permute-start | bytes 1572872 | tf_op jit(solution)/shard_map/ppermute | solution.py:39
  80.2 16.6 %collective-permute-start.24 = (f32[2,128,128]{2,1,0:T(8,128)S(1)}, f32[2,128,128]{2,1,0:T(8,128)S(1)}, u32[]{:S(2)}, u32[]{:S(2)}) collective-permute-start(f32[2,128,128]{2,1,0:T(8,128)S(1)} %get-tuple-element.86), channel_id=1, source_target_pairs={{0,1},{1,0},{2,3},{3,2},{4,5},{5,4},{6,7},{7,6},{8,9},{9,8},{10,11... | collective-permute-start | bytes 393224 | tf_op jit(solution)/shard_map/ppermute | solution.py:39
  (7 other events, 26.0 us)

commit v9 on v8

--- a/solution.py
+++ b/solution.py
@@ -65,25 +65,24 @@
     copy.wait()
 
 
-def layers_body(depth, field, coef, first_x, last_x, first_y, last_y, held, sem):
+def layers_body(depth, field, coef, first_x, last_x, first_y, last_y, near, far, sem):
     planes, rows = field.shape[0], field.shape[1]
-    pieces = sem.shape[0]
-    size = planes // pieces
-    copies = []
-    for number in range(pieces):
-        here = pl.ds(number * size, size)
-        copies.append(pltpu.make_async_copy(field.at[here], held.at[here], sem.at[number]))
-        copies[-1].start()
+    copies = [
+        pltpu.make_async_copy(field.at[:, pl.ds(0, pad), :], near, sem.at[0]),
+        pltpu.make_async_copy(field.at[:, pl.ds(rows - pad, pad), :], far, sem.at[1]),
+        pltpu.make_async_copy(field.at[0], first_x.at[pl.ds(0, rows)], sem.at[2]),
+        pltpu.make_async_copy(field.at[planes - 1], last_x.at[pl.ds(0, rows)], sem.at[3]),
+    ]
+    for copy in copies:
+        copy.start()
     for out in (first_x, last_x, first_y, last_y):
         out[rows : rows + coef.shape[0]] = coef[...]
         out[rows + coef.shape[0] :] = jnp.zeros((out.shape[0] - rows - coef.shape[0], lanes), f32)
     for copy in copies:
         copy.wait()
-    first_x[:rows] = held[0]
-    last_x[:rows] = held[planes - 1]
     for plane in range(planes):
-        first_y[plane * depth : (plane + 1) * depth] = held[plane, :depth]
-        last_y[plane * depth : (plane + 1) * depth] = held[plane, rows - depth :]
+        first_y[plane * depth : (plane + 1) * depth] = near[plane, :depth]
+        last_y[plane * depth : (plane + 1) * depth] = far[plane, pad - depth :]
 
 
 def halves_body(coef, halves, square):
@@ -381,20 +380,20 @@
             [((count,) + plane, f32)],
             [pltpu.SemaphoreType.DMA],
             in_specs=[anywhere] * (1 + len(ties)),
-            vmem=vmem_bytes if ties else first_bytes,
             name=name,
         )(start, *ties)
         return sent(out, "ma", 1, True)
 
-    raw_1 = chosen(low, high - low, "chosen_1")
+    raw_1 = sent(lax.slice_in_dim(start, low, high, axis=0), "ma", 1, True)
 
     coef = coefficients.reshape(3 * nx, rows)
     layer = ((rows + lanes, lanes), f32)
     first_x, last_x, first_y, last_y = call(
         functools.partial(layers_body, depth),
         [layer] * 4,
-        [pltpu.VMEM(flat, f32), pltpu.SemaphoreType.DMA((8,))],
+        [pltpu.VMEM((nx, pad, lanes), f32)] * 2 + [pltpu.SemaphoreType.DMA((4,))],
         in_specs=[anywhere, whole],
+        vmem=first_bytes,
         name="layers",
     )(start, coef)
     low_y = sent(last_y, "gy", 1, True)

time: 98 us -> 98 us (level)
  local copies, waits for them, and re-layouts: 1.38 us -> 4.17 us
  starting transfers between devices: 37 us -> 34.6 us
    pallas_call x1, Pallas kernels: 0.28 us -> 2.69 us  [shards(): call(functools.partial(layers_body, depth), [layer] * 4, [pltpu.VMEM((nx,...]
    ppermute x27, starting transfers between devices: 37 us -> 34.6 us  [sent(): return lax.ppermute(array, axis, pairs)]
    pallas_call x3 -> x2, Pallas kernels: 2.52 us -> 0.26 us  [chosen(): call(functools.partial(chosen_body, begin), [((count,) + plane, f32)], [p...]
    slice x0 -> x1, local copies, waits for them, and re-layouts: none -> 1.24 us  [shards(): raw_1 = sent(lax.slice_in_dim(start, low, high, axis=0), 'ma', 1, True)]
  transfers between devices with their start and end apart: 27 -> 27, of which waited for: 8 -> 7; matrix products, arithmetic and copies ran while one was open for 0% -> 2% of each run, Pallas kernels for 35% -> 38%
where the time goes in v9:
time: 98 us; the launch traced here: 97.6 us
  Pallas kernels  37.8 us (39%)
  starting transfers between devices  34.6 us (35%)
  waiting for transfers between devices  19.8 us (20%)
  local copies, waits for them, and re-layouts  4.17 us (4%)
  between operations  1.17 us (1%)
    ppermute x27, starting transfers between devices, sent(): return lax.ppermute(array, axis, pairs)  34.6 us
    pallas_call x9, Pallas kernels, over_planes(): call(functools.partial(planes_body, depth, tuple(names), tuple(outs), pie...  25.2 us
    ppermute x27, waiting for transfers between devices, sent(): return lax.ppermute(array, axis, pairs)  19.8 us
    pallas_call x4, Pallas kernels, add_last(): call(functools.partial(last_body, first, skip), [(shape, f32)] * 2, [pltp...  4.64 us
    pallas_call x1, Pallas kernels, shards(): call(functools.partial(layers_body, depth), [layer] * 4, [pltpu.VMEM((nx,...  2.69 us
    pallas_call x1, Pallas kernels, shards(): call(functools.partial(diagonal_body, depth), [(halves_shape, f32), ((3,)...  2.67 us
    unnamed x9, local copies, waits for them, and re-layouts  2.07 us
  transfers between devices with their start and end apart: 27, of which 7 were waited for; matrix products, arithmetic and copies ran while one was open for 2% of the time, Pallas kernels for 38%

profile of v9, /device:TPU:0, one launch (start us, length us, event | category | flops | bytes accessed | tf_op | source)
XLA Modules:
  0.0 97.6 jit_solution(2226331996945396374)
XLA Ops:
  1.9 3.0 %collective-permute-start.4 = (f32[14,128,128]{2,1,0:T(8,128)S(1)}, f32[14,128,128]{2,1,0:T(8,128)S(1)}, u32[]{:S(2)}, u32[]{:S(2)}) collective-permute-start(f32[14,128,128]{2,1,0:T(8,128)S(1)} %bitcast.21), channel_id=1, source_target_pairs={{0,1},{1,0},{2,3},{3,2},{4,5},{5,4},{6,7},{7,6},{8,9},{9,8},{10,11... | collective-permute-start | bytes 2752520 | tf_op jit(solution)/shard_map/ppermute | solution.py:39
  6.9 2.7 %layers.1 = (f32[256,128]{1,0:T(8,128)}, f32[256,128]{1,0:T(8,128)}, f32[256,128]{1,0:T(8,128)}, f32[256,128]{1,0:T(8,128)}) custom-call(f32[32,128,128]{2,1,0:T(8,128)} %bitcast.7, f32[96,128]{1,0:T(8,128)} %copy.15.coef), custom_call_target="tpu_custom_call" | custom-call | flops 1000000000 | bytes 2000000 | tf_op jit(solution)/shard_map/layers/pallas_call | solution.py:391
  9.6 3.5 %collective-permute-start = (f32[256,128]{1,0:T(8,128)}, f32[256,128]{1,0:T(8,128)S(1)}, u32[]{:S(2)}, u32[]{:S(2)}) collective-permute-start(f32[256,128]{1,0:T(8,128)} %get-tuple-element.51), channel_id=1, source_target_pairs={{0,8},{8,16},{16,24},{1,9},{9,17},{17,25},{2,10},{10,18},{18,26},{... | collective-permute-start | bytes 393224 | tf_op jit(solution)/shard_map/ppermute | solution.py:39
  14.5 1.7 %collective-permute-start.3 = (f32[256,128]{1,0:T(8,128)}, f32[256,128]{1,0:T(8,128)S(1)}, u32[]{:S(2)}, u32[]{:S(2)}) collective-permute-start(f32[256,128]{1,0:T(8,128)} %get-tuple-element.54), channel_id=1, source_target_pairs={{0,6},{2,0},{4,2},{6,4},{1,7},{3,1},{5,3},{7,5},{8,14},{10,8},{12,... | collective-permute-start | bytes 393224 | tf_op jit(solution)/shard_map/ppermute | solution.py:39
  16.2 1.9 %halves.1.halves_in = f32[3,34,144,128]{3,2,1,0:T(8,128)S(1)} custom-call(f32[96,128]{1,0:T(8,128)S(1)} %copy-done.2), custom_call_target="tpu_custom_call" | custom-call | flops 1000000000 | bytes 2000000 | tf_op jit(solution)/shard_map/halves/pallas_call | solution.py:413
  18.6 1.6 %collective-permute-done.1.high_x.refs_9_ = f32[256,128]{1,0:T(8,128)S(1)} collective-permute-done((f32[256,128]{1,0:T(8,128)}, f32[256,128]{1,0:T(8,128)S(1)}, u32[]{:S(2)}, u32[]{:S(2)}) %collective-permute-start.1) | collective-permute-done | bytes 131104 | tf_op jit(solution)/shard_map/ppermute | solution.py:39
  20.2 2.7 %diagonal.1 = (f32[3,34,144,128]{3,2,1,0:T(8,128)S(1)}, f32[3,32,128,128]{3,2,1,0:T(8,128)S(1)}) custom-call(f32[256,128]{1,0:T(8,128)S(1)} %collective-permute-done.low_x.refs_8_, f32[256,128]{1,0:T(8,128)S(1)} %collective-permute-done.1.high_x.refs_9_, f32[256,128]{1,0:T(8,128)S(1)} %collective-permute-done.2.low_y.refs_6_, ...), custom_call_target="tpu_custom_call", output_to_operand_aliasing={{0}: (4, {})} | custom-call | flops 1000000000 | bytes 2000000 | tf_op jit(solution)/shard_map/diagonal/pallas_call | solution.py:414
  24.4 2.9 %own_1.1.refs_1_.refs_4_.refs_0_ = f32[12,128,128]{2,1,0:T(8,128)S(1)} custom-call(f32[3,34,144,128]{3,2,1,0:T(8,128)S(1)} %get-tuple-element.55.refs_0_, f32[3,32,128,128]{3,2,1,0:T(8,128)S(1)} %get-tuple-element.56.refs_1_, bf16[384,256]{1,0:T(8,128)(2,1)S(1)} %get-tuple-element.57.refs_2_.refs_0_, bf16[384,256]{1,0:T(8,128)(2,1)S(1)} %get-tuple-element.58.refs_3_, ...), custom_call_target="tpu_custom_call" | custom-call | flops 1200000000 | bytes 2400000 | tf_op jit(solution)/shard_map/own_1/pallas_call | solution.py:295
  30.0 2.9 %own_2.1.refs_8_.refs_4_ = f32[12,128,128]{2,1,0:T(8,128)S(1)} custom-call(f32[3,34,144,128]{3,2,1,0:T(8,128)S(1)} %get-tuple-element.55.refs_0_, f32[3,32,128,128]{3,2,1,0:T(8,128)S(1)} %get-tuple-element.56.refs_1_, bf16[384,256]{1,0:T(8,128)(2,1)S(1)} %get-tuple-element.57.refs_2_.refs_0_, bf16[384,256]{1,0:T(8,128)(2,1)S(1)} %get-tuple-element.58.refs_3_, ...), custom_call_target="tpu_custom_call" | custom-call | flops 1200000000 | bytes 2400000 | tf_op jit(solution)/shard_map/own_2/pallas_call | solution.py:295
  33.0 2.8 %middle_1.1 = (f32[12,128,128]{2,1,0:T(8,128)S(1)}, f32[12,4,128]{2,1,0:T(4,128)S(1)}, f32[12,4,128]{2,1,0:T(4,128)S(1)}) custom-call(f32[3,34,144,128]{3,2,1,0:T(8,128)S(1)} %get-tuple-element.55.refs_0_, f32[3,32,128,128]{3,2,1,0:T(8,128)S(1)} %get-tuple-element.56.refs_1_, bf16[384,128]{1,0:T(8,128)(2,1)S(1)} %get-tuple-element.59.refs_2_, ...), custom_call_target="tpu_custom_call" | custom-call | flops 1200000000 | bytes 2400000 | tf_op jit(solution)/shard_map/middle_1/pallas_call | solution.py:295
  37.6 2.1 %own_3.1.refs_8_.refs_4_ = f32[8,128,128]{2,1,0:T(8,128)S(1)} custom-call(f32[3,34,144,128]{3,2,1,0:T(8,128)S(1)} %get-tuple-element.55.refs_0_, f32[3,32,128,128]{3,2,1,0:T(8,128)S(1)} %get-tuple-element.56.refs_1_, bf16[384,256]{1,0:T(8,128)(2,1)S(1)} %get-tuple-element.57.refs_2_.refs_0_, bf16[384,256]{1,0:T(8,128)(2,1)S(1)} %get-tuple-element.58.refs_3_, ...), custom_call_target="tpu_custom_call" | custom-call | flops 800000000 | bytes 1600000 | tf_op jit(solution)/shard_map/own_3/pallas_call | solution.py:295
  39.8 2.7 %second_1.1 = (f32[10,128,128]{2,1,0:T(8,128)S(1)}, f32[10,128,128]{2,1,0:T(8,128)S(1)}, f32[10,128,128]{2,1,0:T(8,128)S(1)}) custom-call(f32[3,34,144,128]{3,2,1,0:T(8,128)S(1)} %get-tuple-element.55.refs_0_, f32[3,32,128,128]{3,2,1,0:T(8,128)S(1)} %get-tuple-element.56.refs_1_, bf16[384,256]{1,0:T(8,128)(2,1)S(1)} %get-tuple-element.57.refs_2_.refs_0_, ...), custom_call_target="tpu_custom_call" | custom-call | flops 1000000000 | bytes 2000000 | tf_op jit(solution)/shard_map/second_1/pallas_call | solution.py:295
  42.5 1.5 %collective-permute-start.21 = (f32[10,128,128]{2,1,0:T(8,128)S(1)}, f32[10,128,128]{2,1,0:T(8,128)S(1)}, u32[]{:S(2)}, u32[]{:S(2)}) collective-permute-start(f32[10,128,128]{2,1,0:T(8,128)S(1)} %get-tuple-element.66.refs_1_), channel_id=1, source_target_pairs={{0,1},{1,0},{2,3},{3,2},{4,5},{5,4},{6,7},{7,6},{8,9},{9,8},{10,11... | collective-permute-start | bytes 1966088 | tf_op jit(solution)/shard_map/ppermute | solution.py:39
  45.8 4.2 %collective-permute-start.13 = (f32[128,128]{1,0:T(8,128)S(1)}, f32[128,128]{1,0:T(8,128)S(1)}, u32[]{:S(2)}, u32[]{:S(2)}) collective-permute-start(f32[128,128]{1,0:T(8,128)S(1)} %get-tuple-element.70), channel_id=1, source_target_pairs={{0,8},{8,16},{16,24},{1,9},{9,17},{17,25},{2,10},{10,18},{18,26},{... | collective-permute-start | bytes 196616 | tf_op jit(solution)/shard_map/ppermute | solution.py:39
  50.1 2.9 %middle_2.1 = (f32[12,128,128]{2,1,0:T(8,128)S(1)}, f32[12,4,128]{2,1,0:T(4,128)S(1)}, f32[12,4,128]{2,1,0:T(4,128)S(1)}) custom-call(f32[3,34,144,128]{3,2,1,0:T(8,128)S(1)} %get-tuple-element.55.refs_0_, f32[3,32,128,128]{3,2,1,0:T(8,128)S(1)} %get-tuple-element.56.refs_1_, bf16[384,128]{1,0:T(8,128)(2,1)S(1)} %get-tuple-element.59.refs_2_, ...), custom_call_target="tpu_custom_call" | custom-call | flops 1200000000 | bytes 2400000 | tf_op jit(solution)/shard_map/middle_2/pallas_call | solution.py:295
  53.1 1.7 %collective-permute-start.18 = (f32[12,4,128]{2,1,0:T(4,128)S(1)}, f32[12,4,128]{2,1,0:T(4,128)S(1)}, u32[]{:S(2)}, u32[]{:S(2)}) collective-permute-start(f32[12,4,128]{2,1,0:T(4,128)S(1)} %get-tuple-element.71.refs_1_), channel_id=1, source_target_pairs={{0,6},{2,0},{4,2},{6,4},{1,7},{3,1},{5,3},{7,5},{8,14},{10,8},{12,... | collective-permute-start | bytes 73736 | tf_op jit(solution)/shard_map/ppermute | solution.py:39
  58.0 3.2 %second_2.1 = (f32[12,128,128]{2,1,0:T(8,128)S(1)}, f32[12,128,128]{2,1,0:T(8,128)S(1)}, f32[12,128,128]{2,1,0:T(8,128)S(1)}) custom-call(f32[3,34,144,128]{3,2,1,0:T(8,128)S(1)} %get-tuple-element.55.refs_0_, f32[3,32,128,128]{3,2,1,0:T(8,128)S(1)} %get-tuple-element.56.refs_1_, bf16[384,256]{1,0:T(8,128)(2,1)S(1)} %get-tuple-element.57.refs_2_.refs_0_, ...), custom_call_target="tpu_custom_call" | custom-call | flops 4000000000 | bytes 8000000 | tf_op jit(solution)/shard_map/second_2/pallas_call | solution.py:295
  62.9 2.2 %middle_3.1 = (f32[8,128,128]{2,1,0:T(8,128)S(1)}, f32[8,4,128]{2,1,0:T(4,128)S(1)}, f32[8,4,128]{2,1,0:T(4,128)S(1)}, f32[128,128]{1,0:T(8,128)S(1)}, f32[128,128]{1,0:T(8,128)S(1)}) custom-call(f32[3,34,144,128]{3,2,1,0:T(8,128)S(1)} %get-tuple-element.55.refs_0_, f32[3,32,128,128]{3,2,1,0:T(8,128)S(1)} %get-tuple-element.56.refs_1_, ...), custom_call_target="tpu_custom_call" | custom-call | flops 800000000 | bytes 1600000 | tf_op jit(solution)/shard_map/middle_3/pallas_call | solution.py:295
  65.1 3.5 %collective-permute-start.19 = (f32[128,128]{1,0:T(8,128)S(1)}, f32[128,128]{1,0:T(8,128)S(1)}, u32[]{:S(2)}, u32[]{:S(2)}) collective-permute-start(f32[128,128]{1,0:T(8,128)S(1)} %get-tuple-element.78), channel_id=1, source_target_pairs={{0,8},{8,16},{16,24},{1,9},{9,17},{17,25},{2,10},{10,18},{18,26},{... | collective-permute-start | bytes 196616 | tf_op jit(solution)/shard_map/ppermute | solution.py:39
  71.7 3.6 %collective-permute-done.20.refs_9_ = f32[128,128]{1,0:T(8,128)S(1)} collective-permute-done((f32[128,128]{1,0:T(8,128)S(1)}, f32[128,128]{1,0:T(8,128)S(1)}, u32[]{:S(2)}, u32[]{:S(2)}) %collective-permute-start.20) | collective-permute-done | bytes 65568 | tf_op jit(solution)/shard_map/ppermute | solution.py:39
  75.4 3.3 %second_3.1 = (f32[10,128,128]{2,1,0:T(8,128)S(1)}, f32[10,128,128]{2,1,0:T(8,128)S(1)}, f32[8,128,128]{2,1,0:T(8,128)S(1)}, f32[2,128,128]{2,1,0:T(8,128)S(1)}) custom-call(f32[3,34,144,128]{3,2,1,0:T(8,128)S(1)} %get-tuple-element.55.refs_0_, f32[3,32,128,128]{3,2,1,0:T(8,128)S(1)} %get-tuple-element.56.refs_1_, ...), custom_call_target="tpu_custom_call" | custom-call | flops 2000000000 | bytes 4000000 | tf_op jit(solution)/shard_map/second_3/pallas_call | solution.py:295
  78.7 1.5 %collective-permute-start.25 = (f32[8,128,128]{2,1,0:T(8,128)S(1)}, f32[8,128,128]{2,1,0:T(8,128)S(1)}, u32[]{:S(2)}, u32[]{:S(2)}) collective-permute-start(f32[8,128,128]{2,1,0:T(8,128)S(1)} %get-tuple-element.87), channel_id=1, source_target_pairs={{0,1},{1,0},{2,3},{3,2},{4,5},{5,4},{6,7},{7,6},{8,9},{9,8},{10,11... | collective-permute-start | bytes 1572872 | tf_op jit(solution)/shard_map/ppermute | solution.py:39
  84.2 9.8 %collective-permute-done.25.came = f32[8,128,128]{2,1,0:T(8,128)S(1)} collective-permute-done((f32[8,128,128]{2,1,0:T(8,128)S(1)}, f32[8,128,128]{2,1,0:T(8,128)S(1)}, u32[]{:S(2)}, u32[]{:S(2)}) %collective-permute-start.25) | collective-permute-done | bytes 524320 | tf_op jit(solution)/shard_map/ppermute | solution.py:39
  95.1 1.5 %collective-permute-done.24.came = f32[2,128,128]{2,1,0:T(8,128)S(1)} collective-permute-done((f32[2,128,128]{2,1,0:T(8,128)S(1)}, f32[2,128,128]{2,1,0:T(8,128)S(1)}, u32[]{:S(2)}, u32[]{:S(2)}) %collective-permute-start.24) | collective-permute-done | bytes 131104 | tf_op jit(solution)/shard_map/ppermute | solution.py:39
  (65 shorter events, 26.7 us)
Async XLA Ops:
  1.9 26.3 %collective-permute-start.4 = (f32[14,128,128]{2,1,0:T(8,128)S(1)}, f32[14,128,128]{2,1,0:T(8,128)S(1)}, u32[]{:S(2)}, u32[]{:S(2)}) collective-permute-start(f32[14,128,128]{2,1,0:T(8,128)S(1)} %bitcast.21), channel_id=1, source_target_pairs={{0,1},{1,0},{2,3},{3,2},{4,5},{5,4},{6,7},{7,6},{8,9},{9,8},{10,11... | collective-permute-start | bytes 2752520 | tf_op jit(solution)/shard_map/ppermute | solution.py:39
  9.6 9.0 %collective-permute-start = (f32[256,128]{1,0:T(8,128)}, f32[256,128]{1,0:T(8,128)S(1)}, u32[]{:S(2)}, u32[]{:S(2)}) collective-permute-start(f32[256,128]{1,0:T(8,128)} %get-tuple-element.51), channel_id=1, source_target_pairs={{0,8},{8,16},{16,24},{1,9},{9,17},{17,25},{2,10},{10,18},{18,26},{... | collective-permute-start | bytes 393224 | tf_op jit(solution)/shard_map/ppermute | solution.py:39
  13.1 7.1 %collective-permute-start.1 = (f32[256,128]{1,0:T(8,128)}, f32[256,128]{1,0:T(8,128)S(1)}, u32[]{:S(2)}, u32[]{:S(2)}) collective-permute-start(f32[256,128]{1,0:T(8,128)} %get-tuple-element.52), channel_id=1, source_target_pairs={{8,0},{16,8},{24,16},{9,1},{17,9},{25,17},{10,2},{18,10},{26,18},{... | collective-permute-start | bytes 393224 | tf_op jit(solution)/shard_map/ppermute | solution.py:39
  14.4 5.8 %collective-permute-start.2 = (f32[256,128]{1,0:T(8,128)}, f32[256,128]{1,0:T(8,128)S(1)}, u32[]{:S(2)}, u32[]{:S(2)}) collective-permute-start(f32[256,128]{1,0:T(8,128)} %get-tuple-element.53), channel_id=1, source_target_pairs={{0,2},{2,4},{4,6},{6,0},{1,3},{3,5},{5,7},{7,1},{8,10},{10,12},{12... | collective-permute-start | bytes 393224 | tf_op jit(solution)/shard_map/ppermute | solution.py:39
  14.5 5.7 %collective-permute-start.3 = (f32[256,128]{1,0:T(8,128)}, f32[256,128]{1,0:T(8,128)S(1)}, u32[]{:S(2)}, u32[]{:S(2)}) collective-permute-start(f32[256,128]{1,0:T(8,128)} %get-tuple-element.54), channel_id=1, source_target_pairs={{0,6},{2,0},{4,2},{6,4},{1,7},{3,1},{5,3},{7,5},{8,14},{10,8},{12,... | collective-permute-start | bytes 393224 | tf_op jit(solution)/shard_map/ppermute | solution.py:39
  22.9 21.1 %collective-permute-start.7 = (f32[12,128,128]{2,1,0:T(8,128)S(1)}, f32[12,128,128]{2,1,0:T(8,128)S(1)}, u32[]{:S(2)}, u32[]{:S(2)}) collective-permute-start(f32[12,128,128]{2,1,0:T(8,128)S(1)} %chosen_2.1), channel_id=1, source_target_pairs={{0,1},{1,0},{2,3},{3,2},{4,5},{5,4},{6,7},{7,6},{8,9},{9,8},{10,11... | collective-permute-start | bytes 2359304 | tf_op jit(solution)/shard_map/ppermute | solution.py:39
  27.6 27.3 %collective-permute-start.12 = (f32[6,128,128]{2,1,0:T(8,128)S(1)}, f32[6,128,128]{2,1,0:T(8,128)S(1)}, u32[]{:S(2)}, u32[]{:S(2)}) collective-permute-start(f32[6,128,128]{2,1,0:T(8,128)S(1)} %chosen_3.1), channel_id=1, source_target_pairs={{0,1},{1,0},{2,3},{3,2},{4,5},{5,4},{6,7},{7,6},{8,9},{9,8},{10,11... | collective-permute-start | bytes 1179656 | tf_op jit(solution)/shard_map/ppermute | solution.py:39
  28.2 4.7 %collective-permute-start.5 = (f32[14,4,128]{2,1,0:T(4,128)S(1)}, f32[14,4,128]{2,1,0:T(4,128)S(1)}, u32[]{:S(2)}, u32[]{:S(2)}) collective-permute-start(f32[14,4,128]{2,1,0:T(4,128)S(1)} %get-tuple-element.61), channel_id=1, source_target_pairs={{0,2},{2,4},{4,6},{6,0},{1,3},{3,5},{5,7},{7,1},{8,10},{10,12},{12... | collective-permute-start | bytes 86024 | tf_op jit(solution)/shard_map/ppermute | solution.py:39
  28.7 4.3 %collective-permute-start.6 = (f32[14,4,128]{2,1,0:T(4,128)S(1)}, f32[14,4,128]{2,1,0:T(4,128)S(1)}, u32[]{:S(2)}, u32[]{:S(2)}) collective-permute-start(f32[14,4,128]{2,1,0:T(4,128)S(1)} %get-tuple-element.62.refs_10_), channel_id=1, source_target_pairs={{0,6},{2,0},{4,2},{6,4},{1,7},{3,1},{5,3},{7,5},{8,14},{10,8},{12,... | collective-permute-start | bytes 86024 | tf_op jit(solution)/shard_map/ppermute | solution.py:39
  35.8 3.9 %collective-permute-start.8 = (f32[12,4,128]{2,1,0:T(4,128)S(1)}, f32[12,4,128]{2,1,0:T(4,128)S(1)}, u32[]{:S(2)}, u32[]{:S(2)}) collective-permute-start(f32[12,4,128]{2,1,0:T(4,128)S(1)} %get-tuple-element.64), channel_id=1, source_target_pairs={{0,2},{2,4},{4,6},{6,0},{1,3},{3,5},{5,7},{7,1},{8,10},{10,12},{12... | collective-permute-start | bytes 73736 | tf_op jit(solution)/shard_map/ppermute | solution.py:39
  42.5 27.4 %collective-permute-start.21 = (f32[10,128,128]{2,1,0:T(8,128)S(1)}, f32[10,128,128]{2,1,0:T(8,128)S(1)}, u32[]{:S(2)}, u32[]{:S(2)}) collective-permute-start(f32[10,128,128]{2,1,0:T(8,128)S(1)} %get-tuple-element.66.refs_1_), channel_id=1, source_target_pairs={{0,1},{1,0},{2,3},{3,2},{4,5},{5,4},{6,7},{7,6},{8,9},{9,8},{10,11... | collective-permute-start | bytes 1966088 | tf_op jit(solution)/shard_map/ppermute | solution.py:39
  44.0 6.1 %collective-permute-start.10 = (f32[12,4,128]{2,1,0:T(4,128)S(1)}, f32[12,4,128]{2,1,0:T(4,128)S(1)}, u32[]{:S(2)}, u32[]{:S(2)}) collective-permute-start(f32[12,4,128]{2,1,0:T(4,128)S(1)} %get-tuple-element.67), channel_id=1, source_target_pairs={{0,2},{2,4},{4,6},{6,0},{1,3},{3,5},{5,7},{7,1},{8,10},{10,12},{12... | collective-permute-start | bytes 73736 | tf_op jit(solution)/shard_map/ppermute | solution.py:39
  45.1 5.0 %collective-permute-start.11 = (f32[12,4,128]{2,1,0:T(4,128)S(1)}, f32[12,4,128]{2,1,0:T(4,128)S(1)}, u32[]{:S(2)}, u32[]{:S(2)}) collective-permute-start(f32[12,4,128]{2,1,0:T(4,128)S(1)} %get-tuple-element.68), channel_id=1, source_target_pairs={{0,6},{2,0},{4,2},{6,4},{1,7},{3,1},{5,3},{7,5},{8,14},{10,8},{12,... | collective-permute-start | bytes 73736 | tf_op jit(solution)/shard_map/ppermute | solution.py:39
  45.8 12.1 %collective-permute-start.13 = (f32[128,128]{1,0:T(8,128)S(1)}, f32[128,128]{1,0:T(8,128)S(1)}, u32[]{:S(2)}, u32[]{:S(2)}) collective-permute-start(f32[128,128]{1,0:T(8,128)S(1)} %get-tuple-element.70), channel_id=1, source_target_pairs={{0,8},{8,16},{16,24},{1,9},{9,17},{17,25},{2,10},{10,18},{18,26},{... | collective-permute-start | bytes 196616 | tf_op jit(solution)/shard_map/ppermute | solution.py:39
  54.8 6.9 %collective-permute-start.15 = (f32[6,4,128]{2,1,0:T(4,128)S(1)}, f32[6,4,128]{2,1,0:T(4,128)S(1)}, u32[]{:S(2)}, u32[]{:S(2)}) collective-permute-start(f32[6,4,128]{2,1,0:T(4,128)S(1)} %get-tuple-element.73), channel_id=1, source_target_pairs={{0,2},{2,4},{4,6},{6,0},{1,3},{3,5},{5,7},{7,1},{8,10},{10,12},{12... | collective-permute-start | bytes 36872 | tf_op jit(solution)/shard_map/ppermute | solution.py:39
  56.3 5.4 %collective-permute-start.16 = (f32[6,4,128]{2,1,0:T(4,128)S(1)}, f32[6,4,128]{2,1,0:T(4,128)S(1)}, u32[]{:S(2)}, u32[]{:S(2)}) collective-permute-start(f32[6,4,128]{2,1,0:T(4,128)S(1)} %get-tuple-element.74.refs_11_), channel_id=1, source_target_pairs={{0,6},{2,0},{4,2},{6,4},{1,7},{3,1},{5,3},{7,5},{8,14},{10,8},{12,... | collective-permute-start | bytes 36872 | tf_op jit(solution)/shard_map/ppermute | solution.py:39
  56.7 6.2 %collective-permute-start.14 = (f32[128,128]{1,0:T(8,128)S(1)}, f32[128,128]{1,0:T(8,128)S(1)}, u32[]{:S(2)}, u32[]{:S(2)}) collective-permute-start(f32[128,128]{1,0:T(8,128)S(1)} %get-tuple-element.72), channel_id=1, source_target_pairs={{8,0},{16,8},{24,16},{9,1},{17,9},{25,17},{10,2},{18,10},{26,18},{... | collective-permute-start | bytes 196616 | tf_op jit(solution)/shard_map/ppermute | solution.py:39
  61.1 21.6 %collective-permute-start.26 = (f32[12,128,128]{2,1,0:T(8,128)S(1)}, f32[12,128,128]{2,1,0:T(8,128)S(1)}, u32[]{:S(2)}, u32[]{:S(2)}) collective-permute-start(f32[12,128,128]{2,1,0:T(8,128)S(1)} %get-tuple-element.76.refs_16_), channel_id=1, source_target_pairs={{0,1},{1,0},{2,3},{3,2},{4,5},{5,4},{6,7},{7,6},{8,9},{9,8},{10,11... | collective-permute-start | bytes 2359304 | tf_op jit(solution)/shard_map/ppermute | solution.py:39
  65.1 6.6 %collective-permute-start.19 = (f32[128,128]{1,0:T(8,128)S(1)}, f32[128,128]{1,0:T(8,128)S(1)}, u32[]{:S(2)}, u32[]{:S(2)}) collective-permute-start(f32[128,128]{1,0:T(8,128)S(1)} %get-tuple-element.78), channel_id=1, source_target_pairs={{0,8},{8,16},{16,24},{1,9},{9,17},{17,25},{2,10},{10,18},{18,26},{... | collective-permute-start | bytes 196616 | tf_op jit(solution)/shard_map/ppermute | solution.py:39
  68.6 6.8 %collective-permute-start.20 = (f32[128,128]{1,0:T(8,128)S(1)}, f32[128,128]{1,0:T(8,128)S(1)}, u32[]{:S(2)}, u32[]{:S(2)}) collective-permute-start(f32[128,128]{1,0:T(8,128)S(1)} %get-tuple-element.79), channel_id=1, source_target_pairs={{8,0},{16,8},{24,16},{9,1},{17,9},{25,17},{10,2},{18,10},{26,18},{... | collective-permute-start | bytes 196616 | tf_op jit(solution)/shard_map/ppermute | solution.py:39
  69.9 5.4 %collective-permute-start.22 = (f32[8,4,128]{2,1,0:T(4,128)S(1)}, f32[8,4,128]{2,1,0:T(4,128)S(1)}, u32[]{:S(2)}, u32[]{:S(2)}) collective-permute-start(f32[8,4,128]{2,1,0:T(4,128)S(1)} %get-tuple-element.82), channel_id=1, source_target_pairs={{0,2},{2,4},{4,6},{6,0},{1,3},{3,5},{5,7},{7,1},{8,10},{10,12},{12... | collective-permute-start | bytes 49160 | tf_op jit(solution)/shard_map/ppermute | solution.py:39
  70.8 4.5 %collective-permute-start.23 = (f32[8,4,128]{2,1,0:T(4,128)S(1)}, f32[8,4,128]{2,1,0:T(4,128)S(1)}, u32[]{:S(2)}, u32[]{:S(2)}) collective-permute-start(f32[8,4,128]{2,1,0:T(4,128)S(1)} %get-tuple-element.83), channel_id=1, source_target_pairs={{0,6},{2,0},{4,2},{6,4},{1,7},{3,1},{5,3},{7,5},{8,14},{10,8},{12,... | collective-permute-start | bytes 49160 | tf_op jit(solution)/shard_map/ppermute | solution.py:39
  78.7 15.3 %collective-permute-start.25 = (f32[8,128,128]{2,1,0:T(8,128)S(1)}, f32[8,128,128]{2,1,0:T(8,128)S(1)}, u32[]{:S(2)}, u32[]{:S(2)}) collective-permute-start(f32[8,128,128]{2,1,0:T(8,128)S(1)} %get-tuple-element.87), channel_id=1, source_target_pairs={{0,1},{1,0},{2,3},{3,2},{4,5},{5,4},{6,7},{7,6},{8,9},{9,8},{10,11... | collective-permute-start | bytes 1572872 | tf_op jit(solution)/shard_map/ppermute | solution.py:39
  80.2 16.4 %collective-permute-start.24 = (f32[2,128,128]{2,1,0:T(8,128)S(1)}, f32[2,128,128]{2,1,0:T(8,128)S(1)}, u32[]{:S(2)}, u32[]{:S(2)}) collective-permute-start(f32[2,128,128]{2,1,0:T(8,128)S(1)} %get-tuple-element.86), channel_id=1, source_target_pairs={{0,1},{1,0},{2,3},{3,2},{4,5},{5,4},{6,7},{7,6},{8,9},{9,8},{10,11... | collective-permute-start | bytes 393224 | tf_op jit(solution)/shard_map/ppermute | solution.py:39
  (7 other events, 29.1 us)
